TPU v7x, 32 devices: a whole 2x2x4 slice. The times are simulated.
32 devices in a mesh: groups: 2 (over y), pts: 16 (over z, x, core).
Axes of the slice: x: 2, y: 2, z: 4, core: 2. Of those that a mesh axis runs over, the one named last changes fastest.
Arguments:
- latents: bfloat16 [2048, 768], P(('groups', 'pts')), parts along dimension 0, may hold values from -160 to 160
- points: bfloat16 [12288, 768], P(('groups', 'pts')), parts along dimension 0, may hold values from -6 to 6
- counts: int32 [32], P(('groups', 'pts')), parts along dimension 0, may hold values from 48 to 384, as said below
- w_query: bfloat16 [768, 768], replicated, may hold values from -0.21875 to 0.21875
- w_key: bfloat16 [768, 768], replicated, may hold values from -0.21875 to 0.21875
- w_value: bfloat16 [768, 768], replicated, may hold values from -0.21875 to 0.21875
- w_out: bfloat16 [768, 768], replicated, may hold values from -0.21875 to 0.21875
- d_out: bfloat16 [2048, 768], P(('groups', 'pts')), parts along dimension 0, may hold values from -6 to 6
Outputs:
- result: bfloat16 [2048, 768], P(('groups', 'pts')), parts along dimension 0
- d_latents: bfloat16 [2048, 768], P(('groups', 'pts')), parts along dimension 0
- d_points: bfloat16 [12288, 768], P(('groups', 'pts')), parts along dimension 0
There are 2 independent parts, one for each index of `groups`. A program takes and returns all parts, laid end to end along the dimension named above; an argument that names none is the same for every part. Nothing has to cross between parts.
Inputs may be any that keep to these rules, and one draw needn't show every extreme that they name: counts[s] live points fill the first slots of block s; in every part one block is full with 384 and another holds only 48.
All inputs are finite; a program needn't handle non-finite values.
Results may differ from a plain program's by a relative error of at most 0.018.
The roundings to bfloat16 on the way count: a program that leaves them out, or rounds other values in their place, can miss the bound.
Values may be sent and summed in bfloat16 or wider, within the bound.
No kernel may reach another device: no remote copies, remote signals or barrier semaphores. Data moves between devices by JAX's collectives and lax.ppermute only.
A program may use at most 128 MiB of HBM per device.

v0:
```python
import jax
import jax.numpy as jnp
from jax import lax
from jax.sharding import PartitionSpec as P

HEADS = 12


def masked_scores(query_head, key_head, live_mask):
    raw = jnp.dot(query_head, key_head.T, preferred_element_type=jnp.float32) * 0.125
    return jnp.where(live_mask[None, :], raw, -jnp.inf)


def body(latents, points, counts, w_query, w_key, w_value, w_out, d_out):
    own_rows, width = latents.shape
    slots = points.shape[0]
    head_dim = width // HEADS
    key_rows = jnp.dot(points, w_key, preferred_element_type=jnp.float32).astype(jnp.bfloat16)
    value_rows = jnp.dot(points, w_value, preferred_element_type=jnp.float32).astype(jnp.bfloat16)
    live_mask = jnp.arange(slots, dtype=jnp.int32) < counts[0]
    query_own = jnp.dot(latents, w_query, preferred_element_type=jnp.float32).astype(jnp.bfloat16)
    query_all = lax.all_gather(query_own, "pts", axis=0, tiled=True)
    query_count = query_all.shape[0]

    def split_heads(matrix):
        return matrix.reshape(matrix.shape[0], HEADS, head_dim).transpose(1, 0, 2)

    def join_heads(stack):
        return stack.transpose(1, 0, 2).reshape(stack.shape[1], width)

    query_heads = split_heads(query_all)
    key_heads = split_heads(key_rows)
    value_heads = split_heads(value_rows)

    def local_max(operands):
        query_head, key_head = operands
        return jnp.max(masked_scores(query_head, key_head, live_mask), axis=1)

    row_max = lax.pmax(lax.map(local_max, (query_heads, key_heads)), "pts")

    def partial_attend(operands):
        query_head, key_head, value_head, max_head = operands
        weights = jnp.exp(masked_scores(query_head, key_head, live_mask) - max_head[:, None])
        numerator = jnp.dot(
            weights.astype(jnp.bfloat16), value_head, preferred_element_type=jnp.float32
        )
        return (jnp.sum(weights, axis=1), numerator)

    totals, numerators = lax.map(partial_attend, (query_heads, key_heads, value_heads, row_max))
    numerator = join_heads(numerators)
    total_cols = totals.T
    start = lax.axis_index("pts") * own_rows
    grad_attended = jnp.dot(d_out, w_out.T, preferred_element_type=jnp.float32).astype(jnp.bfloat16)
    numer_all, total_all = lax.psum((numerator, total_cols), "pts")
    attended_all = (numer_all / jnp.repeat(total_all, head_dim, axis=1)).astype(jnp.bfloat16)
    attended = lax.dynamic_slice_in_dim(attended_all, start, own_rows, 0)
    result = (
        latents.astype(jnp.float32) + jnp.dot(attended, w_out, preferred_element_type=jnp.float32)
    ).astype(jnp.bfloat16)
    grad_all = lax.all_gather(grad_attended, "pts", axis=0, tiled=True)
    delta_all = jnp.sum(
        (grad_all.astype(jnp.float32) * attended_all.astype(jnp.float32)).reshape(
            query_count, HEADS, head_dim
        ),
        axis=2,
    )
    lse_all = row_max.T + jnp.log(total_all)

    def backward_head(operands):
        query_head, key_head, value_head, grad_head, lse_head, delta_head = operands
        probability = jnp.exp(masked_scores(query_head, key_head, live_mask) - lse_head[:, None])
        grad_value = jnp.dot(
            probability.astype(jnp.bfloat16).T, grad_head, preferred_element_type=jnp.float32
        )
        grad_weights = jnp.dot(grad_head, value_head.T, preferred_element_type=jnp.float32)
        grad_scores = (probability * (grad_weights - delta_head[:, None])).astype(jnp.bfloat16)
        grad_query = jnp.dot(grad_scores, key_head, preferred_element_type=jnp.float32) * 0.125
        grad_key = jnp.dot(grad_scores.T, query_head, preferred_element_type=jnp.float32) * 0.125
        return (grad_query, grad_key, grad_value)

    grad_query, grad_key, grad_value = lax.map(
        backward_head,
        (query_heads, key_heads, value_heads, split_heads(grad_all), lse_all.T, delta_all.T),
    )
    grad_query_own = lax.psum_scatter(
        join_heads(grad_query), "pts", scatter_dimension=0, tiled=True
    )
    d_latents = (
        d_out.astype(jnp.float32)
        + jnp.dot(
            grad_query_own.astype(jnp.bfloat16), w_query.T, preferred_element_type=jnp.float32
        )
    ).astype(jnp.bfloat16)
    d_points = (
        jnp.dot(
            join_heads(grad_key).astype(jnp.bfloat16), w_key.T, preferred_element_type=jnp.float32
        )
        + jnp.dot(
            join_heads(grad_value).astype(jnp.bfloat16),
            w_value.T,
            preferred_element_type=jnp.float32,
        )
    ).astype(jnp.bfloat16)
    return (result, d_latents, d_points)


def solution(mesh):
    in_specs = (
        P(("groups", "pts"), None),
        P(("groups", "pts"), None),
        P(("groups", "pts")),
        P(),
        P(),
        P(),
        P(),
        P(("groups", "pts"), None),
    )
    out_specs = (P(("groups", "pts"), None), P(("groups", "pts"), None), P(("groups", "pts"), None))
    return jax.shard_map(body, mesh=mesh, in_specs=in_specs, out_specs=out_specs, check_vma=False)
```

profile of v0, /device:TPU:0, one launch (start us, length us, event | category | flops | bytes accessed | tf_op | source)
XLA Modules:
  0.0 493.8 jit_solution(4530850203376139020)
XLA Ops:
  7.3 2.4 convolution_convert_fusion.3
  9.8 2.0 convolution_convert_fusion.2
  17.7 35.6 %all-gather.3.cloned.1.call-done = bf16[1024,768]{1,0:T(8,128)(2,1)} async-done(((bf16[64,768]{1,0:T(8,128)(2,1)}), bf16[1024,768]{1,0:T(8,128)(2,1)}) %all-gather.3.cloned.1.call-update) | async-done | bytes 1572880 | tf_op jit(solution)/shard_map/all_gather | solution.py:22
  55.0 2.7 copy.38
  57.8 25.9 %while.39 = (s32[]{:T(128)}, f32[12,1024]{1,0:T(8,128)S(1)}, bf16[12,1024,64]{2,1,0:T(8,128)(2,1)}, bf16[12,384,64]{2,1,0:T(8,128)(2,1)}, s32[]{:T(128)}, /*index=5*/s32[]{:T(128)}, s32[]{:T(128)}) while((s32[]{:T(128)}, f32[12,1024]{1,0:T(8,128)S(1)}, bf16[12,1024,64]{2,1,0:T(8,128)(2,1)}, bf16[12,384,64]{2,1,0:T(8,128)(2,1)}, ...), condition=%wide.region_2.3_spmd.clone, body=%wide.region_0.2_spmd.clone.sunk | while | flops 51510656 | bytes 374621 | solution.py:39
  83.6 59.7 %pmax.7 = f32[12,1024]{1,0:T(8,128)S(1)} all-reduce(f32[12,1024]{1,0:T(8,128)S(1)} %get-tuple-element.132), channel_id=1, replica_groups=mesh['groups'=2,'pts'=16] {'pts'}, use_global_device_ids=true, to_apply=%region_3.4 | all-reduce | flops 12288 | bytes 98304 | tf_op jit(solution)/shard_map/pmax | solution.py:39
  143.3 2.1 broadcast.28.clone
  145.4 50.3 %while.40 = (s32[]{:T(128)}, f32[12,1024]{1,0:T(8,128)S(1)}, f32[12,1024,64]{1,2,0:T(8,128)}, bf16[12,1024,64]{2,1,0:T(8,128)(2,1)}, bf16[12,384,64]{2,1,0:T(8,1...) while((s32[]{:T(128)}, f32[12,1024]{1,0:T(8,128)S(1)}, ...), condition=%wide.region_6.7_spmd.clone, body=%wide.region_4.6_spmd.clone.sunk | while | flops 102628736 | bytes 2321273 | solution.py:49
  195.7 3.6 copy.41
  199.4 58.6 %psum.15 = f32[1024,12]{0,1:T(8,128)S(1)} all-reduce(f32[1024,12]{0,1:T(8,128)S(1)} %bitcast.173), channel_id=1, replica_groups=mesh['groups'=2,'pts'=16] {'pts'}, use_global_device_ids=true, to_apply=%region_8.9 | all-reduce | flops 12288 | bytes 98304 | tf_op jit(solution)/shard_map/psum | solution.py:54
  258.0 2.0 broadcast_in_dim.58
  260.0 3.5 copy.42
  263.6 2.7 copy.43
  266.3 34.2 %all-reduce.2.cloned.1.call-done = f32[1024,768]{1,0:T(8,128)} async-done(((f32[1024,768]{1,0:T(8,128)}), f32[1024,768]{1,0:T(8,128)}) %all-reduce.2.cloned.1.call-update) | async-done | bytes 3145744 | tf_op jit(solution)/shard_map/psum | solution.py:54
  300.5 5.6 %convert_multiply_fusion = (f32[1024,768]{1,0:T(8,128)}, bf16[1024,768]{1,0:T(8,128)(2,1)}) fusion(bf16[1024,768]{1,0:T(8,128)(2,1)S(1)} %copy-done.1, f32[1024,768]{1,0:T(8,128)} %all-reduce.2.cloned.1.call-done, f32[1024,768]{1,0:T(8,128)} %copy.42), kind=kLoop, calls=%fused_computation.57 | loop fusion | flops 3932160 | bytes 12582912 | tf_op jit(solution)/shard_map/mul | solution.py:62
  306.1 3.6 copy.44
  309.7 2.3 reduce_sum.18
  311.9 2.1 broadcast.28
  314.0 102.0 %while.41 = (s32[]{:T(128)}, f32[12,1024,64]{1,2,0:T(8,128)}, bf16[12,384,64]{1,2,0:T(8,128)(2,1)}, bf16[12,384,64]{1,2,0:T(8,128)(2,1)S(1)}, bf16[12,1024,64]{2...) while((s32[]{:T(128)}, f32[12,1024,64]{1,2,0:T(8,128)}, ...), condition=%wide.region_11.12_spmd.clone, body=%wide.region_10.11_spmd.clone.sunk | while | flops 254501248 | bytes 8648581 | solution.py:81
  360.0 2.0 fusion.108
  368.5 2.0 fusion.108
  385.5 2.0 fusion.108
  416.0 3.5 copy.49
  426.1 58.9 %reduce-scatter.4.cloned.1.call-done = f32[64,768]{1,0:T(8,128)} async-done(((f32[1024,768]{1,0:T(8,128)}), f32[64,768]{1,0:T(8,128)}) %reduce-scatter.4.cloned.1.call-update) | async-done | bytes 196624
  (223 shorter events, 187.4 us)
Async XLA Ops:
  7.2 4.7 copy-start
  7.2 2.6 copy-start.3
  7.2 4.7 copy-start.9
  7.2 46.1 %all-gather.3.cloned.1.call-start = ((), (), s32[]{:S(2)}) async-start(), calls=%async_computation.1 | async-start | bytes 1671168 | tf_op jit(solution)/shard_map/all_gather | solution.py:22
  9.7 253.8 %all-gather.5.cloned.1.call-start = ((), (), s32[]{:S(2)}) async-start(), calls=%async_computation.3 | async-start | bytes 1671168 | tf_op jit(solution)/shard_map/all_gather | solution.py:60
  11.8 288.6 %all-reduce.2.cloned.1.call-start = ((), (), s32[]{:S(2)}) async-start(), calls=%async_computation.2 | async-start | bytes 6291456 | tf_op jit(solution)/shard_map/psum | solution.py:54
  12.6 1.8 copy-start.5
  199.3 285.7 %reduce-scatter.4.cloned.1.call-start = ((), (), s32[]{:S(2)}) async-start(), calls=%async_computation.4 | async-start | bytes 3342336
  263.6 36.9 %copy-start.1 = (bf16[1024,768]{1,0:T(8,128)(2,1)S(1)}, bf16[1024,768]{1,0:T(8,128)(2,1)}, u32[]{:S(2)}) copy-start(bf16[1024,768]{1,0:T(8,128)(2,1)} %all-gather.5.cloned.1.call-done) | copy-start | bytes 4718596
  419.6 1.3 copy-start.4
  419.6 1.3 copy-start.8
  422.7 1.8 copy-start.6
  424.6 61.6 %copy-start.2 = (bf16[768,768]{1,0:T(8,128)(2,1)S(1)}, bf16[768,768]{1,0:T(8,128)(2,1)}, u32[]{:S(2)}) copy-start(bf16[768,768]{1,0:T(8,128)(2,1)} %param.17) | copy-start | bytes 3538948
  424.6 61.6 %copy-start.7 = (bf16[64,768]{1,0:T(8,128)(2,1)S(1)}, bf16[64,768]{1,0:T(8,128)(2,1)}, u32[]{:S(2)}) copy-start(bf16[64,768]{1,0:T(8,128)(2,1)} %param.21) | copy-start | bytes 294916
Sparse Core Ops, SparseCore 0:
  10.9 42.3 all-gather.2
  56.1 38.5 all-gather.4
  199.4 101.0 all-reduce.1
  419.7 65.2 reduce-scatter.3
where the time goes:
time: 497 us; the launch traced here: 494 us
  matrix products  164 us (33%)
  waiting for transfers between devices  129 us (26%)
  blocking collectives  118 us (24%)
  local copies, waits for them, and re-layouts  36.3 us (7%)
  other arithmetic  31.3 us (6%)
  between operations  14 us (3%)
    pmax x1, blocking collectives, body(): row_max = lax.pmax(lax.map(local_max, (query_heads, key_heads)), 'pts')  59.7 us
    unnamed x5, waiting for transfers between devices  59 us
    psum x1, blocking collectives, body(): numer_all, total_all = lax.psum((numerator, total_cols), 'pts')  58.6 us
    dot_general x36, matrix products, masked_scores(): jnp.dot(query_head, key_head.T, preferred_element_type=jnp.float32) * 0.125  51.5 us
    all_gather x1, waiting for transfers between devices, body(): query_all = lax.all_gather(query_own, 'pts', axis=0, tiled=True)  35.6 us
    psum x1, waiting for transfers between devices, body(): numer_all, total_all = lax.psum((numerator, total_cols), 'pts')  34.2 us
    dot_general x12, matrix products, backward_head(): jnp.dot(grad_scores, key_head, preferred_element_type=jnp.float32) * 0.125  23.7 us
    lt x36, other arithmetic, body(): live_mask = jnp.arange(slots, dtype=jnp.int32) < counts[0]  23.4 us
  transfers between devices with their start and end apart: 4, of which 3 were waited for; matrix products, arithmetic and copies ran while one was open for 22% of the time, Pallas kernels for 0%

commit v1 on v0

v1 whole, which is shorter than its diff:
```python
import functools

import jax
import jax.numpy as jnp
from jax import lax
from jax.experimental import pallas as pl
from jax.experimental.pallas import tpu as pltpu
from jax.sharding import PartitionSpec as P

HEADS = 12
BF16 = jnp.bfloat16
F32 = jnp.float32
NT = (((1,), (1,)), ((), ()))


def dot(a, b):
    return jnp.dot(a, b, preferred_element_type=F32)


def dot_nt(a, b):
    return lax.dot_general(a, b, NT, preferred_element_type=F32)


def low_lanes(shape):
    return lax.broadcasted_iota(jnp.int32, shape, 1) < shape[1] // 2


def keep_half(pair, half):
    low = low_lanes(pair.shape)
    return jnp.where(low if half == 0 else ~low, pair, jnp.zeros_like(pair))


def head_scores(key_pair, half, query_pair, dead):
    raw = dot_nt(keep_half(key_pair, half), query_pair)
    return jnp.where(dead, -jnp.inf, raw)


def forward_kernel(count_ref, q_ref, g_ref, key_ref, value_t_ref, numer_ref, max_ref, stat_ref):
    rows, width = q_ref.shape
    slots = key_ref.shape[0]
    head_dim = width // HEADS
    span = 2 * head_dim
    dead = lax.broadcasted_iota(jnp.int32, (slots, rows), 0) >= count_ref[0]
    for pair in range(HEADS // 2):
        cols = slice(pair * span, (pair + 1) * span)
        query_pair = q_ref[:, cols]
        key_pair = key_ref[:, cols]
        grad_t = g_ref[:, cols].astype(F32).T
        for half in range(2):
            head = 2 * pair + half
            at = slice(head * head_dim, (head + 1) * head_dim)
            scores = head_scores(key_pair, half, query_pair, dead)
            top = jnp.max(scores, axis=0, keepdims=True)
            weights = jnp.exp(scores - top)
            total = jnp.sum(weights, axis=0, keepdims=True)
            numer = dot(value_t_ref[at, :], weights.astype(BF16))
            numer_ref[at, :] = numer
            mine = grad_t[half * head_dim : (half + 1) * head_dim, :]
            inner = jnp.sum(mine * numer, axis=0, keepdims=True)
            max_ref[head : head + 1, :] = top
            stat_ref[head : head + 1, :] = top + jnp.log(total)
            stat_ref[HEADS + head : HEADS + head + 1, :] = inner / total


def scale_kernel(numer_ref, max_ref, stat_ref, out_ref):
    width, rows = numer_ref.shape
    head_dim = width // HEADS
    for pair in range(HEADS // 2):
        parts = []
        for half in range(2):
            head = 2 * pair + half
            scale = jnp.exp(max_ref[head : head + 1, :] - stat_ref[head : head + 1, :])
            parts.append(numer_ref[head * head_dim : (head + 1) * head_dim, :] * scale)
        out_ref[:, 2 * pair * head_dim : 2 * (pair + 1) * head_dim] = (
            jnp.concatenate(parts, axis=0).T.astype(out_ref.dtype)
        )


def backward_kernel(
    first,
    last,
    count_ref,
    q_ref,
    g_ref,
    stat_ref,
    key_ref,
    key_t_ref,
    value_ref,
    *refs,
):
    if first:
        gq_ref, gk_ref, gv_ref = refs
    else:
        gk_in_ref, gv_in_ref, gq_ref, gk_ref, gv_ref = refs
    rows, width = q_ref.shape
    slots = key_ref.shape[0]
    head_dim = width // HEADS
    span = 2 * head_dim
    dead = lax.broadcasted_iota(jnp.int32, (slots, rows), 0) >= count_ref[0]
    low = low_lanes((slots, span))
    for pair in range(HEADS // 2):
        cols = slice(pair * span, (pair + 1) * span)
        query_pair = q_ref[:, cols]
        grad_pair = g_ref[:, cols]
        key_pair = key_ref[:, cols]
        value_pair = value_ref[:, cols]
        gk, gv, gq = [], [], []
        for half in range(2):
            head = 2 * pair + half
            scores = head_scores(key_pair, half, query_pair, dead)
            prob = jnp.exp(scores - stat_ref[head : head + 1, :])
            gv.append(dot(prob.astype(BF16), grad_pair))
            gw = dot_nt(keep_half(value_pair, half), grad_pair)
            ds = (prob * (gw - stat_ref[HEADS + head : HEADS + head + 1, :])).astype(BF16)
            gk.append(dot(ds, query_pair))
            gq.append(dot(key_t_ref[head * head_dim : (head + 1) * head_dim, :], ds))
        gq_ref[:, cols] = jnp.concatenate(gq, axis=0).T.astype(gq_ref.dtype)
        gk_sum = jnp.where(low, gk[0], gk[1])
        gv_sum = jnp.where(low, gv[0], gv[1])
        if not first:
            gk_sum += gk_in_ref[:, cols]
            gv_sum += gv_in_ref[:, cols]
        if last:
            gk_sum *= 0.125
        gk_ref[:, cols] = gk_sum.astype(gk_ref.dtype)
        gv_ref[:, cols] = gv_sum.astype(gv_ref.dtype)


def call(kernel, ins, out_shapes, flops=0, exps=0):
    vmem = pl.BlockSpec(memory_space=pltpu.VMEM)
    smem = pl.BlockSpec(memory_space=pltpu.SMEM)
    specs = [smem if a.dtype == jnp.int32 else vmem for a in ins]
    moved = sum(a.size * a.dtype.itemsize for a in list(ins) + list(out_shapes))
    return pl.pallas_call(
        kernel,
        in_specs=specs,
        out_specs=[vmem] * len(out_shapes),
        out_shape=out_shapes,
        compiler_params=pltpu.CompilerParams(vmem_limit_bytes=40 << 20),
        cost_estimate=pl.CostEstimate(flops=flops, transcendentals=exps, bytes_accessed=moved),
    )(*ins)


def body(size, latents, points, counts, w_query, w_key, w_value, w_out, d_out):
    own, width = latents.shape
    slots = points.shape[0]
    shape = jax.ShapeDtypeStruct
    direct = [0, size // 4, size // 2, size // 4 + size // 2]
    middle = []
    bit = size // 8
    while bit >= 4:
        middle.append(bit)
        bit //= 2

    def swap(array, mask):
        return lax.ppermute(array, "pts", [(i, i ^ mask) for i in range(size)])

    query_own = dot(latents, w_query).astype(BF16)
    grad_own = dot(d_out, w_out.T).astype(BF16)

    def gather(block):
        near = jnp.concatenate([block] + [swap(block, m) for m in direct[1:]], axis=0)
        for mask in middle:
            near = jnp.concatenate([near, swap(near, mask)], axis=0)
        across = swap(near, 2)
        return [near, across, swap(near, 1), swap(across, 1)]

    query = gather(query_own)
    grad = gather(grad_own)
    keys = dot(points, w_key).astype(BF16) * jnp.asarray(0.125, BF16)
    values = dot(points, w_value).astype(BF16)
    keys_t = keys.T
    values_t = values.T
    rows = query[0].shape[0]
    work = 2 * rows * slots * width

    def forward(i):
        return call(
            forward_kernel,
            [counts, query[i], grad[i], keys, values_t],
            [shape((width, rows), F32), shape((HEADS, rows), F32), shape((2 * HEADS, rows), F32)],
            flops=8 * work,
            exps=rows * slots * HEADS,
        )

    numer, tops, stats = [None] * 4, [None] * 4, [None] * 4
    for i in (0, 2, 1, 3):
        numer[i], tops[i], stats[i] = forward(i)

    def merge(*parts):
        lse = [p[:HEADS] for p in parts]
        top = functools.reduce(jnp.maximum, lse)
        scale = [jnp.exp(x - top) for x in lse]
        total = sum(scale)
        delta = sum(s * p[HEADS:] for s, p in zip(scale, parts)) / total
        return jnp.concatenate([top + jnp.log(total), delta], axis=0)

    came = swap(jnp.stack([stats[2], stats[3]]), 1)
    mine = merge(stats[0], came[0])
    other = merge(stats[1], came[1])
    mine = merge(mine, swap(other, 2))
    for mask in reversed(middle):
        half = mine.shape[1] // 2
        mine = merge(mine[:, :half], swap(mine[:, half:], mask))
    quarter = mine.shape[1] // 4

    def turned(array, p):
        blocks = [array[:, t * quarter : (t + 1) * quarter] for t in range(4)]
        return jnp.concatenate([blocks[t ^ p] for t in range(4)], axis=1)

    mine = merge(mine, *[turned(swap(mine, direct[p]), p) for p in range(1, 4)])
    for mask in middle:
        mine = jnp.concatenate([mine, swap(mine, mask)], axis=1)
    both = jnp.stack([mine, swap(mine, 2)])
    far = swap(both, 1)
    final = [both[0], both[1], far[0], far[1]]

    def scaled(i, dtype):
        return call(scale_kernel, [numer[i], tops[i], final[i]], [shape((rows, width), dtype)])[0]

    def total_of(near, across):
        summed = near + swap(across.astype(BF16), 2).astype(F32)
        for mask in reversed(middle):
            half = summed.shape[0] // 2
            summed = summed[:half] + swap(summed[half:].astype(BF16), mask).astype(F32)
        out = summed[:own]
        for p in range(1, 4):
            sent = summed[p * own : (p + 1) * own].astype(BF16)
            out = out + swap(sent, direct[p]).astype(F32)
        return out

    def add(array, came):
        return array + came.astype(F32)

    sent = swap(jnp.concatenate([scaled(2, BF16), scaled(3, BF16)], axis=0), 1)
    attended = total_of(
        add(scaled(0, F32), sent[:rows]), add(scaled(1, F32), sent[rows:])
    ).astype(BF16)
    result = (latents.astype(F32) + dot(attended, w_out)).astype(BF16)

    def backward(i, sums, dtype, last=False):
        kind = BF16 if last else F32
        outs = [shape((rows, width), dtype), shape((slots, width), kind), shape((slots, width), kind)]
        gq, gk, gv = call(
            functools.partial(backward_kernel, not sums, last),
            [counts, query[i], grad[i], final[i], keys, keys_t, values] + sums,
            outs,
            flops=14 * work,
            exps=rows * slots * HEADS,
        )
        return gq, [gk, gv]

    gq_2, sums = backward(2, [], BF16)
    sent_2 = swap(gq_2, 1)
    gq_3, sums = backward(3, sums, BF16)
    sent_3 = swap(gq_3, 1)
    gq_1, sums = backward(1, sums, F32)
    across = add(gq_1, sent_3)
    gq_0, sums = backward(0, sums, F32, last=True)
    grad_query = total_of(add(gq_0, sent_2), across)
    d_latents = (d_out.astype(F32) + dot(grad_query.astype(BF16), w_query.T)).astype(BF16)
    d_points = (dot(sums[0], w_key.T) + dot(sums[1], w_value.T)).astype(BF16)
    return (result, d_latents, d_points)


def solution(mesh):
    part = P(("groups", "pts"), None)
    in_specs = (part, part, P(("groups", "pts")), P(), P(), P(), P(), part)
    return jax.shard_map(
        functools.partial(body, mesh.shape["pts"]),
        mesh=mesh,
        in_specs=in_specs,
        out_specs=(part, part, part),
        check_vma=False,
    )
```

time: 497 us -> 135 us (0.27)
  matrix products: 164 us -> 9.26 us
  blocking collectives: 118 us -> 0 us
  waiting for transfers between devices: 129 us -> 39.9 us
  Pallas kernels: 0 us -> 44.4 us
  starting transfers between devices: 0.16 us -> 36.1 us
  local copies, waits for them, and re-layouts: 36.3 us -> 1.39 us
  other arithmetic: 31.3 us -> 2.22 us
  between operations: 14 us -> 1.72 us
    dot_general x104 -> x8, matrix products: 164 us -> 9.26 us  [dot(): return jnp.dot(a, b, preferred_element_type=F32)]
    pmax x1 -> x0, blocking collectives: 59.7 us -> none  [body(): row_max = lax.pmax(lax.map(local_max, (query_heads, key_heads)), 'pts')]
    unnamed x5 -> x0, waiting for transfers between devices: 59 us -> none
    psum x1 -> x0, blocking collectives: 58.6 us -> none  [body(): numer_all, total_all = lax.psum((numerator, total_cols), 'pts')]
    pallas_call x0 -> x12, Pallas kernels: none -> 44.4 us  [call(): pl.pallas_call(kernel, in_specs=specs, out_specs=[vmem] * len(out_shapes)...]
    ppermute x0 -> x30, waiting for transfers between devices: none -> 39.9 us  [swap(): return lax.ppermute(array, 'pts', [(i, i ^ mask) for i in range(size)])]
    ppermute x0 -> x30, starting transfers between devices: none -> 36.1 us  [swap(): return lax.ppermute(array, 'pts', [(i, i ^ mask) for i in range(size)])]
    all_gather x2 -> x0, waiting for transfers between devices: 35.6 us -> none  [the longest x1 35.6 us: body(): query_all = lax.all_gather(query_own, 'pts', axis=0, tiled=True)]
  transfers between devices with their start and end apart: 4 -> 30, of which waited for: 3 -> 15; matrix products, arithmetic and copies ran while one was open for 22% -> 7% of each run, Pallas kernels for 0% -> 29%
where the time goes in v1:
time: 135 us
  Pallas kernels  44.4 us (33%)
  waiting for transfers between devices  39.9 us (30%)
  starting transfers between devices  36.1 us (27%)
  matrix products  9.26 us (7%)
  other arithmetic  2.22 us (2%)
  between operations  1.72 us (1%)
  local copies, waits for them, and re-layouts  1.39 us (1%)
    pallas_call x12, Pallas kernels, call(): pl.pallas_call(kernel, in_specs=specs, out_specs=[vmem] * len(out_shapes)...  44.4 us
    ppermute x30, waiting for transfers between devices, swap(): return lax.ppermute(array, 'pts', [(i, i ^ mask) for i in range(size)])  39.9 us
    ppermute x30, starting transfers between devices, swap(): return lax.ppermute(array, 'pts', [(i, i ^ mask) for i in range(size)])  36.1 us
    dot_general x8, matrix products, dot(): return jnp.dot(a, b, preferred_element_type=F32)  9.26 us
  transfers between devices with their start and end apart: 30, of which 15 were waited for; matrix products, arithmetic and copies ran while one was open for 7% of the time, Pallas kernels for 29%

profile of v1, /device:TPU:0, one launch (start us, length us, event | category | flops | bytes accessed | tf_op | source)
XLA Modules:
  0.0 135.0 jit_solution(4892007879137233354)
XLA Ops:
  2.5 5.1 %collective-permute-start.2 = (bf16[64,768]{1,0:T(8,128)(2,1)S(1)}, bf16[64,768]{1,0:T(8,128)(2,1)S(1)}, u32[]{:S(2)}, u32[]{:S(2)}) collective-permute-start(bf16[64,768]{1,0:T(8,128)(2,1)S(1)} %convolution_convert_fusion.3), channel_id=1, source_target_pairs={{0,12},{1,13},{2,14},{3,15},{4,8},{5,9},{6,10},{7,11},{8,4},{9,5},... | collective-permute-start | bytes 294920 | tf_op jit(solution)/shard_map/ppermute | solution.py:156
  8.7 3.8 %collective-permute-start.5 = (bf16[64,768]{1,0:T(8,128)(2,1)S(1)}, bf16[64,768]{1,0:T(8,128)(2,1)S(1)}, u32[]{:S(2)}, u32[]{:S(2)}) collective-permute-start(bf16[64,768]{1,0:T(8,128)(2,1)S(1)} %convolution_convert_fusion.2), channel_id=1, source_target_pairs={{0,12},{1,13},{2,14},{3,15},{4,8},{5,9},{6,10},{7,11},{8,4},{9,5},... | collective-permute-start | bytes 294920 | tf_op jit(solution)/shard_map/ppermute | solution.py:156
  12.6 6.0 %collective-permute-start.3 = (bf16[64,768]{1,0:T(8,128)(2,1)S(1)}, bf16[64,768]{1,0:T(8,128)(2,1)S(1)}, u32[]{:S(2)}, u32[]{:S(2)}) collective-permute-start(bf16[64,768]{1,0:T(8,128)(2,1)S(1)} %convolution_convert_fusion.2), channel_id=1, source_target_pairs={{0,4},{1,5},{2,6},{3,7},{4,0},{5,1},{6,2},{7,3},{8,12},{9,13},{10,... | collective-permute-start | bytes 294920 | tf_op jit(solution)/shard_map/ppermute | solution.py:156
  18.5 2.5 %collective-permute-done.1 = bf16[64,768]{1,0:T(8,128)(2,1)S(1)} collective-permute-done((bf16[64,768]{1,0:T(8,128)(2,1)S(1)}, bf16[64,768]{1,0:T(8,128)(2,1)S(1)}, u32[]{:S(2)}, u32[]{:S(2)}) %collective-permute-start.1) | collective-permute-done | bytes 98336 | tf_op jit(solution)/shard_map/ppermute | solution.py:156
  28.8 5.1 %collective-permute-done.8.q_ref = bf16[256,768]{1,0:T(8,128)(2,1)} collective-permute-done((bf16[256,768]{1,0:T(8,128)(2,1)}, bf16[256,768]{1,0:T(8,128)(2,1)}, u32[]{:S(2)}, u32[]{:S(2)}) %collective-permute-start.8) | collective-permute-done | bytes 393248 | tf_op jit(solution)/shard_map/ppermute | solution.py:156
  33.9 5.1 %collective-permute-done.10.g_ref = bf16[256,768]{1,0:T(8,128)(2,1)} collective-permute-done((bf16[256,768]{1,0:T(8,128)(2,1)}, bf16[256,768]{1,0:T(8,128)(2,1)}, u32[]{:S(2)}, u32[]{:S(2)}) %collective-permute-start.10) | collective-permute-done | bytes 393248 | tf_op jit(solution)/shard_map/ppermute | solution.py:156
  39.0 2.1 %fusion.1 = bf16[384,768]{0,1:T(8,128)(2,1)S(1)} fusion(bf16[384,768]{1,0:T(8,128)(2,1)S(1)} %copy-done.9, bf16[768,768]{1,0:T(8,128)(2,1)} %param.12), kind=kOutput, calls=%fused_computation.4 | convolution fusion | flops 453574656 | bytes 2359296 | tf_op jit(solution)/shard_map/dot_general | solution.py:17
  41.4 5.4 %shard_map.104 = (f32[768,256]{1,0:T(8,128)S(1)}, f32[12,256]{1,0:T(8,128)S(1)}, f32[24,256]{1,0:T(8,128)S(1)}) custom-call(s32[1]{0:T(128)S(6)} %copy.25.count_ref, bf16[256,768]{1,0:T(8,128)(2,1)} %collective-permute-done.6.q_ref, bf16[256,768]{1,0:T(8,128)(2,1)} %collective-permute-done.7.g_ref, bf16[384,768]{1,0:T(8,128)(2,1)S(1)} %copy.12.key_ref, ...), custom_call_target="tpu_custom_call" | custom-call | flops 1207959552 | bytes 2789380 | tf_op jit(solution)/shard_map/pallas_call | solution.py:134
  46.8 5.4 %shard_map.105 = (f32[768,256]{1,0:T(8,128)S(1)}, f32[12,256]{1,0:T(8,128)S(1)}, f32[24,256]{1,0:T(8,128)S(1)}) custom-call(s32[1]{0:T(128)S(6)} %copy.25.count_ref, bf16[256,768]{1,0:T(8,128)(2,1)} %collective-permute-done.9.q_ref, bf16[256,768]{1,0:T(8,128)(2,1)} %collective-permute-done.11.g_ref, bf16[384,768]{1,0:T(8,128)(2,1)S(1)} %copy.12.key_ref, ...), custom_call_target="tpu_custom_call" | custom-call | flops 1207959552 | bytes 2789380 | tf_op jit(solution)/shard_map/pallas_call | solution.py:134
  52.8 5.6 %shard_map.106 = (f32[768,256]{1,0:T(8,128)S(1)}, f32[12,256]{1,0:T(8,128)S(1)}, f32[24,256]{1,0:T(8,128)S(1)}) custom-call(s32[1]{0:T(128)S(6)} %copy.25.count_ref, bf16[256,768]{1,0:T(8,128)(2,1)} %collective-permute-done.8.q_ref, bf16[256,768]{1,0:T(8,128)(2,1)} %collective-permute-done.10.g_ref, bf16[384,768]{1,0:T(8,128)(2,1)S(1)} %copy.12.key_ref, ...), custom_call_target="tpu_custom_call" | custom-call | flops 1207959552 | bytes 2789380 | tf_op jit(solution)/shard_map/pallas_call | solution.py:134
  60.0 5.4 %shard_map.103 = (f32[768,256]{1,0:T(8,128)S(1)}, f32[12,256]{1,0:T(8,128)S(1)}, f32[24,256]{1,0:T(8,128)S(1)}) custom-call(s32[1]{0:T(128)S(6)} %copy.25.count_ref, bf16[256,768]{1,0:T(8,128)(2,1)} %pad_maximum_fusion.1.q_ref, bf16[256,768]{1,0:T(8,128)(2,1)} %pad_maximum_fusion.2.g_ref, bf16[384,768]{1,0:T(8,128)(2,1)S(1)} %copy.12.key_ref, ...), custom_call_target="tpu_custom_call" | custom-call | flops 1207959552 | bytes 2789380 | tf_op jit(solution)/shard_map/pallas_call | solution.py:134
  65.5 2.1 %collective-permute-start.16 = (f32[24,256]{1,0:T(8,128)S(1)}, f32[24,256]{1,0:T(8,128)S(1)}, u32[]{:S(2)}, u32[]{:S(2)}) collective-permute-start(f32[24,256]{1,0:T(8,128)S(1)} %pad_maximum_fusion.6), channel_id=1, source_target_pairs={{0,12},{1,13},{2,14},{3,15},{4,8},{5,9},{6,10},{7,11},{8,4},{9,5},... | collective-permute-start | bytes 73736 | tf_op jit(solution)/shard_map/ppermute | solution.py:156
  67.6 2.4 %collective-permute-start.14 = (f32[24,256]{1,0:T(8,128)S(1)}, f32[24,256]{1,0:T(8,128)S(1)}, u32[]{:S(2)}, u32[]{:S(2)}) collective-permute-start(f32[24,256]{1,0:T(8,128)S(1)} %pad_maximum_fusion.6), channel_id=1, source_target_pairs={{0,4},{1,5},{2,6},{3,7},{4,0},{5,1},{6,2},{7,3},{8,12},{9,13},{10,... | collective-permute-start | bytes 73736 | tf_op jit(solution)/shard_map/ppermute | solution.py:156
  73.0 3.3 %collective-permute-done.17.stat_ref = f32[24,256]{1,0:T(8,128)S(1)} collective-permute-done((f32[24,256]{1,0:T(8,128)S(1)}, f32[24,256]{1,0:T(8,128)S(1)}, u32[]{:S(2)}, u32[]{:S(2)}) %collective-permute-start.17) | collective-permute-done | bytes 24608 | tf_op jit(solution)/shard_map/ppermute | solution.py:156
  78.1 5.3 %shard_map.111 = (bf16[256,768]{1,0:T(8,128)(2,1)S(1)}, f32[384,768]{1,0:T(8,128)S(1)}, f32[384,768]{1,0:T(8,128)S(1)}) custom-call(s32[1]{0:T(128)S(6)} %copy.25.count_ref, bf16[256,768]{1,0:T(8,128)(2,1)} %collective-permute-done.6.q_ref, bf16[256,768]{1,0:T(8,128)(2,1)} %collective-permute-done.7.g_ref, f32[24,256]{1,0:T(8,128)S(1)} %get-tuple-element.67.stat_ref, ...), custom_call_target="tpu_custom_call" | custom-call | flops 2113929216 | bytes 5332996 | tf_op jit(solution)/shard_map/pallas_call | solution.py:134
  83.5 5.6 %shard_map.112 = (bf16[256,768]{1,0:T(8,128)(2,1)S(1)}, f32[384,768]{1,0:T(8,128)S(1)}, f32[384,768]{1,0:T(8,128)S(1)}) custom-call(s32[1]{0:T(128)S(6)} %copy.25.count_ref, bf16[256,768]{1,0:T(8,128)(2,1)} %collective-permute-done.9.q_ref, bf16[256,768]{1,0:T(8,128)(2,1)} %collective-permute-done.11.g_ref, f32[24,256]{1,0:T(8,128)S(1)} %get-tuple-element.68.stat_ref, ...), custom_call_target="tpu_custom_call" | custom-call | flops 2113929216 | bytes 7692292 | tf_op jit(solution)/shard_map/pallas_call | solution.py:134
  89.7 5.4 %shard_map.113 = (f32[256,768]{1,0:T(8,128)S(1)}, f32[384,768]{1,0:T(8,128)S(1)}, f32[384,768]{1,0:T(8,128)S(1)}) custom-call(s32[1]{0:T(128)S(6)} %copy.25.count_ref, bf16[256,768]{1,0:T(8,128)(2,1)} %collective-permute-done.8.q_ref, bf16[256,768]{1,0:T(8,128)(2,1)} %collective-permute-done.10.g_ref, f32[24,256]{1,0:T(8,128)S(1)} %collective-permute-done.17.stat_ref, ...), custom_call_target="tpu_custom_call" | custom-call | flops 2113929216 | bytes 8085508 | tf_op jit(solution)/shard_map/pallas_call | solution.py:134
  95.1 5.3 %shard_map.114 = (f32[256,768]{1,0:T(8,128)S(1)}, bf16[384,768]{1,0:T(8,128)(2,1)S(1)}, bf16[384,768]{1,0:T(8,128)(2,1)S(1)}) custom-call(s32[1]{0:T(128)S(6)} %copy.25.count_ref, bf16[256,768]{1,0:T(8,128)(2,1)} %pad_maximum_fusion.1.q_ref, bf16[256,768]{1,0:T(8,128)(2,1)} %pad_maximum_fusion.2.g_ref, f32[24,256]{1,0:T(8,128)S(1)} %pad_maximum_fusion.9.stat_ref, ...), custom_call_target="tpu_custom_call" | custom-call | flops 2113929216 | bytes 6905860 | tf_op jit(solution)/shard_map/pallas_call | solution.py:134
  105.0 8.3 %collective-permute-done.26 = bf16[256,768]{1,0:T(8,128)(2,1)S(1)} collective-permute-done((bf16[256,768]{1,0:T(8,128)(2,1)S(1)}, bf16[256,768]{1,0:T(8,128)(2,1)S(1)}, u32[]{:S(2)}, u32[]{:S(2)}) %collective-permute-start.26) | collective-permute-done | bytes 393248 | tf_op jit(solution)/shard_map/ppermute | solution.py:156
  115.1 2.0 %collective-permute-start.29 = (bf16[64,768]{1,0:T(8,128)(2,1)S(1)}, bf16[64,768]{1,0:T(8,128)(2,1)S(1)}, u32[]{:S(2)}, u32[]{:S(2)}) collective-permute-start(bf16[64,768]{1,0:T(8,128)(2,1)S(1)} %get-tuple-element.56), channel_id=1, source_target_pairs={{0,12},{1,13},{2,14},{3,15},{4,8},{5,9},{6,10},{7,11},{8,4},{9,5},... | collective-permute-start | bytes 294920 | tf_op jit(solution)/shard_map/ppermute | solution.py:156
  117.2 3.9 %collective-permute-done.20 = bf16[256,768]{1,0:T(8,128)(2,1)S(1)} collective-permute-done((bf16[256,768]{1,0:T(8,128)(2,1)S(1)}, bf16[256,768]{1,0:T(8,128)(2,1)S(1)}, u32[]{:S(2)}, u32[]{:S(2)}) %collective-permute-start.20) | collective-permute-done | bytes 393248 | tf_op jit(solution)/shard_map/ppermute | solution.py:156
  123.0 2.0 %collective-permute-start.23 = (bf16[64,768]{1,0:T(8,128)(2,1)S(1)}, bf16[64,768]{1,0:T(8,128)(2,1)S(1)}, u32[]{:S(2)}, u32[]{:S(2)}) collective-permute-start(bf16[64,768]{1,0:T(8,128)(2,1)S(1)} %get-tuple-element.59), channel_id=1, source_target_pairs={{0,12},{1,13},{2,14},{3,15},{4,8},{5,9},{6,10},{7,11},{8,4},{9,5},... | collective-permute-start | bytes 294920 | tf_op jit(solution)/shard_map/ppermute | solution.py:156
  128.1 2.7 %collective-permute-done.23 = bf16[64,768]{1,0:T(8,128)(2,1)S(1)} collective-permute-done((bf16[64,768]{1,0:T(8,128)(2,1)S(1)}, bf16[64,768]{1,0:T(8,128)(2,1)S(1)}, u32[]{:S(2)}, u32[]{:S(2)}) %collective-permute-start.23) | collective-permute-done | bytes 98336 | tf_op jit(solution)/shard_map/ppermute | solution.py:156
  130.8 3.2 %collective-permute-done.22 = bf16[64,768]{1,0:T(8,128)(2,1)S(1)} collective-permute-done((bf16[64,768]{1,0:T(8,128)(2,1)S(1)}, bf16[64,768]{1,0:T(8,128)(2,1)S(1)}, u32[]{:S(2)}, u32[]{:S(2)}) %collective-permute-start.22) | collective-permute-done | bytes 98336 | tf_op jit(solution)/shard_map/ppermute | solution.py:156
  (101 shorter events, 30.1 us)
Async XLA Ops:
  2.5 10.1 %collective-permute-start.2 = (bf16[64,768]{1,0:T(8,128)(2,1)S(1)}, bf16[64,768]{1,0:T(8,128)(2,1)S(1)}, u32[]{:S(2)}, u32[]{:S(2)}) collective-permute-start(bf16[64,768]{1,0:T(8,128)(2,1)S(1)} %convolution_convert_fusion.3), channel_id=1, source_target_pairs={{0,12},{1,13},{2,14},{3,15},{4,8},{5,9},{6,10},{7,11},{8,4},{9,5},... | collective-permute-start | bytes 294920 | tf_op jit(solution)/shard_map/ppermute | solution.py:156
  7.6 13.4 %collective-permute-start.1 = (bf16[64,768]{1,0:T(8,128)(2,1)S(1)}, bf16[64,768]{1,0:T(8,128)(2,1)S(1)}, u32[]{:S(2)}, u32[]{:S(2)}) collective-permute-start(bf16[64,768]{1,0:T(8,128)(2,1)S(1)} %convolution_convert_fusion.3), channel_id=1, source_target_pairs={{0,8},{1,9},{2,10},{3,11},{4,12},{5,13},{6,14},{7,15},{8,0},{9,1},... | collective-permute-start | bytes 294920 | tf_op jit(solution)/shard_map/ppermute | solution.py:156
  7.6 13.4 %collective-permute-start = (bf16[64,768]{1,0:T(8,128)(2,1)S(1)}, bf16[64,768]{1,0:T(8,128)(2,1)S(1)}, u32[]{:S(2)}, u32[]{:S(2)}) collective-permute-start(bf16[64,768]{1,0:T(8,128)(2,1)S(1)} %convolution_convert_fusion.3), channel_id=1, source_target_pairs={{0,4},{1,5},{2,6},{3,7},{4,0},{5,1},{6,2},{7,3},{8,12},{9,13},{10,... | collective-permute-start | bytes 294920 | tf_op jit(solution)/shard_map/ppermute | solution.py:156
  8.7 14.6 %collective-permute-start.5 = (bf16[64,768]{1,0:T(8,128)(2,1)S(1)}, bf16[64,768]{1,0:T(8,128)(2,1)S(1)}, u32[]{:S(2)}, u32[]{:S(2)}) collective-permute-start(bf16[64,768]{1,0:T(8,128)(2,1)S(1)} %convolution_convert_fusion.2), channel_id=1, source_target_pairs={{0,12},{1,13},{2,14},{3,15},{4,8},{5,9},{6,10},{7,11},{8,4},{9,5},... | collective-permute-start | bytes 294920 | tf_op jit(solution)/shard_map/ppermute | solution.py:156
  12.5 11.7 %collective-permute-start.4 = (bf16[64,768]{1,0:T(8,128)(2,1)S(1)}, bf16[64,768]{1,0:T(8,128)(2,1)S(1)}, u32[]{:S(2)}, u32[]{:S(2)}) collective-permute-start(bf16[64,768]{1,0:T(8,128)(2,1)S(1)} %convolution_convert_fusion.2), channel_id=1, source_target_pairs={{0,8},{1,9},{2,10},{3,11},{4,12},{5,13},{6,14},{7,15},{8,0},{9,1},... | collective-permute-start | bytes 294920 | tf_op jit(solution)/shard_map/ppermute | solution.py:156
  12.6 11.7 %collective-permute-start.3 = (bf16[64,768]{1,0:T(8,128)(2,1)S(1)}, bf16[64,768]{1,0:T(8,128)(2,1)S(1)}, u32[]{:S(2)}, u32[]{:S(2)}) collective-permute-start(bf16[64,768]{1,0:T(8,128)(2,1)S(1)} %convolution_convert_fusion.2), channel_id=1, source_target_pairs={{0,4},{1,5},{2,6},{3,7},{4,0},{5,1},{6,2},{7,3},{8,12},{9,13},{10,... | collective-permute-start | bytes 294920 | tf_op jit(solution)/shard_map/ppermute | solution.py:156
  21.8 12.1 %collective-permute-start.8 = (bf16[256,768]{1,0:T(8,128)(2,1)}, bf16[256,768]{1,0:T(8,128)(2,1)}, u32[]{:S(2)}, u32[]{:S(2)}) collective-permute-start(bf16[256,768]{1,0:T(8,128)(2,1)} %pad_maximum_fusion.1.q_ref), channel_id=1, source_target_pairs={{0,2},{1,3},{2,0},{3,1},{4,6},{5,7},{6,4},{7,5},{8,10},{9,11},{10,... | collective-permute-start | bytes 1179656 | tf_op jit(solution)/shard_map/ppermute | solution.py:156
  25.1 13.9 %collective-permute-start.10 = (bf16[256,768]{1,0:T(8,128)(2,1)}, bf16[256,768]{1,0:T(8,128)(2,1)}, u32[]{:S(2)}, u32[]{:S(2)}) collective-permute-start(bf16[256,768]{1,0:T(8,128)(2,1)} %pad_maximum_fusion.2.g_ref), channel_id=1, source_target_pairs={{0,2},{1,3},{2,0},{3,1},{4,6},{5,7},{6,4},{7,5},{8,10},{9,11},{10,... | collective-permute-start | bytes 1179656 | tf_op jit(solution)/shard_map/ppermute | solution.py:156
  26.6 14.8 %collective-permute-start.6 = (bf16[256,768]{1,0:T(8,128)(2,1)}, bf16[256,768]{1,0:T(8,128)(2,1)}, u32[]{:S(2)}, u32[]{:S(2)}) collective-permute-start(bf16[256,768]{1,0:T(8,128)(2,1)} %pad_maximum_fusion.1.q_ref), channel_id=1, source_target_pairs={{0,1},{1,0},{2,3},{3,2},{4,5},{5,4},{6,7},{7,6},{8,9},{9,8},{10,11... | collective-permute-start | bytes 1179656 | tf_op jit(solution)/shard_map/ppermute | solution.py:156
  26.6 14.8 %collective-permute-start.7 = (bf16[256,768]{1,0:T(8,128)(2,1)}, bf16[256,768]{1,0:T(8,128)(2,1)}, u32[]{:S(2)}, u32[]{:S(2)}) collective-permute-start(bf16[256,768]{1,0:T(8,128)(2,1)} %pad_maximum_fusion.2.g_ref), channel_id=1, source_target_pairs={{0,1},{1,0},{2,3},{3,2},{4,5},{5,4},{6,7},{7,6},{8,9},{9,8},{10,11... | collective-permute-start | bytes 1179656 | tf_op jit(solution)/shard_map/ppermute | solution.py:156
  33.9 12.9 %collective-permute-start.9 = (bf16[256,768]{1,0:T(8,128)(2,1)}, bf16[256,768]{1,0:T(8,128)(2,1)}, u32[]{:S(2)}, u32[]{:S(2)}) collective-permute-start(bf16[256,768]{1,0:T(8,128)(2,1)} %collective-permute-done.8.q_ref), channel_id=1, source_target_pairs={{0,1},{1,0},{2,3},{3,2},{4,5},{5,4},{6,7},{7,6},{8,9},{9,8},{10,11... | collective-permute-start | bytes 1179656 | tf_op jit(solution)/shard_map/ppermute | solution.py:156
  39.0 7.8 %collective-permute-start.11 = (bf16[256,768]{1,0:T(8,128)(2,1)}, bf16[256,768]{1,0:T(8,128)(2,1)}, u32[]{:S(2)}, u32[]{:S(2)}) collective-permute-start(bf16[256,768]{1,0:T(8,128)(2,1)} %collective-permute-done.10.g_ref), channel_id=1, source_target_pairs={{0,1},{1,0},{2,3},{3,2},{4,5},{5,4},{6,7},{7,6},{8,9},{9,8},{10,11... | collective-permute-start | bytes 1179656 | tf_op jit(solution)/shard_map/ppermute | solution.py:156
  58.4 7.0 %collective-permute-start.13 = (f32[24,256]{1,0:T(8,128)S(1)}, f32[24,256]{1,0:T(8,128)S(1)}, u32[]{:S(2)}, u32[]{:S(2)}) collective-permute-start(f32[24,256]{1,0:T(8,128)S(1)} %pad_maximum_fusion.5), channel_id=1, source_target_pairs={{0,2},{1,3},{2,0},{3,1},{4,6},{5,7},{6,4},{7,5},{8,10},{9,11},{10,... | collective-permute-start | bytes 73736 | tf_op jit(solution)/shard_map/ppermute | solution.py:156
  77.9 26.0 %collective-permute-start.19 = (bf16[512,768]{1,0:T(8,128)(2,1)S(1)}, bf16[512,768]{1,0:T(8,128)(2,1)S(1)}, u32[]{:S(2)}, u32[]{:S(2)}) collective-permute-start(bf16[512,768]{1,0:T(8,128)(2,1)S(1)} %pad_maximum_fusion), channel_id=1, source_target_pairs={{0,1},{1,0},{2,3},{3,2},{4,5},{5,4},{6,7},{7,6},{8,9},{9,8},{10,11... | collective-permute-start | bytes 2359304 | tf_op jit(solution)/shard_map/ppermute | solution.py:156
  89.1 12.0 %collective-permute-start.25 = (bf16[256,768]{1,0:T(8,128)(2,1)S(1)}, bf16[256,768]{1,0:T(8,128)(2,1)S(1)}, u32[]{:S(2)}, u32[]{:S(2)}) collective-permute-start(bf16[256,768]{1,0:T(8,128)(2,1)S(1)} %get-tuple-element.48), channel_id=1, source_target_pairs={{0,1},{1,0},{2,3},{3,2},{4,5},{5,4},{6,7},{7,6},{8,9},{9,8},{10,11... | collective-permute-start | bytes 1179656 | tf_op jit(solution)/shard_map/ppermute | solution.py:156
  89.6 15.4 %collective-permute-start.24 = (bf16[256,768]{1,0:T(8,128)(2,1)S(1)}, bf16[256,768]{1,0:T(8,128)(2,1)S(1)}, u32[]{:S(2)}, u32[]{:S(2)}) collective-permute-start(bf16[256,768]{1,0:T(8,128)(2,1)S(1)} %get-tuple-element.46), channel_id=1, source_target_pairs={{0,1},{1,0},{2,3},{3,2},{4,5},{5,4},{6,7},{7,6},{8,9},{9,8},{10,11... | collective-permute-start | bytes 1179656 | tf_op jit(solution)/shard_map/ppermute | solution.py:156
  101.2 12.0 %collective-permute-start.26 = (bf16[256,768]{1,0:T(8,128)(2,1)S(1)}, bf16[256,768]{1,0:T(8,128)(2,1)S(1)}, u32[]{:S(2)}, u32[]{:S(2)}) collective-permute-start(bf16[256,768]{1,0:T(8,128)(2,1)S(1)} %add_convert_fusion), channel_id=1, source_target_pairs={{0,2},{1,3},{2,0},{3,1},{4,6},{5,7},{6,4},{7,5},{8,10},{9,11},{10,... | collective-permute-start | bytes 1179656 | tf_op jit(solution)/shard_map/ppermute | solution.py:156
  104.0 17.1 %collective-permute-start.20 = (bf16[256,768]{1,0:T(8,128)(2,1)S(1)}, bf16[256,768]{1,0:T(8,128)(2,1)S(1)}, u32[]{:S(2)}, u32[]{:S(2)}) collective-permute-start(bf16[256,768]{1,0:T(8,128)(2,1)S(1)} %add_convert_fusion.1), channel_id=1, source_target_pairs={{0,2},{1,3},{2,0},{3,1},{4,6},{5,7},{6,4},{7,5},{8,10},{9,11},{10,... | collective-permute-start | bytes 1179656 | tf_op jit(solution)/shard_map/ppermute | solution.py:156
  113.4 11.6 %collective-permute-start.27 = (bf16[64,768]{1,0:T(8,128)(2,1)S(1)}, bf16[64,768]{1,0:T(8,128)(2,1)S(1)}, u32[]{:S(2)}, u32[]{:S(2)}) collective-permute-start(bf16[64,768]{1,0:T(8,128)(2,1)S(1)} %get-tuple-element.55), channel_id=1, source_target_pairs={{0,4},{1,5},{2,6},{3,7},{4,0},{5,1},{6,2},{7,3},{8,12},{9,13},{10,... | collective-permute-start | bytes 294920 | tf_op jit(solution)/shard_map/ppermute | solution.py:156
  115.1 9.9 %collective-permute-start.29 = (bf16[64,768]{1,0:T(8,128)(2,1)S(1)}, bf16[64,768]{1,0:T(8,128)(2,1)S(1)}, u32[]{:S(2)}, u32[]{:S(2)}) collective-permute-start(bf16[64,768]{1,0:T(8,128)(2,1)S(1)} %get-tuple-element.56), channel_id=1, source_target_pairs={{0,12},{1,13},{2,14},{3,15},{4,8},{5,9},{6,10},{7,11},{8,4},{9,5},... | collective-permute-start | bytes 294920 | tf_op jit(solution)/shard_map/ppermute | solution.py:156
  117.2 9.3 %collective-permute-start.28 = (bf16[64,768]{1,0:T(8,128)(2,1)S(1)}, bf16[64,768]{1,0:T(8,128)(2,1)S(1)}, u32[]{:S(2)}, u32[]{:S(2)}) collective-permute-start(bf16[64,768]{1,0:T(8,128)(2,1)S(1)} %get-tuple-element.57), channel_id=1, source_target_pairs={{0,8},{1,9},{2,10},{3,11},{4,12},{5,13},{6,14},{7,15},{8,0},{9,1},... | collective-permute-start | bytes 294920 | tf_op jit(solution)/shard_map/ppermute | solution.py:156
  121.3 6.9 %collective-permute-start.21 = (bf16[64,768]{1,0:T(8,128)(2,1)S(1)}, bf16[64,768]{1,0:T(8,128)(2,1)S(1)}, u32[]{:S(2)}, u32[]{:S(2)}) collective-permute-start(bf16[64,768]{1,0:T(8,128)(2,1)S(1)} %get-tuple-element.58), channel_id=1, source_target_pairs={{0,4},{1,5},{2,6},{3,7},{4,0},{5,1},{6,2},{7,3},{8,12},{9,13},{10,... | collective-permute-start | bytes 294920 | tf_op jit(solution)/shard_map/ppermute | solution.py:156
  123.0 7.8 %collective-permute-start.23 = (bf16[64,768]{1,0:T(8,128)(2,1)S(1)}, bf16[64,768]{1,0:T(8,128)(2,1)S(1)}, u32[]{:S(2)}, u32[]{:S(2)}) collective-permute-start(bf16[64,768]{1,0:T(8,128)(2,1)S(1)} %get-tuple-element.59), channel_id=1, source_target_pairs={{0,12},{1,13},{2,14},{3,15},{4,8},{5,9},{6,10},{7,11},{8,4},{9,5},... | collective-permute-start | bytes 294920 | tf_op jit(solution)/shard_map/ppermute | solution.py:156
  125.0 9.0 %collective-permute-start.22 = (bf16[64,768]{1,0:T(8,128)(2,1)S(1)}, bf16[64,768]{1,0:T(8,128)(2,1)S(1)}, u32[]{:S(2)}, u32[]{:S(2)}) collective-permute-start(bf16[64,768]{1,0:T(8,128)(2,1)S(1)} %get-tuple-element.60), channel_id=1, source_target_pairs={{0,8},{1,9},{2,10},{3,11},{4,12},{5,13},{6,14},{7,15},{8,0},{9,1},... | collective-permute-start | bytes 294920 | tf_op jit(solution)/shard_map/ppermute | solution.py:156
  (16 other events, 148.8 us)

commit v2 on v1

v2 whole, which is shorter than its diff:
```python
import functools

import jax
import jax.numpy as jnp
from jax import lax
from jax.experimental import pallas as pl
from jax.experimental.pallas import tpu as pltpu
from jax.sharding import PartitionSpec as P

HEADS = 12
BF16 = jnp.bfloat16
F32 = jnp.float32
NT = (((1,), (1,)), ((), ()))


def dot(a, b):
    return jnp.dot(a, b, preferred_element_type=F32)


def dot_nt(a, b):
    return lax.dot_general(a, b, NT, preferred_element_type=F32)


def low_lanes(shape):
    return lax.broadcasted_iota(jnp.int32, shape, 1) < shape[1] // 2


def keep_half(pair, half):
    low = low_lanes(pair.shape)
    return jnp.where(low if half == 0 else ~low, pair, jnp.zeros_like(pair))


def head_scores(key_pair, half, query_pair, dead):
    raw = dot_nt(keep_half(key_pair, half), query_pair)
    return jnp.where(dead, -jnp.inf, raw)


def forward_kernel(
    count_ref, q_ref, g_ref, key_ref, value_t_ref, numer_ref, max_ref, stat_ref, score_ref, weight_ref
):
    rows, width = q_ref.shape
    slots = key_ref.shape[0]
    head_dim = width // HEADS
    span = 2 * head_dim
    depth = score_ref.shape[0]
    dead = lax.broadcasted_iota(jnp.int32, (slots, rows), 0) >= count_ref[0]
    tops, totals = [None] * HEADS, [None] * HEADS

    def score(head):
        pair, half = divmod(head, 2)
        cols = slice(pair * span, (pair + 1) * span)
        score_ref[head % depth] = dot_nt(keep_half(key_ref[:, cols], half), q_ref[:, cols])

    def weigh(head):
        scores = jnp.where(dead, -jnp.inf, score_ref[head % depth])
        tops[head] = jnp.max(scores, axis=0, keepdims=True)
        weights = jnp.exp(scores - tops[head])
        totals[head] = jnp.sum(weights, axis=0, keepdims=True)
        weight_ref[head % depth] = weights.astype(BF16)

    def attend(head):
        pair, half = divmod(head, 2)
        at = slice(head * head_dim, (head + 1) * head_dim)
        numer = dot(value_t_ref[at, :], weight_ref[head % depth])
        numer_ref[at, :] = numer
        grad_t = g_ref[:, pair * span : (pair + 1) * span].astype(F32).T
        mine = grad_t[half * head_dim : (half + 1) * head_dim, :]
        inner = jnp.sum(mine * numer, axis=0, keepdims=True)
        max_ref[head : head + 1, :] = tops[head]
        stat_ref[head : head + 1, :] = tops[head] + jnp.log(totals[head])
        stat_ref[HEADS + head : HEADS + head + 1, :] = inner / totals[head]

    for step in range(HEADS + 2):
        if step < HEADS:
            score(step)
        if 0 <= step - 1 < HEADS:
            weigh(step - 1)
        if 0 <= step - 2:
            attend(step - 2)


def scale_kernel(numer_ref, max_ref, stat_ref, out_ref):
    width, rows = numer_ref.shape
    head_dim = width // HEADS
    for pair in range(HEADS // 2):
        parts = []
        for half in range(2):
            head = 2 * pair + half
            scale = jnp.exp(max_ref[head : head + 1, :] - stat_ref[head : head + 1, :])
            parts.append(numer_ref[head * head_dim : (head + 1) * head_dim, :] * scale)
        out_ref[:, 2 * pair * head_dim : 2 * (pair + 1) * head_dim] = (
            jnp.concatenate(parts, axis=0).T.astype(out_ref.dtype)
        )


def backward_kernel(first, last, count_ref, q_ref, g_ref, stat_ref, key_ref, key_t_ref, value_ref, *refs):
    if not first:
        gk_in_ref, gv_in_ref, *refs = refs
    gq_ref, gk_ref, gv_ref, score_ref, gw_ref, prob_ref, ds_ref = refs
    rows, width = q_ref.shape
    slots = key_ref.shape[0]
    head_dim = width // HEADS
    span = 2 * head_dim
    depth = score_ref.shape[0]
    dead = lax.broadcasted_iota(jnp.int32, (slots, rows), 0) >= count_ref[0]
    low = low_lanes((slots, span))
    gq, gk, gv = [None] * HEADS, [None] * HEADS, [None] * HEADS

    def score(head):
        pair, half = divmod(head, 2)
        cols = slice(pair * span, (pair + 1) * span)
        score_ref[head % depth] = dot_nt(keep_half(key_ref[:, cols], half), q_ref[:, cols])
        gw_ref[head % depth] = dot_nt(keep_half(value_ref[:, cols], half), g_ref[:, cols])

    def weigh(head):
        scores = jnp.where(dead, -jnp.inf, score_ref[head % depth])
        prob = jnp.exp(scores - stat_ref[head : head + 1, :])
        delta = stat_ref[HEADS + head : HEADS + head + 1, :]
        prob_ref[head % depth] = prob.astype(BF16)
        ds_ref[head % depth] = (prob * (gw_ref[head % depth] - delta)).astype(BF16)

    def collect(head):
        pair, half = divmod(head, 2)
        cols = slice(pair * span, (pair + 1) * span)
        gv[head] = dot(prob_ref[head % depth], g_ref[:, cols])
        gk[head] = dot(ds_ref[head % depth], q_ref[:, cols])
        gq[head] = dot(key_t_ref[head * head_dim : (head + 1) * head_dim, :], ds_ref[head % depth])
        if half == 0:
            return
        gq_ref[:, cols] = jnp.concatenate(gq[head - 1 : head + 1], axis=0).T.astype(gq_ref.dtype)
        gk_sum = jnp.where(low, gk[head - 1], gk[head])
        gv_sum = jnp.where(low, gv[head - 1], gv[head])
        if not first:
            gk_sum += gk_in_ref[:, cols]
            gv_sum += gv_in_ref[:, cols]
        if last:
            gk_sum *= 0.125
        gk_ref[:, cols] = gk_sum.astype(gk_ref.dtype)
        gv_ref[:, cols] = gv_sum.astype(gv_ref.dtype)

    for step in range(HEADS + 2):
        if 0 <= step - 2:
            collect(step - 2)
        if 0 <= step - 1 < HEADS:
            weigh(step - 1)
        if step < HEADS:
            score(step)


def after(array, *others):
    return lax.optimization_barrier((array, *others))[0]


def call(kernel, ins, out_shapes, scratch=(), flops=0, exps=0):
    vmem = pl.BlockSpec(memory_space=pltpu.VMEM)
    smem = pl.BlockSpec(memory_space=pltpu.SMEM)
    specs = [smem if a.dtype == jnp.int32 else vmem for a in ins]
    moved = sum(a.size * a.dtype.itemsize for a in list(ins) + list(out_shapes))
    return pl.pallas_call(
        kernel,
        in_specs=specs,
        out_specs=[vmem] * len(out_shapes),
        out_shape=out_shapes,
        scratch_shapes=scratch,
        compiler_params=pltpu.CompilerParams(vmem_limit_bytes=40 << 20),
        cost_estimate=pl.CostEstimate(flops=flops, transcendentals=exps, bytes_accessed=moved),
    )(*ins)


def body(size, latents, points, counts, w_query, w_key, w_value, w_out, d_out):
    own, width = latents.shape
    slots = points.shape[0]
    shape = jax.ShapeDtypeStruct
    direct = [0, size // 4, size // 2, size // 4 + size // 2]
    middle = []
    bit = size // 8
    while bit >= 4:
        middle.append(bit)
        bit //= 2

    def swap(array, mask):
        return lax.ppermute(array, "pts", [(i, i ^ mask) for i in range(size)])

    query_own = dot(latents, w_query).astype(BF16)
    grad_own = dot(d_out, w_out.T).astype(BF16)

    def near_of(block, came):
        near = jnp.concatenate([block] + came, axis=0)
        for mask in middle:
            near = jnp.concatenate([near, swap(near, mask)], axis=0)
        return near

    came_q = [swap(query_own, m) for m in direct[1:]]
    grad_own = after(grad_own, came_q[0])
    came_g = [swap(grad_own, m) for m in direct[1:]]
    keys = dot(points, w_key).astype(BF16) * jnp.asarray(0.125, BF16)
    values = dot(points, w_value).astype(BF16)
    keys_t = keys.T
    values_t = values.T
    came_q[2] = after(came_q[2], keys, values_t)
    near_q = near_of(query_own, came_q)
    near_g = near_of(grad_own, came_g)
    query = [near_q, swap(near_q, 2), swap(near_q, 1)]
    grad = [near_g, swap(near_g, 2), swap(near_g, 1)]
    rows = query[0].shape[0]
    work = 2 * rows * slots * width

    def forward(i):
        return call(
            forward_kernel,
            [counts, query[i], grad[i], keys, values_t],
            [shape((width, rows), F32), shape((HEADS, rows), F32), shape((2 * HEADS, rows), F32)],
            [pltpu.VMEM((3, slots, rows), F32), pltpu.VMEM((3, slots, rows), BF16)],
            flops=8 * work,
            exps=rows * slots * HEADS,
        )

    numer, tops, stats = [None] * 4, [None] * 4, [None] * 4
    for i in (0, 2):
        numer[i], tops[i], stats[i] = forward(i)
    query[1] = after(query[1], stats[0])
    grad[1] = after(grad[1], stats[2])
    query.append(swap(query[1], 1))
    grad.append(swap(grad[1], 1))
    for i in (1, 3):
        numer[i], tops[i], stats[i] = forward(i)

    def merge(*parts):
        lse = [p[:HEADS] for p in parts]
        top = functools.reduce(jnp.maximum, lse)
        scale = [jnp.exp(x - top) for x in lse]
        total = sum(scale)
        delta = sum(s * p[HEADS:] for s, p in zip(scale, parts)) / total
        return jnp.concatenate([top + jnp.log(total), delta], axis=0)

    came = swap(jnp.stack([stats[2], stats[3]]), 1)
    mine = merge(stats[0], came[0])
    other = merge(stats[1], came[1])
    mine = merge(mine, swap(other, 2))
    for mask in reversed(middle):
        half = mine.shape[1] // 2
        mine = merge(mine[:, :half], swap(mine[:, half:], mask))
    quarter = mine.shape[1] // 4

    def turned(array, p):
        blocks = [array[:, t * quarter : (t + 1) * quarter] for t in range(4)]
        return jnp.concatenate([blocks[t ^ p] for t in range(4)], axis=1)

    mine = merge(mine, *[turned(swap(mine, direct[p]), p) for p in range(1, 4)])
    for mask in middle:
        mine = jnp.concatenate([mine, swap(mine, mask)], axis=1)
    both = jnp.stack([mine, swap(mine, 2)])
    far = swap(both, 1)
    final = [both[0], both[1], far[0], far[1]]

    def scaled(i, dtype):
        return call(scale_kernel, [numer[i], tops[i], final[i]], [shape((rows, width), dtype)])[0]

    def add(array, came):
        return array + came.astype(F32)

    def inner_sums(near, across):
        summed = add(near, across)
        for mask in reversed(middle):
            half = summed.shape[0] // 2
            summed = add(summed[:half], swap(summed[half:].astype(BF16), mask))
        out = [summed[p * own : (p + 1) * own] for p in range(4)]
        return [out[0]] + [x.astype(BF16) for x in out[1:]]

    def outer_sum(blocks):
        out = blocks[0]
        for p in range(1, 4):
            out = add(out, swap(blocks[p], direct[p]))
        return out

    def backward(i, sums, dtype, behind=(), last=False):
        kind = BF16 if last else F32
        outs = [shape((rows, width), dtype), shape((slots, width), kind), shape((slots, width), kind)]
        stat = after(final[i], *behind)
        gq, gk, gv = call(
            functools.partial(backward_kernel, not sums, last),
            [counts, query[i], grad[i], stat, keys, keys_t, values] + sums,
            outs,
            [pltpu.VMEM((2, slots, rows), F32)] * 2 + [pltpu.VMEM((2, slots, rows), BF16)] * 2,
            flops=14 * work,
            exps=rows * slots * HEADS,
        )
        return gq, [gk, gv]

    near_0, near_1 = scaled(0, F32), scaled(1, F32)
    sent_a = swap(jnp.concatenate([scaled(2, BF16), scaled(3, BF16)], axis=0), 1)
    gq_3, sums = backward(3, [], BF16, [near_0, near_1])
    sent_3 = swap(gq_3, 1)
    across_a = add(near_1, sent_a[rows:]).astype(BF16)
    came_a = swap(across_a, 2)
    gq_1, sums = backward(1, sums, F32, [across_a])
    across = add(gq_1, sent_3).astype(BF16)
    came = swap(across, 2)
    blocks_a = inner_sums(add(near_0, sent_a[:rows]), came_a)
    gq_2, sums = backward(2, sums, BF16, [across, blocks_a[3]])
    sent_2 = swap(gq_2, 1)
    gq_0, sums = backward(0, sums, F32, last=True)
    attended = outer_sum(blocks_a).astype(BF16)
    result = (latents.astype(F32) + dot(attended, w_out)).astype(BF16)
    grad_query = outer_sum(inner_sums(add(gq_0, sent_2), came))
    d_latents = (d_out.astype(F32) + dot(grad_query.astype(BF16), w_query.T)).astype(BF16)
    d_points = (dot(sums[0], w_key.T) + dot(sums[1], w_value.T)).astype(BF16)
    return (result, d_latents, d_points)


def solution(mesh):
    part = P(("groups", "pts"), None)
    in_specs = (part, part, P(("groups", "pts")), P(), P(), P(), P(), part)
    return jax.shard_map(
        functools.partial(body, mesh.shape["pts"]),
        mesh=mesh,
        in_specs=in_specs,
        out_specs=(part, part, part),
        check_vma=False,
    )
```

time: 135 us -> 110 us (0.81)
  Pallas kernels: 44.4 us -> 29.5 us
  waiting for transfers between devices: 39.9 us -> 32.8 us
  starting transfers between devices: 36.1 us -> 32.1 us
  local copies, waits for them, and re-layouts: 1.39 us -> 4.38 us
    pallas_call x12, Pallas kernels: 44.4 us -> 29.5 us  [call(): pl.pallas_call(kernel, in_specs=specs, out_specs=[vmem] * len(out_shapes)...]
    ppermute x30, waiting for transfers between devices: 39.9 us -> 32.8 us  [swap(): return lax.ppermute(array, 'pts', [(i, i ^ mask) for i in range(size)])]
    ppermute x30, starting transfers between devices: 36.1 us -> 32.1 us  [swap(): return lax.ppermute(array, 'pts', [(i, i ^ mask) for i in range(size)])]
    unnamed x20 -> x23, local copies, waits for them, and re-layouts: 0.64 us -> 2.99 us
  transfers between devices with their start and end apart: 30 -> 30, of which waited for: 15 -> 14; matrix products, arithmetic and copies ran while one was open for 7% -> 9% of each run, Pallas kernels for 29% -> 24%
where the time goes in v2:
time: 110 us
  waiting for transfers between devices  32.8 us (30%)
  starting transfers between devices  32.1 us (29%)
  Pallas kernels  29.5 us (27%)
  matrix products  8 us (7%)
  local copies, waits for them, and re-layouts  4.38 us (4%)
  between operations  1.68 us (2%)
  other arithmetic  1.44 us (1%)
    ppermute x30, waiting for transfers between devices, swap(): return lax.ppermute(array, 'pts', [(i, i ^ mask) for i in range(size)])  32.8 us
    ppermute x30, starting transfers between devices, swap(): return lax.ppermute(array, 'pts', [(i, i ^ mask) for i in range(size)])  32.1 us
    pallas_call x12, Pallas kernels, call(): pl.pallas_call(kernel, in_specs=specs, out_specs=[vmem] * len(out_shapes)...  29.5 us
    dot_general x8, matrix products, dot(): return jnp.dot(a, b, preferred_element_type=F32)  8 us
    unnamed x23, local copies, waits for them, and re-layouts  2.99 us
  transfers between devices with their start and end apart: 30, of which 14 were waited for; matrix products, arithmetic and copies ran while one was open for 9% of the time, Pallas kernels for 24%

profile of v2, /device:TPU:0, one launch (start us, length us, event | category | flops | bytes accessed | tf_op | source)
XLA Modules:
  0.0 109.8 jit_solution(12231427325678854502)
XLA Ops:
  0.7 1.8 %convolution_convert_fusion.3 = bf16[64,768]{1,0:T(8,128)(2,1)S(1)} fusion(bf16[64,768]{1,0:T(8,128)(2,1)} %param.8, bf16[768,768]{1,0:T(8,128)(2,1)} %param.11), kind=kOutput, calls=%fused_computation.8 | convolution fusion | flops 75546624 | bytes 1376256 | tf_op jit(solution)/shard_map/dot_general | solution.py:17
  2.5 5.1 %collective-permute-start.2 = (bf16[64,768]{1,0:T(8,128)(2,1)S(1)}, bf16[64,768]{1,0:T(8,128)(2,1)S(1)}, u32[]{:S(2)}, u32[]{:S(2)}) collective-permute-start(bf16[64,768]{1,0:T(8,128)(2,1)S(1)} %convolution_convert_fusion.3), channel_id=1, source_target_pairs={{0,12},{1,13},{2,14},{3,15},{4,8},{5,9},{6,10},{7,11},{8,4},{9,5},... | collective-permute-start | bytes 294920 | tf_op jit(solution)/shard_map/ppermute | solution.py:182
  10.6 3.2 %collective-permute-done = bf16[64,768]{1,0:T(8,128)(2,1)S(1)} collective-permute-done((bf16[64,768]{1,0:T(8,128)(2,1)S(1)}, bf16[64,768]{1,0:T(8,128)(2,1)S(1)}, u32[]{:S(2)}, u32[]{:S(2)}) %collective-permute-start) | collective-permute-done | bytes 98336 | tf_op jit(solution)/shard_map/ppermute | solution.py:182
  13.9 2.6 %collective-permute-start.5 = (bf16[64,768]{1,0:T(8,128)(2,1)S(1)}, bf16[64,768]{1,0:T(8,128)(2,1)S(1)}, u32[]{:S(2)}, u32[]{:S(2)}) collective-permute-start(bf16[64,768]{1,0:T(8,128)(2,1)S(1)} %convolution_convert_fusion.2), channel_id=1, source_target_pairs={{0,12},{1,13},{2,14},{3,15},{4,8},{5,9},{6,10},{7,11},{8,4},{9,5},... | collective-permute-start | bytes 294920 | tf_op jit(solution)/shard_map/ppermute | solution.py:182
  23.3 2.4 %collective-permute-done.4 = bf16[64,768]{1,0:T(8,128)(2,1)S(1)} collective-permute-done((bf16[64,768]{1,0:T(8,128)(2,1)S(1)}, bf16[64,768]{1,0:T(8,128)(2,1)S(1)}, u32[]{:S(2)}, u32[]{:S(2)}) %collective-permute-start.4) | collective-permute-done | bytes 98336 | tf_op jit(solution)/shard_map/ppermute | solution.py:182
  29.7 3.4 %shard_map.103 = (f32[768,256]{1,0:T(8,128)S(1)}, f32[12,256]{1,0:T(8,128)S(1)}, f32[24,256]{1,0:T(8,128)S(1)}) custom-call(s32[1]{0:T(128)S(6)} %copy.28.count_ref, bf16[256,768]{1,0:T(8,128)(2,1)} %pad_maximum_fusion.1.q_ref, bf16[256,768]{1,0:T(8,128)(2,1)} %constant_dynamic-update-slice_fusion.g_ref, bf16[384,768]{1,0:T(8,128)(2,1)S(1)} %copy.12.key_ref, ...), custom_call_target="tpu_custom_call" | custom-call | flops 1207959552 | bytes 2789380 | tf_op jit(solution)/shard_map/pallas_call | solution.py:159
  33.4 3.4 %shard_map.104 = (f32[768,256]{1,0:T(8,128)S(1)}, f32[12,256]{1,0:T(8,128)S(1)}, f32[24,256]{1,0:T(8,128)S(1)}) custom-call(s32[1]{0:T(128)S(6)} %copy.28.count_ref, bf16[256,768]{1,0:T(8,128)(2,1)} %collective-permute-done.6.q_ref, bf16[256,768]{1,0:T(8,128)(2,1)} %collective-permute-done.7.g_ref, bf16[384,768]{1,0:T(8,128)(2,1)S(1)} %copy.12.key_ref, ...), custom_call_target="tpu_custom_call" | custom-call | flops 1207959552 | bytes 2789380 | tf_op jit(solution)/shard_map/pallas_call | solution.py:159
  36.8 2.1 %collective-permute-done.10.g_ref = bf16[256,768]{1,0:T(8,128)(2,1)} collective-permute-done((bf16[256,768]{1,0:T(8,128)(2,1)}, bf16[256,768]{1,0:T(8,128)(2,1)}, u32[]{:S(2)}, u32[]{:S(2)}) %collective-permute-start.10) | collective-permute-done | bytes 393248 | tf_op jit(solution)/shard_map/ppermute | solution.py:182
  38.8 1.9 %collective-permute-done.11.g_ref = bf16[256,768]{1,0:T(8,128)(2,1)S(1)} collective-permute-done((bf16[256,768]{1,0:T(8,128)(2,1)}, bf16[256,768]{1,0:T(8,128)(2,1)S(1)}, u32[]{:S(2)}, u32[]{:S(2)}) %collective-permute-start.11) | collective-permute-done | bytes 393248 | tf_op jit(solution)/shard_map/ppermute | solution.py:182
  40.8 2.3 %shard_map.105 = (f32[768,256]{1,0:T(8,128)S(1)}, f32[12,256]{1,0:T(8,128)S(1)}, f32[24,256]{1,0:T(8,128)S(1)}) custom-call(s32[1]{0:T(128)S(6)} %copy.28.count_ref, bf16[256,768]{1,0:T(8,128)(2,1)S(1)} %collective-permute-done.9.q_ref, bf16[256,768]{1,0:T(8,128)(2,1)S(1)} %collective-permute-done.11.g_ref, bf16[384,768]{1,0:T(8,128)(2,1)S(1)} %copy.12.key_ref, ...), custom_call_target="tpu_custom_call" | custom-call | flops 1207959552 | bytes 2789380 | tf_op jit(solution)/shard_map/pallas_call | solution.py:159
  43.3 3.4 %shard_map.106 = (f32[768,256]{1,0:T(8,128)S(1)}, f32[12,256]{1,0:T(8,128)S(1)}, f32[24,256]{1,0:T(8,128)S(1)}) custom-call(s32[1]{0:T(128)S(6)} %copy.28.count_ref, bf16[256,768]{1,0:T(8,128)(2,1)} %collective-permute-done.8.q_ref, bf16[256,768]{1,0:T(8,128)(2,1)} %collective-permute-done.10.g_ref, bf16[384,768]{1,0:T(8,128)(2,1)S(1)} %copy.12.key_ref, ...), custom_call_target="tpu_custom_call" | custom-call | flops 1207959552 | bytes 2789380 | tf_op jit(solution)/shard_map/pallas_call | solution.py:159
  48.3 2.3 %collective-permute-done.13 = f32[24,256]{1,0:T(8,128)S(1)} collective-permute-done((f32[24,256]{1,0:T(8,128)S(1)}, f32[24,256]{1,0:T(8,128)S(1)}, u32[]{:S(2)}, u32[]{:S(2)}) %collective-permute-start.13) | collective-permute-done | bytes 24608 | tf_op jit(solution)/shard_map/ppermute | solution.py:182
  50.7 1.7 %collective-permute-start.16 = (f32[24,256]{1,0:T(8,128)S(1)}, f32[24,256]{1,0:T(8,128)S(1)}, u32[]{:S(2)}, u32[]{:S(2)}) collective-permute-start(f32[24,256]{1,0:T(8,128)S(1)} %pad_maximum_fusion.5), channel_id=1, source_target_pairs={{0,12},{1,13},{2,14},{3,15},{4,8},{5,9},{6,10},{7,11},{8,4},{9,5},... | collective-permute-start | bytes 73736 | tf_op jit(solution)/shard_map/ppermute | solution.py:182
  52.4 2.8 %collective-permute-start.14 = (f32[24,256]{1,0:T(8,128)S(1)}, f32[24,256]{1,0:T(8,128)S(1)}, u32[]{:S(2)}, u32[]{:S(2)}) collective-permute-start(f32[24,256]{1,0:T(8,128)S(1)} %pad_maximum_fusion.5), channel_id=1, source_target_pairs={{0,4},{1,5},{2,6},{3,7},{4,0},{5,1},{6,2},{7,3},{8,12},{9,13},{10,... | collective-permute-start | bytes 73736 | tf_op jit(solution)/shard_map/ppermute | solution.py:182
  59.0 2.3 %collective-permute-done.17.stat_ref = f32[24,256]{1,0:T(8,128)S(1)} collective-permute-done((f32[24,256]{1,0:T(8,128)S(1)}, f32[24,256]{1,0:T(8,128)S(1)}, u32[]{:S(2)}, u32[]{:S(2)}) %collective-permute-start.17) | collective-permute-done | bytes 24608 | tf_op jit(solution)/shard_map/ppermute | solution.py:182
  63.8 3.1 %shard_map.111 = (bf16[256,768]{1,0:T(8,128)(2,1)S(1)}, f32[384,768]{1,0:T(8,128)S(1)}, f32[384,768]{1,0:T(8,128)S(1)}) custom-call(s32[1]{0:T(128)S(6)} %copy.28.count_ref, bf16[256,768]{1,0:T(8,128)(2,1)S(1)} %collective-permute-done.9.q_ref, bf16[256,768]{1,0:T(8,128)(2,1)S(1)} %collective-permute-done.11.g_ref, ...), custom_call_target="tpu_custom_call" | custom-call | flops 2113929216 | bytes 5332996 | tf_op jit(solution)/shard_map/pallas_call | solution.py:159
  69.0 4.3 %shard_map.112 = (f32[256,768]{1,0:T(8,128)S(1)}, f32[384,768]{1,0:T(8,128)S(1)}, f32[384,768]{1,0:T(8,128)S(1)}) custom-call(s32[1]{0:T(128)S(6)} %copy.28.count_ref, bf16[256,768]{1,0:T(8,128)(2,1)} %collective-permute-done.8.q_ref, bf16[256,768]{1,0:T(8,128)(2,1)} %collective-permute-done.10.g_ref, f32[24,256]{1,0:T(8,128)S(1)} %collective-permute-done.17.stat_ref, ...), custom_call_target="tpu_custom_call" | custom-call | flops 2113929216 | bytes 8085508 | tf_op jit(solution)/shard_map/pallas_call | solution.py:159
  74.0 5.5 %collective-permute-done.20 = bf16[256,768]{1,0:T(8,128)(2,1)S(1)} collective-permute-done((bf16[256,768]{1,0:T(8,128)(2,1)S(1)}, bf16[256,768]{1,0:T(8,128)(2,1)S(1)}, u32[]{:S(2)}, u32[]{:S(2)}) %collective-permute-start.20) | collective-permute-done | bytes 393248 | tf_op jit(solution)/shard_map/ppermute | solution.py:182
  79.6 2.0 %collective-permute-start.23 = (bf16[64,768]{1,0:T(8,128)(2,1)S(1)}, bf16[64,768]{1,0:T(8,128)(2,1)S(1)}, u32[]{:S(2)}, u32[]{:S(2)}) collective-permute-start(bf16[64,768]{1,0:T(8,128)(2,1)S(1)} %get-tuple-element.73), channel_id=1, source_target_pairs={{0,12},{1,13},{2,14},{3,15},{4,8},{5,9},{6,10},{7,11},{8,4},{9,5},... | collective-permute-start | bytes 294920 | tf_op jit(solution)/shard_map/ppermute | solution.py:182
  82.2 1.9 %collective-permute-start.22 = (bf16[64,768]{1,0:T(8,128)(2,1)S(1)}, bf16[64,768]{1,0:T(8,128)(2,1)S(1)}, u32[]{:S(2)}, u32[]{:S(2)}) collective-permute-start(bf16[64,768]{1,0:T(8,128)(2,1)S(1)} %get-tuple-element.74), channel_id=1, source_target_pairs={{0,8},{1,9},{2,10},{3,11},{4,12},{5,13},{6,14},{7,15},{8,0},{9,1},... | collective-permute-start | bytes 294920 | tf_op jit(solution)/shard_map/ppermute | solution.py:182
  84.1 4.2 %shard_map.113 = (bf16[256,768]{1,0:T(8,128)(2,1)S(1)}, f32[384,768]{1,0:T(8,128)S(1)}, f32[384,768]{1,0:T(8,128)S(1)}) custom-call(s32[1]{0:T(128)S(6)} %copy.28.count_ref, bf16[256,768]{1,0:T(8,128)(2,1)} %collective-permute-done.6.q_ref, bf16[256,768]{1,0:T(8,128)(2,1)} %collective-permute-done.7.g_ref, f32[24,256]{1,0:T(8,128)S(1)} %get-tuple-element.56.stat_ref, ...), custom_call_target="tpu_custom_call" | custom-call | flops 2113929216 | bytes 7692292 | tf_op jit(solution)/shard_map/pallas_call | solution.py:159
  88.4 4.5 %shard_map.114 = (f32[256,768]{1,0:T(8,128)S(1)}, bf16[384,768]{1,0:T(8,128)(2,1)S(1)}, bf16[384,768]{1,0:T(8,128)(2,1)S(1)}) custom-call(s32[1]{0:T(128)S(6)} %copy.28.count_ref, bf16[256,768]{1,0:T(8,128)(2,1)} %pad_maximum_fusion.1.q_ref, bf16[256,768]{1,0:T(8,128)(2,1)} %constant_dynamic-update-slice_fusion.g_ref, ...), custom_call_target="tpu_custom_call" | custom-call | flops 2113929216 | bytes 6905860 | tf_op jit(solution)/shard_map/pallas_call | solution.py:159
  101.2 3.2 %collective-permute-done.29 = bf16[64,768]{1,0:T(8,128)(2,1)S(1)} collective-permute-done((bf16[64,768]{1,0:T(8,128)(2,1)S(1)}, bf16[64,768]{1,0:T(8,128)(2,1)S(1)}, u32[]{:S(2)}, u32[]{:S(2)}) %collective-permute-start.29) | collective-permute-done | bytes 98336 | tf_op jit(solution)/shard_map/ppermute | solution.py:182
  104.4 4.3 %collective-permute-done.28 = bf16[64,768]{1,0:T(8,128)(2,1)S(1)} collective-permute-done((bf16[64,768]{1,0:T(8,128)(2,1)S(1)}, bf16[64,768]{1,0:T(8,128)(2,1)S(1)}, u32[]{:S(2)}, u32[]{:S(2)}) %collective-permute-start.28) | collective-permute-done | bytes 98336 | tf_op jit(solution)/shard_map/ppermute | solution.py:182
  (104 shorter events, 34.4 us)
Async XLA Ops:
  2.5 15.8 %collective-permute-start.2 = (bf16[64,768]{1,0:T(8,128)(2,1)S(1)}, bf16[64,768]{1,0:T(8,128)(2,1)S(1)}, u32[]{:S(2)}, u32[]{:S(2)}) collective-permute-start(bf16[64,768]{1,0:T(8,128)(2,1)S(1)} %convolution_convert_fusion.3), channel_id=1, source_target_pairs={{0,12},{1,13},{2,14},{3,15},{4,8},{5,9},{6,10},{7,11},{8,4},{9,5},... | collective-permute-start | bytes 294920 | tf_op jit(solution)/shard_map/ppermute | solution.py:182
  7.6 10.7 %collective-permute-start.1 = (bf16[64,768]{1,0:T(8,128)(2,1)S(1)}, bf16[64,768]{1,0:T(8,128)(2,1)S(1)}, u32[]{:S(2)}, u32[]{:S(2)}) collective-permute-start(bf16[64,768]{1,0:T(8,128)(2,1)S(1)} %convolution_convert_fusion.3), channel_id=1, source_target_pairs={{0,8},{1,9},{2,10},{3,11},{4,12},{5,13},{6,14},{7,15},{8,0},{9,1},... | collective-permute-start | bytes 294920 | tf_op jit(solution)/shard_map/ppermute | solution.py:182
  7.6 6.3 %collective-permute-start = (bf16[64,768]{1,0:T(8,128)(2,1)S(1)}, bf16[64,768]{1,0:T(8,128)(2,1)S(1)}, u32[]{:S(2)}, u32[]{:S(2)}) collective-permute-start(bf16[64,768]{1,0:T(8,128)(2,1)S(1)} %convolution_convert_fusion.3), channel_id=1, source_target_pairs={{0,4},{1,5},{2,6},{3,7},{4,0},{5,1},{6,2},{7,3},{8,12},{9,13},{10,... | collective-permute-start | bytes 294920 | tf_op jit(solution)/shard_map/ppermute | solution.py:182
  13.9 12.5 %collective-permute-start.5 = (bf16[64,768]{1,0:T(8,128)(2,1)S(1)}, bf16[64,768]{1,0:T(8,128)(2,1)S(1)}, u32[]{:S(2)}, u32[]{:S(2)}) collective-permute-start(bf16[64,768]{1,0:T(8,128)(2,1)S(1)} %convolution_convert_fusion.2), channel_id=1, source_target_pairs={{0,12},{1,13},{2,14},{3,15},{4,8},{5,9},{6,10},{7,11},{8,4},{9,5},... | collective-permute-start | bytes 294920 | tf_op jit(solution)/shard_map/ppermute | solution.py:182
  16.5 9.3 %collective-permute-start.4 = (bf16[64,768]{1,0:T(8,128)(2,1)S(1)}, bf16[64,768]{1,0:T(8,128)(2,1)S(1)}, u32[]{:S(2)}, u32[]{:S(2)}) collective-permute-start(bf16[64,768]{1,0:T(8,128)(2,1)S(1)} %convolution_convert_fusion.2), channel_id=1, source_target_pairs={{0,8},{1,9},{2,10},{3,11},{4,12},{5,13},{6,14},{7,15},{8,0},{9,1},... | collective-permute-start | bytes 294920 | tf_op jit(solution)/shard_map/ppermute | solution.py:182
  17.8 4.8 %collective-permute-start.3 = (bf16[64,768]{1,0:T(8,128)(2,1)S(1)}, bf16[64,768]{1,0:T(8,128)(2,1)S(1)}, u32[]{:S(2)}, u32[]{:S(2)}) collective-permute-start(bf16[64,768]{1,0:T(8,128)(2,1)S(1)} %convolution_convert_fusion.2), channel_id=1, source_target_pairs={{0,4},{1,5},{2,6},{3,7},{4,0},{5,1},{6,2},{7,3},{8,12},{9,13},{10,... | collective-permute-start | bytes 294920 | tf_op jit(solution)/shard_map/ppermute | solution.py:182
  19.1 14.0 %collective-permute-start.8 = (bf16[256,768]{1,0:T(8,128)(2,1)}, bf16[256,768]{1,0:T(8,128)(2,1)}, u32[]{:S(2)}, u32[]{:S(2)}) collective-permute-start(bf16[256,768]{1,0:T(8,128)(2,1)} %pad_maximum_fusion.1.q_ref), channel_id=1, source_target_pairs={{0,2},{1,3},{2,0},{3,1},{4,6},{5,7},{6,4},{7,5},{8,10},{9,11},{10,... | collective-permute-start | bytes 1179656 | tf_op jit(solution)/shard_map/ppermute | solution.py:182
  20.5 12.8 %collective-permute-start.6 = (bf16[256,768]{1,0:T(8,128)(2,1)}, bf16[256,768]{1,0:T(8,128)(2,1)}, u32[]{:S(2)}, u32[]{:S(2)}) collective-permute-start(bf16[256,768]{1,0:T(8,128)(2,1)} %pad_maximum_fusion.1.q_ref), channel_id=1, source_target_pairs={{0,1},{1,0},{2,3},{3,2},{4,5},{5,4},{6,7},{7,6},{8,9},{9,8},{10,11... | collective-permute-start | bytes 1179656 | tf_op jit(solution)/shard_map/ppermute | solution.py:182
  27.0 6.4 %collective-permute-start.7 = (bf16[256,768]{1,0:T(8,128)(2,1)}, bf16[256,768]{1,0:T(8,128)(2,1)}, u32[]{:S(2)}, u32[]{:S(2)}) collective-permute-start(bf16[256,768]{1,0:T(8,128)(2,1)} %constant_dynamic-update-slice_fusion.g_ref), channel_id=1, source_target_pairs={{0,1},{1,0},{2,3},{3,2},{4,5},{5,4},{6,7},{7,6},{8,9},{9,8},{10,11... | collective-permute-start | bytes 1179656 | tf_op jit(solution)/shard_map/ppermute | solution.py:182
  27.0 11.8 %collective-permute-start.10 = (bf16[256,768]{1,0:T(8,128)(2,1)}, bf16[256,768]{1,0:T(8,128)(2,1)}, u32[]{:S(2)}, u32[]{:S(2)}) collective-permute-start(bf16[256,768]{1,0:T(8,128)(2,1)} %constant_dynamic-update-slice_fusion.g_ref), channel_id=1, source_target_pairs={{0,2},{1,3},{2,0},{3,1},{4,6},{5,7},{6,4},{7,5},{8,10},{9,11},{10,... | collective-permute-start | bytes 1179656 | tf_op jit(solution)/shard_map/ppermute | solution.py:182
  33.1 5.7 %collective-permute-start.9 = (bf16[256,768]{1,0:T(8,128)(2,1)}, bf16[256,768]{1,0:T(8,128)(2,1)S(1)}, u32[]{:S(2)}, u32[]{:S(2)}) collective-permute-start(bf16[256,768]{1,0:T(8,128)(2,1)} %collective-permute-done.8.q_ref), channel_id=1, source_target_pairs={{0,1},{1,0},{2,3},{3,2},{4,5},{5,4},{6,7},{7,6},{8,9},{9,8},{10,11... | collective-permute-start | bytes 1179656 | tf_op jit(solution)/shard_map/ppermute | solution.py:182
  50.7 5.8 %collective-permute-start.16 = (f32[24,256]{1,0:T(8,128)S(1)}, f32[24,256]{1,0:T(8,128)S(1)}, u32[]{:S(2)}, u32[]{:S(2)}) collective-permute-start(f32[24,256]{1,0:T(8,128)S(1)} %pad_maximum_fusion.5), channel_id=1, source_target_pairs={{0,12},{1,13},{2,14},{3,15},{4,8},{5,9},{6,10},{7,11},{8,4},{9,5},... | collective-permute-start | bytes 73736 | tf_op jit(solution)/shard_map/ppermute | solution.py:182
  52.4 5.0 %collective-permute-start.15 = (f32[24,256]{1,0:T(8,128)S(1)}, f32[24,256]{1,0:T(8,128)S(1)}, u32[]{:S(2)}, u32[]{:S(2)}) collective-permute-start(f32[24,256]{1,0:T(8,128)S(1)} %pad_maximum_fusion.5), channel_id=1, source_target_pairs={{0,8},{1,9},{2,10},{3,11},{4,12},{5,13},{6,14},{7,15},{8,0},{9,1},... | collective-permute-start | bytes 73736 | tf_op jit(solution)/shard_map/ppermute | solution.py:182
  52.4 4.9 %collective-permute-start.14 = (f32[24,256]{1,0:T(8,128)S(1)}, f32[24,256]{1,0:T(8,128)S(1)}, u32[]{:S(2)}, u32[]{:S(2)}) collective-permute-start(f32[24,256]{1,0:T(8,128)S(1)} %pad_maximum_fusion.5), channel_id=1, source_target_pairs={{0,4},{1,5},{2,6},{3,7},{4,0},{5,1},{6,2},{7,3},{8,12},{9,13},{10,... | collective-permute-start | bytes 73736 | tf_op jit(solution)/shard_map/ppermute | solution.py:182
  67.0 6.3 %collective-permute-start.24 = (bf16[256,768]{1,0:T(8,128)(2,1)S(1)}, bf16[256,768]{1,0:T(8,128)(2,1)S(1)}, u32[]{:S(2)}, u32[]{:S(2)}) collective-permute-start(bf16[256,768]{1,0:T(8,128)(2,1)S(1)} %get-tuple-element.55), channel_id=1, source_target_pairs={{0,1},{1,0},{2,3},{3,2},{4,5},{5,4},{6,7},{7,6},{8,9},{9,8},{10,11... | collective-permute-start | bytes 1179656 | tf_op jit(solution)/shard_map/ppermute | solution.py:182
  67.5 12.0 %collective-permute-start.20 = (bf16[256,768]{1,0:T(8,128)(2,1)S(1)}, bf16[256,768]{1,0:T(8,128)(2,1)S(1)}, u32[]{:S(2)}, u32[]{:S(2)}) collective-permute-start(bf16[256,768]{1,0:T(8,128)(2,1)S(1)} %add_convert_fusion.1), channel_id=1, source_target_pairs={{0,2},{1,3},{2,0},{3,1},{4,6},{5,7},{6,4},{7,5},{8,10},{9,11},{10,... | collective-permute-start | bytes 1179656 | tf_op jit(solution)/shard_map/ppermute | solution.py:182
  73.4 22.3 %collective-permute-start.26 = (bf16[256,768]{1,0:T(8,128)(2,1)S(1)}, bf16[256,768]{1,0:T(8,128)(2,1)S(1)}, u32[]{:S(2)}, u32[]{:S(2)}) collective-permute-start(bf16[256,768]{1,0:T(8,128)(2,1)S(1)} %add_convert_fusion), channel_id=1, source_target_pairs={{0,2},{1,3},{2,0},{3,1},{4,6},{5,7},{6,4},{7,5},{8,10},{9,11},{10,... | collective-permute-start | bytes 1179656 | tf_op jit(solution)/shard_map/ppermute | solution.py:182
  79.6 19.8 %collective-permute-start.23 = (bf16[64,768]{1,0:T(8,128)(2,1)S(1)}, bf16[64,768]{1,0:T(8,128)(2,1)S(1)}, u32[]{:S(2)}, u32[]{:S(2)}) collective-permute-start(bf16[64,768]{1,0:T(8,128)(2,1)S(1)} %get-tuple-element.73), channel_id=1, source_target_pairs={{0,12},{1,13},{2,14},{3,15},{4,8},{5,9},{6,10},{7,11},{8,4},{9,5},... | collective-permute-start | bytes 294920 | tf_op jit(solution)/shard_map/ppermute | solution.py:182
  81.6 16.8 %collective-permute-start.21 = (bf16[64,768]{1,0:T(8,128)(2,1)S(1)}, bf16[64,768]{1,0:T(8,128)(2,1)S(1)}, u32[]{:S(2)}, u32[]{:S(2)}) collective-permute-start(bf16[64,768]{1,0:T(8,128)(2,1)S(1)} %get-tuple-element.72), channel_id=1, source_target_pairs={{0,4},{1,5},{2,6},{3,7},{4,0},{5,1},{6,2},{7,3},{8,12},{9,13},{10,... | collective-permute-start | bytes 294920 | tf_op jit(solution)/shard_map/ppermute | solution.py:182
  82.2 17.3 %collective-permute-start.22 = (bf16[64,768]{1,0:T(8,128)(2,1)S(1)}, bf16[64,768]{1,0:T(8,128)(2,1)S(1)}, u32[]{:S(2)}, u32[]{:S(2)}) collective-permute-start(bf16[64,768]{1,0:T(8,128)(2,1)S(1)} %get-tuple-element.74), channel_id=1, source_target_pairs={{0,8},{1,9},{2,10},{3,11},{4,12},{5,13},{6,14},{7,15},{8,0},{9,1},... | collective-permute-start | bytes 294920 | tf_op jit(solution)/shard_map/ppermute | solution.py:182
  88.3 7.4 %collective-permute-start.25 = (bf16[256,768]{1,0:T(8,128)(2,1)S(1)}, bf16[256,768]{1,0:T(8,128)(2,1)S(1)}, u32[]{:S(2)}, u32[]{:S(2)}) collective-permute-start(bf16[256,768]{1,0:T(8,128)(2,1)S(1)} %get-tuple-element.62), channel_id=1, source_target_pairs={{0,1},{1,0},{2,3},{3,2},{4,5},{5,4},{6,7},{7,6},{8,9},{9,8},{10,11... | collective-permute-start | bytes 1179656 | tf_op jit(solution)/shard_map/ppermute | solution.py:182
  95.9 5.3 %collective-permute-start.27 = (bf16[64,768]{1,0:T(8,128)(2,1)S(1)}, bf16[64,768]{1,0:T(8,128)(2,1)S(1)}, u32[]{:S(2)}, u32[]{:S(2)}) collective-permute-start(bf16[64,768]{1,0:T(8,128)(2,1)S(1)} %get-tuple-element.69), channel_id=1, source_target_pairs={{0,4},{1,5},{2,6},{3,7},{4,0},{5,1},{6,2},{7,3},{8,12},{9,13},{10,... | collective-permute-start | bytes 294920 | tf_op jit(solution)/shard_map/ppermute | solution.py:182
  96.8 7.5 %collective-permute-start.29 = (bf16[64,768]{1,0:T(8,128)(2,1)S(1)}, bf16[64,768]{1,0:T(8,128)(2,1)S(1)}, u32[]{:S(2)}, u32[]{:S(2)}) collective-permute-start(bf16[64,768]{1,0:T(8,128)(2,1)S(1)} %get-tuple-element.70), channel_id=1, source_target_pairs={{0,12},{1,13},{2,14},{3,15},{4,8},{5,9},{6,10},{7,11},{8,4},{9,5},... | collective-permute-start | bytes 294920 | tf_op jit(solution)/shard_map/ppermute | solution.py:182
  98.4 10.2 %collective-permute-start.28 = (bf16[64,768]{1,0:T(8,128)(2,1)S(1)}, bf16[64,768]{1,0:T(8,128)(2,1)S(1)}, u32[]{:S(2)}, u32[]{:S(2)}) collective-permute-start(bf16[64,768]{1,0:T(8,128)(2,1)S(1)} %get-tuple-element.71), channel_id=1, source_target_pairs={{0,8},{1,9},{2,10},{3,11},{4,12},{5,13},{6,14},{7,15},{8,0},{9,1},... | collective-permute-start | bytes 294920 | tf_op jit(solution)/shard_map/ppermute | solution.py:182
  (16 other events, 77.4 us)

commit v3 on v0

v3 whole, which is shorter than its diff:
```python
import functools

import jax
import jax.numpy as jnp
from jax import lax
from jax.experimental import pallas as pl
from jax.experimental.pallas import tpu as pltpu
from jax.sharding import PartitionSpec as P

HEADS = 12
TEAM = 4
MINE = HEADS // TEAM
BF16 = jnp.bfloat16
F32 = jnp.float32
LANES = 128
NT = (((1,), (1,)), ((), ()))


def dot(a, b):
    return jnp.dot(a, b, preferred_element_type=F32)


def dot_nt(a, b):
    return lax.dot_general(a, b, NT, preferred_element_type=F32)


def after(array, *others):
    return lax.optimization_barrier((array, *others))[0]


def low_lanes(shape):
    return lax.broadcasted_iota(jnp.int32, shape, 1) < shape[1] // 2


def lanes_of(part):
    start = part // 2 * LANES
    return slice(start, start + LANES)


def keep_part(array, part):
    low = low_lanes(array.shape)
    return jnp.where(low if part % 2 == 0 else ~low, array, jnp.zeros_like(array))


def block_of(refs, block, slots):
    start = block % 2 * slots
    return refs[block // 2].at[start : start + slots]


def columns_of(refs, block, slots):
    start = block % 2 * slots
    return refs[block // 2].at[:, start : start + slots]


def forward_kernel(
    count_ref, qg_ref, kv_0, kv_1, kv_t_0, kv_t_1, numer_ref, max_ref, stat_ref, score_ref, weight_ref
):
    kv_refs, kv_t_refs = (kv_0, kv_1), (kv_t_0, kv_t_1)
    rows = qg_ref.shape[0]
    dim = kv_t_0.shape[0] // (2 * MINE)
    slots = kv_0.shape[0] // 2
    depth = score_ref.shape[0]
    slot = lax.broadcasted_iota(jnp.int32, (slots, rows), 0)
    units = [(head, block) for head in range(MINE) for block in range(TEAM)]
    tops, totals, numers = {}, {}, {}

    def score(step):
        head, block = units[step]
        keys = keep_part(block_of(kv_refs, block, slots)[:, lanes_of(head)], head)
        score_ref[step % depth] = dot_nt(keys, qg_ref[:, lanes_of(head)])

    def weigh(step):
        scores = jnp.where(slot >= count_ref[units[step][1]], -jnp.inf, score_ref[step % depth])
        tops[step] = jnp.max(scores, axis=0, keepdims=True)
        weights = jnp.exp(scores - tops[step])
        totals[step] = jnp.sum(weights, axis=0, keepdims=True)
        weight_ref[step % depth] = weights.astype(BF16)

    def attend(step):
        head, block = units[step]
        part = MINE + head
        at = slice(part * dim, (part + 1) * dim)
        numers[step] = dot(columns_of(kv_t_refs, block, slots)[at, :], weight_ref[step % depth])
        if block < TEAM - 1:
            return
        steps = range(step - TEAM + 1, step + 1)
        top = functools.reduce(jnp.maximum, [tops[s] for s in steps])
        scale = {s: jnp.exp(tops[s] - top) for s in steps}
        total = sum(scale[s] * totals[s] for s in steps)
        numer = sum(scale[s] * numers[s] for s in steps)
        numer_ref[head * dim : (head + 1) * dim, :] = numer
        half = part % 2 * dim
        grad_t = qg_ref[:, lanes_of(part)].astype(F32).T[half : half + dim, :]
        inner = jnp.sum(grad_t * numer, axis=0, keepdims=True)
        max_ref[head : head + 1, :] = top
        stat_ref[head : head + 1, :] = top + jnp.log(total)
        stat_ref[MINE + head : MINE + head + 1, :] = inner / total

    for step in range(len(units) + 2):
        if step < len(units):
            score(step)
        if 0 <= step - 1 < len(units):
            weigh(step - 1)
        if 0 <= step - 2:
            attend(step - 2)


def backward_kernel(first, last, count_ref, qg_ref, stat_ref, kv_0, kv_1, kv_t_0, kv_t_1, *refs):
    kv_refs, kv_t_refs = (kv_0, kv_1), (kv_t_0, kv_t_1)
    if not first:
        sum_in_refs, refs = refs[:2], refs[2:]
    gq_ref, *sum_refs, score_ref, gw_ref, prob_ref, ds_ref = refs
    rows = qg_ref.shape[0]
    dim = kv_t_0.shape[0] // (2 * MINE)
    slots = kv_0.shape[0] // 2
    depth = score_ref.shape[0]
    slot = lax.broadcasted_iota(jnp.int32, (slots, rows), 0)
    low = low_lanes((slots, LANES))
    units = [(head, block) for block in range(TEAM) for head in range(MINE)]
    gq, held = {}, {}

    def product(block, part):
        rows_of = block_of(kv_refs, block, slots)
        return dot_nt(keep_part(rows_of[:, lanes_of(part)], part), qg_ref[:, lanes_of(part)])

    def score(step):
        head, block = units[step]
        score_ref[step % depth] = product(block, head)
        gw_ref[step % depth] = product(block, MINE + head)

    def weigh(step):
        head, block = units[step]
        scores = jnp.where(slot >= count_ref[block], -jnp.inf, score_ref[step % depth])
        prob = jnp.exp(scores - stat_ref[head : head + 1, :])
        delta = stat_ref[MINE + head : MINE + head + 1, :]
        prob_ref[step % depth] = prob.astype(BF16)
        ds_ref[step % depth] = (prob * (gw_ref[step % depth] - delta)).astype(BF16)

    def store(block, part, value):
        held[block, part] = value
        first_part = part // 2 * 2
        if (block, first_part) not in held or (block, first_part + 1) not in held:
            return
        pair = [held.pop((block, p)) for p in (first_part, first_part + 1)]
        if last:
            pair = [x * 0.125 if p < MINE else x for p, x in zip((first_part, first_part + 1), pair)]
        total = jnp.where(low, pair[0], pair[1])
        if not first:
            before = block_of(sum_in_refs, block, slots)[:, lanes_of(part)]
            if last:
                scales = [0.125 if p < MINE else 1.0 for p in (first_part, first_part + 1)]
                before = before * (scales[0] if scales[0] == scales[1] else jnp.where(low, *scales))
            total += before
        block_of(sum_refs, block, slots)[:, lanes_of(part)] = total.astype(sum_refs[0].dtype)

    def collect(step):
        head, block = units[step]
        store(block, head, dot(ds_ref[step % depth], qg_ref[:, lanes_of(head)]))
        store(block, MINE + head, dot(prob_ref[step % depth], qg_ref[:, lanes_of(MINE + head)]))
        keys_t = columns_of(kv_t_refs, block, slots)[head * dim : (head + 1) * dim, :]
        term = dot(keys_t, ds_ref[step % depth])
        gq[head] = gq[head] + term if head in gq else term
        if block == TEAM - 1:
            gq_ref[head * dim : (head + 1) * dim, :] = gq[head].astype(gq_ref.dtype)

    for step in range(len(units) + 2):
        if 0 <= step - 2:
            collect(step - 2)
        if 0 <= step - 1 < len(units):
            weigh(step - 1)
        if step < len(units):
            score(step)


def call(kernel, ins, out_shapes, scratch, flops, exps):
    vmem = pl.BlockSpec(memory_space=pltpu.VMEM)
    smem = pl.BlockSpec(memory_space=pltpu.SMEM)
    moved = sum(a.size * a.dtype.itemsize for a in list(ins) + list(out_shapes))
    return pl.pallas_call(
        kernel,
        in_specs=[smem if a.dtype == jnp.int32 else vmem for a in ins],
        out_specs=[vmem] * len(out_shapes),
        out_shape=out_shapes,
        scratch_shapes=scratch,
        compiler_params=pltpu.CompilerParams(vmem_limit_bytes=40 << 20),
        cost_estimate=pl.CostEstimate(flops=flops, transcendentals=exps, bytes_accessed=moved),
    )(*ins)


def body(size, latents, points, counts, w_query, w_key, w_value, w_out, d_out):
    own, width = latents.shape
    slots = points.shape[0]
    mine = width // TEAM
    shape = jax.ShapeDtypeStruct
    direct = [0, size // 4, size // 2, size // 4 + size // 2]
    middle = []
    bit = size // 8
    while bit >= TEAM:
        middle.append(bit)
        bit //= 2
    place = lax.axis_index("pts")
    even_core, even_x = place % 2 == 0, place // 2 % 2 == 0

    def swap(array, mask):
        return lax.ppermute(array, "pts", [(i, i ^ mask) for i in range(size)])

    def sort(test, a, b):
        return jnp.where(test, a, b), jnp.where(test, b, a)

    def spread(one, two, behind=None):
        quarter = [
            jnp.concatenate([a[:, i * mine : (i + 1) * mine] for a in (one, two)], axis=1)
            for i in range(TEAM)
        ]
        keep, send = sort(
            even_core,
            jnp.concatenate([quarter[0], quarter[2]], axis=1),
            jnp.concatenate([quarter[1], quarter[3]], axis=1),
        )
        if behind is not None:
            send = after(send, behind)
        both = jnp.concatenate([keep, swap(send, 1)], axis=0)
        keep, send = sort(even_x, both[:, : 2 * mine], both[:, 2 * mine :])
        return keep, send

    query_own = dot(latents, w_query).astype(BF16)
    grad_own = dot(d_out, w_out.T).astype(BF16)
    keep_qg, send_qg = spread(query_own, grad_own)
    came_qg = swap(send_qg, 2)
    points = after(points, keep_qg)
    keys = dot(points, w_key).astype(BF16) * jnp.asarray(0.125, BF16)
    values = dot(points, w_value).astype(BF16)
    keep_kv, send_kv = spread(keys, values, came_qg)
    came_kv = swap(send_kv, 2)
    qg = jnp.concatenate([keep_qg, came_qg], axis=0)
    for mask in middle:
        qg = jnp.concatenate([qg, swap(qg, mask)], axis=0)
    qg = [qg] + [swap(qg, m) for m in direct[1:]]
    pair = jnp.concatenate([counts, swap(counts, 1)])
    pair = after(pair, keep_kv)
    count_all = jnp.concatenate([pair, swap(pair, 2)])
    kv = [keep_kv, came_kv, keep_kv.T, came_kv.T]
    rows = qg[0].shape[0]
    team_slots = TEAM * slots
    work = 2 * rows * team_slots * mine

    numer, tops, stats = [None] * 4, [None] * 4, [None] * 4
    for p in range(4):
        if p:
            qg[p] = after(qg[p], stats[p - 1])
        numer[p], tops[p], stats[p] = call(
            forward_kernel,
            [count_all, qg[p]] + kv,
            [shape((mine, rows), F32), shape((MINE, rows), F32), shape((2 * MINE, rows), F32)],
            [pltpu.VMEM((3, slots, rows), F32), pltpu.VMEM((3, slots, rows), BF16)],
            flops=8 * work,
            exps=rows * team_slots * MINE,
        )

    def merge(*parts):
        lse = [p[..., :MINE, :] for p in parts]
        top = functools.reduce(jnp.maximum, lse)
        scale = [jnp.exp(x - top) for x in lse]
        total = sum(scale)
        delta = sum(s * p[..., MINE:, :] for s, p in zip(scale, parts)) / total
        return jnp.concatenate([top + jnp.log(total), delta], axis=-2)

    stat = jnp.stack(stats)
    came = [stat] + [swap(stat, m) for m in direct[1:]]
    final = jnp.stack([merge(*[came[p][q ^ p] for p in range(4)]) for q in range(4)])
    for mask in reversed(middle):
        half = final.shape[-1] // 2
        final = merge(final[..., :half], swap(final[..., half:], mask))
    for mask in middle:
        final = jnp.concatenate([final, swap(final, mask)], axis=-1)

    def add(array, came):
        return array.astype(F32) + came.astype(F32)

    def scaled(p):
        scale = jnp.exp(tops[p] - final[p, :MINE])
        return (numer[p].reshape(MINE, -1, rows) * scale[:, None, :]).reshape(mine, rows)

    scaled_a = [scaled(p) for p in range(4)]
    came_a = scaled_a[:1] + [swap(scaled_a[p].astype(BF16), direct[p]) for p in range(1, 4)]

    def backward(p, sums, behind=(), last=False):
        kind = BF16 if last else F32
        gq, *sums = call(
            functools.partial(backward_kernel, not sums, last),
            [count_all, qg[p], after(final[p], *behind)] + kv + sums,
            [shape((mine, rows), F32 if p == 0 else BF16)] + [shape((team_slots // 2, 2 * mine), kind)] * 2,
            [pltpu.VMEM((2, slots, rows), F32)] * 2 + [pltpu.VMEM((2, slots, rows), BF16)] * 2,
            flops=14 * work,
            exps=rows * team_slots * MINE,
        )
        return gq, sums

    came_q = [None] * 4
    gq, sums = backward(3, [], scaled_a[1:])
    came_q[3] = swap(gq, direct[3])
    gq, sums = backward(2, sums, [came_a[3]])
    came_q[2] = swap(gq, direct[2])
    gq, sums = backward(1, sums, [came_a[2], came_q[3]])
    came_q[1] = swap(gq, direct[1])
    came_q[0], gkv = backward(0, sums, [came_a[1], came_q[2]], last=True)

    came = swap(gkv[1], 2)
    low, high = sort(even_x, gkv[0], came)
    sides = jnp.concatenate([low, high], axis=1)
    came = swap(sides[slots:], 1)
    even, odd = sort(even_core, sides[:slots], came)

    def columns(which):
        at = [i * 2 * mine + which * mine for i in range(2)]
        return jnp.concatenate([a[:, i : i + mine] for i in at for a in (even, odd)], axis=1)

    d_points = (dot(columns(0), w_key.T) + dot(columns(1), w_value.T)).astype(BF16)

    both = jnp.stack([functools.reduce(add, came_a), functools.reduce(add, came_q)])
    for mask in reversed(middle):
        half = both.shape[-1] // 2
        both = add(both[..., :half], swap(both[..., half:].astype(BF16), mask))
    both = both.astype(BF16)
    came = swap(both[..., 2 * own :], 2)
    low, high = sort(even_x, both[..., : 2 * own], came)
    sides = jnp.stack([low, high], axis=1)
    came = swap(sides[..., own:], 1)
    even, odd = sort(even_core, sides[..., :own], came)
    joined = jnp.stack([even, odd], axis=2).reshape(2, width, own)
    result = (latents.astype(F32) + dot(joined[0].T, w_out)).astype(BF16)
    d_latents = (d_out.astype(F32) + dot(joined[1].T, w_query.T)).astype(BF16)
    return (result, d_latents, d_points)


def solution(mesh):
    part = P(("groups", "pts"), None)
    in_specs = (part, part, P(("groups", "pts")), P(), P(), P(), P(), part)
    return jax.shard_map(
        functools.partial(body, mesh.shape["pts"]),
        mesh=mesh,
        in_specs=in_specs,
        out_specs=(part, part, part),
        check_vma=False,
    )
```

time: 497 us -> 113 us (0.23)
  matrix products: 164 us -> 9.32 us
  blocking collectives: 118 us -> 0 us
  waiting for transfers between devices: 129 us -> 24.4 us
  Pallas kernels: 0 us -> 29.9 us
  starting transfers between devices: 0.16 us -> 26.6 us
  other arithmetic: 31.3 us -> 6.64 us
  local copies, waits for them, and re-layouts: 36.3 us -> 13.6 us
  between operations: 14 us -> 1.73 us
    dot_general x104 -> x8, matrix products: 164 us -> 9.32 us  [dot(): return jnp.dot(a, b, preferred_element_type=F32)]
    pmax x1 -> x0, blocking collectives: 59.7 us -> none  [body(): row_max = lax.pmax(lax.map(local_max, (query_heads, key_heads)), 'pts')]
    unnamed x5 -> x0, waiting for transfers between devices: 59 us -> none
    psum x1 -> x0, blocking collectives: 58.6 us -> none  [body(): numer_all, total_all = lax.psum((numerator, total_cols), 'pts')]
    all_gather x2 -> x0, waiting for transfers between devices: 35.6 us -> none  [the longest x1 35.6 us: body(): query_all = lax.all_gather(query_own, 'pts', axis=0, tiled=True)]
    psum x1 -> x0, waiting for transfers between devices: 34.2 us -> none  [body(): numer_all, total_all = lax.psum((numerator, total_cols), 'pts')]
    pallas_call x0 -> x8, Pallas kernels: none -> 29.9 us  [call(): pl.pallas_call(kernel, in_specs=[smem if a.dtype == jnp.int32 else vmem f...]
    ppermute x0 -> x22, starting transfers between devices: none -> 26.6 us  [swap(): return lax.ppermute(array, 'pts', [(i, i ^ mask) for i in range(size)])]
  transfers between devices with their start and end apart: 4 -> 22, of which waited for: 3 -> 12; matrix products, arithmetic and copies ran while one was open for 22% -> 17% of each run, Pallas kernels for 0% -> 24%
where the time goes in v3:
time: 113 us; the launch traced here: 112 us
  Pallas kernels  29.9 us (26%)
  starting transfers between devices  26.6 us (24%)
  waiting for transfers between devices  24.4 us (22%)
  local copies, waits for them, and re-layouts  13.6 us (12%)
  matrix products  9.32 us (8%)
  other arithmetic  6.64 us (6%)
  between operations  1.73 us (2%)
    pallas_call x8, Pallas kernels, call(): pl.pallas_call(kernel, in_specs=[smem if a.dtype == jnp.int32 else vmem f...  29.9 us
    ppermute x22, starting transfers between devices, swap(): return lax.ppermute(array, 'pts', [(i, i ^ mask) for i in range(size)])  26.6 us
    ppermute x22, waiting for transfers between devices, swap(): return lax.ppermute(array, 'pts', [(i, i ^ mask) for i in range(size)])  24.4 us
    dot_general x8, matrix products, dot(): return jnp.dot(a, b, preferred_element_type=F32)  9.32 us
    unnamed x30, local copies, waits for them, and re-layouts  3.37 us
    pallas_call x2, local copies, waits for them, and re-layouts, call(): pl.pallas_call(kernel, in_specs=[smem if a.dtype == jnp.int32 else vmem f...  2.38 us
  transfers between devices with their start and end apart: 22, of which 12 were waited for; matrix products, arithmetic and copies ran while one was open for 17% of the time, Pallas kernels for 24%

profile of v3, /device:TPU:0, one launch (start us, length us, event | category | flops | bytes accessed | tf_op | source)
XLA Modules:
  0.0 112.2 jit_solution(17801706478733031030)
XLA Ops:
  0.7 1.8 %convolution_convert_fusion.3 = bf16[64,768]{1,0:T(8,128)(2,1)S(1)} fusion(bf16[64,768]{1,0:T(8,128)(2,1)} %param.8, bf16[768,768]{1,0:T(8,128)(2,1)} %param.11), kind=kOutput, calls=%fused_computation.12 | convolution fusion | flops 75546624 | bytes 1376256 | tf_op jit(solution)/shard_map/dot_general | solution.py:20
  4.8 2.9 %collective-permute-start.2 = (bf16[128,384]{1,0:T(8,128)(2,1)S(1)}, bf16[128,384]{1,0:T(8,128)(2,1)S(1)}, u32[]{:S(2)}, u32[]{:S(2)}) collective-permute-start(bf16[128,384]{1,0:T(8,128)(2,1)S(1)} %get-tuple-element.111), channel_id=1, source_target_pairs={{0,2},{1,3},{2,0},{3,1},{4,6},{5,7},{6,4},{7,5},{8,10},{9,11},{10,... | collective-permute-start | bytes 294920 | tf_op jit(solution)/shard_map/ppermute | solution.py:205
  11.0 2.0 %collective-permute-done.3 = bf16[384,768]{0,1:T(8,128)(2,1)S(1)} collective-permute-done((bf16[384,768]{0,1:T(8,128)(2,1)S(1)}, bf16[384,768]{0,1:T(8,128)(2,1)S(1)}, u32[]{:S(2)}, u32[]{:S(2)}) %collective-permute-start.3) | collective-permute-done | bytes 589856 | tf_op jit(solution)/shard_map/ppermute | solution.py:205
  17.6 3.6 %collective-permute-start.8 = (bf16[256,384]{1,0:T(8,128)(2,1)}, bf16[256,384]{1,0:T(8,128)(2,1)}, u32[]{:S(2)}, u32[]{:S(2)}) collective-permute-start(bf16[256,384]{1,0:T(8,128)(2,1)} %pad_maximum_fusion.6.qg_ref), channel_id=1, source_target_pairs={{0,12},{1,13},{2,14},{3,15},{4,8},{5,9},{6,10},{7,11},{8,4},{9,5},... | collective-permute-start | bytes 589832 | tf_op jit(solution)/shard_map/ppermute | solution.py:205
  22.9 5.9 %collective-permute-done.4 = s32[2]{0:T(128)S(1)} collective-permute-done((s32[2]{0:T(128)S(1)}, s32[2]{0:T(128)S(1)}, u32[]{:S(2)}, u32[]{:S(2)}) %collective-permute-start.4) | collective-permute-done | bytes 40 | tf_op jit(solution)/shard_map/ppermute | solution.py:205
  29.1 3.3 %shard_map.103 = (f32[192,256]{1,0:T(8,128)S(1)}, f32[3,256]{1,0:T(4,128)S(1)}, f32[6,256]{1,0:T(8,128)S(1)}) custom-call(s32[4]{0:T(128)S(1)} %pad_add_fusion.1.count_ref, bf16[256,384]{1,0:T(8,128)(2,1)} %pad_maximum_fusion.6.qg_ref, bf16[768,384]{1,0:T(8,128)(2,1)S(1)} %copy.34.kv_0, bf16[768,384]{1,0:T(8,128)(2,1)S(1)} %copy.35.kv_1, ...), custom_call_target="tpu_custom_call" | custom-call | flops 1207959552 | bytes 2761744 | tf_op jit(solution)/shard_map/pallas_call | solution.py:179
  32.4 2.2 %collective-permute-done.6.qg_ref = bf16[256,384]{1,0:T(8,128)(2,1)} collective-permute-done((bf16[256,384]{1,0:T(8,128)(2,1)}, bf16[256,384]{1,0:T(8,128)(2,1)}, u32[]{:S(2)}, u32[]{:S(2)}) %collective-permute-start.6) | collective-permute-done | bytes 196640 | tf_op jit(solution)/shard_map/ppermute | solution.py:205
  34.6 3.3 %shard_map.104 = (f32[192,256]{1,0:T(8,128)S(1)}, f32[3,256]{1,0:T(4,128)S(1)}, f32[6,256]{1,0:T(8,128)S(1)}) custom-call(s32[4]{0:T(128)S(1)} %pad_add_fusion.1.count_ref, bf16[256,384]{1,0:T(8,128)(2,1)} %collective-permute-done.6.qg_ref, bf16[768,384]{1,0:T(8,128)(2,1)S(1)} %copy.34.kv_0, bf16[768,384]{1,0:T(8,128)(2,1)S(1)} %copy.35.kv_1, ...), custom_call_target="tpu_custom_call" | custom-call | flops 1207959552 | bytes 2761744 | tf_op jit(solution)/shard_map/pallas_call | solution.py:179
  38.6 3.3 %shard_map.105 = (f32[192,256]{1,0:T(8,128)S(1)}, f32[3,256]{1,0:T(4,128)S(1)}, f32[6,256]{1,0:T(8,128)S(1)}) custom-call(s32[4]{0:T(128)S(1)} %pad_add_fusion.1.count_ref, bf16[256,384]{1,0:T(8,128)(2,1)} %collective-permute-done.7.qg_ref, bf16[768,384]{1,0:T(8,128)(2,1)S(1)} %copy.34.kv_0, bf16[768,384]{1,0:T(8,128)(2,1)S(1)} %copy.35.kv_1, ...), custom_call_target="tpu_custom_call" | custom-call | flops 1207959552 | bytes 2761744 | tf_op jit(solution)/shard_map/pallas_call | solution.py:179
  41.9 3.5 %shard_map.106 = (f32[192,256]{1,0:T(8,128)S(1)}, f32[3,256]{1,0:T(4,128)S(1)}, f32[6,256]{1,0:T(8,128)S(1)}) custom-call(s32[4]{0:T(128)S(1)} %pad_add_fusion.1.count_ref, bf16[256,384]{1,0:T(8,128)(2,1)} %collective-permute-done.8.qg_ref, bf16[768,384]{1,0:T(8,128)(2,1)S(1)} %copy.34.kv_0, bf16[768,384]{1,0:T(8,128)(2,1)S(1)} %copy.35.kv_1, ...), custom_call_target="tpu_custom_call" | custom-call | flops 1207959552 | bytes 2761744 | tf_op jit(solution)/shard_map/pallas_call | solution.py:179
  45.4 2.5 %collective-permute-start.11 = (f32[4,6,256]{2,1,0:T(8,128)S(1)}, f32[4,6,256]{2,1,0:T(8,128)S(1)}, u32[]{:S(2)}, u32[]{:S(2)}) collective-permute-start(f32[4,6,256]{2,1,0:T(8,128)S(1)} %pad_maximum_fusion.11), channel_id=1, source_target_pairs={{0,12},{1,13},{2,14},{3,15},{4,8},{5,9},{6,10},{7,11},{8,4},{9,5},... | collective-permute-start | bytes 73736 | tf_op jit(solution)/shard_map/ppermute | solution.py:205
  55.4 2.4 %collective-permute-start.14 = (bf16[192,256]{1,0:T(8,128)(2,1)S(1)}, bf16[192,256]{1,0:T(8,128)(2,1)S(1)}, u32[]{:S(2)}, u32[]{:S(2)}) collective-permute-start(bf16[192,256]{1,0:T(8,128)(2,1)S(1)} %bitcast_multiply_fusion), channel_id=1, source_target_pairs={{0,12},{1,13},{2,14},{3,15},{4,8},{5,9},{6,10},{7,11},{8,4},{9,5},... | collective-permute-start | bytes 294920 | tf_op jit(solution)/shard_map/ppermute | solution.py:205
  57.8 4.0 %shard_map.107 = (bf16[192,256]{1,0:T(8,128)(2,1)S(1)}, f32[768,384]{1,0:T(8,128)S(1)}, f32[768,384]{1,0:T(8,128)S(1)}) custom-call(s32[4]{0:T(128)S(1)} %pad_add_fusion.1.count_ref, bf16[256,384]{1,0:T(8,128)(2,1)} %collective-permute-done.8.qg_ref, f32[6,256]{1,0:T(8,128)S(1)} %get-tuple-element.56.stat_ref, bf16[768,384]{1,0:T(8,128)(2,1)S(1)} %copy.34.kv_0, ...), custom_call_target="tpu_custom_call" | custom-call | flops 2113929216 | bytes 5019664 | tf_op jit(solution)/shard_map/pallas_call | solution.py:179
  63.4 4.1 %shard_map.108 = (bf16[192,256]{1,0:T(8,128)(2,1)S(1)}, f32[768,384]{1,0:T(8,128)S(1)}, f32[768,384]{1,0:T(8,128)S(1)}) custom-call(s32[4]{0:T(128)S(1)} %pad_add_fusion.1.count_ref, bf16[256,384]{1,0:T(8,128)(2,1)} %collective-permute-done.7.qg_ref, f32[6,256]{1,0:T(8,128)S(1)} %get-tuple-element.55.stat_ref, bf16[768,384]{1,0:T(8,128)(2,1)S(1)} %copy.34.kv_0, ...), custom_call_target="tpu_custom_call" | custom-call | flops 2113929216 | bytes 7378960 | tf_op jit(solution)/shard_map/pallas_call | solution.py:179
  67.5 3.7 %collective-permute-start.15 = (bf16[192,256]{1,0:T(8,128)(2,1)S(1)}, bf16[192,256]{1,0:T(8,128)(2,1)S(1)}, u32[]{:S(2)}, u32[]{:S(2)}) collective-permute-start(bf16[192,256]{1,0:T(8,128)(2,1)S(1)} %get-tuple-element.59), channel_id=1, source_target_pairs={{0,8},{1,9},{2,10},{3,11},{4,12},{5,13},{6,14},{7,15},{8,0},{9,1},... | collective-permute-start | bytes 294920 | tf_op jit(solution)/shard_map/ppermute | solution.py:205
  71.2 4.1 %shard_map.109 = (bf16[192,256]{1,0:T(8,128)(2,1)S(1)}, f32[768,384]{1,0:T(8,128)S(1)}, f32[768,384]{1,0:T(8,128)S(1)}) custom-call(s32[4]{0:T(128)S(1)} %pad_add_fusion.1.count_ref, bf16[256,384]{1,0:T(8,128)(2,1)} %collective-permute-done.6.qg_ref, f32[6,256]{1,0:T(8,128)S(1)} %get-tuple-element.62.stat_ref, bf16[768,384]{1,0:T(8,128)(2,1)S(1)} %copy.34.kv_0, ...), custom_call_target="tpu_custom_call" | custom-call | flops 2113929216 | bytes 7378960 | tf_op jit(solution)/shard_map/pallas_call | solution.py:179
  75.5 4.4 %shard_map.110 = (f32[192,256]{1,0:T(8,128)S(1)}, bf16[768,384]{1,0:T(8,128)(2,1)S(1)}, bf16[768,384]{1,0:T(8,128)(2,1)S(1)}) custom-call(s32[4]{0:T(128)S(1)} %pad_add_fusion.1.count_ref, bf16[256,384]{1,0:T(8,128)(2,1)} %pad_maximum_fusion.6.qg_ref, f32[6,256]{1,0:T(8,128)S(1)} %get-tuple-element.60.stat_ref, bf16[768,384]{1,0:T(8,128)(2,1)S(1)} %copy.34.kv_0, ...), custom_call_target="tpu_custom_call" | custom-call | flops 2113929216 | bytes 6297616 | tf_op jit(solution)/shard_map/pallas_call | solution.py:179
  82.2 2.1 %copy.52 = bf16[768,384]{0,1:T(8,128)(2,1)} copy(bf16[768,384]{1,0:T(8,128)(2,1)} %copy-done.3) | data formatting | bytes 1179648 | tf_op jit(solution)/shard_map/pallas_call | solution.py:179
  90.1 6.0 %collective-permute-done.20 = bf16[768,384]{0,1:T(8,128)(2,1)S(1)} collective-permute-done((bf16[768,384]{0,1:T(8,128)(2,1)}, bf16[768,384]{0,1:T(8,128)(2,1)S(1)}, u32[]{:S(2)}, u32[]{:S(2)}) %collective-permute-start.20) | collective-permute-done | bytes 589856 | tf_op jit(solution)/shard_map/ppermute | solution.py:205
  97.9 1.7 %copy.51 = bf16[1,2,2,192,64]{3,2,1,4,0:T(2,128)(2,1)} copy(bf16[1,2,2,192,64]{4,3,0,1,2:T(8,128)(2,1)} %get-tuple-element.103) | data formatting | bytes 196608 | tf_op jit(solution)/shard_map/slice | solution.py:332
  99.7 1.7 %squeeze.17 = bf16[768,64]{0,1:T(8,128)(2,1)} reshape(bf16[1,2,2,192,64]{3,2,1,4,0:T(2,128)(2,1)} %copy.51) | data formatting | bytes 196608 | tf_op jit(solution)/shard_map/squeeze | solution.py:332
  101.3 1.7 %copy.50 = bf16[1,2,2,192,64]{3,2,1,4,0:T(2,128)(2,1)} copy(bf16[1,2,2,192,64]{4,3,0,1,2:T(8,128)(2,1)} %get-tuple-element.104) | data formatting | bytes 196608 | tf_op jit(solution)/shard_map/slice | solution.py:331
  103.1 1.7 %squeeze.16 = bf16[768,64]{0,1:T(8,128)(2,1)} reshape(bf16[1,2,2,192,64]{3,2,1,4,0:T(2,128)(2,1)} %copy.50) | data formatting | bytes 196608 | tf_op jit(solution)/shard_map/squeeze | solution.py:331
  104.8 2.2 %fusion.3 = bf16[64,768]{1,0:T(8,128)(2,1)} fusion(bf16[768,64]{0,1:T(8,128)(2,1)} %squeeze.17, bf16[768,768]{1,0:T(8,128)(2,1)S(1)} %copy-done.4, bf16[64,768]{1,0:T(8,128)(2,1)} %param.15), kind=kOutput, calls=%fused_computation.14 | convolution fusion | flops 75644928 | bytes 1474560 | tf_op jit(solution)/shard_map/dot_general | solution.py:20
  (112 shorter events, 36.5 us)
Async XLA Ops:
  0.6 7.1 %copy-start = (bf16[768,768]{1,0:T(8,128)(2,1)S(1)}, bf16[768,768]{1,0:T(8,128)(2,1)}, u32[]{:S(2)}) copy-start(bf16[768,768]{1,0:T(8,128)(2,1)} %param.13) | copy-start | bytes 3538948
  3.3 1.5 %collective-permute-start.1 = (bf16[64,768]{1,0:T(8,128)(2,1)S(1)}, bf16[64,768]{1,0:T(8,128)(2,1)S(1)}, u32[]{:S(2)}, u32[]{:S(2)}) collective-permute-start(bf16[64,768]{1,0:T(8,128)(2,1)S(1)} %get-tuple-element.110), channel_id=1, source_target_pairs={{0,1},{1,0},{2,3},{3,2},{4,5},{5,4},{6,7},{7,6},{8,9},{9,8},{10,11... | collective-permute-start | bytes 294920 | tf_op jit(solution)/shard_map/ppermute | solution.py:205
  4.8 6.2 %collective-permute-start.2 = (bf16[128,384]{1,0:T(8,128)(2,1)S(1)}, bf16[128,384]{1,0:T(8,128)(2,1)S(1)}, u32[]{:S(2)}, u32[]{:S(2)}) collective-permute-start(bf16[128,384]{1,0:T(8,128)(2,1)S(1)} %get-tuple-element.111), channel_id=1, source_target_pairs={{0,2},{1,3},{2,0},{3,1},{4,6},{5,7},{6,4},{7,5},{8,10},{9,11},{10,... | collective-permute-start | bytes 294920 | tf_op jit(solution)/shard_map/ppermute | solution.py:205
  11.0 2.1 %collective-permute-start.3 = (bf16[384,768]{0,1:T(8,128)(2,1)S(1)}, bf16[384,768]{0,1:T(8,128)(2,1)S(1)}, u32[]{:S(2)}, u32[]{:S(2)}) collective-permute-start(bf16[384,768]{0,1:T(8,128)(2,1)S(1)} %get-tuple-element.38), channel_id=1, source_target_pairs={{0,1},{1,0},{2,3},{3,2},{4,5},{5,4},{6,7},{7,6},{8,9},{9,8},{10,11... | collective-permute-start | bytes 1769480 | tf_op jit(solution)/shard_map/ppermute | solution.py:205
  13.2 15.6 %collective-permute-start.5 = (bf16[768,384]{0,1:T(8,128)(2,1)S(1)}, bf16[768,384]{0,1:T(8,128)(2,1)S(1)}, u32[]{:S(2)}, u32[]{:S(2)}) collective-permute-start(bf16[768,384]{0,1:T(8,128)(2,1)S(1)} %get-tuple-element.83), channel_id=1, source_target_pairs={{0,2},{1,3},{2,0},{3,1},{4,6},{5,7},{6,4},{7,5},{8,10},{9,11},{10,... | collective-permute-start | bytes 1769480 | tf_op jit(solution)/shard_map/ppermute | solution.py:205
  14.8 1.4 %collective-permute-start = (s32[1]{0:T(128)}, s32[1]{0:T(128)}, u32[]{:S(2)}, u32[]{:S(2)}) collective-permute-start(s32[1]{0:T(128)} %param.10), channel_id=1, source_target_pairs={{0,1},{1,0},{2,3},{3,2},{4,5},{5,4},{6,7},{7,6},{8,9},{9,8},{10,11... | collective-permute-start | bytes 20 | tf_op jit(solution)/shard_map/ppermute | solution.py:205
  17.6 24.3 %collective-permute-start.8 = (bf16[256,384]{1,0:T(8,128)(2,1)}, bf16[256,384]{1,0:T(8,128)(2,1)}, u32[]{:S(2)}, u32[]{:S(2)}) collective-permute-start(bf16[256,384]{1,0:T(8,128)(2,1)} %pad_maximum_fusion.6.qg_ref), channel_id=1, source_target_pairs={{0,12},{1,13},{2,14},{3,15},{4,8},{5,9},{6,10},{7,11},{8,4},{9,5},... | collective-permute-start | bytes 589832 | tf_op jit(solution)/shard_map/ppermute | solution.py:205
  21.2 17.4 %collective-permute-start.7 = (bf16[256,384]{1,0:T(8,128)(2,1)}, bf16[256,384]{1,0:T(8,128)(2,1)}, u32[]{:S(2)}, u32[]{:S(2)}) collective-permute-start(bf16[256,384]{1,0:T(8,128)(2,1)} %pad_maximum_fusion.6.qg_ref), channel_id=1, source_target_pairs={{0,8},{1,9},{2,10},{3,11},{4,12},{5,13},{6,14},{7,15},{8,0},{9,1},... | collective-permute-start | bytes 589832 | tf_op jit(solution)/shard_map/ppermute | solution.py:205
  21.2 13.4 %collective-permute-start.6 = (bf16[256,384]{1,0:T(8,128)(2,1)}, bf16[256,384]{1,0:T(8,128)(2,1)}, u32[]{:S(2)}, u32[]{:S(2)}) collective-permute-start(bf16[256,384]{1,0:T(8,128)(2,1)} %pad_maximum_fusion.6.qg_ref), channel_id=1, source_target_pairs={{0,4},{1,5},{2,6},{3,7},{4,0},{5,1},{6,2},{7,3},{8,12},{9,13},{10,... | collective-permute-start | bytes 589832 | tf_op jit(solution)/shard_map/ppermute | solution.py:205
  22.3 6.4 %collective-permute-start.4 = (s32[2]{0:T(128)S(1)}, s32[2]{0:T(128)S(1)}, u32[]{:S(2)}, u32[]{:S(2)}) collective-permute-start(s32[2]{0:T(128)S(1)} %pad_add_fusion), channel_id=1, source_target_pairs={{0,2},{1,3},{2,0},{3,1},{4,6},{5,7},{6,4},{7,5},{8,10},{9,11},{10,... | collective-permute-start | bytes 32 | tf_op jit(solution)/shard_map/ppermute | solution.py:205
  45.4 5.9 %collective-permute-start.11 = (f32[4,6,256]{2,1,0:T(8,128)S(1)}, f32[4,6,256]{2,1,0:T(8,128)S(1)}, u32[]{:S(2)}, u32[]{:S(2)}) collective-permute-start(f32[4,6,256]{2,1,0:T(8,128)S(1)} %pad_maximum_fusion.11), channel_id=1, source_target_pairs={{0,12},{1,13},{2,14},{3,15},{4,8},{5,9},{6,10},{7,11},{8,4},{9,5},... | collective-permute-start | bytes 73736 | tf_op jit(solution)/shard_map/ppermute | solution.py:205
  47.9 4.9 %collective-permute-start.10 = (f32[4,6,256]{2,1,0:T(8,128)S(1)}, f32[4,6,256]{2,1,0:T(8,128)S(1)}, u32[]{:S(2)}, u32[]{:S(2)}) collective-permute-start(f32[4,6,256]{2,1,0:T(8,128)S(1)} %pad_maximum_fusion.11), channel_id=1, source_target_pairs={{0,8},{1,9},{2,10},{3,11},{4,12},{5,13},{6,14},{7,15},{8,0},{9,1},... | collective-permute-start | bytes 73736 | tf_op jit(solution)/shard_map/ppermute | solution.py:205
  48.6 4.3 %collective-permute-start.9 = (f32[4,6,256]{2,1,0:T(8,128)S(1)}, f32[4,6,256]{2,1,0:T(8,128)S(1)}, u32[]{:S(2)}, u32[]{:S(2)}) collective-permute-start(f32[4,6,256]{2,1,0:T(8,128)S(1)} %pad_maximum_fusion.11), channel_id=1, source_target_pairs={{0,4},{1,5},{2,6},{3,7},{4,0},{5,1},{6,2},{7,3},{8,12},{9,13},{10,... | collective-permute-start | bytes 73736 | tf_op jit(solution)/shard_map/ppermute | solution.py:205
  53.1 22.3 %collective-permute-start.12 = (bf16[192,256]{1,0:T(8,128)(2,1)S(1)}, bf16[192,256]{1,0:T(8,128)(2,1)S(1)}, u32[]{:S(2)}, u32[]{:S(2)}) collective-permute-start(bf16[192,256]{1,0:T(8,128)(2,1)S(1)} %bitcast_multiply_fusion.2), channel_id=1, source_target_pairs={{0,4},{1,5},{2,6},{3,7},{4,0},{5,1},{6,2},{7,3},{8,12},{9,13},{10,... | collective-permute-start | bytes 294920 | tf_op jit(solution)/shard_map/ppermute | solution.py:205
  54.0 17.2 %collective-permute-start.13 = (bf16[192,256]{1,0:T(8,128)(2,1)S(1)}, bf16[192,256]{1,0:T(8,128)(2,1)S(1)}, u32[]{:S(2)}, u32[]{:S(2)}) collective-permute-start(bf16[192,256]{1,0:T(8,128)(2,1)S(1)} %bitcast_multiply_fusion.1), channel_id=1, source_target_pairs={{0,8},{1,9},{2,10},{3,11},{4,12},{5,13},{6,14},{7,15},{8,0},{9,1},... | collective-permute-start | bytes 294920 | tf_op jit(solution)/shard_map/ppermute | solution.py:205
  55.4 8.0 %collective-permute-start.14 = (bf16[192,256]{1,0:T(8,128)(2,1)S(1)}, bf16[192,256]{1,0:T(8,128)(2,1)S(1)}, u32[]{:S(2)}, u32[]{:S(2)}) collective-permute-start(bf16[192,256]{1,0:T(8,128)(2,1)S(1)} %bitcast_multiply_fusion), channel_id=1, source_target_pairs={{0,12},{1,13},{2,14},{3,15},{4,8},{5,9},{6,10},{7,11},{8,4},{9,5},... | collective-permute-start | bytes 294920 | tf_op jit(solution)/shard_map/ppermute | solution.py:205
  61.8 9.4 %collective-permute-start.16 = (bf16[192,256]{1,0:T(8,128)(2,1)S(1)}, bf16[192,256]{1,0:T(8,128)(2,1)S(1)}, u32[]{:S(2)}, u32[]{:S(2)}) collective-permute-start(bf16[192,256]{1,0:T(8,128)(2,1)S(1)} %get-tuple-element.61), channel_id=1, source_target_pairs={{0,12},{1,13},{2,14},{3,15},{4,8},{5,9},{6,10},{7,11},{8,4},{9,5},... | collective-permute-start | bytes 294920 | tf_op jit(solution)/shard_map/ppermute | solution.py:205
  67.5 8.0 %collective-permute-start.15 = (bf16[192,256]{1,0:T(8,128)(2,1)S(1)}, bf16[192,256]{1,0:T(8,128)(2,1)S(1)}, u32[]{:S(2)}, u32[]{:S(2)}) collective-permute-start(bf16[192,256]{1,0:T(8,128)(2,1)S(1)} %get-tuple-element.59), channel_id=1, source_target_pairs={{0,8},{1,9},{2,10},{3,11},{4,12},{5,13},{6,14},{7,15},{8,0},{9,1},... | collective-permute-start | bytes 294920 | tf_op jit(solution)/shard_map/ppermute | solution.py:205
  75.3 5.4 %collective-permute-start.17 = (bf16[192,256]{1,0:T(8,128)(2,1)S(1)}, bf16[192,256]{1,0:T(8,128)(2,1)S(1)}, u32[]{:S(2)}, u32[]{:S(2)}) collective-permute-start(bf16[192,256]{1,0:T(8,128)(2,1)S(1)} %get-tuple-element.68), channel_id=1, source_target_pairs={{0,4},{1,5},{2,6},{3,7},{4,0},{5,1},{6,2},{7,3},{8,12},{9,13},{10,... | collective-permute-start | bytes 294920 | tf_op jit(solution)/shard_map/ppermute | solution.py:205
  81.6 5.8 %collective-permute-start.18 = (bf16[2,192,128]{2,1,0:T(8,128)(2,1)S(1)}, bf16[2,192,128]{2,1,0:T(8,128)(2,1)S(1)}, u32[]{:S(2)}, u32[]{:S(2)}) collective-permute-start(bf16[2,192,128]{2,1,0:T(8,128)(2,1)S(1)} %pad_maximum_fusion.7), channel_id=1, source_target_pairs={{0,2},{1,3},{2,0},{3,1},{4,6},{5,7},{6,4},{7,5},{8,10},{9,11},{10,... | collective-permute-start | bytes 294920 | tf_op jit(solution)/shard_map/ppermute | solution.py:205
  84.3 11.8 %collective-permute-start.20 = (bf16[768,384]{0,1:T(8,128)(2,1)}, bf16[768,384]{0,1:T(8,128)(2,1)S(1)}, u32[]{:S(2)}, u32[]{:S(2)}) collective-permute-start(bf16[768,384]{0,1:T(8,128)(2,1)} %copy.52), channel_id=1, source_target_pairs={{0,2},{1,3},{2,0},{3,1},{4,6},{5,7},{6,4},{7,5},{8,10},{9,11},{10,... | collective-permute-start | bytes 1769480 | tf_op jit(solution)/shard_map/ppermute | solution.py:205
  87.5 1.6 %collective-permute-start.19 = (bf16[2,2,192,64]{3,2,0,1:T(8,128)(2,1)S(1)}, bf16[2,2,192,64]{3,2,0,1:T(8,128)(2,1)}, u32[]{:S(2)}, u32[]{:S(2)}) collective-permute-start(bf16[2,2,192,64]{3,2,0,1:T(8,128)(2,1)S(1)} %pad_maximum_fusion.5), channel_id=1, source_target_pairs={{0,1},{1,0},{2,3},{3,2},{4,5},{5,4},{6,7},{7,6},{8,9},{9,8},{10,11... | collective-permute-start | bytes 294920 | tf_op jit(solution)/shard_map/ppermute | solution.py:205
  97.1 7.7 %copy-start.4 = (bf16[768,768]{1,0:T(8,128)(2,1)S(1)}, bf16[768,768]{1,0:T(8,128)(2,1)}, u32[]{:S(2)}) copy-start(bf16[768,768]{1,0:T(8,128)(2,1)} %param.11) | copy-start | bytes 3538948
  97.1 10.9 %collective-permute-start.21 = (bf16[384,768]{0,1:T(8,128)(2,1)}, bf16[384,768]{0,1:T(8,128)(2,1)}, u32[]{:S(2)}, u32[]{:S(2)}) collective-permute-start(bf16[384,768]{0,1:T(8,128)(2,1)} %pad_maximum_fusion), channel_id=1, source_target_pairs={{0,1},{1,0},{2,3},{3,2},{4,5},{5,4},{6,7},{7,6},{8,9},{9,8},{10,11... | collective-permute-start | bytes 1769480 | tf_op jit(solution)/shard_map/ppermute | solution.py:205
  (13 other events, 37.6 us)

commit v4 on v3

v4 whole, which is shorter than its diff:
```python
import functools

import jax
import jax.numpy as jnp
from jax import lax
from jax.experimental import pallas as pl
from jax.experimental.pallas import tpu as pltpu
from jax.sharding import PartitionSpec as P

HEADS = 12
TEAM = 4
MINE = HEADS // TEAM
BF16 = jnp.bfloat16
F32 = jnp.float32
LANES = 128
NT = (((1,), (1,)), ((), ()))


def dot(a, b):
    return jnp.dot(a, b, preferred_element_type=F32)


def dot_nt(a, b):
    return lax.dot_general(a, b, NT, preferred_element_type=F32)


def after(array, *others):
    return lax.optimization_barrier((array, *others))[0]


def low_lanes(shape):
    return lax.broadcasted_iota(jnp.int32, shape, 1) < shape[1] // 2


def lanes_of(part):
    start = part // 2 * LANES
    return slice(start, start + LANES)


def keep_part(array, part):
    low = low_lanes(array.shape)
    return jnp.where(low if part % 2 == 0 else ~low, array, jnp.zeros_like(array))


def block_of(refs, block, slots):
    start = block % 2 * slots
    return refs[block // 2].at[start : start + slots]


def columns_of(refs, block, slots):
    start = block % 2 * slots
    return refs[block // 2].at[:, start : start + slots]


def forward_kernel(
    count_ref, qg_ref, kv_0, kv_1, kv_t_0, kv_t_1, numer_ref, max_ref, stat_ref, score_ref, weight_ref
):
    kv_refs, kv_t_refs = (kv_0, kv_1), (kv_t_0, kv_t_1)
    rows = qg_ref.shape[0]
    dim = kv_t_0.shape[0] // (2 * MINE)
    slots = kv_0.shape[0] // 2
    depth = score_ref.shape[0]
    slot = lax.broadcasted_iota(jnp.int32, (slots, rows), 0)
    units = [(head, block) for head in range(MINE) for block in range(TEAM)]
    tops, totals, numers = {}, {}, {}

    def score(step):
        head, block = units[step]
        keys = keep_part(block_of(kv_refs, block, slots)[:, lanes_of(head)], head)
        score_ref[step % depth] = dot_nt(keys, qg_ref[:, lanes_of(head)])

    def weigh(step):
        scores = jnp.where(slot >= count_ref[units[step][1]], -jnp.inf, score_ref[step % depth])
        tops[step] = jnp.max(scores, axis=0, keepdims=True)
        weights = jnp.exp(scores - tops[step])
        totals[step] = jnp.sum(weights, axis=0, keepdims=True)
        weight_ref[step % depth] = weights.astype(BF16)

    def attend(step):
        head, block = units[step]
        part = MINE + head
        at = slice(part * dim, (part + 1) * dim)
        numers[step] = dot(columns_of(kv_t_refs, block, slots)[at, :], weight_ref[step % depth])
        if block < TEAM - 1:
            return
        steps = range(step - TEAM + 1, step + 1)
        top = functools.reduce(jnp.maximum, [tops[s] for s in steps])
        scale = {s: jnp.exp(tops[s] - top) for s in steps}
        total = sum(scale[s] * totals[s] for s in steps)
        numer = sum(scale[s] * numers[s] for s in steps)
        numer_ref[head * dim : (head + 1) * dim, :] = numer
        half = part % 2 * dim
        grad_t = qg_ref[:, lanes_of(part)].astype(F32).T[half : half + dim, :]
        inner = jnp.sum(grad_t * numer, axis=0, keepdims=True)
        max_ref[head : head + 1, :] = top
        stat_ref[head : head + 1, :] = top + jnp.log(total)
        stat_ref[MINE + head : MINE + head + 1, :] = inner / total

    for step in range(len(units) + 2):
        if step < len(units):
            score(step)
        if 0 <= step - 1 < len(units):
            weigh(step - 1)
        if 0 <= step - 2:
            attend(step - 2)


def backward_kernel(chunks, first, last, count_ref, *refs):
    qg_refs, stat_refs, refs = refs[:chunks], refs[chunks : 2 * chunks], refs[2 * chunks :]
    kv_ref, kv_t_ref, *refs = refs
    if not first:
        sum_in_ref, *refs = refs
    gq_in_refs = ()
    if len(refs) > chunks + 6:
        gq_in_refs, refs = refs[:chunks], refs[chunks:]
    gq_refs, (sum_ref, total_ref, score_ref, gw_ref, prob_ref, ds_ref) = refs[:chunks], refs[chunks:]
    rows = qg_refs[0].shape[0]
    dim = kv_t_ref.shape[0] // (2 * MINE)
    slots = kv_ref.shape[0] // 2
    depth = score_ref.shape[0]
    slot = lax.broadcasted_iota(jnp.int32, (slots, rows), 0)
    low = low_lanes((slots, LANES))
    units = [(c, head, block) for c in range(chunks) for block in range(2) for head in range(MINE)]
    gq, held = {}, {}

    def product(chunk, block, part):
        keys = kv_ref[block * slots : (block + 1) * slots, lanes_of(part)]
        return dot_nt(keep_part(keys, part), qg_refs[chunk][:, lanes_of(part)])

    def score(step):
        chunk, head, block = units[step]
        score_ref[step % depth] = product(chunk, block, head)
        gw_ref[step % depth] = product(chunk, block, MINE + head)

    def weigh(step):
        chunk, head, block = units[step]
        scores = jnp.where(slot >= count_ref[block], -jnp.inf, score_ref[step % depth])
        prob = jnp.exp(scores - stat_refs[chunk][head : head + 1, :])
        delta = stat_refs[chunk][MINE + head : MINE + head + 1, :]
        prob_ref[step % depth] = prob.astype(BF16)
        ds_ref[step % depth] = (prob * (gw_ref[step % depth] - delta)).astype(BF16)

    def store(chunk, block, part, value):
        held[part] = value
        pair = part // 2 * 2, part // 2 * 2 + 1
        if not all(p in held for p in pair):
            return
        at = slice(block * slots, (block + 1) * slots), lanes_of(part)
        total = jnp.where(low, held.pop(pair[0]), held.pop(pair[1]))
        if chunk > 0:
            total += total_ref[at]
        elif not first:
            total += sum_in_ref[at]
        if chunk < chunks - 1:
            total_ref[at] = total
            return
        if last:
            scales = [0.125 if p < MINE else 1.0 for p in pair]
            total *= scales[0] if scales[0] == scales[1] else jnp.where(low, *scales)
        sum_ref[at] = total.astype(sum_ref.dtype)

    def collect(step):
        chunk, head, block = units[step]
        qg_ref = qg_refs[chunk]
        store(chunk, block, head, dot(ds_ref[step % depth], qg_ref[:, lanes_of(head)]))
        store(chunk, block, MINE + head, dot(prob_ref[step % depth], qg_ref[:, lanes_of(MINE + head)]))
        at = slice(head * dim, (head + 1) * dim)
        term = dot(kv_t_ref[at, block * slots : (block + 1) * slots], ds_ref[step % depth])
        if block == 0:
            gq[head] = term + gq_in_refs[chunk][at, :] if gq_in_refs else term
        else:
            gq_refs[chunk][at, :] = (gq[head] + term).astype(gq_refs[chunk].dtype)

    for step in range(len(units) + 2):
        if 0 <= step - 2:
            collect(step - 2)
        if 0 <= step - 1 < len(units):
            weigh(step - 1)
        if step < len(units):
            score(step)


def queries_kernel(place_ref, near_ref, far_ref, core_ref, latents_ref, d_out_ref, w_out_ref, w_query_ref,
                   result_ref, d_latents_ref, joined_ref):
    own = latents_ref.shape[0]
    mine = near_ref.shape[1]
    even_core = place_ref[0] % 2
    even_x = place_ref[0] // 2 % 2
    for kind in range(2):
        for across in range(2):
            for core in range(2):
                quarter = 2 * (even_x ^ across) + (even_core ^ core)
                piece = core_ref[across, kind] if core else (near_ref, far_ref)[across][kind, :, :own]
                joined_ref[pl.ds(pl.multiple_of(quarter * mine, mine), mine), :] = piece.astype(F32)
        joined = joined_ref[...].T.astype(BF16)
        if kind == 0:
            result_ref[...] = (latents_ref[...].astype(F32) + dot(joined, w_out_ref[...])).astype(BF16)
        else:
            d_latents_ref[...] = (
                d_out_ref[...].astype(F32) + dot_nt(joined, w_query_ref[...])
            ).astype(BF16)


def points_kernel(place_ref, near_ref, far_ref, core_ref, weight_ref, out_ref):
    slots = out_ref.shape[0]
    even_core = place_ref[0] % 2
    even_x = place_ref[0] // 2 % 2
    total = None
    for across in range(2):
        for core in range(2):
            quarter = 2 * (even_x ^ across) + (even_core ^ core)
            piece = core_ref[across] if core else (near_ref, far_ref)[across][:slots, :]
            term = dot(piece, weight_ref[quarter])
            total = term if total is None else total + term
    out_ref[...] = total.astype(BF16)


def call(kernel, ins, out_shapes, scratch=(), flops=0, exps=0):
    vmem = pl.BlockSpec(memory_space=pltpu.VMEM)
    smem = pl.BlockSpec(memory_space=pltpu.SMEM)
    moved = sum(a.size * a.dtype.itemsize for a in list(ins) + list(out_shapes))
    return pl.pallas_call(
        kernel,
        in_specs=[smem if a.dtype == jnp.int32 else vmem for a in ins],
        out_specs=[vmem] * len(out_shapes),
        out_shape=out_shapes,
        scratch_shapes=scratch,
        compiler_params=pltpu.CompilerParams(vmem_limit_bytes=40 << 20),
        cost_estimate=pl.CostEstimate(flops=flops, transcendentals=exps, bytes_accessed=moved),
    )(*ins)


def body(size, latents, points, counts, w_query, w_key, w_value, w_out, d_out):
    own, width = latents.shape
    slots = points.shape[0]
    mine = width // TEAM
    shape = jax.ShapeDtypeStruct
    near_bit, far_bit = size // 4, size // 2
    middle = []
    bit = size // 8
    while bit >= TEAM:
        middle.append(bit)
        bit //= 2
    place = lax.axis_index("pts").astype(jnp.int32).reshape(1)
    even_core, even_x = place[0] % 2 == 0, place[0] // 2 % 2 == 0

    def swap(array, mask):
        return lax.ppermute(array, "pts", [(i, i ^ mask) for i in range(size)])

    def sort(test, a, b):
        return jnp.where(test, a, b), jnp.where(test, b, a)

    def halves(one, two):
        quarter = [
            jnp.concatenate([a[:, i * mine : (i + 1) * mine] for a in (one, two)], axis=1)
            for i in range(TEAM)
        ]
        return sort(
            even_core,
            jnp.concatenate([quarter[0], quarter[2]], axis=1),
            jnp.concatenate([quarter[1], quarter[3]], axis=1),
        )

    def spread(keep, send):
        both = jnp.concatenate([keep, swap(send, 1)], axis=0)
        return sort(even_x, both[:, : 2 * mine], both[:, 2 * mine :])

    keys = dot(points, w_key).astype(BF16) * jnp.asarray(0.125, BF16)
    values = dot(points, w_value).astype(BF16)
    keep_kv, send_kv = halves(keys, values)
    extra = 16
    high = jnp.broadcast_to((counts // 16).astype(BF16), (extra, width))
    rest = jnp.broadcast_to((counts % 16).astype(BF16), (extra, width))
    latents_in = after(latents, send_kv)
    query_own = jnp.concatenate([dot(latents_in, w_query).astype(BF16), high], axis=0)
    grad_own = jnp.concatenate([dot(d_out, w_out.T).astype(BF16), rest], axis=0)
    keep_qg, send_qg = spread(*halves(query_own, grad_own))
    came_qg = swap(send_qg, 2)
    keep_kv, send_kv = spread(keep_kv, send_kv)
    came_kv = swap(send_kv, 2)
    each = own + extra
    blocks = [a[i * each : (i + 1) * each] for a in (keep_qg, came_qg) for i in range(2)]
    qg = jnp.concatenate([a[:own] for a in blocks], axis=0)
    count = jnp.stack([16 * a[own, 0].astype(jnp.int32) + a[own, mine].astype(jnp.int32) for a in blocks])
    for mask in middle:
        qg = jnp.concatenate([qg, swap(qg, mask)], axis=0)
    qg = [qg, swap(qg, near_bit), swap(qg, far_bit)]
    qg.append(swap(qg[2], near_bit))
    kv = [keep_kv, came_kv, keep_kv.T, came_kv.T]
    weights = jnp.concatenate(
        [w.T.reshape(TEAM, mine, width) for w in (w_key, w_value)], axis=1
    )
    weights = after(weights, came_qg)
    rows = qg[0].shape[0]
    team_slots = TEAM * slots
    work = 2 * rows * team_slots * mine

    numer, tops, stats = [None] * 4, [None] * 4, [None] * 4
    for p in range(4):
        if p:
            qg[p] = after(qg[p], stats[p - 1])
        numer[p], tops[p], stats[p] = call(
            forward_kernel,
            [count, qg[p]] + kv,
            [shape((mine, rows), F32), shape((MINE, rows), F32), shape((2 * MINE, rows), F32)],
            [pltpu.VMEM((3, slots, rows), F32), pltpu.VMEM((3, slots, rows), BF16)],
            flops=8 * work,
            exps=rows * team_slots * MINE,
        )

    def merge(*parts):
        lse = [p[..., :MINE, :] for p in parts]
        top = functools.reduce(jnp.maximum, lse)
        scale = [jnp.exp(x - top) for x in lse]
        total = sum(scale)
        delta = sum(s * p[..., MINE:, :] for s, p in zip(scale, parts)) / total
        return jnp.concatenate([top + jnp.log(total), delta], axis=-2)

    stat = jnp.stack(stats)
    came = [stat] + [swap(stat, m) for m in (near_bit, far_bit, near_bit + far_bit)]
    final = [merge(*[came[p][q ^ p] for p in range(4)]) for q in range(4)]
    if middle:
        final = jnp.stack(final)
        for mask in reversed(middle):
            half = final.shape[-1] // 2
            final = merge(final[..., :half], swap(final[..., half:], mask))
        for mask in middle:
            final = jnp.concatenate([final, swap(final, mask)], axis=-1)
        final = [final[q] for q in range(4)]

    def add(array, came):
        return array.astype(F32) + came.astype(F32)

    def scaled(p):
        scale = jnp.exp(tops[p] - final[p][:MINE])
        return (numer[p].reshape(MINE, -1, rows) * scale[:, None, :]).reshape(mine, rows)

    def backward(chunks, side, sums=(), partial=(), behind=(), first=True, last=False, kinds=()):
        stat = [final[p] for p in chunks]
        stat[0] = after(stat[0], *behind)
        kept = (team_slots // 2, 2 * mine)
        return call(
            functools.partial(backward_kernel, len(chunks), first, last),
            [count[2 * side : 2 * side + 2]]
            + [qg[p] for p in chunks]
            + stat
            + [kv[side], kv[2 + side]]
            + list(sums)
            + list(partial),
            [shape((mine, rows), k) for k in kinds] + [shape(kept, BF16 if last else F32)],
            [pltpu.VMEM(kept if len(chunks) > 1 else (8, LANES), F32)]
            + [pltpu.VMEM((2, slots, rows), F32)] * 2
            + [pltpu.VMEM((2, slots, rows), BF16)] * 2,
            flops=7 * work * len(chunks),
            exps=rows * team_slots // 2 * MINE * len(chunks),
        )

    scaled_3 = scaled(3).astype(BF16)
    scaled_2 = scaled(2)
    came_a3 = swap(scaled_3, near_bit)
    order = (3, 2, 1, 0)
    *partial, gkv_far = backward(order, 1, behind=[scaled_2, scaled_3], last=True, kinds=[F32] * 4)
    came_far = swap(gkv_far, 2)
    came_a2 = swap(add(scaled_2, came_a3).astype(BF16), far_bit)
    came_a1 = swap(scaled(1).astype(BF16), near_bit)
    gq_3, total = backward((3,), 0, partial=partial[:1], behind=[gkv_far], kinds=[BF16])
    came_3 = swap(gq_3, near_bit)
    gq_2, total = backward((2,), 0, [total], partial[1:2], [came_a2], False, kinds=[F32])
    sent_2 = add(gq_2, came_3).astype(BF16)
    came_2 = swap(sent_2, far_bit)
    gq_1, total = backward((1,), 0, [total], partial[2:3], [came_a1, sent_2], False, kinds=[BF16])
    came_1 = swap(gq_1, near_bit)
    gq_0, gkv_near = backward((0,), 0, [total], partial[3:], (), False, True, kinds=[F32])
    attended = add(add(scaled(0), came_a1), came_a2)
    grad_query = add(add(gq_0, came_1), came_2)

    both = jnp.stack([attended, grad_query])
    for mask in reversed(middle):
        half = both.shape[-1] // 2
        both = add(both[..., :half], swap(both[..., half:].astype(BF16), mask))
    both = both.astype(BF16)
    far = swap(both[..., 2 * own :], 2)
    near = both[..., : 2 * own]
    core = swap(jnp.stack([near[..., own:], far[..., own:]]), 1)
    result, d_latents = call(
        queries_kernel,
        [place, near, far, core, latents, d_out, w_out, w_query],
        [shape((own, width), BF16)] * 2,
        [pltpu.VMEM((width, own), F32)],
        flops=4 * own * width * width,
    )

    core = swap(jnp.stack([gkv_near[slots:], came_far[slots:]]), 1)
    (d_points,) = call(
        points_kernel,
        [place, gkv_near, came_far, core, weights],
        [shape((slots, width), BF16)],
        flops=4 * slots * width * width,
    )
    return (result, d_latents, d_points)


def solution(mesh):
    part = P(("groups", "pts"), None)
    in_specs = (part, part, P(("groups", "pts")), P(), P(), P(), P(), part)
    return jax.shard_map(
        functools.partial(body, mesh.shape["pts"]),
        mesh=mesh,
        in_specs=in_specs,
        out_specs=(part, part, part),
        check_vma=False,
    )
```

time: 113 us -> 109 us (0.965)
  waiting for transfers between devices: 24.4 us -> 18.1 us
  Pallas kernels: 29.9 us -> 35.8 us
  matrix products: 9.32 us -> 3.84 us
  between operations: 1.73 us -> 6.97 us
  starting transfers between devices: 26.6 us -> 23.8 us
    ppermute x22 -> x20, waiting for transfers between devices: 24.4 us -> 18.1 us  [swap(): return lax.ppermute(array, 'pts', [(i, i ^ mask) for i in range(size)])]
    pallas_call x8 -> x11, Pallas kernels: 29.9 us -> 35.8 us  [call(): pl.pallas_call(kernel, in_specs=[smem if a.dtype == jnp.int32 else vmem f...]
    dot_general x8 -> x4, matrix products: 9.32 us -> 3.84 us  [dot(): return jnp.dot(a, b, preferred_element_type=F32)]
    transpose x0 -> x2, local copies, waits for them, and re-layouts: none -> 4.75 us  [body(): w.T.reshape(TEAM, mine, width)]
    squeeze x2 -> x0, local copies, waits for them, and re-layouts: 3.4 us -> none  [the longest x1 1.71 us: body(): result = (latents.astype(F32) + dot(joined[0].T, w_out)).astype(BF16)]
    select_n x6 -> x4, other arithmetic: 1.97 us -> 5.37 us  [sort(): return (jnp.where(test, a, b), jnp.where(test, b, a))]
    ppermute x22 -> x20, starting transfers between devices: 26.6 us -> 23.8 us  [swap(): return lax.ppermute(array, 'pts', [(i, i ^ mask) for i in range(size)])]
    pallas_call x2 -> x0, local copies, waits for them, and re-layouts: 2.38 us -> none  [call(): pl.pallas_call(kernel, in_specs=[smem if a.dtype == jnp.int32 else vmem f...]
  transfers between devices with their start and end apart: 22 -> 20, of which waited for: 12 -> 11; matrix products, arithmetic and copies ran while one was open for 17% -> 15% of each run, Pallas kernels for 24% -> 28%
where the time goes in v4:
time: 109 us; the launch traced here: 108 us
  Pallas kernels  35.8 us (33%)
  starting transfers between devices  23.8 us (22%)
  waiting for transfers between devices  18.1 us (17%)
  local copies, waits for them, and re-layouts  12.8 us (12%)
  other arithmetic  7.03 us (6%)
  between operations  6.97 us (6%)
  matrix products  3.84 us (4%)
    pallas_call x11, Pallas kernels, call(): pl.pallas_call(kernel, in_specs=[smem if a.dtype == jnp.int32 else vmem f...  35.8 us
    ppermute x20, starting transfers between devices, swap(): return lax.ppermute(array, 'pts', [(i, i ^ mask) for i in range(size)])  23.8 us
    ppermute x20, waiting for transfers between devices, swap(): return lax.ppermute(array, 'pts', [(i, i ^ mask) for i in range(size)])  18.1 us
    select_n x4, other arithmetic, sort(): return (jnp.where(test, a, b), jnp.where(test, b, a))  5.37 us
    transpose x2, local copies, waits for them, and re-layouts, body(): w.T.reshape(TEAM, mine, width)  4.75 us
    dot_general x4, matrix products, dot(): return jnp.dot(a, b, preferred_element_type=F32)  3.84 us
    unnamed x28, local copies, waits for them, and re-layouts  3.23 us
  transfers between devices with their start and end apart: 20, of which 11 were waited for; matrix products, arithmetic and copies ran while one was open for 15% of the time, Pallas kernels for 28%

profile of v4, /device:TPU:0, one launch (start us, length us, event | category | flops | bytes accessed | tf_op | source)
XLA Modules:
  0.0 108.4 jit_solution(3791872616912877029)
XLA Ops:
  1.7 2.2 %convolution_convert_fusion = bf16[384,768]{0,1:T(8,128)(2,1)S(1)} fusion(bf16[384,768]{1,0:T(8,128)(2,1)S(1)} %copy-done, bf16[768,768]{1,0:T(8,128)(2,1)} %param.13), kind=kOutput, calls=%fused_computation.1 | convolution fusion | flops 453279744 | bytes 2359296 | tf_op jit(solution)/shard_map/dot_general | solution.py:20
  9.1 2.4 %copy.27 = bf16[768,768]{1,0:T(8,128)(2,1)} copy(bf16[768,768]{0,1:T(8,128)(2,1)} %bitcast.309) | data formatting | bytes 2359296 | tf_op jit(solution)/shard_map/transpose | solution.py:291
  11.5 2.4 %copy.26 = bf16[768,768]{1,0:T(8,128)(2,1)} copy(bf16[768,768]{0,1:T(8,128)(2,1)} %bitcast.310) | data formatting | bytes 2359296 | tf_op jit(solution)/shard_map/transpose | solution.py:291
  18.1 2.9 %collective-permute-start.1 = (bf16[160,384]{1,0:T(8,128)(2,1)S(1)}, bf16[160,384]{1,0:T(8,128)(2,1)S(1)}, u32[]{:S(2)}, u32[]{:S(2)}) collective-permute-start(bf16[160,384]{1,0:T(8,128)(2,1)S(1)} %get-tuple-element.108), channel_id=1, source_target_pairs={{0,2},{1,3},{2,0},{3,1},{4,6},{5,7},{6,4},{7,5},{8,10},{9,11},{10,... | collective-permute-start | bytes 368648 | tf_op jit(solution)/shard_map/ppermute | solution.py:248
  21.0 2.5 %broadcast_select_fusion = (bf16[768,384]{0,1:T(8,128)(2,1)}, bf16[768,384]{0,1:T(8,128)(2,1)S(1)}) fusion(pred[]{:T(512)S(6)} %eq.11, bf16[384,768]{0,1:T(8,128)(2,1)} %collective-permute-done.2, bf16[384,768]{0,1:T(8,128)(2,1)} %get-tuple-element.95), kind=kLoop, calls=%fused_computation.13 | loop fusion | flops 4128768 | bytes 2359297 | tf_op jit(solution)/shard_map/jit(_where)/select_n | solution.py:251
  25.3 2.8 %collective-permute-start.5 = (bf16[256,384]{1,0:T(8,128)(2,1)}, bf16[256,384]{1,0:T(8,128)(2,1)}, u32[]{:S(2)}, u32[]{:S(2)}) collective-permute-start(bf16[256,384]{1,0:T(8,128)(2,1)} %pad_maximum_fusion.5.qg_ref.refs_3_.refs_0_), channel_id=1, source_target_pairs={{0,8},{1,9},{2,10},{3,11},{4,12},{5,13},{6,14},{7,15},{8,0},{9,1},... | collective-permute-start | bytes 589832 | tf_op jit(solution)/shard_map/ppermute | solution.py:248
  33.1 4.2 %collective-permute-done.5.qg_ref.refs_1_.refs_0_ = bf16[256,384]{1,0:T(8,128)(2,1)} collective-permute-done((bf16[256,384]{1,0:T(8,128)(2,1)}, bf16[256,384]{1,0:T(8,128)(2,1)}, u32[]{:S(2)}, u32[]{:S(2)}) %collective-permute-start.5) | collective-permute-done | bytes 196640 | tf_op jit(solution)/shard_map/ppermute | solution.py:248
  38.9 2.1 %copy.14.kv_1.refs_8_ = bf16[768,384]{1,0:T(8,128)(2,1)} copy(bf16[768,384]{0,1:T(8,128)(2,1)} %collective-permute-done.3) | data formatting | bytes 1179648 | tf_op jit(solution)/shard_map/ppermute | solution.py:248
  43.1 3.6 %shard_map.103 = (f32[192,256]{1,0:T(8,128)S(1)}, f32[3,256]{1,0:T(4,128)S(1)}, f32[6,256]{1,0:T(8,128)S(1)}) custom-call(s32[4]{0:T(128)S(1)} %pad_add_fusion.count_ref, bf16[256,384]{1,0:T(8,128)(2,1)} %pad_maximum_fusion.5.qg_ref.refs_3_.refs_0_, bf16[768,384]{1,0:T(8,128)(2,1)S(1)} %copy-done.3, bf16[768,384]{1,0:T(8,128)(2,1)S(1)} %copy-done.5, ...), custom_call_target="tpu_custom_call" | custom-call | flops 1207959552 | bytes 2761744 | tf_op jit(solution)/shard_map/pallas_call | solution.py:222
  46.7 3.5 %shard_map.104 = (f32[192,256]{1,0:T(8,128)S(1)}, f32[3,256]{1,0:T(4,128)S(1)}, f32[6,256]{1,0:T(8,128)S(1)}) custom-call(s32[4]{0:T(128)S(1)} %pad_add_fusion.count_ref, bf16[256,384]{1,0:T(8,128)(2,1)} %collective-permute-done.4.qg_ref.refs_2_.refs_0_, bf16[768,384]{1,0:T(8,128)(2,1)S(1)} %copy-done.4, bf16[768,384]{1,0:T(8,128)(2,1)S(1)} %copy-done.5, ...), custom_call_target="tpu_custom_call" | custom-call | flops 1207959552 | bytes 2761744 | tf_op jit(solution)/shard_map/pallas_call | solution.py:222
  50.3 3.5 %shard_map.105 = (f32[192,256]{1,0:T(8,128)S(1)}, f32[3,256]{1,0:T(4,128)S(1)}, f32[6,256]{1,0:T(8,128)S(1)}) custom-call(s32[4]{0:T(128)S(1)} %pad_add_fusion.count_ref, bf16[256,384]{1,0:T(8,128)(2,1)} %collective-permute-done.5.qg_ref.refs_1_.refs_0_, bf16[768,384]{1,0:T(8,128)(2,1)S(1)} %copy-done.4, bf16[768,384]{1,0:T(8,128)(2,1)S(1)} %copy-done.5, ...), custom_call_target="tpu_custom_call" | custom-call | flops 1207959552 | bytes 2761744 | tf_op jit(solution)/shard_map/pallas_call | solution.py:222
  53.8 3.5 %shard_map.106 = (f32[192,256]{1,0:T(8,128)S(1)}, f32[3,256]{1,0:T(4,128)S(1)}, f32[6,256]{1,0:T(8,128)S(1)}) custom-call(s32[4]{0:T(128)S(1)} %pad_add_fusion.count_ref, bf16[256,384]{1,0:T(8,128)(2,1)} %collective-permute-done.6.qg_ref.refs_0_, bf16[768,384]{1,0:T(8,128)(2,1)S(1)} %copy-done.4, bf16[768,384]{1,0:T(8,128)(2,1)S(1)} %copy-done.5, ...), custom_call_target="tpu_custom_call" | custom-call | flops 1207959552 | bytes 2761744 | tf_op jit(solution)/shard_map/pallas_call | solution.py:222
  57.4 3.7 %collective-permute-start.9 = (f32[4,6,256]{2,1,0:T(8,128)S(1)}, f32[4,6,256]{2,1,0:T(8,128)S(1)}, u32[]{:S(2)}, u32[]{:S(2)}) collective-permute-start(f32[4,6,256]{2,1,0:T(8,128)S(1)} %pad_maximum_fusion.11), channel_id=1, source_target_pairs={{0,12},{1,13},{2,14},{3,15},{4,8},{5,9},{6,10},{7,11},{8,4},{9,5},... | collective-permute-start | bytes 73736 | tf_op jit(solution)/shard_map/ppermute | solution.py:248
  63.2 2.7 %collective-permute-done.8 = f32[4,6,256]{2,1,0:T(8,128)S(1)} collective-permute-done((f32[4,6,256]{2,1,0:T(8,128)S(1)}, f32[4,6,256]{2,1,0:T(8,128)S(1)}, u32[]{:S(2)}, u32[]{:S(2)}) %collective-permute-start.8) | collective-permute-done | bytes 24608 | tf_op jit(solution)/shard_map/ppermute | solution.py:248
  66.4 1.9 %collective-permute-start.11 = (bf16[192,256]{1,0:T(8,128)(2,1)S(1)}, bf16[192,256]{1,0:T(8,128)(2,1)S(1)}, u32[]{:S(2)}, u32[]{:S(2)}) collective-permute-start(bf16[192,256]{1,0:T(8,128)(2,1)S(1)} %fusion.2), channel_id=1, source_target_pairs={{0,4},{1,5},{2,6},{3,7},{4,0},{5,1},{6,2},{7,3},{8,12},{9,13},{10,... | collective-permute-start | bytes 294920 | tf_op jit(solution)/shard_map/ppermute | solution.py:248
  68.3 3.5 %collective-permute-done.11 = bf16[192,256]{1,0:T(8,128)(2,1)S(1)} collective-permute-done((bf16[192,256]{1,0:T(8,128)(2,1)S(1)}, bf16[192,256]{1,0:T(8,128)(2,1)S(1)}, u32[]{:S(2)}, u32[]{:S(2)}) %collective-permute-start.11) | collective-permute-done | bytes 98336 | tf_op jit(solution)/shard_map/ppermute | solution.py:248
  71.9 7.7 %shard_map.107 = (f32[192,256]{1,0:T(8,128)S(1)}, f32[192,256]{1,0:T(8,128)S(1)}, f32[192,256]{1,0:T(8,128)S(1)}, f32[192,256]{1,0:T(8,128)S(1)}, bf16[768,384]{1,0:T(8,128)(2,1)S(1)}) custom-call(s32[2]{0:T(128)S(1)} %pad_add_fusion.2.count_ref, bf16[256,384]{1,0:T(8,128)(2,1)} %collective-permute-done.6.qg_ref.refs_0_, ...), custom_call_target="tpu_custom_call" | custom-call | flops 4227858432 | bytes 3366920 | tf_op jit(solution)/shard_map/pallas_call | solution.py:222
  80.4 2.0 %collective-permute-start.12 = (bf16[192,256]{1,0:T(8,128)(2,1)S(1)}, bf16[192,256]{1,0:T(8,128)(2,1)S(1)}, u32[]{:S(2)}, u32[]{:S(2)}) collective-permute-start(bf16[192,256]{1,0:T(8,128)(2,1)S(1)} %add_convert_fusion.2), channel_id=1, source_target_pairs={{0,8},{1,9},{2,10},{3,11},{4,12},{5,13},{6,14},{7,15},{8,0},{9,1},... | collective-permute-start | bytes 294920 | tf_op jit(solution)/shard_map/ppermute | solution.py:248
  82.4 2.5 %shard_map.108 = (bf16[192,256]{1,0:T(8,128)(2,1)S(1)}, f32[768,384]{1,0:T(8,128)S(1)}) custom-call(s32[2]{0:T(128)S(1)} %pad_add_fusion.1.count_ref, bf16[256,384]{1,0:T(8,128)(2,1)} %collective-permute-done.6.qg_ref.refs_0_, f32[6,256]{1,0:T(8,128)S(1)} %pad_maximum_fusion.15.refs_4_.refs_1_, bf16[768,384]{1,0:T(8,128)(2,1)S(1)} %copy-done.4, ...), custom_call_target="tpu_custom_call" | custom-call | flops 1056964608 | bytes 2856968 | tf_op jit(solution)/shard_map/pallas_call | solution.py:222
  87.0 2.6 %shard_map.109 = (f32[192,256]{1,0:T(8,128)S(1)}, f32[768,384]{1,0:T(8,128)S(1)}) custom-call(s32[2]{0:T(128)S(1)} %pad_add_fusion.1.count_ref, bf16[256,384]{1,0:T(8,128)(2,1)} %collective-permute-done.5.qg_ref.refs_1_.refs_0_, f32[6,256]{1,0:T(8,128)S(1)} %pad_maximum_fusion.14.refs_5_.refs_1_, bf16[768,384]{1,0:T(8,128)(2,1)S(1)} %copy-done.4, ...), custom_call_target="tpu_custom_call" | custom-call | flops 1056964608 | bytes 4134920 | tf_op jit(solution)/shard_map/pallas_call | solution.py:222
  91.1 2.6 %shard_map.110 = (bf16[192,256]{1,0:T(8,128)(2,1)S(1)}, f32[768,384]{1,0:T(8,128)S(1)}) custom-call(s32[2]{0:T(128)S(1)} %pad_add_fusion.1.count_ref, bf16[256,384]{1,0:T(8,128)(2,1)} %collective-permute-done.4.qg_ref.refs_2_.refs_0_, f32[6,256]{1,0:T(8,128)S(1)} %pad_maximum_fusion.13.refs_6_.refs_1_, bf16[768,384]{1,0:T(8,128)(2,1)S(1)} %copy-done.4, ...), custom_call_target="tpu_custom_call" | custom-call | flops 1056964608 | bytes 4036616 | tf_op jit(solution)/shard_map/pallas_call | solution.py:222
  95.4 2.6 %shard_map.111 = (f32[192,256]{1,0:T(8,128)S(1)}, bf16[768,384]{1,0:T(8,128)(2,1)S(1)}) custom-call(s32[2]{0:T(128)S(1)} %pad_add_fusion.1.count_ref, bf16[256,384]{1,0:T(8,128)(2,1)} %pad_maximum_fusion.5.qg_ref.refs_3_.refs_0_, f32[6,256]{1,0:T(8,128)S(1)} %pad_maximum_fusion.12.refs_7_.refs_1_, bf16[768,384]{1,0:T(8,128)(2,1)S(1)} %copy-done.4, ...), custom_call_target="tpu_custom_call" | custom-call | flops 1056964608 | bytes 3545096 | tf_op jit(solution)/shard_map/pallas_call | solution.py:222
  100.5 2.7 %collective-permute-done.16.far_ref = bf16[2,192,128]{2,1,0:T(8,128)(2,1)S(1)} collective-permute-done((bf16[2,192,128]{2,1,0:T(8,128)(2,1)S(1)}, bf16[2,192,128]{2,1,0:T(8,128)(2,1)S(1)}, u32[]{:S(2)}, u32[]{:S(2)}) %collective-permute-start.16) | collective-permute-done | bytes 98336 | tf_op jit(solution)/shard_map/ppermute | solution.py:248
  106.2 2.2 %shard_map.113 = bf16[384,768]{1,0:T(8,128)(2,1)} custom-call(s32[1]{0:T(128)} %bitcast.place_ref, bf16[768,384]{1,0:T(8,128)(2,1)S(1)} %get-tuple-element.73.near_ref, bf16[768,384]{1,0:T(8,128)(2,1)S(1)} %collective-permute-done.18.far_ref, bf16[2,384,384]{2,1,0:T(8,128)(2,1)S(1)} %collective-permute-done.19.core_ref, ...), custom_call_target="tpu_custom_call" | custom-call | flops 905969664 | bytes 4718596 | tf_op jit(solution)/shard_map/pallas_call | solution.py:222
  (101 shorter events, 29.1 us)
Async XLA Ops:
  5.9 15.1 %collective-permute-start.2 = (bf16[384,768]{0,1:T(8,128)(2,1)S(1)}, bf16[384,768]{0,1:T(8,128)(2,1)}, u32[]{:S(2)}, u32[]{:S(2)}) collective-permute-start(bf16[384,768]{0,1:T(8,128)(2,1)S(1)} %get-tuple-element.96), channel_id=1, source_target_pairs={{0,1},{1,0},{2,3},{3,2},{4,5},{5,4},{6,7},{7,6},{8,9},{9,8},{10,11... | collective-permute-start | bytes 1769480 | tf_op jit(solution)/shard_map/ppermute | solution.py:248
  9.0 4.9 %collective-permute-start = (bf16[80,768]{1,0:T(8,128)(2,1)}, bf16[80,768]{1,0:T(8,128)(2,1)}, u32[]{:S(2)}, u32[]{:S(2)}) collective-permute-start(bf16[80,768]{1,0:T(8,128)(2,1)} %get-tuple-element.106), channel_id=1, source_target_pairs={{0,1},{1,0},{2,3},{3,2},{4,5},{5,4},{6,7},{7,6},{8,9},{9,8},{10,11... | collective-permute-start | bytes 368648 | tf_op jit(solution)/shard_map/ppermute | solution.py:248
  18.1 6.5 %collective-permute-start.1 = (bf16[160,384]{1,0:T(8,128)(2,1)S(1)}, bf16[160,384]{1,0:T(8,128)(2,1)S(1)}, u32[]{:S(2)}, u32[]{:S(2)}) collective-permute-start(bf16[160,384]{1,0:T(8,128)(2,1)S(1)} %get-tuple-element.108), channel_id=1, source_target_pairs={{0,2},{1,3},{2,0},{3,1},{4,6},{5,7},{6,4},{7,5},{8,10},{9,11},{10,... | collective-permute-start | bytes 368648 | tf_op jit(solution)/shard_map/ppermute | solution.py:248
  23.5 15.4 %collective-permute-start.3 = (bf16[768,384]{0,1:T(8,128)(2,1)}, bf16[768,384]{0,1:T(8,128)(2,1)}, u32[]{:S(2)}, u32[]{:S(2)}) collective-permute-start(bf16[768,384]{0,1:T(8,128)(2,1)} %get-tuple-element.93), channel_id=1, source_target_pairs={{0,2},{1,3},{2,0},{3,1},{4,6},{5,7},{6,4},{7,5},{8,10},{9,11},{10,... | collective-permute-start | bytes 1769480 | tf_op jit(solution)/shard_map/ppermute | solution.py:248
  25.3 11.9 %collective-permute-start.5 = (bf16[256,384]{1,0:T(8,128)(2,1)}, bf16[256,384]{1,0:T(8,128)(2,1)}, u32[]{:S(2)}, u32[]{:S(2)}) collective-permute-start(bf16[256,384]{1,0:T(8,128)(2,1)} %pad_maximum_fusion.5.qg_ref.refs_3_.refs_0_), channel_id=1, source_target_pairs={{0,8},{1,9},{2,10},{3,11},{4,12},{5,13},{6,14},{7,15},{8,0},{9,1},... | collective-permute-start | bytes 589832 | tf_op jit(solution)/shard_map/ppermute | solution.py:248
  28.2 18.6 %collective-permute-start.4 = (bf16[256,384]{1,0:T(8,128)(2,1)}, bf16[256,384]{1,0:T(8,128)(2,1)}, u32[]{:S(2)}, u32[]{:S(2)}) collective-permute-start(bf16[256,384]{1,0:T(8,128)(2,1)} %pad_maximum_fusion.5.qg_ref.refs_3_.refs_0_), channel_id=1, source_target_pairs={{0,4},{1,5},{2,6},{3,7},{4,0},{5,1},{6,2},{7,3},{8,12},{9,13},{10,... | collective-permute-start | bytes 589832 | tf_op jit(solution)/shard_map/ppermute | solution.py:248
  37.3 16.6 %collective-permute-start.6 = (bf16[256,384]{1,0:T(8,128)(2,1)}, bf16[256,384]{1,0:T(8,128)(2,1)}, u32[]{:S(2)}, u32[]{:S(2)}) collective-permute-start(bf16[256,384]{1,0:T(8,128)(2,1)} %collective-permute-done.5.qg_ref.refs_1_.refs_0_), channel_id=1, source_target_pairs={{0,4},{1,5},{2,6},{3,7},{4,0},{5,1},{6,2},{7,3},{8,12},{9,13},{10,... | collective-permute-start | bytes 589832 | tf_op jit(solution)/shard_map/ppermute | solution.py:248
  43.1 3.6 %copy-start.4 = (bf16[768,384]{1,0:T(8,128)(2,1)S(1)}, bf16[768,384]{1,0:T(8,128)(2,1)}, u32[]{:S(2)}) copy-start(bf16[768,384]{1,0:T(8,128)(2,1)} %copy.13.kv_0.refs_2_) | copy-start | bytes 1769476
  57.4 14.5 %copy-start.6 = (bf16[768,384]{1,0:T(8,128)(2,1)S(1)}, bf16[768,384]{1,0:T(8,128)(2,1)}, u32[]{:S(2)}) copy-start(bf16[768,384]{1,0:T(8,128)(2,1)} %copy.14.kv_1.refs_8_) | copy-start | bytes 1769476
  57.4 5.8 %collective-permute-start.9 = (f32[4,6,256]{2,1,0:T(8,128)S(1)}, f32[4,6,256]{2,1,0:T(8,128)S(1)}, u32[]{:S(2)}, u32[]{:S(2)}) collective-permute-start(f32[4,6,256]{2,1,0:T(8,128)S(1)} %pad_maximum_fusion.11), channel_id=1, source_target_pairs={{0,12},{1,13},{2,14},{3,15},{4,8},{5,9},{6,10},{7,11},{8,4},{9,5},... | collective-permute-start | bytes 73736 | tf_op jit(solution)/shard_map/ppermute | solution.py:248
  61.0 4.9 %collective-permute-start.8 = (f32[4,6,256]{2,1,0:T(8,128)S(1)}, f32[4,6,256]{2,1,0:T(8,128)S(1)}, u32[]{:S(2)}, u32[]{:S(2)}) collective-permute-start(f32[4,6,256]{2,1,0:T(8,128)S(1)} %pad_maximum_fusion.11), channel_id=1, source_target_pairs={{0,8},{1,9},{2,10},{3,11},{4,12},{5,13},{6,14},{7,15},{8,0},{9,1},... | collective-permute-start | bytes 73736 | tf_op jit(solution)/shard_map/ppermute | solution.py:248
  61.0 4.9 %collective-permute-start.7 = (f32[4,6,256]{2,1,0:T(8,128)S(1)}, f32[4,6,256]{2,1,0:T(8,128)S(1)}, u32[]{:S(2)}, u32[]{:S(2)}) collective-permute-start(f32[4,6,256]{2,1,0:T(8,128)S(1)} %pad_maximum_fusion.11), channel_id=1, source_target_pairs={{0,4},{1,5},{2,6},{3,7},{4,0},{5,1},{6,2},{7,3},{8,12},{9,13},{10,... | collective-permute-start | bytes 73736 | tf_op jit(solution)/shard_map/ppermute | solution.py:248
  66.1 25.0 %collective-permute-start.10 = (bf16[192,256]{1,0:T(8,128)(2,1)S(1)}, bf16[192,256]{1,0:T(8,128)(2,1)S(1)}, u32[]{:S(2)}, u32[]{:S(2)}) collective-permute-start(bf16[192,256]{1,0:T(8,128)(2,1)S(1)} %fusion.3), channel_id=1, source_target_pairs={{0,4},{1,5},{2,6},{3,7},{4,0},{5,1},{6,2},{7,3},{8,12},{9,13},{10,... | collective-permute-start | bytes 294920 | tf_op jit(solution)/shard_map/ppermute | solution.py:248
  66.4 5.4 %collective-permute-start.11 = (bf16[192,256]{1,0:T(8,128)(2,1)S(1)}, bf16[192,256]{1,0:T(8,128)(2,1)S(1)}, u32[]{:S(2)}, u32[]{:S(2)}) collective-permute-start(bf16[192,256]{1,0:T(8,128)(2,1)S(1)} %fusion.2), channel_id=1, source_target_pairs={{0,4},{1,5},{2,6},{3,7},{4,0},{5,1},{6,2},{7,3},{8,12},{9,13},{10,... | collective-permute-start | bytes 294920 | tf_op jit(solution)/shard_map/ppermute | solution.py:248
  79.6 20.5 %collective-permute-start.18 = (bf16[768,384]{1,0:T(8,128)(2,1)S(1)}, bf16[768,384]{1,0:T(8,128)(2,1)S(1)}, u32[]{:S(2)}, u32[]{:S(2)}) collective-permute-start(bf16[768,384]{1,0:T(8,128)(2,1)S(1)} %get-tuple-element.57), channel_id=1, source_target_pairs={{0,2},{1,3},{2,0},{3,1},{4,6},{5,7},{6,4},{7,5},{8,10},{9,11},{10,... | collective-permute-start | bytes 1769480 | tf_op jit(solution)/shard_map/ppermute | solution.py:248
  80.4 6.6 %collective-permute-start.12 = (bf16[192,256]{1,0:T(8,128)(2,1)S(1)}, bf16[192,256]{1,0:T(8,128)(2,1)S(1)}, u32[]{:S(2)}, u32[]{:S(2)}) collective-permute-start(bf16[192,256]{1,0:T(8,128)(2,1)S(1)} %add_convert_fusion.2), channel_id=1, source_target_pairs={{0,8},{1,9},{2,10},{3,11},{4,12},{5,13},{6,14},{7,15},{8,0},{9,1},... | collective-permute-start | bytes 294920 | tf_op jit(solution)/shard_map/ppermute | solution.py:248
  85.0 4.7 %collective-permute-start.13 = (bf16[192,256]{1,0:T(8,128)(2,1)S(1)}, bf16[192,256]{1,0:T(8,128)(2,1)S(1)}, u32[]{:S(2)}, u32[]{:S(2)}) collective-permute-start(bf16[192,256]{1,0:T(8,128)(2,1)S(1)} %get-tuple-element.63), channel_id=1, source_target_pairs={{0,4},{1,5},{2,6},{3,7},{4,0},{5,1},{6,2},{7,3},{8,12},{9,13},{10,... | collective-permute-start | bytes 294920 | tf_op jit(solution)/shard_map/ppermute | solution.py:248
  89.7 8.7 %collective-permute-start.15 = (bf16[192,256]{1,0:T(8,128)(2,1)S(1)}, bf16[192,256]{1,0:T(8,128)(2,1)S(1)}, u32[]{:S(2)}, u32[]{:S(2)}) collective-permute-start(bf16[192,256]{1,0:T(8,128)(2,1)S(1)} %add_convert_fusion.1), channel_id=1, source_target_pairs={{0,8},{1,9},{2,10},{3,11},{4,12},{5,13},{6,14},{7,15},{8,0},{9,1},... | collective-permute-start | bytes 294920 | tf_op jit(solution)/shard_map/ppermute | solution.py:248
  93.7 4.7 %collective-permute-start.14 = (bf16[192,256]{1,0:T(8,128)(2,1)S(1)}, bf16[192,256]{1,0:T(8,128)(2,1)S(1)}, u32[]{:S(2)}, u32[]{:S(2)}) collective-permute-start(bf16[192,256]{1,0:T(8,128)(2,1)S(1)} %get-tuple-element.70), channel_id=1, source_target_pairs={{0,4},{1,5},{2,6},{3,7},{4,0},{5,1},{6,2},{7,3},{8,12},{9,13},{10,... | collective-permute-start | bytes 294920 | tf_op jit(solution)/shard_map/ppermute | solution.py:248
  98.5 4.7 %collective-permute-start.16 = (bf16[2,192,128]{2,1,0:T(8,128)(2,1)S(1)}, bf16[2,192,128]{2,1,0:T(8,128)(2,1)S(1)}, u32[]{:S(2)}, u32[]{:S(2)}) collective-permute-start(bf16[2,192,128]{2,1,0:T(8,128)(2,1)S(1)} %get-tuple-element.109), channel_id=1, source_target_pairs={{0,2},{1,3},{2,0},{3,1},{4,6},{5,7},{6,4},{7,5},{8,10},{9,11},{10,... | collective-permute-start | bytes 294920 | tf_op jit(solution)/shard_map/ppermute | solution.py:248
  100.2 3.2 %copy-start.12 = (bf16[768,768]{1,0:T(8,128)(2,1)S(1)}, bf16[768,768]{1,0:T(8,128)(2,1)}, u32[]{:S(2)}) copy-start(bf16[768,768]{1,0:T(8,128)(2,1)} %copy.26) | copy-start | bytes 3538948
  100.2 3.2 %copy-start.11 = (bf16[768,768]{1,0:T(8,128)(2,1)S(1)}, bf16[768,768]{1,0:T(8,128)(2,1)}, u32[]{:S(2)}) copy-start(bf16[768,768]{1,0:T(8,128)(2,1)} %copy.27) | copy-start | bytes 3538948
  100.3 5.9 %collective-permute-start.19 = (bf16[2,384,384]{2,1,0:T(8,128)(2,1)S(1)}, bf16[2,384,384]{2,1,0:T(8,128)(2,1)S(1)}, u32[]{:S(2)}, u32[]{:S(2)}) collective-permute-start(bf16[2,384,384]{2,1,0:T(8,128)(2,1)S(1)} %pad_maximum_fusion.4), channel_id=1, source_target_pairs={{0,1},{1,0},{2,3},{3,2},{4,5},{5,4},{6,7},{7,6},{8,9},{9,8},{10,11... | collective-permute-start | bytes 1769480 | tf_op jit(solution)/shard_map/ppermute | solution.py:248
  103.3 1.5 %collective-permute-start.17 = (bf16[2,2,192,64]{3,2,1,0:T(8,128)(2,1)S(1)}, bf16[2,2,192,64]{3,2,1,0:T(8,128)(2,1)S(1)}, u32[]{:S(2)}, u32[]{:S(2)}) collective-permute-start(bf16[2,2,192,64]{3,2,1,0:T(8,128)(2,1)S(1)} %pad_maximum_fusion.6), channel_id=1, source_target_pairs={{0,1},{1,0},{2,3},{3,2},{4,5},{5,4},{6,7},{7,6},{8,9},{9,8},{10,11... | collective-permute-start | bytes 294920 | tf_op jit(solution)/shard_map/ppermute | solution.py:248
  (10 other events, 16.2 us)

commit v5 on v4

v5 whole, which is shorter than its diff:
```python
import functools

import jax
import jax.numpy as jnp
from jax import lax
from jax.experimental import pallas as pl
from jax.experimental.pallas import tpu as pltpu
from jax.sharding import PartitionSpec as P

HEADS = 12
TEAM = 4
MINE = HEADS // TEAM
BF16 = jnp.bfloat16
F32 = jnp.float32
LANES = 128
NT = (((1,), (1,)), ((), ()))


def dot(a, b):
    return jnp.dot(a, b, preferred_element_type=F32)


def dot_nt(a, b):
    return lax.dot_general(a, b, NT, preferred_element_type=F32)


def after(array, *others):
    return lax.optimization_barrier((array, *others))[0]


def low_lanes(shape):
    return lax.broadcasted_iota(jnp.int32, shape, 1) < shape[1] // 2


def lanes_of(part):
    start = part // 2 * LANES
    return slice(start, start + LANES)


def keep_part(array, part):
    low = low_lanes(array.shape)
    return jnp.where(low if part % 2 == 0 else ~low, array, jnp.zeros_like(array))


def team_place(place_ref, quarter):
    relative = (place_ref[0] % TEAM) ^ quarter
    return relative % 2, relative // 2


def store_quarters(place_ref, keep_ref, send_ref, one, two, at):
    mine = one.shape[1] // TEAM
    for quarter in range(TEAM):
        cols = slice(quarter * mine, (quarter + 1) * mine)
        piece = jnp.concatenate([one[:, cols], two[:, cols]], axis=1)
        core, across = team_place(place_ref, quarter)
        for ref, which in ((keep_ref, 0), (send_ref, 1)):

            @pl.when(core == which)
            def _():
                ref[across, at, :] = piece


def slots_kernel(place_ref, points_ref, w_key_ref, w_value_ref, keep_ref, send_ref):
    keys = dot(points_ref[...], w_key_ref[...]).astype(BF16) * jnp.asarray(0.125, BF16)
    values = dot(points_ref[...], w_value_ref[...]).astype(BF16)
    store_quarters(place_ref, keep_ref, send_ref, keys, values, slice(0, keys.shape[0]))


def rows_kernel(
    place_ref, count_ref, latents_ref, d_out_ref, w_query_ref, w_out_ref, keep_ref, send_ref
):
    own = latents_ref.shape[0]
    query = dot(latents_ref[...], w_query_ref[...]).astype(BF16)
    grad = dot_nt(d_out_ref[...], w_out_ref[...]).astype(BF16)
    store_quarters(place_ref, keep_ref, send_ref, query, grad, slice(0, own))
    extra = keep_ref.shape[1] - own, keep_ref.shape[2]
    first = lax.broadcasted_iota(jnp.int32, extra, 1) < extra[1] // 2
    count = jnp.where(first, count_ref[0] // 16, count_ref[0] % 16).astype(F32).astype(BF16)
    for ref in (keep_ref, send_ref):
        for across in range(2):
            ref[across, own:, :] = count


def dead_slots(slot, count_ref, block):
    count = jnp.concatenate([count_ref[block : block + 1, :]] * (slot.shape[1] // LANES), axis=1)
    return slot >= count


def forward_kernel(
    count_ref, qg_ref, keep_ref, core_ref, far_ref, near_t_ref, far_t_ref,
    numer_ref, max_ref, stat_ref, score_ref, weight_ref
):
    rows = qg_ref.shape[0]
    slots = keep_ref.shape[1]
    dim = keep_ref.shape[2] // (2 * MINE)
    depth = score_ref.shape[0]
    kv_refs = [keep_ref.at[0], core_ref.at[0], far_ref.at[0], far_ref.at[1]]
    kv_t_refs = [near_t_ref.at[0], near_t_ref.at[1], far_t_ref.at[0], far_t_ref.at[1]]
    slot = lax.broadcasted_iota(jnp.int32, (slots, rows), 0).astype(F32)
    units = [(head, block) for head in range(MINE) for block in range(TEAM)]
    tops, totals, numers = {}, {}, {}

    def score(step):
        head, block = units[step]
        keys = keep_part(kv_refs[block][:, lanes_of(head)], head)
        score_ref[step % depth] = dot_nt(keys, qg_ref[:, lanes_of(head)])

    def weigh(step):
        dead = dead_slots(slot, count_ref, units[step][1])
        scores = jnp.where(dead, -jnp.inf, score_ref[step % depth])
        tops[step] = jnp.max(scores, axis=0, keepdims=True)
        weights = jnp.exp(scores - tops[step])
        totals[step] = jnp.sum(weights, axis=0, keepdims=True)
        weight_ref[step % depth] = weights.astype(BF16)

    def attend(step):
        head, block = units[step]
        part = MINE + head
        at = slice(part * dim, (part + 1) * dim)
        numers[step] = dot(kv_t_refs[block][at, :], weight_ref[step % depth])
        if block < TEAM - 1:
            return
        steps = range(step - TEAM + 1, step + 1)
        top = functools.reduce(jnp.maximum, [tops[s] for s in steps])
        scale = {s: jnp.exp(tops[s] - top) for s in steps}
        total = sum(scale[s] * totals[s] for s in steps)
        numer = sum(scale[s] * numers[s] for s in steps)
        numer_ref[head * dim : (head + 1) * dim, :] = numer
        half = part % 2 * dim
        grad_t = qg_ref[:, lanes_of(part)].astype(F32).T[half : half + dim, :]
        inner = jnp.sum(grad_t * numer, axis=0, keepdims=True)
        max_ref[head : head + 1, :] = top
        stat_ref[head : head + 1, :] = top + jnp.log(total)
        stat_ref[MINE + head : MINE + head + 1, :] = inner / total

    for step in range(len(units) + 2):
        if step < len(units):
            score(step)
        if 0 <= step - 1 < len(units):
            weigh(step - 1)
        if 0 <= step - 2:
            attend(step - 2)


def backward_kernel(chunks, start, side, first, last, count_ref, *refs):
    qg_refs, stat_refs, refs = refs[:chunks], refs[chunks : 2 * chunks], refs[2 * chunks :]
    even_ref, odd_ref, kv_t_ref, *refs = refs
    kv_refs = even_ref.at[0], odd_ref.at[side]
    if not first:
        sum_in_ref, *refs = refs
    gq_in_ref = None
    if side == 0:
        gq_in_ref, *refs = refs
    gq_ref, sum_ref, total_ref, score_ref, gw_ref, prob_ref, ds_ref = refs
    rows = qg_refs[0].shape[0]
    slots, dim = even_ref.shape[1], even_ref.shape[2] // (2 * MINE)
    depth = score_ref.shape[0]
    slot = lax.broadcasted_iota(jnp.int32, (slots, rows), 0).astype(F32)
    low = low_lanes((slots, LANES))
    units = [(c, head, block) for c in range(chunks) for block in range(2) for head in range(MINE)]
    gq, held = {}, {}

    def product(chunk, block, part):
        return dot_nt(keep_part(kv_refs[block][:, lanes_of(part)], part), qg_refs[chunk][:, lanes_of(part)])

    def score(step):
        chunk, head, block = units[step]
        score_ref[step % depth] = product(chunk, block, head)
        gw_ref[step % depth] = product(chunk, block, MINE + head)

    def weigh(step):
        chunk, head, block = units[step]
        dead = dead_slots(slot, count_ref, 2 * side + block)
        scores = jnp.where(dead, -jnp.inf, score_ref[step % depth])
        prob = jnp.exp(scores - stat_refs[chunk][head : head + 1, :])
        delta = stat_refs[chunk][MINE + head : MINE + head + 1, :]
        prob_ref[step % depth] = prob.astype(BF16)
        ds_ref[step % depth] = (prob * (gw_ref[step % depth] - delta)).astype(BF16)

    def store(chunk, block, part, value):
        held[part] = value
        pair = part // 2 * 2, part // 2 * 2 + 1
        if not all(p in held for p in pair):
            return
        at = block, slice(0, slots), lanes_of(part)
        total = jnp.where(low, held.pop(pair[0]), held.pop(pair[1]))
        if chunk > 0:
            total += total_ref[at]
        elif not first:
            total += sum_in_ref[at]
        if chunk < chunks - 1:
            total_ref[at] = total
            return
        if last:
            scales = [0.125 if p < MINE else 1.0 for p in pair]
            total *= scales[0] if scales[0] == scales[1] else jnp.where(low, *scales)
        sum_ref[at] = total.astype(sum_ref.dtype)

    def collect(step):
        chunk, head, block = units[step]
        qg_ref = qg_refs[chunk]
        store(chunk, block, head, dot(ds_ref[step % depth], qg_ref[:, lanes_of(head)]))
        store(chunk, block, MINE + head, dot(prob_ref[step % depth], qg_ref[:, lanes_of(MINE + head)]))
        at = slice(head * dim, (head + 1) * dim)
        term = dot(kv_t_ref[block, at, :], ds_ref[step % depth])
        if block == 0:
            gq[head] = term if gq_in_ref is None else term + gq_in_ref[start + chunk, at, :]
        else:
            gq_ref[chunk, at, :] = (gq[head] + term).astype(gq_ref.dtype)

    for step in range(len(units) + 2):
        if 0 <= step - 2:
            collect(step - 2)
        if 0 <= step - 1 < len(units):
            weigh(step - 1)
        if step < len(units):
            score(step)


def queries_kernel(
    place_ref, near_ref, far_ref, core_ref, latents_ref, d_out_ref, w_out_ref, w_query_ref,
    result_ref, d_latents_ref, joined_ref
):
    own = latents_ref.shape[0]
    mine = near_ref.shape[1]
    for kind in range(2):
        for relative in range(TEAM):
            core, across = relative % 2, relative // 2
            quarter = (place_ref[0] % TEAM) ^ relative
            piece = core_ref[across, kind] if core else (near_ref, far_ref)[across][kind, :, :own]
            joined_ref[pl.ds(pl.multiple_of(quarter * mine, mine), mine), :] = piece.astype(F32)
        joined = joined_ref[...].T.astype(BF16)
        if kind == 0:
            result_ref[...] = (latents_ref[...].astype(F32) + dot(joined, w_out_ref[...])).astype(BF16)
        else:
            d_latents_ref[...] = (
                d_out_ref[...].astype(F32) + dot_nt(joined, w_query_ref[...])
            ).astype(BF16)


def points_kernel(
    place_ref, near_ref, far_ref, core_ref, w_key_ref, w_value_ref, out_ref, key_ref, value_ref
):
    mine = key_ref.shape[1] // TEAM
    for relative in range(TEAM):
        core, across = relative % 2, relative // 2
        piece = core_ref[across] if core else (near_ref, far_ref)[across][0]
        for quarter in range(TEAM):

            @pl.when((place_ref[0] % TEAM) ^ relative == quarter)
            def _():
                key_ref[:, quarter * mine : (quarter + 1) * mine] = piece[:, :mine]
                value_ref[:, quarter * mine : (quarter + 1) * mine] = piece[:, mine:]

    total = dot_nt(key_ref[...], w_key_ref[...]) + dot_nt(value_ref[...], w_value_ref[...])
    out_ref[...] = total.astype(BF16)


def call(kernel, ins, out_shapes, scratch=(), flops=0, exps=0):
    vmem = pl.BlockSpec(memory_space=pltpu.VMEM)
    smem = pl.BlockSpec(memory_space=pltpu.SMEM)
    moved = sum(a.size * a.dtype.itemsize for a in list(ins) + list(out_shapes))
    return pl.pallas_call(
        kernel,
        in_specs=[smem if a.dtype == jnp.int32 else vmem for a in ins],
        out_specs=[vmem] * len(out_shapes),
        out_shape=out_shapes,
        scratch_shapes=scratch,
        compiler_params=pltpu.CompilerParams(vmem_limit_bytes=40 << 20),
        cost_estimate=pl.CostEstimate(flops=flops // 8, transcendentals=exps // 8, bytes_accessed=moved // 8),
    )(*ins)


def body(size, latents, points, counts, w_query, w_key, w_value, w_out, d_out):
    own, width = latents.shape
    slots = points.shape[0]
    mine = width // TEAM
    shape = jax.ShapeDtypeStruct
    near_bit, far_bit = size // 4, size // 2
    middle = []
    bit = size // 8
    while bit >= TEAM:
        middle.append(bit)
        bit //= 2
    place = lax.axis_index("pts").astype(jnp.int32).reshape(1)

    def swap(array, mask):
        return lax.ppermute(array, "pts", [(i, i ^ mask) for i in range(size)])

    each = own + 16
    keep_qg, send_qg = call(
        rows_kernel,
        [place, counts, latents, d_out, w_query, w_out],
        [shape((2, each, 2 * mine), BF16)] * 2,
        flops=4 * own * width * width,
    )
    keep, send = call(
        slots_kernel,
        [place, after(points, send_qg), w_key, w_value],
        [shape((2, slots, 2 * mine), BF16)] * 2,
        flops=4 * slots * width * width,
    )
    core_qg = swap(send_qg, 1)
    far_qg = swap(jnp.stack([keep_qg[1], core_qg[1]]), 2)
    core = swap(send, 1)
    far = swap(jnp.stack([keep[1], core[1]]), 2)
    blocks = [keep_qg[0], core_qg[0], far_qg[0], far_qg[1]]
    qg = jnp.concatenate([a[:own] for a in blocks], axis=0)
    tail = jnp.concatenate([a[own : own + 1] for a in blocks], axis=0).astype(F32)
    count = 16 * tail[:, :LANES] + tail[:, mine : mine + LANES]
    for mask in middle:
        qg = jnp.concatenate([qg, swap(qg, mask)], axis=0)
    qg = [qg, swap(qg, near_bit), swap(qg, far_bit)]
    qg.append(swap(qg[2], near_bit))
    near_t = jnp.stack([keep[0].T, core[0].T])
    far_t = jnp.swapaxes(far, 1, 2)
    rows = qg[0].shape[0]
    team_slots = TEAM * slots
    work = 2 * rows * team_slots * mine

    numer, tops, stats = [None] * 4, [None] * 4, [None] * 4
    for p in range(4):
        if p:
            qg[p] = after(qg[p], stats[p - 1])
        numer[p], tops[p], stats[p] = call(
            forward_kernel,
            [count, qg[p], keep, core, far, near_t, far_t],
            [shape((mine, rows), F32), shape((MINE, rows), F32), shape((2 * MINE, rows), F32)],
            [pltpu.VMEM((3, slots, rows), F32), pltpu.VMEM((3, slots, rows), BF16)],
            flops=8 * work,
            exps=rows * team_slots * MINE,
        )

    def merge(*parts):
        lse = [p[..., :MINE, :] for p in parts]
        top = functools.reduce(jnp.maximum, lse)
        scale = [jnp.exp(x - top) for x in lse]
        total = sum(scale)
        delta = sum(s * p[..., MINE:, :] for s, p in zip(scale, parts)) / total
        return jnp.concatenate([top + jnp.log(total), delta], axis=-2)

    stat = jnp.stack(stats)
    came = [stat] + [swap(stat, m) for m in (near_bit, far_bit, near_bit + far_bit)]
    final = [merge(*[came[p][q ^ p] for p in range(4)]) for q in range(4)]
    if middle:
        final = jnp.stack(final)
        for mask in reversed(middle):
            half = final.shape[-1] // 2
            final = merge(final[..., :half], swap(final[..., half:], mask))
        for mask in middle:
            final = jnp.concatenate([final, swap(final, mask)], axis=-1)
        final = [final[q] for q in range(4)]

    def add(array, came):
        return array.astype(F32) + came.astype(F32)

    def scaled(p):
        scale = jnp.exp(tops[p] - final[p][:MINE])
        return (numer[p].reshape(MINE, -1, rows) * scale[:, None, :]).reshape(mine, rows)

    order = (3, 2, 1, 0)

    def backward(chunks, side, kind, sums=(), partial=(), last=False):
        kept = (2, slots, 2 * mine)
        return call(
            functools.partial(
                backward_kernel, len(chunks), order.index(chunks[0]), side, not sums, last
            ),
            [count]
            + [qg[p] for p in chunks]
            + [final[p] for p in chunks]
            + ([far, far, far_t] if side else [keep, core, near_t])
            + list(sums)
            + list(partial),
            [shape((len(chunks), mine, rows), kind), shape(kept, BF16 if last else F32)],
            [pltpu.VMEM(kept if len(chunks) > 1 else (1, 8, LANES), F32)]
            + [pltpu.VMEM((2, slots, rows), F32)] * 2
            + [pltpu.VMEM((2, slots, rows), BF16)] * 2,
            flops=7 * work * len(chunks),
            exps=rows * team_slots // 2 * MINE * len(chunks),
        )

    came_a = swap(jnp.stack([scaled(3), scaled(2)]).astype(BF16), far_bit)
    partial, gkv_far = backward(order, 1, F32, last=True)
    came_a, partial = lax.optimization_barrier((came_a, partial))
    came_far = swap(gkv_far, 2)
    near_a = swap(add(scaled(1), came_a[0]).astype(BF16), near_bit)
    gq, total = backward((3, 2), 0, BF16, partial=[partial])
    came_q = swap(gq, far_bit)
    gq, total = backward((1,), 0, F32, [total], [partial])
    near_q = swap(add(gq[0], came_q[0]).astype(BF16), near_bit)
    gq, gkv_near = backward((0,), 0, F32, [total], [partial], True)
    attended = add(add(scaled(0), near_a), came_a[1])
    grad_query = add(add(gq[0], near_q), came_q[1])

    both = jnp.stack([attended, grad_query])
    for mask in reversed(middle):
        half = both.shape[-1] // 2
        both = add(both[..., :half], swap(both[..., half:].astype(BF16), mask))
    both, came_far = lax.optimization_barrier((both.astype(BF16), came_far))
    far_both = swap(both[..., 2 * own :], 2)
    near_both = both[..., : 2 * own]

    core_gkv = swap(jnp.stack([gkv_near[1], came_far[1]]), 1)
    (d_points,) = call(
        points_kernel,
        [place, gkv_near, came_far, core_gkv, w_key, w_value],
        [shape((slots, width), BF16)],
        [pltpu.VMEM((slots, width), BF16)] * 2,
        flops=4 * slots * width * width,
    )
    far_both, d_points = lax.optimization_barrier((far_both, d_points))
    core_both = swap(jnp.stack([near_both[..., own:], far_both[..., own:]]), 1)
    result, d_latents = call(
        queries_kernel,
        [place, near_both, far_both, core_both, latents, d_out, w_out, w_query],
        [shape((own, width), BF16)] * 2,
        [pltpu.VMEM((width, own), F32)],
        flops=4 * own * width * width,
    )
    return (result, d_latents, d_points)


def solution(mesh):
    part = P(("groups", "pts"), None)
    in_specs = (part, part, P(("groups", "pts")), P(), P(), P(), P(), part)
    return jax.shard_map(
        functools.partial(body, mesh.shape["pts"]),
        mesh=mesh,
        in_specs=in_specs,
        out_specs=(part, part, part),
        check_vma=False,
    )
```

time: 109 us -> 89.6 us (0.82)
  other arithmetic: 7.03 us -> 1.57 us
  waiting for transfers between devices: 18.1 us -> 23.4 us
  between operations: 6.97 us -> 1.72 us
  local copies, waits for them, and re-layouts: 12.8 us -> 8.08 us
  Pallas kernels: 35.8 us -> 31.7 us
  matrix products: 3.84 us -> 0 us
    select_n x4 -> x0, other arithmetic: 5.37 us -> none  [sort(): return (jnp.where(test, a, b), jnp.where(test, b, a))]
    ppermute x20 -> x18, waiting for transfers between devices: 18.1 us -> 23.4 us  [swap(): return lax.ppermute(array, 'pts', [(i, i ^ mask) for i in range(size)])]
    transpose x2 -> x0, local copies, waits for them, and re-layouts: 4.75 us -> none  [body(): w.T.reshape(TEAM, mine, width)]
    pallas_call x11 -> x12, Pallas kernels: 35.8 us -> 31.7 us  [call(): pl.pallas_call(kernel, in_specs=[smem if a.dtype == jnp.int32 else vmem f...]
    dot_general x4 -> x0, matrix products: 3.84 us -> none  [dot(): return jnp.dot(a, b, preferred_element_type=F32)]
    unnamed x28 -> x26, local copies, waits for them, and re-layouts: 3.23 us -> 5.6 us
    ppermute x1 -> x2, local copies, waits for them, and re-layouts: 2.12 us -> 0.64 us  [swap(): return lax.ppermute(array, 'pts', [(i, i ^ mask) for i in range(size)])]
    slice x5 -> x8, local copies, waits for them, and re-layouts: 1.52 us -> 0.13 us  [the longest x2 0.06 us: body(): core_gkv = swap(jnp.stack([gkv_near[1], came_far[1]]), 1)]
  transfers between devices with their start and end apart: 20 -> 18, of which waited for: 11 -> 10; matrix products, arithmetic and copies ran while one was open for 15% -> 4% of each run, Pallas kernels for 28% -> 25%
where the time goes in v5:
time: 89.6 us; the launch traced here: 89.2 us
  Pallas kernels  31.7 us (35%)
  waiting for transfers between devices  23.4 us (26%)
  starting transfers between devices  22.8 us (25%)
  local copies, waits for them, and re-layouts  8.08 us (9%)
  between operations  1.72 us (2%)
  other arithmetic  1.57 us (2%)
    pallas_call x12, Pallas kernels, call(): pl.pallas_call(kernel, in_specs=[smem if a.dtype == jnp.int32 else vmem f...  31.7 us
    ppermute x18, waiting for transfers between devices, swap(): return lax.ppermute(array, 'pts', [(i, i ^ mask) for i in range(size)])  23.4 us
    ppermute x18, starting transfers between devices, swap(): return lax.ppermute(array, 'pts', [(i, i ^ mask) for i in range(size)])  22.8 us
    unnamed x26, local copies, waits for them, and re-layouts  5.6 us
  transfers between devices with their start and end apart: 18, of which 10 were waited for; matrix products, arithmetic and copies ran while one was open for 4% of the time, Pallas kernels for 25%

profile of v5, /device:TPU:0, one launch (start us, length us, event | category | flops | bytes accessed | tf_op | source)
XLA Modules:
  0.0 89.2 jit_solution(10677303616207815332)
XLA Ops:
  8.3 1.5 %shard_map.104 = (bf16[2,384,384]{2,1,0:T(8,128)(2,1)S(1)}, bf16[2,384,384]{2,1,0:T(8,128)(2,1)S(1)}) custom-call(s32[1]{0:T(128)} %bitcast.place_ref, bf16[384,768]{1,0:T(8,128)(2,1)S(1)} %copy-done.8, bf16[768,768]{1,0:T(8,128)(2,1)S(1)} %copy-done, bf16[768,768]{1,0:T(8,128)(2,1)S(1)} %copy-done.2), custom_call_target="tpu_custom_call" | custom-call | flops 113246208 | bytes 516096 | tf_op jit(solution)/shard_map/pallas_call | solution.py:263
  11.8 2.6 %collective-permute-start.1 = (bf16[2,80,384]{2,1,0:T(8,128)(2,1)S(1)}, bf16[2,80,384]{2,1,0:T(8,128)(2,1)S(1)}, u32[]{:S(2)}, u32[]{:S(2)}) collective-permute-start(bf16[2,80,384]{2,1,0:T(8,128)(2,1)S(1)} %pad_maximum_fusion.7), channel_id=1, source_target_pairs={{0,2},{1,3},{2,0},{3,1},{4,6},{5,7},{6,4},{7,5},{8,10},{9,11},{10,... | collective-permute-start | bytes 368648 | tf_op jit(solution)/shard_map/ppermute | solution.py:288
  15.4 1.6 %collective-permute-start.3 = (bf16[2,384,384]{1,2,0:T(8,128)(2,1)}, bf16[2,384,384]{1,2,0:T(8,128)(2,1)S(1)}, u32[]{:S(2)}, u32[]{:S(2)}) collective-permute-start(bf16[2,384,384]{1,2,0:T(8,128)(2,1)} %pad_maximum_fusion), channel_id=1, source_target_pairs={{0,2},{1,3},{2,0},{3,1},{4,6},{5,7},{6,4},{7,5},{8,10},{9,11},{10,... | collective-permute-start | bytes 1769480 | tf_op jit(solution)/shard_map/ppermute | solution.py:288
  18.4 3.0 %collective-permute-start.5 = (bf16[256,384]{1,0:T(8,128)(2,1)S(1)}, bf16[256,384]{1,0:T(8,128)(2,1)S(1)}, u32[]{:S(2)}, u32[]{:S(2)}) collective-permute-start(bf16[256,384]{1,0:T(8,128)(2,1)S(1)} %pad_maximum_fusion.3.qg_ref.refs_3_.refs_0_), channel_id=1, source_target_pairs={{0,8},{1,9},{2,10},{3,11},{4,12},{5,13},{6,14},{7,15},{8,0},{9,1},... | collective-permute-start | bytes 589832 | tf_op jit(solution)/shard_map/ppermute | solution.py:288
  21.4 1.6 %collective-permute-start.4 = (bf16[256,384]{1,0:T(8,128)(2,1)S(1)}, bf16[256,384]{1,0:T(8,128)(2,1)S(1)}, u32[]{:S(2)}, u32[]{:S(2)}) collective-permute-start(bf16[256,384]{1,0:T(8,128)(2,1)S(1)} %pad_maximum_fusion.3.qg_ref.refs_3_.refs_0_), channel_id=1, source_target_pairs={{0,4},{1,5},{2,6},{3,7},{4,0},{5,1},{6,2},{7,3},{8,12},{9,13},{10,... | collective-permute-start | bytes 589832 | tf_op jit(solution)/shard_map/ppermute | solution.py:288
  23.0 7.4 %collective-permute-done.5.qg_ref.refs_1_ = bf16[256,384]{1,0:T(8,128)(2,1)S(1)} collective-permute-done((bf16[256,384]{1,0:T(8,128)(2,1)S(1)}, bf16[256,384]{1,0:T(8,128)(2,1)S(1)}, u32[]{:S(2)}, u32[]{:S(2)}) %collective-permute-start.5) | collective-permute-done | bytes 196640 | tf_op jit(solution)/shard_map/ppermute | solution.py:288
  31.9 2.3 %shard_map.105 = (f32[192,256]{1,0:T(8,128)S(1)}, f32[3,256]{1,0:T(4,128)S(1)}, f32[6,256]{1,0:T(8,128)S(1)}) custom-call(f32[4,128]{1,0:T(4,128)S(1)} %fusion.36.count_ref, bf16[256,384]{1,0:T(8,128)(2,1)S(1)} %pad_maximum_fusion.3.qg_ref.refs_3_.refs_0_, bf16[2,384,384]{2,1,0:T(8,128)(2,1)S(1)} %get-tuple-element.42.keep_ref.refs_4_.refs_2_, ...), custom_call_target="tpu_custom_call" | custom-call | flops 150994944 | bytes 419200 | tf_op jit(solution)/shard_map/pallas_call | solution.py:263
  34.2 2.3 %shard_map.106 = (f32[192,256]{1,0:T(8,128)S(1)}, f32[3,256]{1,0:T(4,128)S(1)}, f32[6,256]{1,0:T(8,128)S(1)}) custom-call(f32[4,128]{1,0:T(4,128)S(1)} %fusion.36.count_ref, bf16[256,384]{1,0:T(8,128)(2,1)S(1)} %collective-permute-done.4.qg_ref.refs_2_.refs_0_, bf16[2,384,384]{2,1,0:T(8,128)(2,1)S(1)} %get-tuple-element.42.keep_ref.refs_4_.refs_2_, ...), custom_call_target="tpu_custom_call" | custom-call | flops 150994944 | bytes 419200 | tf_op jit(solution)/shard_map/pallas_call | solution.py:263
  36.6 2.3 %shard_map.107 = (f32[192,256]{1,0:T(8,128)S(1)}, f32[3,256]{1,0:T(4,128)S(1)}, f32[6,256]{1,0:T(8,128)S(1)}) custom-call(f32[4,128]{1,0:T(4,128)S(1)} %fusion.36.count_ref, bf16[256,384]{1,0:T(8,128)(2,1)S(1)} %collective-permute-done.5.qg_ref.refs_1_, bf16[2,384,384]{2,1,0:T(8,128)(2,1)S(1)} %get-tuple-element.42.keep_ref.refs_4_.refs_2_, ...), custom_call_target="tpu_custom_call" | custom-call | flops 150994944 | bytes 419200 | tf_op jit(solution)/shard_map/pallas_call | solution.py:263
  38.9 3.2 %shard_map.108 = (f32[192,256]{1,0:T(8,128)S(1)}, f32[3,256]{1,0:T(4,128)S(1)}, f32[6,256]{1,0:T(8,128)S(1)}) custom-call(f32[4,128]{1,0:T(4,128)S(1)} %fusion.36.count_ref, bf16[256,384]{1,0:T(8,128)(2,1)} %collective-permute-done.6.qg_ref.refs_0_, bf16[2,384,384]{2,1,0:T(8,128)(2,1)S(1)} %get-tuple-element.42.keep_ref.refs_4_.refs_2_, ...), custom_call_target="tpu_custom_call" | custom-call | flops 150994944 | bytes 419200 | tf_op jit(solution)/shard_map/pallas_call | solution.py:263
  42.2 3.4 %collective-permute-start.9 = (f32[4,6,256]{2,1,0:T(8,128)S(1)}, f32[4,6,256]{2,1,0:T(8,128)S(1)}, u32[]{:S(2)}, u32[]{:S(2)}) collective-permute-start(f32[4,6,256]{2,1,0:T(8,128)S(1)} %pad_maximum_fusion.8), channel_id=1, source_target_pairs={{0,12},{1,13},{2,14},{3,15},{4,8},{5,9},{6,10},{7,11},{8,4},{9,5},... | collective-permute-start | bytes 73736 | tf_op jit(solution)/shard_map/ppermute | solution.py:288
  48.0 2.8 %collective-permute-done.8 = f32[4,6,256]{2,1,0:T(8,128)S(1)} collective-permute-done((f32[4,6,256]{2,1,0:T(8,128)S(1)}, f32[4,6,256]{2,1,0:T(8,128)S(1)}, u32[]{:S(2)}, u32[]{:S(2)}) %collective-permute-start.8) | collective-permute-done | bytes 24608 | tf_op jit(solution)/shard_map/ppermute | solution.py:288
  50.9 1.7 %collective-permute-start.10 = (bf16[2,192,256]{2,1,0:T(8,128)(2,1)S(1)}, bf16[2,192,256]{2,1,0:T(8,128)(2,1)S(1)}, u32[]{:S(2)}, u32[]{:S(2)}) collective-permute-start(bf16[2,192,256]{2,1,0:T(8,128)(2,1)S(1)} %pad_maximum_fusion.4), channel_id=1, source_target_pairs={{0,8},{1,9},{2,10},{3,11},{4,12},{5,13},{6,14},{7,15},{8,0},{9,1},... | collective-permute-start | bytes 589832 | tf_op jit(solution)/shard_map/ppermute | solution.py:288
  52.8 7.2 %shard_map.109 = (f32[4,192,256]{2,1,0:T(8,128)S(1)}, bf16[2,384,384]{2,1,0:T(8,128)(2,1)S(1)}) custom-call(f32[4,128]{1,0:T(4,128)S(1)} %fusion.36.count_ref, bf16[256,384]{1,0:T(8,128)(2,1)} %collective-permute-done.6.qg_ref.refs_0_, bf16[256,384]{1,0:T(8,128)(2,1)S(1)} %collective-permute-done.5.qg_ref.refs_1_, ...), custom_call_target="tpu_custom_call" | custom-call | flops 528482304 | bytes 494848 | tf_op jit(solution)/shard_map/pallas_call | solution.py:263
  60.6 4.1 %shard_map.110 = (bf16[2,192,256]{2,1,0:T(8,128)(2,1)S(1)}, f32[2,384,384]{2,1,0:T(8,128)S(1)}) custom-call(f32[4,128]{1,0:T(4,128)S(1)} %fusion.36.count_ref, bf16[256,384]{1,0:T(8,128)(2,1)} %collective-permute-done.6.qg_ref.refs_0_, bf16[256,384]{1,0:T(8,128)(2,1)S(1)} %collective-permute-done.5.qg_ref.refs_1_, ...), custom_call_target="tpu_custom_call" | custom-call | flops 264241152 | bytes 542464 | tf_op jit(solution)/shard_map/pallas_call | solution.py:263
  65.4 1.5 %collective-permute-start.14 = (bf16[2,384,384]{2,1,0:T(8,128)(2,1)S(1)}, bf16[2,384,384]{2,1,0:T(8,128)(2,1)S(1)}, u32[]{:S(2)}, u32[]{:S(2)}) collective-permute-start(bf16[2,384,384]{2,1,0:T(8,128)(2,1)S(1)} %get-tuple-element.67), channel_id=1, source_target_pairs={{0,2},{1,3},{2,0},{3,1},{4,6},{5,7},{6,4},{7,5},{8,10},{9,11},{10,... | collective-permute-start | bytes 1769480 | tf_op jit(solution)/shard_map/ppermute | solution.py:288
  66.9 2.3 %collective-permute-start.11 = (bf16[192,256]{1,0:T(8,128)(2,1)S(1)}, bf16[192,256]{1,0:T(8,128)(2,1)S(1)}, u32[]{:S(2)}, u32[]{:S(2)}) collective-permute-start(bf16[192,256]{1,0:T(8,128)(2,1)S(1)} %fusion.2), channel_id=1, source_target_pairs={{0,4},{1,5},{2,6},{3,7},{4,0},{5,1},{6,2},{7,3},{8,12},{9,13},{10,... | collective-permute-start | bytes 294920 | tf_op jit(solution)/shard_map/ppermute | solution.py:288
  69.2 1.7 %shard_map.111 = (f32[1,192,256]{2,1,0:T(8,128)S(1)}, f32[2,384,384]{2,1,0:T(8,128)S(1)}) custom-call(f32[4,128]{1,0:T(4,128)S(1)} %fusion.36.count_ref, bf16[256,384]{1,0:T(8,128)(2,1)S(1)} %collective-permute-done.4.qg_ref.refs_2_.refs_0_, f32[6,256]{1,0:T(8,128)S(1)} %get-tuple-element.106.refs_6_.refs_1_, ...), custom_call_target="tpu_custom_call" | custom-call | flops 132120576 | bytes 664576 | tf_op jit(solution)/shard_map/pallas_call | solution.py:263
  70.9 4.8 %collective-permute-done.12 = bf16[2,192,256]{2,1,0:T(8,128)(2,1)S(1)} collective-permute-done((bf16[2,192,256]{2,1,0:T(8,128)(2,1)S(1)}, bf16[2,192,256]{2,1,0:T(8,128)(2,1)S(1)}, u32[]{:S(2)}, u32[]{:S(2)}) %collective-permute-start.12) | collective-permute-done | bytes 196640 | tf_op jit(solution)/shard_map/ppermute | solution.py:288
  75.8 1.7 %shard_map.112 = (f32[1,192,256]{2,1,0:T(8,128)S(1)}, bf16[2,384,384]{2,1,0:T(8,128)(2,1)S(1)}) custom-call(f32[4,128]{1,0:T(4,128)S(1)} %fusion.36.count_ref, bf16[256,384]{1,0:T(8,128)(2,1)S(1)} %pad_maximum_fusion.3.qg_ref.refs_3_.refs_0_, f32[6,256]{1,0:T(8,128)S(1)} %get-tuple-element.107.refs_7_.refs_1_, ...), custom_call_target="tpu_custom_call" | custom-call | flops 132120576 | bytes 590848 | tf_op jit(solution)/shard_map/pallas_call | solution.py:263
  77.6 2.9 %collective-permute-done.13 = bf16[192,256]{1,0:T(8,128)(2,1)S(1)} collective-permute-done((bf16[192,256]{1,0:T(8,128)(2,1)S(1)}, bf16[192,256]{1,0:T(8,128)(2,1)S(1)}, u32[]{:S(2)}, u32[]{:S(2)}) %collective-permute-start.13) | collective-permute-done | bytes 98336 | tf_op jit(solution)/shard_map/ppermute | solution.py:288
  80.9 1.5 %collective-permute-start.15 = (bf16[2,192,128]{2,1,0:T(8,128)(2,1)S(1)}, bf16[2,192,128]{2,1,0:T(8,128)(2,1)S(1)}, u32[]{:S(2)}, u32[]{:S(2)}) collective-permute-start(bf16[2,192,128]{2,1,0:T(8,128)(2,1)S(1)} %get-tuple-element.91), channel_id=1, source_target_pairs={{0,2},{1,3},{2,0},{3,1},{4,6},{5,7},{6,4},{7,5},{8,10},{9,11},{10,... | collective-permute-start | bytes 294920 | tf_op jit(solution)/shard_map/ppermute | solution.py:288
  82.8 2.9 %shard_map.113 = bf16[384,768]{1,0:T(8,128)(2,1)} custom-call(s32[1]{0:T(128)} %bitcast.place_ref, bf16[2,384,384]{2,1,0:T(8,128)(2,1)S(1)} %get-tuple-element.69.near_ref, bf16[2,384,384]{2,1,0:T(8,128)(2,1)S(1)} %collective-permute-done.14.far_ref, bf16[2,384,384]{2,1,0:T(8,128)(2,1)S(1)} %collective-permute-done.16.core_ref, ...), custom_call_target="tpu_custom_call" | custom-call | flops 113246208 | bytes 589824 | tf_op jit(solution)/shard_map/pallas_call | solution.py:263
  86.3 1.4 %collective-permute-done.17.core_ref = bf16[2,2,192,64]{3,2,1,0:T(8,128)(2,1)S(1)} collective-permute-done((bf16[2,2,192,64]{3,2,1,0:T(8,128)(2,1)S(1)}, bf16[2,2,192,64]{3,2,1,0:T(8,128)(2,1)S(1)}, u32[]{:S(2)}, u32[]{:S(2)}) %collective-permute-start.17) | collective-permute-done | bytes 98336 | tf_op jit(solution)/shard_map/ppermute | solution.py:288
  (91 shorter events, 19.5 us)
Async XLA Ops:
  6.5 5.2 %collective-permute-start = (bf16[2,80,384]{2,1,0:T(8,128)(2,1)S(1)}, bf16[2,80,384]{2,1,0:T(8,128)(2,1)S(1)}, u32[]{:S(2)}, u32[]{:S(2)}) collective-permute-start(bf16[2,80,384]{2,1,0:T(8,128)(2,1)S(1)} %get-tuple-element.40), channel_id=1, source_target_pairs={{0,1},{1,0},{2,3},{3,2},{4,5},{5,4},{6,7},{7,6},{8,9},{9,8},{10,11... | collective-permute-start | bytes 368648 | tf_op jit(solution)/shard_map/ppermute | solution.py:288
  10.9 3.5 %collective-permute-start.2 = (bf16[2,384,384]{1,2,0:T(8,128)(2,1)}, bf16[2,384,384]{1,2,0:T(8,128)(2,1)S(1)}, u32[]{:S(2)}, u32[]{:S(2)}) collective-permute-start(bf16[2,384,384]{1,2,0:T(8,128)(2,1)} %copy.11), channel_id=1, source_target_pairs={{0,1},{1,0},{2,3},{3,2},{4,5},{5,4},{6,7},{7,6},{8,9},{9,8},{10,11... | collective-permute-start | bytes 1769480 | tf_op jit(solution)/shard_map/ppermute | solution.py:288
  11.8 6.5 %collective-permute-start.1 = (bf16[2,80,384]{2,1,0:T(8,128)(2,1)S(1)}, bf16[2,80,384]{2,1,0:T(8,128)(2,1)S(1)}, u32[]{:S(2)}, u32[]{:S(2)}) collective-permute-start(bf16[2,80,384]{2,1,0:T(8,128)(2,1)S(1)} %pad_maximum_fusion.7), channel_id=1, source_target_pairs={{0,2},{1,3},{2,0},{3,1},{4,6},{5,7},{6,4},{7,5},{8,10},{9,11},{10,... | collective-permute-start | bytes 368648 | tf_op jit(solution)/shard_map/ppermute | solution.py:288
  15.4 16.2 %collective-permute-start.3 = (bf16[2,384,384]{1,2,0:T(8,128)(2,1)}, bf16[2,384,384]{1,2,0:T(8,128)(2,1)S(1)}, u32[]{:S(2)}, u32[]{:S(2)}) collective-permute-start(bf16[2,384,384]{1,2,0:T(8,128)(2,1)} %pad_maximum_fusion), channel_id=1, source_target_pairs={{0,2},{1,3},{2,0},{3,1},{4,6},{5,7},{6,4},{7,5},{8,10},{9,11},{10,... | collective-permute-start | bytes 1769480 | tf_op jit(solution)/shard_map/ppermute | solution.py:288
  18.4 12.0 %collective-permute-start.5 = (bf16[256,384]{1,0:T(8,128)(2,1)S(1)}, bf16[256,384]{1,0:T(8,128)(2,1)S(1)}, u32[]{:S(2)}, u32[]{:S(2)}) collective-permute-start(bf16[256,384]{1,0:T(8,128)(2,1)S(1)} %pad_maximum_fusion.3.qg_ref.refs_3_.refs_0_), channel_id=1, source_target_pairs={{0,8},{1,9},{2,10},{3,11},{4,12},{5,13},{6,14},{7,15},{8,0},{9,1},... | collective-permute-start | bytes 589832 | tf_op jit(solution)/shard_map/ppermute | solution.py:288
  21.4 12.8 %collective-permute-start.4 = (bf16[256,384]{1,0:T(8,128)(2,1)S(1)}, bf16[256,384]{1,0:T(8,128)(2,1)S(1)}, u32[]{:S(2)}, u32[]{:S(2)}) collective-permute-start(bf16[256,384]{1,0:T(8,128)(2,1)S(1)} %pad_maximum_fusion.3.qg_ref.refs_3_.refs_0_), channel_id=1, source_target_pairs={{0,4},{1,5},{2,6},{3,7},{4,0},{5,1},{6,2},{7,3},{8,12},{9,13},{10,... | collective-permute-start | bytes 589832 | tf_op jit(solution)/shard_map/ppermute | solution.py:288
  30.4 8.5 %collective-permute-start.6 = (bf16[256,384]{1,0:T(8,128)(2,1)S(1)}, bf16[256,384]{1,0:T(8,128)(2,1)}, u32[]{:S(2)}, u32[]{:S(2)}) collective-permute-start(bf16[256,384]{1,0:T(8,128)(2,1)S(1)} %collective-permute-done.5.qg_ref.refs_1_), channel_id=1, source_target_pairs={{0,4},{1,5},{2,6},{3,7},{4,0},{5,1},{6,2},{7,3},{8,12},{9,13},{10,... | collective-permute-start | bytes 589832 | tf_op jit(solution)/shard_map/ppermute | solution.py:288
  42.2 5.8 %collective-permute-start.9 = (f32[4,6,256]{2,1,0:T(8,128)S(1)}, f32[4,6,256]{2,1,0:T(8,128)S(1)}, u32[]{:S(2)}, u32[]{:S(2)}) collective-permute-start(f32[4,6,256]{2,1,0:T(8,128)S(1)} %pad_maximum_fusion.8), channel_id=1, source_target_pairs={{0,12},{1,13},{2,14},{3,15},{4,8},{5,9},{6,10},{7,11},{8,4},{9,5},... | collective-permute-start | bytes 73736 | tf_op jit(solution)/shard_map/ppermute | solution.py:288
  45.6 5.2 %collective-permute-start.8 = (f32[4,6,256]{2,1,0:T(8,128)S(1)}, f32[4,6,256]{2,1,0:T(8,128)S(1)}, u32[]{:S(2)}, u32[]{:S(2)}) collective-permute-start(f32[4,6,256]{2,1,0:T(8,128)S(1)} %pad_maximum_fusion.8), channel_id=1, source_target_pairs={{0,8},{1,9},{2,10},{3,11},{4,12},{5,13},{6,14},{7,15},{8,0},{9,1},... | collective-permute-start | bytes 73736 | tf_op jit(solution)/shard_map/ppermute | solution.py:288
  45.7 5.0 %collective-permute-start.7 = (f32[4,6,256]{2,1,0:T(8,128)S(1)}, f32[4,6,256]{2,1,0:T(8,128)S(1)}, u32[]{:S(2)}, u32[]{:S(2)}) collective-permute-start(f32[4,6,256]{2,1,0:T(8,128)S(1)} %pad_maximum_fusion.8), channel_id=1, source_target_pairs={{0,4},{1,5},{2,6},{3,7},{4,0},{5,1},{6,2},{7,3},{8,12},{9,13},{10,... | collective-permute-start | bytes 73736 | tf_op jit(solution)/shard_map/ppermute | solution.py:288
  50.9 9.7 %collective-permute-start.10 = (bf16[2,192,256]{2,1,0:T(8,128)(2,1)S(1)}, bf16[2,192,256]{2,1,0:T(8,128)(2,1)S(1)}, u32[]{:S(2)}, u32[]{:S(2)}) collective-permute-start(bf16[2,192,256]{2,1,0:T(8,128)(2,1)S(1)} %pad_maximum_fusion.4), channel_id=1, source_target_pairs={{0,8},{1,9},{2,10},{3,11},{4,12},{5,13},{6,14},{7,15},{8,0},{9,1},... | collective-permute-start | bytes 589832 | tf_op jit(solution)/shard_map/ppermute | solution.py:288
  64.7 11.0 %collective-permute-start.12 = (bf16[2,192,256]{2,1,0:T(8,128)(2,1)S(1)}, bf16[2,192,256]{2,1,0:T(8,128)(2,1)S(1)}, u32[]{:S(2)}, u32[]{:S(2)}) collective-permute-start(bf16[2,192,256]{2,1,0:T(8,128)(2,1)S(1)} %get-tuple-element.66), channel_id=1, source_target_pairs={{0,8},{1,9},{2,10},{3,11},{4,12},{5,13},{6,14},{7,15},{8,0},{9,1},... | collective-permute-start | bytes 589832 | tf_op jit(solution)/shard_map/ppermute | solution.py:288
  65.4 15.3 %collective-permute-start.14 = (bf16[2,384,384]{2,1,0:T(8,128)(2,1)S(1)}, bf16[2,384,384]{2,1,0:T(8,128)(2,1)S(1)}, u32[]{:S(2)}, u32[]{:S(2)}) collective-permute-start(bf16[2,384,384]{2,1,0:T(8,128)(2,1)S(1)} %get-tuple-element.67), channel_id=1, source_target_pairs={{0,2},{1,3},{2,0},{3,1},{4,6},{5,7},{6,4},{7,5},{8,10},{9,11},{10,... | collective-permute-start | bytes 1769480 | tf_op jit(solution)/shard_map/ppermute | solution.py:288
  66.9 10.6 %collective-permute-start.11 = (bf16[192,256]{1,0:T(8,128)(2,1)S(1)}, bf16[192,256]{1,0:T(8,128)(2,1)S(1)}, u32[]{:S(2)}, u32[]{:S(2)}) collective-permute-start(bf16[192,256]{1,0:T(8,128)(2,1)S(1)} %fusion.2), channel_id=1, source_target_pairs={{0,4},{1,5},{2,6},{3,7},{4,0},{5,1},{6,2},{7,3},{8,12},{9,13},{10,... | collective-permute-start | bytes 294920 | tf_op jit(solution)/shard_map/ppermute | solution.py:288
  75.7 4.8 %collective-permute-start.13 = (bf16[192,256]{1,0:T(8,128)(2,1)S(1)}, bf16[192,256]{1,0:T(8,128)(2,1)S(1)}, u32[]{:S(2)}, u32[]{:S(2)}) collective-permute-start(bf16[192,256]{1,0:T(8,128)(2,1)S(1)} %fusion.6), channel_id=1, source_target_pairs={{0,4},{1,5},{2,6},{3,7},{4,0},{5,1},{6,2},{7,3},{8,12},{9,13},{10,... | collective-permute-start | bytes 294920 | tf_op jit(solution)/shard_map/ppermute | solution.py:288
  80.6 2.2 %copy-start.1 = (bf16[768,768]{1,0:T(8,128)(2,1)S(1)}, bf16[768,768]{1,0:T(8,128)(2,1)}, u32[]{:S(2)}) copy-start(bf16[768,768]{1,0:T(8,128)(2,1)} %w_key_ref.3) | copy-start | bytes 3538948
  80.6 2.2 %copy-start.3 = (bf16[768,768]{1,0:T(8,128)(2,1)S(1)}, bf16[768,768]{1,0:T(8,128)(2,1)}, u32[]{:S(2)}) copy-start(bf16[768,768]{1,0:T(8,128)(2,1)} %w_value_ref.3) | copy-start | bytes 3538948
  80.7 2.1 %collective-permute-start.16 = (bf16[2,384,384]{2,1,0:T(8,128)(2,1)S(1)}, bf16[2,384,384]{2,1,0:T(8,128)(2,1)S(1)}, u32[]{:S(2)}, u32[]{:S(2)}) collective-permute-start(bf16[2,384,384]{2,1,0:T(8,128)(2,1)S(1)} %pad_maximum_fusion.2), channel_id=1, source_target_pairs={{0,1},{1,0},{2,3},{3,2},{4,5},{5,4},{6,7},{7,6},{8,9},{9,8},{10,11... | collective-permute-start | bytes 1769480 | tf_op jit(solution)/shard_map/ppermute | solution.py:288
  80.9 5.3 %collective-permute-start.15 = (bf16[2,192,128]{2,1,0:T(8,128)(2,1)S(1)}, bf16[2,192,128]{2,1,0:T(8,128)(2,1)S(1)}, u32[]{:S(2)}, u32[]{:S(2)}) collective-permute-start(bf16[2,192,128]{2,1,0:T(8,128)(2,1)S(1)} %get-tuple-element.91), channel_id=1, source_target_pairs={{0,2},{1,3},{2,0},{3,1},{4,6},{5,7},{6,4},{7,5},{8,10},{9,11},{10,... | collective-permute-start | bytes 294920 | tf_op jit(solution)/shard_map/ppermute | solution.py:288
  82.5 5.3 %copy-start.10 = (bf16[64,768]{1,0:T(8,128)(2,1)S(1)}, bf16[64,768]{1,0:T(8,128)(2,1)}, u32[]{:S(2)}) copy-start(bf16[64,768]{1,0:T(8,128)(2,1)} %latents_ref.3) | copy-start | bytes 294916
  82.5 5.3 %copy-start.12 = (bf16[64,768]{1,0:T(8,128)(2,1)S(1)}, bf16[64,768]{1,0:T(8,128)(2,1)}, u32[]{:S(2)}) copy-start(bf16[64,768]{1,0:T(8,128)(2,1)} %d_out_ref.3) | copy-start | bytes 294916
  82.8 5.0 %copy-start.5 = (bf16[768,768]{1,0:T(8,128)(2,1)S(1)}, bf16[768,768]{1,0:T(8,128)(2,1)}, u32[]{:S(2)}) copy-start(bf16[768,768]{1,0:T(8,128)(2,1)} %w_query_ref.3) | copy-start | bytes 3538948
  82.8 5.0 %copy-start.7 = (bf16[768,768]{1,0:T(8,128)(2,1)S(1)}, bf16[768,768]{1,0:T(8,128)(2,1)}, u32[]{:S(2)}) copy-start(bf16[768,768]{1,0:T(8,128)(2,1)} %w_out_ref.3) | copy-start | bytes 3538948
  86.3 1.5 %collective-permute-start.17 = (bf16[2,2,192,64]{3,2,1,0:T(8,128)(2,1)S(1)}, bf16[2,2,192,64]{3,2,1,0:T(8,128)(2,1)S(1)}, u32[]{:S(2)}, u32[]{:S(2)}) collective-permute-start(bf16[2,2,192,64]{3,2,1,0:T(8,128)(2,1)S(1)} %pad_maximum_fusion.6), channel_id=1, source_target_pairs={{0,1},{1,0},{2,3},{3,2},{4,5},{5,4},{6,7},{7,6},{8,9},{9,8},{10,11... | collective-permute-start | bytes 294920 | tf_op jit(solution)/shard_map/ppermute | solution.py:288
  (7 other events, 8.5 us)

commit v6 on v5

--- a/solution.py
+++ b/solution.py
@@ -24,10 +24,6 @@
     return lax.dot_general(a, b, NT, preferred_element_type=F32)
 
 
-def after(array, *others):
-    return lax.optimization_barrier((array, *others))[0]
-
-
 def low_lanes(shape):
     return lax.broadcasted_iota(jnp.int32, shape, 1) < shape[1] // 2
 
@@ -67,10 +63,30 @@
 
 
 def rows_kernel(
-    place_ref, count_ref, latents_ref, d_out_ref, w_query_ref, w_out_ref, keep_ref, send_ref
+    place_ref, count_ref, latents_hbm, d_out_hbm, w_query_hbm, w_out_hbm,
+    keep_ref, send_ref, latents_ref, d_out_ref, w_query_ref, w_out_ref, sems
 ):
-    own = latents_ref.shape[0]
+    own, pieces = latents_ref.shape[0], sems.shape[1] - 1
+    loads = []
+    for i, (small, small_to, big, big_to) in enumerate(
+        (
+            (latents_hbm, latents_ref, w_query_hbm, w_query_ref),
+            (d_out_hbm, d_out_ref, w_out_hbm, w_out_ref),
+        )
+    ):
+        step = big.shape[0] // pieces
+        group = [pltpu.make_async_copy(small, small_to, sems.at[i, pieces])]
+        for k in range(pieces):
+            at = slice(k * step, (k + 1) * step)
+            group.append(pltpu.make_async_copy(big.at[at], big_to.at[at], sems.at[i, k]))
+        for copy in group:
+            copy.start()
+        loads.append(group)
+    for copy in loads[0]:
+        copy.wait()
     query = dot(latents_ref[...], w_query_ref[...]).astype(BF16)
+    for copy in loads[1]:
+        copy.wait()
     grad = dot_nt(d_out_ref[...], w_out_ref[...]).astype(BF16)
     store_quarters(place_ref, keep_ref, send_ref, query, grad, slice(0, own))
     extra = keep_ref.shape[1] - own, keep_ref.shape[2]
@@ -79,6 +95,11 @@
     for ref in (keep_ref, send_ref):
         for across in range(2):
             ref[across, own:, :] = count
+
+
+def turn_kernel(picks, *refs):
+    for i, (ref, which) in enumerate(picks):
+        refs[-1][i] = refs[ref][which].T
 
 
 def dead_slots(slot, count_ref, block):
@@ -256,13 +277,14 @@
     out_ref[...] = total.astype(BF16)
 
 
-def call(kernel, ins, out_shapes, scratch=(), flops=0, exps=0):
+def call(kernel, ins, out_shapes, scratch=(), flops=0, exps=0, space=pltpu.VMEM):
     vmem = pl.BlockSpec(memory_space=pltpu.VMEM)
+    other = pl.BlockSpec(memory_space=space)
     smem = pl.BlockSpec(memory_space=pltpu.SMEM)
     moved = sum(a.size * a.dtype.itemsize for a in list(ins) + list(out_shapes))
     return pl.pallas_call(
         kernel,
-        in_specs=[smem if a.dtype == jnp.int32 else vmem for a in ins],
+        in_specs=[smem if a.dtype == jnp.int32 else other for a in ins],
         out_specs=[vmem] * len(out_shapes),
         out_shape=out_shapes,
         scratch_shapes=scratch,
@@ -292,11 +314,15 @@
         rows_kernel,
         [place, counts, latents, d_out, w_query, w_out],
         [shape((2, each, 2 * mine), BF16)] * 2,
+        [pltpu.VMEM((own, width), BF16)] * 2
+        + [pltpu.VMEM((width, width), BF16)] * 2
+        + [pltpu.SemaphoreType.DMA((2, 5))],
         flops=4 * own * width * width,
+        space=pltpu.HBM,
     )
     keep, send = call(
         slots_kernel,
-        [place, after(points, send_qg), w_key, w_value],
+        [place, points, w_key, w_value],
         [shape((2, slots, 2 * mine), BF16)] * 2,
         flops=4 * slots * width * width,
     )
@@ -311,17 +337,18 @@
     for mask in middle:
         qg = jnp.concatenate([qg, swap(qg, mask)], axis=0)
     qg = [qg, swap(qg, near_bit), swap(qg, far_bit)]
-    qg.append(swap(qg[2], near_bit))
-    near_t = jnp.stack([keep[0].T, core[0].T])
-    far_t = jnp.swapaxes(far, 1, 2)
+    turned = [shape((2, 2 * mine, slots), BF16)]
+    (near_t,) = call(functools.partial(turn_kernel, ((0, 0), (1, 0))), [keep, core], turned)
+    (far_t,) = call(functools.partial(turn_kernel, ((0, 0), (0, 1))), [far], turned)
     rows = qg[0].shape[0]
     team_slots = TEAM * slots
     work = 2 * rows * team_slots * mine
 
     numer, tops, stats = [None] * 4, [None] * 4, [None] * 4
     for p in range(4):
-        if p:
-            qg[p] = after(qg[p], stats[p - 1])
+        if p == 2:
+            qg[2], stats[0] = lax.optimization_barrier((qg[2], stats[0]))
+            qg.append(swap(qg[2], near_bit))
         numer[p], tops[p], stats[p] = call(
             forward_kernel,
             [count, qg[p], keep, core, far, near_t, far_t],
@@ -340,10 +367,12 @@
         return jnp.concatenate([top + jnp.log(total), delta], axis=-2)
 
     stat = jnp.stack(stats)
-    came = [stat] + [swap(stat, m) for m in (near_bit, far_bit, near_bit + far_bit)]
-    final = [merge(*[came[p][q ^ p] for p in range(4)]) for q in range(4)]
+    for mask, turn in ((near_bit, 1), (far_bit, 2)):
+        came = swap(stat, mask)
+        stat = merge(stat, jnp.stack([came[q ^ turn] for q in range(4)]))
+    final = [stat[q] for q in range(4)]
     if middle:
-        final = jnp.stack(final)
+        final = stat
         for mask in reversed(middle):
             half = final.shape[-1] // 2
             final = merge(final[..., :half], swap(final[..., half:], mask))
@@ -385,13 +414,17 @@
     came_a, partial = lax.optimization_barrier((came_a, partial))
     came_far = swap(gkv_far, 2)
     near_a = swap(add(scaled(1), came_a[0]).astype(BF16), near_bit)
-    gq, total = backward((3, 2), 0, BF16, partial=[partial])
-    came_q = swap(gq, far_bit)
-    gq, total = backward((1,), 0, F32, [total], [partial])
-    near_q = swap(add(gq[0], came_q[0]).astype(BF16), near_bit)
+    gq, total = backward((3,), 0, BF16, partial=[partial])
+    came = swap(gq[0], near_bit)
+    gq, total = backward((2,), 0, F32, [total], [partial])
+    sent, total = lax.optimization_barrier((add(gq[0], came).astype(BF16), total))
+    far_q = swap(sent, far_bit)
+    gq, total = backward((1,), 0, BF16, [total], [partial])
+    near_q = swap(gq[0], near_bit)
+    came_far, total = lax.optimization_barrier((came_far, total))
     gq, gkv_near = backward((0,), 0, F32, [total], [partial], True)
     attended = add(add(scaled(0), near_a), came_a[1])
-    grad_query = add(add(gq[0], near_q), came_q[1])
+    grad_query = add(add(gq[0], near_q), far_q)
 
     both = jnp.stack([attended, grad_query])
     for mask in reversed(middle):

time: 89.6 us -> 89.3 us (level)
  starting transfers between devices: 22.8 us -> 27.9 us
  local copies, waits for them, and re-layouts: 8.08 us -> 5.82 us
  Pallas kernels: 31.7 us -> 30.5 us
  other arithmetic: 1.57 us -> 0.65 us
  waiting for transfers between devices: 23.4 us -> 22.5 us
    ppermute x18, starting transfers between devices: 22.8 us -> 27.9 us  [swap(): return lax.ppermute(array, 'pts', [(i, i ^ mask) for i in range(size)])]
    pallas_call x2 -> x0, local copies, waits for them, and re-layouts: 1.38 us -> none  [call(): pl.pallas_call(kernel, in_specs=[smem if a.dtype == jnp.int32 else vmem f...]
    pallas_call x12 -> x15, Pallas kernels: 31.7 us -> 30.5 us  [call(): pl.pallas_call(kernel, in_specs=[smem if a.dtype == jnp.int32 else other...]
    unnamed x26 -> x22, local copies, waits for them, and re-layouts: 5.6 us -> 5.41 us
  transfers between devices with their start and end apart: 18 -> 18, of which waited for: 10 -> 10; matrix products, arithmetic and copies ran while one was open for 4% -> 1% of each run, Pallas kernels for 25% -> 28%
where the time goes in v6:
time: 89.3 us; the launch traced here: 89 us
  Pallas kernels  30.5 us (34%)
  starting transfers between devices  27.9 us (31%)
  waiting for transfers between devices  22.5 us (25%)
  local copies, waits for them, and re-layouts  5.82 us (7%)
  between operations  1.67 us (2%)
    pallas_call x15, Pallas kernels, call(): pl.pallas_call(kernel, in_specs=[smem if a.dtype == jnp.int32 else other...  30.5 us
    ppermute x18, starting transfers between devices, swap(): return lax.ppermute(array, 'pts', [(i, i ^ mask) for i in range(size)])  27.9 us
    ppermute x18, waiting for transfers between devices, swap(): return lax.ppermute(array, 'pts', [(i, i ^ mask) for i in range(size)])  22.5 us
    unnamed x22, local copies, waits for them, and re-layouts  5.41 us
  transfers between devices with their start and end apart: 18, of which 10 were waited for; matrix products, arithmetic and copies ran while one was open for 1% of the time, Pallas kernels for 28%

profile of v6, /device:TPU:0, one launch (start us, length us, event | category | flops | bytes accessed | tf_op | source)
XLA Modules:
  0.0 89.0 jit_solution(12415255934126055628)
XLA Ops:
  5.6 2.0 %shard_map.103 = (bf16[2,80,384]{2,1,0:T(8,128)(2,1)S(1)}, bf16[2,80,384]{2,1,0:T(8,128)(2,1)S(1)}) custom-call(s32[1]{0:T(128)} %bitcast.place_ref, s32[1]{0:T(128)S(6)} %copy.11.count_ref, bf16[64,768]{1,0:T(8,128)(2,1)S(1)} %copy-done.7, bf16[64,768]{1,0:T(8,128)(2,1)S(1)} %copy-done.9, bf16[768,768]{1,0:T(8,128)(2,1)S(1)} %copy-done.2, ...), custom_call_target="tpu_custom_call" | custom-call | flops 18874368 | bytes 350209 | tf_op jit(solution)/shard_map/pallas_call | solution.py:285
  11.0 3.0 %collective-permute-start.1 = (bf16[2,80,384]{2,1,0:T(8,128)(2,1)S(1)}, bf16[2,80,384]{2,1,0:T(8,128)(2,1)S(1)}, u32[]{:S(2)}, u32[]{:S(2)}) collective-permute-start(bf16[2,80,384]{2,1,0:T(8,128)(2,1)S(1)} %pad_maximum_fusion.6), channel_id=1, source_target_pairs={{0,2},{1,3},{2,0},{3,1},{4,6},{5,7},{6,4},{7,5},{8,10},{9,11},{10,... | collective-permute-start | bytes 368648 | tf_op jit(solution)/shard_map/ppermute | solution.py:310
  15.7 2.5 %collective-permute-done.1 = bf16[2,80,384]{2,1,0:T(8,128)(2,1)S(1)} collective-permute-done((bf16[2,80,384]{2,1,0:T(8,128)(2,1)S(1)}, bf16[2,80,384]{2,1,0:T(8,128)(2,1)S(1)}, u32[]{:S(2)}, u32[]{:S(2)}) %collective-permute-start.1) | collective-permute-done | bytes 122912 | tf_op jit(solution)/shard_map/ppermute | solution.py:310
  18.2 2.0 %collective-permute-start.5 = (bf16[256,384]{1,0:T(8,128)(2,1)S(1)}, bf16[256,384]{1,0:T(8,128)(2,1)S(1)}, u32[]{:S(2)}, u32[]{:S(2)}) collective-permute-start(bf16[256,384]{1,0:T(8,128)(2,1)S(1)} %pad_maximum_fusion.2.qg_ref.refs_3_.refs_0_), channel_id=1, source_target_pairs={{0,4},{1,5},{2,6},{3,7},{4,0},{5,1},{6,2},{7,3},{8,12},{9,13},{10,... | collective-permute-start | bytes 589832 | tf_op jit(solution)/shard_map/ppermute | solution.py:310
  20.2 2.6 %collective-permute-start.4 = (bf16[256,384]{1,0:T(8,128)(2,1)S(1)}, bf16[256,384]{1,0:T(8,128)(2,1)S(1)}, u32[]{:S(2)}, u32[]{:S(2)}) collective-permute-start(bf16[256,384]{1,0:T(8,128)(2,1)S(1)} %pad_maximum_fusion.2.qg_ref.refs_3_.refs_0_), channel_id=1, source_target_pairs={{0,8},{1,9},{2,10},{3,11},{4,12},{5,13},{6,14},{7,15},{8,0},{9,1},... | collective-permute-start | bytes 589832 | tf_op jit(solution)/shard_map/ppermute | solution.py:310
  23.0 7.2 %collective-permute-done.3.refs_0_.far_ref.refs_8_.refs_9_ = bf16[2,384,384]{2,1,0:T(8,128)(2,1)S(1)} collective-permute-done((bf16[2,384,384]{2,1,0:T(8,128)(2,1)S(1)}, bf16[2,384,384]{2,1,0:T(8,128)(2,1)S(1)}, u32[]{:S(2)}, u32[]{:S(2)}) %collective-permute-start.3) | collective-permute-done | bytes 589856 | tf_op jit(solution)/shard_map/ppermute | solution.py:310
  30.4 2.3 %shard_map.107 = (f32[192,256]{1,0:T(8,128)S(1)}, f32[3,256]{1,0:T(4,128)S(1)}, f32[6,256]{1,0:T(8,128)S(1)}) custom-call(f32[4,128]{1,0:T(4,128)S(1)} %fusion.30.count_ref, bf16[256,384]{1,0:T(8,128)(2,1)S(1)} %pad_maximum_fusion.2.qg_ref.refs_3_.refs_0_, bf16[2,384,384]{2,1,0:T(8,128)(2,1)S(1)} %get-tuple-element.45.refs_0_.keep_ref.refs_2_, ...), custom_call_target="tpu_custom_call" | custom-call | flops 150994944 | bytes 419200 | tf_op jit(solution)/shard_map/pallas_call | solution.py:285
  32.8 1.9 %collective-permute-start.6 = (bf16[256,384]{1,0:T(8,128)(2,1)S(1)}, bf16[256,384]{1,0:T(8,128)(2,1)S(1)}, u32[]{:S(2)}, u32[]{:S(2)}) collective-permute-start(bf16[256,384]{1,0:T(8,128)(2,1)S(1)} %collective-permute-done.4.qg_ref.refs_1_.refs_0_), channel_id=1, source_target_pairs={{0,4},{1,5},{2,6},{3,7},{4,0},{5,1},{6,2},{7,3},{8,12},{9,13},{10,... | collective-permute-start | bytes 589832 | tf_op jit(solution)/shard_map/ppermute | solution.py:310
  34.6 2.3 %shard_map.109 = (f32[192,256]{1,0:T(8,128)S(1)}, f32[3,256]{1,0:T(4,128)S(1)}, f32[6,256]{1,0:T(8,128)S(1)}) custom-call(f32[4,128]{1,0:T(4,128)S(1)} %fusion.30.count_ref, bf16[256,384]{1,0:T(8,128)(2,1)S(1)} %collective-permute-done.4.qg_ref.refs_1_.refs_0_, bf16[2,384,384]{2,1,0:T(8,128)(2,1)S(1)} %get-tuple-element.45.refs_0_.keep_ref.refs_2_, ...), custom_call_target="tpu_custom_call" | custom-call | flops 150994944 | bytes 419200 | tf_op jit(solution)/shard_map/pallas_call | solution.py:285
  37.0 2.4 %shard_map.108 = (f32[192,256]{1,0:T(8,128)S(1)}, f32[3,256]{1,0:T(4,128)S(1)}, f32[6,256]{1,0:T(8,128)S(1)}) custom-call(f32[4,128]{1,0:T(4,128)S(1)} %fusion.30.count_ref, bf16[256,384]{1,0:T(8,128)(2,1)S(1)} %collective-permute-done.5.qg_ref.refs_2_.refs_0_, bf16[2,384,384]{2,1,0:T(8,128)(2,1)S(1)} %get-tuple-element.45.refs_0_.keep_ref.refs_2_, ...), custom_call_target="tpu_custom_call" | custom-call | flops 150994944 | bytes 419200 | tf_op jit(solution)/shard_map/pallas_call | solution.py:285
  39.4 2.3 %shard_map.110 = (f32[192,256]{1,0:T(8,128)S(1)}, f32[3,256]{1,0:T(4,128)S(1)}, f32[6,256]{1,0:T(8,128)S(1)}) custom-call(f32[4,128]{1,0:T(4,128)S(1)} %fusion.30.count_ref, bf16[256,384]{1,0:T(8,128)(2,1)S(1)} %collective-permute-done.6.qg_ref.refs_0_, bf16[2,384,384]{2,1,0:T(8,128)(2,1)S(1)} %get-tuple-element.45.refs_0_.keep_ref.refs_2_, ...), custom_call_target="tpu_custom_call" | custom-call | flops 150994944 | bytes 419200 | tf_op jit(solution)/shard_map/pallas_call | solution.py:285
  41.7 1.6 %collective-permute-start.7 = (f32[4,6,256]{2,1,0:T(8,128)S(1)}, f32[4,6,256]{2,1,0:T(8,128)S(1)}, u32[]{:S(2)}, u32[]{:S(2)}) collective-permute-start(f32[4,6,256]{2,1,0:T(8,128)S(1)} %pad_maximum_fusion.7), channel_id=1, source_target_pairs={{0,4},{1,5},{2,6},{3,7},{4,0},{5,1},{6,2},{7,3},{8,12},{9,13},{10,... | collective-permute-start | bytes 73736 | tf_op jit(solution)/shard_map/ppermute | solution.py:310
  43.3 2.4 %collective-permute-done.7 = f32[4,6,256]{2,1,0:T(8,128)S(1)} collective-permute-done((f32[4,6,256]{2,1,0:T(8,128)S(1)}, f32[4,6,256]{2,1,0:T(8,128)S(1)}, u32[]{:S(2)}, u32[]{:S(2)}) %collective-permute-start.7) | collective-permute-done | bytes 24608 | tf_op jit(solution)/shard_map/ppermute | solution.py:310
  45.8 2.7 %collective-permute-start.8 = (f32[4,6,256]{2,1,0:T(8,128)S(1)}, f32[4,6,256]{2,1,0:T(8,128)S(1)}, u32[]{:S(2)}, u32[]{:S(2)}) collective-permute-start(f32[4,6,256]{2,1,0:T(8,128)S(1)} %pad_maximum_fusion.9), channel_id=1, source_target_pairs={{0,8},{1,9},{2,10},{3,11},{4,12},{5,13},{6,14},{7,15},{8,0},{9,1},... | collective-permute-start | bytes 73736 | tf_op jit(solution)/shard_map/ppermute | solution.py:310
  48.5 2.2 %collective-permute-done.8 = f32[4,6,256]{2,1,0:T(8,128)S(1)} collective-permute-done((f32[4,6,256]{2,1,0:T(8,128)S(1)}, f32[4,6,256]{2,1,0:T(8,128)S(1)}, u32[]{:S(2)}, u32[]{:S(2)}) %collective-permute-start.8) | collective-permute-done | bytes 24608 | tf_op jit(solution)/shard_map/ppermute | solution.py:310
  50.8 2.7 %collective-permute-start.9 = (bf16[2,192,256]{2,1,0:T(8,128)(2,1)S(1)}, bf16[2,192,256]{2,1,0:T(8,128)(2,1)S(1)}, u32[]{:S(2)}, u32[]{:S(2)}) collective-permute-start(bf16[2,192,256]{2,1,0:T(8,128)(2,1)S(1)} %pad_maximum_fusion.3), channel_id=1, source_target_pairs={{0,8},{1,9},{2,10},{3,11},{4,12},{5,13},{6,14},{7,15},{8,0},{9,1},... | collective-permute-start | bytes 589832 | tf_op jit(solution)/shard_map/ppermute | solution.py:310
  53.6 6.3 %shard_map.111 = (f32[4,192,256]{2,1,0:T(8,128)S(1)}, bf16[2,384,384]{2,1,0:T(8,128)(2,1)S(1)}) custom-call(f32[4,128]{1,0:T(4,128)S(1)} %fusion.30.count_ref, bf16[256,384]{1,0:T(8,128)(2,1)S(1)} %collective-permute-done.6.qg_ref.refs_0_, bf16[256,384]{1,0:T(8,128)(2,1)S(1)} %collective-permute-done.4.qg_ref.refs_1_.refs_0_, ...), custom_call_target="tpu_custom_call" | custom-call | flops 528482304 | bytes 494848 | tf_op jit(solution)/shard_map/pallas_call | solution.py:285
  61.4 1.7 %shard_map.112 = (bf16[1,192,256]{2,1,0:T(8,128)(2,1)S(1)}, f32[2,384,384]{2,1,0:T(8,128)S(1)}) custom-call(f32[4,128]{1,0:T(4,128)S(1)} %fusion.30.count_ref, bf16[256,384]{1,0:T(8,128)(2,1)S(1)} %collective-permute-done.6.qg_ref.refs_0_, f32[6,256]{1,0:T(8,128)S(1)} %get-tuple-element.94.refs_4_.refs_1_, ...), custom_call_target="tpu_custom_call" | custom-call | flops 132120576 | bytes 504832 | tf_op jit(solution)/shard_map/pallas_call | solution.py:285
  63.1 4.3 %collective-permute-start.12 = (bf16[192,256]{1,0:T(8,128)(2,1)S(1)}, bf16[192,256]{1,0:T(8,128)(2,1)S(1)}, u32[]{:S(2)}, u32[]{:S(2)}) collective-permute-start(bf16[192,256]{1,0:T(8,128)(2,1)S(1)} %bitcast.105), channel_id=1, source_target_pairs={{0,4},{1,5},{2,6},{3,7},{4,0},{5,1},{6,2},{7,3},{8,12},{9,13},{10,... | collective-permute-start | bytes 294920 | tf_op jit(solution)/shard_map/ppermute | solution.py:310
  67.5 1.7 %shard_map.113 = (f32[1,192,256]{2,1,0:T(8,128)S(1)}, f32[2,384,384]{2,1,0:T(8,128)S(1)}) custom-call(f32[4,128]{1,0:T(4,128)S(1)} %fusion.30.count_ref, bf16[256,384]{1,0:T(8,128)(2,1)S(1)} %collective-permute-done.4.qg_ref.refs_1_.refs_0_, f32[6,256]{1,0:T(8,128)S(1)} %get-tuple-element.95.refs_5_.refs_1_, ...), custom_call_target="tpu_custom_call" | custom-call | flops 132120576 | bytes 664576 | tf_op jit(solution)/shard_map/pallas_call | solution.py:285
  70.5 1.7 %shard_map.114 = (bf16[1,192,256]{2,1,0:T(8,128)(2,1)S(1)}, f32[2,384,384]{2,1,0:T(8,128)S(1)}) custom-call(f32[4,128]{1,0:T(4,128)S(1)} %fusion.30.count_ref, bf16[256,384]{1,0:T(8,128)(2,1)S(1)} %collective-permute-done.5.qg_ref.refs_2_.refs_0_, f32[6,256]{1,0:T(8,128)S(1)} %get-tuple-element.96.refs_6_.refs_1_, ...), custom_call_target="tpu_custom_call" | custom-call | flops 132120576 | bytes 652288 | tf_op jit(solution)/shard_map/pallas_call | solution.py:285
  74.6 1.7 %shard_map.115 = (f32[1,192,256]{2,1,0:T(8,128)S(1)}, bf16[2,384,384]{2,1,0:T(8,128)(2,1)S(1)}) custom-call(f32[4,128]{1,0:T(4,128)S(1)} %fusion.30.count_ref, bf16[256,384]{1,0:T(8,128)(2,1)S(1)} %pad_maximum_fusion.2.qg_ref.refs_3_.refs_0_, f32[6,256]{1,0:T(8,128)S(1)} %get-tuple-element.93.refs_7_.refs_1_, ...), custom_call_target="tpu_custom_call" | custom-call | flops 132120576 | bytes 590848 | tf_op jit(solution)/shard_map/pallas_call | solution.py:285
  76.9 3.4 %collective-permute-done.14 = bf16[192,256]{1,0:T(8,128)(2,1)S(1)} collective-permute-done((bf16[192,256]{1,0:T(8,128)(2,1)S(1)}, bf16[192,256]{1,0:T(8,128)(2,1)S(1)}, u32[]{:S(2)}, u32[]{:S(2)}) %collective-permute-start.14) | collective-permute-done | bytes 98336 | tf_op jit(solution)/shard_map/ppermute | solution.py:310
  82.6 2.7 %shard_map.116 = bf16[384,768]{1,0:T(8,128)(2,1)} custom-call(s32[1]{0:T(128)} %bitcast.place_ref, bf16[2,384,384]{2,1,0:T(8,128)(2,1)S(1)} %get-tuple-element.77.near_ref, bf16[2,384,384]{2,1,0:T(8,128)(2,1)S(1)} %collective-permute-done.11.far_ref, bf16[2,384,384]{2,1,0:T(8,128)(2,1)S(1)} %collective-permute-done.16.core_ref, ...), custom_call_target="tpu_custom_call" | custom-call | flops 113246208 | bytes 589824 | tf_op jit(solution)/shard_map/pallas_call | solution.py:285
  (86 shorter events, 21.9 us)
Async XLA Ops:
  5.6 2.6 %copy-start = (bf16[768,768]{1,0:T(8,128)(2,1)S(1)}, bf16[768,768]{1,0:T(8,128)(2,1)}, u32[]{:S(2)}) copy-start(bf16[768,768]{1,0:T(8,128)(2,1)} %w_key_ref.3) | copy-start | bytes 3538948
  5.6 2.6 %copy-start.1 = (bf16[768,768]{1,0:T(8,128)(2,1)S(1)}, bf16[768,768]{1,0:T(8,128)(2,1)}, u32[]{:S(2)}) copy-start(bf16[768,768]{1,0:T(8,128)(2,1)} %w_value_ref.3) | copy-start | bytes 3538948
  7.7 3.3 %collective-permute-start = (bf16[2,80,384]{2,1,0:T(8,128)(2,1)S(1)}, bf16[2,80,384]{2,1,0:T(8,128)(2,1)S(1)}, u32[]{:S(2)}, u32[]{:S(2)}) collective-permute-start(bf16[2,80,384]{2,1,0:T(8,128)(2,1)S(1)} %get-tuple-element.44), channel_id=1, source_target_pairs={{0,1},{1,0},{2,3},{3,2},{4,5},{5,4},{6,7},{7,6},{8,9},{9,8},{10,11... | collective-permute-start | bytes 368648 | tf_op jit(solution)/shard_map/ppermute | solution.py:310
  10.8 3.3 %collective-permute-start.2 = (bf16[2,384,384]{2,1,0:T(8,128)(2,1)S(1)}, bf16[2,384,384]{2,1,0:T(8,128)(2,1)S(1)}, u32[]{:S(2)}, u32[]{:S(2)}) collective-permute-start(bf16[2,384,384]{2,1,0:T(8,128)(2,1)S(1)} %get-tuple-element.46), channel_id=1, source_target_pairs={{0,1},{1,0},{2,3},{3,2},{4,5},{5,4},{6,7},{7,6},{8,9},{9,8},{10,11... | collective-permute-start | bytes 1769480 | tf_op jit(solution)/shard_map/ppermute | solution.py:310
  11.0 7.1 %collective-permute-start.1 = (bf16[2,80,384]{2,1,0:T(8,128)(2,1)S(1)}, bf16[2,80,384]{2,1,0:T(8,128)(2,1)S(1)}, u32[]{:S(2)}, u32[]{:S(2)}) collective-permute-start(bf16[2,80,384]{2,1,0:T(8,128)(2,1)S(1)} %pad_maximum_fusion.6), channel_id=1, source_target_pairs={{0,2},{1,3},{2,0},{3,1},{4,6},{5,7},{6,4},{7,5},{8,10},{9,11},{10,... | collective-permute-start | bytes 368648 | tf_op jit(solution)/shard_map/ppermute | solution.py:310
  14.2 16.0 %collective-permute-start.3 = (bf16[2,384,384]{2,1,0:T(8,128)(2,1)S(1)}, bf16[2,384,384]{2,1,0:T(8,128)(2,1)S(1)}, u32[]{:S(2)}, u32[]{:S(2)}) collective-permute-start(bf16[2,384,384]{2,1,0:T(8,128)(2,1)S(1)} %pad_maximum_fusion), channel_id=1, source_target_pairs={{0,2},{1,3},{2,0},{3,1},{4,6},{5,7},{6,4},{7,5},{8,10},{9,11},{10,... | collective-permute-start | bytes 1769480 | tf_op jit(solution)/shard_map/ppermute | solution.py:310
  18.2 18.8 %collective-permute-start.5 = (bf16[256,384]{1,0:T(8,128)(2,1)S(1)}, bf16[256,384]{1,0:T(8,128)(2,1)S(1)}, u32[]{:S(2)}, u32[]{:S(2)}) collective-permute-start(bf16[256,384]{1,0:T(8,128)(2,1)S(1)} %pad_maximum_fusion.2.qg_ref.refs_3_.refs_0_), channel_id=1, source_target_pairs={{0,4},{1,5},{2,6},{3,7},{4,0},{5,1},{6,2},{7,3},{8,12},{9,13},{10,... | collective-permute-start | bytes 589832 | tf_op jit(solution)/shard_map/ppermute | solution.py:310
  20.2 12.6 %collective-permute-start.4 = (bf16[256,384]{1,0:T(8,128)(2,1)S(1)}, bf16[256,384]{1,0:T(8,128)(2,1)S(1)}, u32[]{:S(2)}, u32[]{:S(2)}) collective-permute-start(bf16[256,384]{1,0:T(8,128)(2,1)S(1)} %pad_maximum_fusion.2.qg_ref.refs_3_.refs_0_), channel_id=1, source_target_pairs={{0,8},{1,9},{2,10},{3,11},{4,12},{5,13},{6,14},{7,15},{8,0},{9,1},... | collective-permute-start | bytes 589832 | tf_op jit(solution)/shard_map/ppermute | solution.py:310
  32.8 6.6 %collective-permute-start.6 = (bf16[256,384]{1,0:T(8,128)(2,1)S(1)}, bf16[256,384]{1,0:T(8,128)(2,1)S(1)}, u32[]{:S(2)}, u32[]{:S(2)}) collective-permute-start(bf16[256,384]{1,0:T(8,128)(2,1)S(1)} %collective-permute-done.4.qg_ref.refs_1_.refs_0_), channel_id=1, source_target_pairs={{0,4},{1,5},{2,6},{3,7},{4,0},{5,1},{6,2},{7,3},{8,12},{9,13},{10,... | collective-permute-start | bytes 589832 | tf_op jit(solution)/shard_map/ppermute | solution.py:310
  41.7 4.0 %collective-permute-start.7 = (f32[4,6,256]{2,1,0:T(8,128)S(1)}, f32[4,6,256]{2,1,0:T(8,128)S(1)}, u32[]{:S(2)}, u32[]{:S(2)}) collective-permute-start(f32[4,6,256]{2,1,0:T(8,128)S(1)} %pad_maximum_fusion.7), channel_id=1, source_target_pairs={{0,4},{1,5},{2,6},{3,7},{4,0},{5,1},{6,2},{7,3},{8,12},{9,13},{10,... | collective-permute-start | bytes 73736 | tf_op jit(solution)/shard_map/ppermute | solution.py:310
  45.8 4.9 %collective-permute-start.8 = (f32[4,6,256]{2,1,0:T(8,128)S(1)}, f32[4,6,256]{2,1,0:T(8,128)S(1)}, u32[]{:S(2)}, u32[]{:S(2)}) collective-permute-start(f32[4,6,256]{2,1,0:T(8,128)S(1)} %pad_maximum_fusion.9), channel_id=1, source_target_pairs={{0,8},{1,9},{2,10},{3,11},{4,12},{5,13},{6,14},{7,15},{8,0},{9,1},... | collective-permute-start | bytes 73736 | tf_op jit(solution)/shard_map/ppermute | solution.py:310
  50.8 10.6 %collective-permute-start.9 = (bf16[2,192,256]{2,1,0:T(8,128)(2,1)S(1)}, bf16[2,192,256]{2,1,0:T(8,128)(2,1)S(1)}, u32[]{:S(2)}, u32[]{:S(2)}) collective-permute-start(bf16[2,192,256]{2,1,0:T(8,128)(2,1)S(1)} %pad_maximum_fusion.3), channel_id=1, source_target_pairs={{0,8},{1,9},{2,10},{3,11},{4,12},{5,13},{6,14},{7,15},{8,0},{9,1},... | collective-permute-start | bytes 589832 | tf_op jit(solution)/shard_map/ppermute | solution.py:310
  59.8 14.7 %collective-permute-start.11 = (bf16[2,384,384]{2,1,0:T(8,128)(2,1)S(1)}, bf16[2,384,384]{2,1,0:T(8,128)(2,1)S(1)}, u32[]{:S(2)}, u32[]{:S(2)}) collective-permute-start(bf16[2,384,384]{2,1,0:T(8,128)(2,1)S(1)} %get-tuple-element.63), channel_id=1, source_target_pairs={{0,2},{1,3},{2,0},{3,1},{4,6},{5,7},{6,4},{7,5},{8,10},{9,11},{10,... | collective-permute-start | bytes 1769480 | tf_op jit(solution)/shard_map/ppermute | solution.py:310
  63.1 7.4 %collective-permute-start.12 = (bf16[192,256]{1,0:T(8,128)(2,1)S(1)}, bf16[192,256]{1,0:T(8,128)(2,1)S(1)}, u32[]{:S(2)}, u32[]{:S(2)}) collective-permute-start(bf16[192,256]{1,0:T(8,128)(2,1)S(1)} %bitcast.105), channel_id=1, source_target_pairs={{0,4},{1,5},{2,6},{3,7},{4,0},{5,1},{6,2},{7,3},{8,12},{9,13},{10,... | collective-permute-start | bytes 294920 | tf_op jit(solution)/shard_map/ppermute | solution.py:310
  67.4 7.1 %collective-permute-start.10 = (bf16[192,256]{1,0:T(8,128)(2,1)S(1)}, bf16[192,256]{1,0:T(8,128)(2,1)S(1)}, u32[]{:S(2)}, u32[]{:S(2)}) collective-permute-start(bf16[192,256]{1,0:T(8,128)(2,1)S(1)} %fusion.1), channel_id=1, source_target_pairs={{0,4},{1,5},{2,6},{3,7},{4,0},{5,1},{6,2},{7,3},{8,12},{9,13},{10,... | collective-permute-start | bytes 294920 | tf_op jit(solution)/shard_map/ppermute | solution.py:310
  72.2 4.7 %collective-permute-start.13 = (bf16[192,256]{1,0:T(8,128)(2,1)S(1)}, bf16[192,256]{1,0:T(8,128)(2,1)S(1)}, u32[]{:S(2)}, u32[]{:S(2)}) collective-permute-start(bf16[192,256]{1,0:T(8,128)(2,1)S(1)} %bitcast.104), channel_id=1, source_target_pairs={{0,4},{1,5},{2,6},{3,7},{4,0},{5,1},{6,2},{7,3},{8,12},{9,13},{10,... | collective-permute-start | bytes 294920 | tf_op jit(solution)/shard_map/ppermute | solution.py:310
  73.8 6.5 %collective-permute-start.14 = (bf16[192,256]{1,0:T(8,128)(2,1)S(1)}, bf16[192,256]{1,0:T(8,128)(2,1)S(1)}, u32[]{:S(2)}, u32[]{:S(2)}) collective-permute-start(bf16[192,256]{1,0:T(8,128)(2,1)S(1)} %fusion.4), channel_id=1, source_target_pairs={{0,8},{1,9},{2,10},{3,11},{4,12},{5,13},{6,14},{7,15},{8,0},{9,1},... | collective-permute-start | bytes 294920 | tf_op jit(solution)/shard_map/ppermute | solution.py:310
  80.5 2.1 %collective-permute-start.16 = (bf16[2,384,384]{2,1,0:T(8,128)(2,1)S(1)}, bf16[2,384,384]{2,1,0:T(8,128)(2,1)S(1)}, u32[]{:S(2)}, u32[]{:S(2)}) collective-permute-start(bf16[2,384,384]{2,1,0:T(8,128)(2,1)S(1)} %pad_maximum_fusion.1), channel_id=1, source_target_pairs={{0,1},{1,0},{2,3},{3,2},{4,5},{5,4},{6,7},{7,6},{8,9},{9,8},{10,11... | collective-permute-start | bytes 1769480 | tf_op jit(solution)/shard_map/ppermute | solution.py:310
  80.7 5.3 %collective-permute-start.15 = (bf16[2,192,128]{2,1,0:T(8,128)(2,1)S(1)}, bf16[2,192,128]{2,1,0:T(8,128)(2,1)S(1)}, u32[]{:S(2)}, u32[]{:S(2)}) collective-permute-start(bf16[2,192,128]{2,1,0:T(8,128)(2,1)S(1)} %get-tuple-element.83), channel_id=1, source_target_pairs={{0,2},{1,3},{2,0},{3,1},{4,6},{5,7},{6,4},{7,5},{8,10},{9,11},{10,... | collective-permute-start | bytes 294920 | tf_op jit(solution)/shard_map/ppermute | solution.py:310
  81.7 5.9 %copy-start.8 = (bf16[64,768]{1,0:T(8,128)(2,1)S(1)}, bf16[64,768]{1,0:T(8,128)(2,1)}, u32[]{:S(2)}) copy-start(bf16[64,768]{1,0:T(8,128)(2,1)} %latents_ref.1) | copy-start | bytes 294916
  81.7 5.9 %copy-start.10 = (bf16[64,768]{1,0:T(8,128)(2,1)S(1)}, bf16[64,768]{1,0:T(8,128)(2,1)}, u32[]{:S(2)}) copy-start(bf16[64,768]{1,0:T(8,128)(2,1)} %d_out_ref.1) | copy-start | bytes 294916
  82.6 5.0 %copy-start.3 = (bf16[768,768]{1,0:T(8,128)(2,1)S(1)}, bf16[768,768]{1,0:T(8,128)(2,1)}, u32[]{:S(2)}) copy-start(bf16[768,768]{1,0:T(8,128)(2,1)} %w_query_ref.1) | copy-start | bytes 3538948
  82.6 5.0 %copy-start.5 = (bf16[768,768]{1,0:T(8,128)(2,1)S(1)}, bf16[768,768]{1,0:T(8,128)(2,1)}, u32[]{:S(2)}) copy-start(bf16[768,768]{1,0:T(8,128)(2,1)} %w_out_ref.1) | copy-start | bytes 3538948
  86.1 1.5 %collective-permute-start.17 = (bf16[2,2,192,64]{3,2,1,0:T(8,128)(2,1)S(1)}, bf16[2,2,192,64]{3,2,1,0:T(8,128)(2,1)S(1)}, u32[]{:S(2)}, u32[]{:S(2)}) collective-permute-start(bf16[2,2,192,64]{3,2,1,0:T(8,128)(2,1)S(1)} %pad_maximum_fusion.5), channel_id=1, source_target_pairs={{0,1},{1,0},{2,3},{3,2},{4,5},{5,4},{6,7},{7,6},{8,9},{9,8},{10,11... | collective-permute-start | bytes 294920 | tf_op jit(solution)/shard_map/ppermute | solution.py:310
  (5 other events, 5.4 us)

commit v7 on v6

--- a/solution.py
+++ b/solution.py
@@ -56,45 +56,62 @@
                 ref[across, at, :] = piece
 
 
-def slots_kernel(place_ref, points_ref, w_key_ref, w_value_ref, keep_ref, send_ref):
+def load(source, target, sems, pieces):
+    step = source.shape[0] // pieces
+    copies = []
+    for k in range(pieces):
+        at = slice(k * step, (k + 1) * step)
+        copies.append(pltpu.make_async_copy(source.at[at], target.at[at], sems.at[k]))
+        copies[-1].start()
+    return copies
+
+
+def project_kernel(
+    place_ref, count_ref, latents_hbm, d_out_hbm, points_hbm, w_query_hbm, w_out_hbm, w_key_hbm, w_value_hbm,
+    keep_qg_ref, send_qg_ref, keep_ref, send_ref,
+    latents_ref, d_out_ref, points_ref, w_query_ref, w_out_ref, w_key_ref, w_value_ref, sems
+):
+    pieces = sems.shape[1]
+    own = latents_ref.shape[0]
+    loads = [
+        load(latents_hbm, latents_ref, sems.at[0], 1),
+        load(w_query_hbm, w_query_ref, sems.at[1], pieces),
+        load(d_out_hbm, d_out_ref, sems.at[2], 1),
+        load(w_out_hbm, w_out_ref, sems.at[3], pieces),
+        load(points_hbm, points_ref, sems.at[4], pieces),
+        load(w_key_hbm, w_key_ref, sems.at[5], pieces),
+        load(w_value_hbm, w_value_ref, sems.at[6], pieces),
+    ]
+
+    def arrived(*which):
+        for i in which:
+            for copy in loads[i]:
+                copy.wait()
+
+    extra = keep_qg_ref.shape[1] - own, keep_qg_ref.shape[2]
+    first = lax.broadcasted_iota(jnp.int32, extra, 1) < extra[1] // 2
+    count = jnp.where(first, count_ref[0] // 16, count_ref[0] % 16).astype(F32).astype(BF16)
+    for ref in (keep_qg_ref, send_qg_ref):
+        for across in range(2):
+            ref[across, own:, :] = count
+    arrived(0, 1)
+    query = dot(latents_ref[...], w_query_ref[...]).astype(BF16)
+    arrived(2, 3)
+    grad = dot_nt(d_out_ref[...], w_out_ref[...]).astype(BF16)
+    store_quarters(place_ref, keep_qg_ref, send_qg_ref, query, grad, slice(0, own))
+    arrived(4, 5)
     keys = dot(points_ref[...], w_key_ref[...]).astype(BF16) * jnp.asarray(0.125, BF16)
+    arrived(6)
     values = dot(points_ref[...], w_value_ref[...]).astype(BF16)
     store_quarters(place_ref, keep_ref, send_ref, keys, values, slice(0, keys.shape[0]))
 
 
-def rows_kernel(
-    place_ref, count_ref, latents_hbm, d_out_hbm, w_query_hbm, w_out_hbm,
-    keep_ref, send_ref, latents_ref, d_out_ref, w_query_ref, w_out_ref, sems
-):
-    own, pieces = latents_ref.shape[0], sems.shape[1] - 1
-    loads = []
-    for i, (small, small_to, big, big_to) in enumerate(
-        (
-            (latents_hbm, latents_ref, w_query_hbm, w_query_ref),
-            (d_out_hbm, d_out_ref, w_out_hbm, w_out_ref),
-        )
-    ):
-        step = big.shape[0] // pieces
-        group = [pltpu.make_async_copy(small, small_to, sems.at[i, pieces])]
-        for k in range(pieces):
-            at = slice(k * step, (k + 1) * step)
-            group.append(pltpu.make_async_copy(big.at[at], big_to.at[at], sems.at[i, k]))
-        for copy in group:
-            copy.start()
-        loads.append(group)
-    for copy in loads[0]:
-        copy.wait()
-    query = dot(latents_ref[...], w_query_ref[...]).astype(BF16)
-    for copy in loads[1]:
-        copy.wait()
-    grad = dot_nt(d_out_ref[...], w_out_ref[...]).astype(BF16)
-    store_quarters(place_ref, keep_ref, send_ref, query, grad, slice(0, own))
-    extra = keep_ref.shape[1] - own, keep_ref.shape[2]
-    first = lax.broadcasted_iota(jnp.int32, extra, 1) < extra[1] // 2
-    count = jnp.where(first, count_ref[0] // 16, count_ref[0] % 16).astype(F32).astype(BF16)
-    for ref in (keep_ref, send_ref):
-        for across in range(2):
-            ref[across, own:, :] = count
+def weights_kernel(w_key_ref, w_value_ref, out_ref):
+    mine = out_ref.shape[1] // 2
+    for i, ref in enumerate((w_key_ref, w_value_ref)):
+        turned = ref[...].T
+        for quarter in range(TEAM):
+            out_ref[quarter, i * mine : (i + 1) * mine, :] = turned[quarter * mine : (quarter + 1) * mine]
 
 
 def turn_kernel(picks, *refs):
@@ -259,25 +276,17 @@
             ).astype(BF16)
 
 
-def points_kernel(
-    place_ref, near_ref, far_ref, core_ref, w_key_ref, w_value_ref, out_ref, key_ref, value_ref
-):
-    mine = key_ref.shape[1] // TEAM
+def points_kernel(place_ref, near_ref, far_ref, core_ref, weight_ref, out_ref):
+    total = None
     for relative in range(TEAM):
         core, across = relative % 2, relative // 2
         piece = core_ref[across] if core else (near_ref, far_ref)[across][0]
-        for quarter in range(TEAM):
-
-            @pl.when((place_ref[0] % TEAM) ^ relative == quarter)
-            def _():
-                key_ref[:, quarter * mine : (quarter + 1) * mine] = piece[:, :mine]
-                value_ref[:, quarter * mine : (quarter + 1) * mine] = piece[:, mine:]
-
-    total = dot_nt(key_ref[...], w_key_ref[...]) + dot_nt(value_ref[...], w_value_ref[...])
+        term = dot(piece, weight_ref[(place_ref[0] % TEAM) ^ relative])
+        total = term if total is None else total + term
     out_ref[...] = total.astype(BF16)
 
 
-def call(kernel, ins, out_shapes, scratch=(), flops=0, exps=0, space=pltpu.VMEM):
+def call(kernel, ins, out_shapes, scratch=(), flops=0, exps=0, space=pltpu.VMEM, grant=40):
     vmem = pl.BlockSpec(memory_space=pltpu.VMEM)
     other = pl.BlockSpec(memory_space=space)
     smem = pl.BlockSpec(memory_space=pltpu.SMEM)
@@ -288,7 +297,7 @@
         out_specs=[vmem] * len(out_shapes),
         out_shape=out_shapes,
         scratch_shapes=scratch,
-        compiler_params=pltpu.CompilerParams(vmem_limit_bytes=40 << 20),
+        compiler_params=pltpu.CompilerParams(vmem_limit_bytes=grant << 20),
         cost_estimate=pl.CostEstimate(flops=flops // 8, transcendentals=exps // 8, bytes_accessed=moved // 8),
     )(*ins)
 
@@ -310,21 +319,15 @@
         return lax.ppermute(array, "pts", [(i, i ^ mask) for i in range(size)])
 
     each = own + 16
-    keep_qg, send_qg = call(
-        rows_kernel,
-        [place, counts, latents, d_out, w_query, w_out],
-        [shape((2, each, 2 * mine), BF16)] * 2,
-        [pltpu.VMEM((own, width), BF16)] * 2
-        + [pltpu.VMEM((width, width), BF16)] * 2
-        + [pltpu.SemaphoreType.DMA((2, 5))],
-        flops=4 * own * width * width,
+    inputs = [latents, d_out, points, w_query, w_out, w_key, w_value]
+    keep_qg, send_qg, keep, send = call(
+        project_kernel,
+        [place, counts] + inputs,
+        [shape((2, each, 2 * mine), BF16)] * 2 + [shape((2, slots, 2 * mine), BF16)] * 2,
+        [pltpu.VMEM(a.shape, BF16) for a in inputs] + [pltpu.SemaphoreType.DMA((len(inputs), 4))],
+        flops=4 * (own + slots) * width * width,
         space=pltpu.HBM,
-    )
-    keep, send = call(
-        slots_kernel,
-        [place, points, w_key, w_value],
-        [shape((2, slots, 2 * mine), BF16)] * 2,
-        flops=4 * slots * width * width,
+        grant=60,
     )
     core_qg = swap(send_qg, 1)
     far_qg = swap(jnp.stack([keep_qg[1], core_qg[1]]), 2)
@@ -336,9 +339,13 @@
     count = 16 * tail[:, :LANES] + tail[:, mine : mine + LANES]
     for mask in middle:
         qg = jnp.concatenate([qg, swap(qg, mask)], axis=0)
-    qg = [qg, swap(qg, near_bit), swap(qg, far_bit)]
+    qg, w_key, w_value = lax.optimization_barrier((qg, w_key, w_value))
+    far_qg = swap(qg, far_bit)
+    qg = [qg, swap(qg, near_bit), far_qg]
+    (weights,) = call(weights_kernel, [w_key, w_value], [shape((TEAM, 2 * mine, width), BF16)])
     turned = [shape((2, 2 * mine, slots), BF16)]
     (near_t,) = call(functools.partial(turn_kernel, ((0, 0), (1, 0))), [keep, core], turned)
+    near_t, weights = lax.optimization_barrier((near_t, weights))
     (far_t,) = call(functools.partial(turn_kernel, ((0, 0), (0, 1))), [far], turned)
     rows = qg[0].shape[0]
     team_slots = TEAM * slots
@@ -437,9 +444,8 @@
     core_gkv = swap(jnp.stack([gkv_near[1], came_far[1]]), 1)
     (d_points,) = call(
         points_kernel,
-        [place, gkv_near, came_far, core_gkv, w_key, w_value],
+        [place, gkv_near, came_far, core_gkv, weights],
         [shape((slots, width), BF16)],
-        [pltpu.VMEM((slots, width), BF16)] * 2,
         flops=4 * slots * width * width,
     )
     far_both, d_points = lax.optimization_barrier((far_both, d_points))

time: 89.3 us -> 89.4 us (level)
  Pallas kernels: 30.5 us -> 33.1 us
  local copies, waits for them, and re-layouts: 5.82 us -> 4.03 us
  starting transfers between devices: 27.9 us -> 26.2 us
  waiting for transfers between devices: 22.5 us -> 23.4 us
    unnamed x22 -> x14, local copies, waits for them, and re-layouts: 5.41 us -> 0.35 us
    pallas_call x15, Pallas kernels: 30.5 us -> 33.1 us  [call(): pl.pallas_call(kernel, in_specs=[smem if a.dtype == jnp.int32 else other...]
    ppermute x18, starting transfers between devices: 27.9 us -> 26.2 us  [swap(): return lax.ppermute(array, 'pts', [(i, i ^ mask) for i in range(size)])]
    slice x2, local copies, waits for them, and re-layouts: 0.06 us -> 1.02 us  [body(): far = swap(jnp.stack([keep[1], core[1]]), 2)]
  transfers between devices with their start and end apart: 18 -> 18, of which waited for: 10 -> 10; matrix products, arithmetic and copies ran while one was open for 1% -> 4% of each run, Pallas kernels for 28% -> 26%
where the time goes in v7:
time: 89.4 us; the launch traced here: 89 us
  Pallas kernels  33.1 us (37%)
  starting transfers between devices  26.2 us (29%)
  waiting for transfers between devices  23.4 us (26%)
  local copies, waits for them, and re-layouts  4.03 us (5%)
  between operations  1.68 us (2%)
    pallas_call x15, Pallas kernels, call(): pl.pallas_call(kernel, in_specs=[smem if a.dtype == jnp.int32 else other...  33.1 us
    ppermute x18, starting transfers between devices, swap(): return lax.ppermute(array, 'pts', [(i, i ^ mask) for i in range(size)])  26.2 us
    ppermute x18, waiting for transfers between devices, swap(): return lax.ppermute(array, 'pts', [(i, i ^ mask) for i in range(size)])  23.4 us
  transfers between devices with their start and end apart: 18, of which 10 were waited for; matrix products, arithmetic and copies ran while one was open for 4% of the time, Pallas kernels for 26%

profile of v7, /device:TPU:0, one launch (start us, length us, event | category | flops | bytes accessed | tf_op | source)
XLA Modules:
  0.0 89.0 jit_solution(12905869354492171168)
XLA Ops:
  1.3 5.9 %shard_map.103 = (bf16[2,80,384]{2,1,0:T(8,128)(2,1)}, bf16[2,80,384]{2,1,0:T(8,128)(2,1)}, bf16[2,384,384]{2,1,0:T(8,128)(2,1)}, bf16[2,384,384]{2,1,0:T(8,128)(2,1)}) custom-call(s32[1]{0:T(128)} %bitcast.place_ref, s32[1]{0:T(128)S(6)} %copy.11.count_ref, bf16[64,768]{1,0:T(8,128)(2,1)} %latents_ref.1, bf16[64,768]{1,0:T(8,128)(2,1)} %d_out_ref.1, ...), custom_call_target="tpu_custom_call" | custom-call | flops 132120576 | bytes 866305 | tf_op jit(solution)/shard_map/pallas_call | solution.py:294
  11.1 3.0 %collective-permute-start.1 = (bf16[2,80,384]{2,1,0:T(8,128)(2,1)S(1)}, bf16[2,80,384]{2,1,0:T(8,128)(2,1)S(1)}, u32[]{:S(2)}, u32[]{:S(2)}) collective-permute-start(bf16[2,80,384]{2,1,0:T(8,128)(2,1)S(1)} %pad_maximum_fusion.6), channel_id=1, source_target_pairs={{0,2},{1,3},{2,0},{3,1},{4,6},{5,7},{6,4},{7,5},{8,10},{9,11},{10,... | collective-permute-start | bytes 368648 | tf_op jit(solution)/shard_map/ppermute | solution.py:319
  14.4 3.9 %collective-permute-done.1 = bf16[2,80,384]{2,1,0:T(8,128)(2,1)S(1)} collective-permute-done((bf16[2,80,384]{2,1,0:T(8,128)(2,1)S(1)}, bf16[2,80,384]{2,1,0:T(8,128)(2,1)S(1)}, u32[]{:S(2)}, u32[]{:S(2)}) %collective-permute-start.1) | collective-permute-done | bytes 122912 | tf_op jit(solution)/shard_map/ppermute | solution.py:319
  18.3 2.2 %collective-permute-start.5 = (bf16[256,384]{1,0:T(8,128)(2,1)S(1)}, bf16[256,384]{1,0:T(8,128)(2,1)S(1)}, u32[]{:S(2)}, u32[]{:S(2)}) collective-permute-start(bf16[256,384]{1,0:T(8,128)(2,1)S(1)} %pad_maximum_fusion.2.qg_ref.refs_3_.refs_0_), channel_id=1, source_target_pairs={{0,4},{1,5},{2,6},{3,7},{4,0},{5,1},{6,2},{7,3},{8,12},{9,13},{10,... | collective-permute-start | bytes 589832 | tf_op jit(solution)/shard_map/ppermute | solution.py:319
  20.5 2.6 %collective-permute-start.4 = (bf16[256,384]{1,0:T(8,128)(2,1)S(1)}, bf16[256,384]{1,0:T(8,128)(2,1)S(1)}, u32[]{:S(2)}, u32[]{:S(2)}) collective-permute-start(bf16[256,384]{1,0:T(8,128)(2,1)S(1)} %pad_maximum_fusion.2.qg_ref.refs_3_.refs_0_), channel_id=1, source_target_pairs={{0,8},{1,9},{2,10},{3,11},{4,12},{5,13},{6,14},{7,15},{8,0},{9,1},... | collective-permute-start | bytes 589832 | tf_op jit(solution)/shard_map/ppermute | solution.py:319
  24.4 5.9 %collective-permute-done.3.refs_0_.far_ref.refs_8_.refs_9_ = bf16[2,384,384]{2,1,0:T(8,128)(2,1)S(1)} collective-permute-done((bf16[2,384,384]{2,1,0:T(8,128)(2,1)S(1)}, bf16[2,384,384]{2,1,0:T(8,128)(2,1)S(1)}, u32[]{:S(2)}, u32[]{:S(2)}) %collective-permute-start.3) | collective-permute-done | bytes 589856 | tf_op jit(solution)/shard_map/ppermute | solution.py:319
  30.5 2.3 %shard_map.107 = (f32[192,256]{1,0:T(8,128)S(1)}, f32[3,256]{1,0:T(4,128)S(1)}, f32[6,256]{1,0:T(8,128)S(1)}) custom-call(f32[4,128]{1,0:T(4,128)S(1)} %fusion.30.count_ref, bf16[256,384]{1,0:T(8,128)(2,1)S(1)} %pad_maximum_fusion.2.qg_ref.refs_3_.refs_0_, bf16[2,384,384]{2,1,0:T(8,128)(2,1)S(1)} %copy-done, ...), custom_call_target="tpu_custom_call" | custom-call | flops 150994944 | bytes 419200 | tf_op jit(solution)/shard_map/pallas_call | solution.py:294
  32.9 1.9 %collective-permute-start.6 = (bf16[256,384]{1,0:T(8,128)(2,1)S(1)}, bf16[256,384]{1,0:T(8,128)(2,1)S(1)}, u32[]{:S(2)}, u32[]{:S(2)}) collective-permute-start(bf16[256,384]{1,0:T(8,128)(2,1)S(1)} %collective-permute-done.4.qg_ref.refs_1_.refs_0_), channel_id=1, source_target_pairs={{0,4},{1,5},{2,6},{3,7},{4,0},{5,1},{6,2},{7,3},{8,12},{9,13},{10,... | collective-permute-start | bytes 589832 | tf_op jit(solution)/shard_map/ppermute | solution.py:319
  34.8 2.3 %shard_map.109 = (f32[192,256]{1,0:T(8,128)S(1)}, f32[3,256]{1,0:T(4,128)S(1)}, f32[6,256]{1,0:T(8,128)S(1)}) custom-call(f32[4,128]{1,0:T(4,128)S(1)} %fusion.30.count_ref, bf16[256,384]{1,0:T(8,128)(2,1)S(1)} %collective-permute-done.4.qg_ref.refs_1_.refs_0_, bf16[2,384,384]{2,1,0:T(8,128)(2,1)S(1)} %copy-done, ...), custom_call_target="tpu_custom_call" | custom-call | flops 150994944 | bytes 419200 | tf_op jit(solution)/shard_map/pallas_call | solution.py:294
  37.1 2.3 %shard_map.108 = (f32[192,256]{1,0:T(8,128)S(1)}, f32[3,256]{1,0:T(4,128)S(1)}, f32[6,256]{1,0:T(8,128)S(1)}) custom-call(f32[4,128]{1,0:T(4,128)S(1)} %fusion.30.count_ref, bf16[256,384]{1,0:T(8,128)(2,1)S(1)} %collective-permute-done.5.qg_ref.refs_2_.refs_0_, bf16[2,384,384]{2,1,0:T(8,128)(2,1)S(1)} %copy-done, ...), custom_call_target="tpu_custom_call" | custom-call | flops 150994944 | bytes 419200 | tf_op jit(solution)/shard_map/pallas_call | solution.py:294
  39.5 2.3 %shard_map.110 = (f32[192,256]{1,0:T(8,128)S(1)}, f32[3,256]{1,0:T(4,128)S(1)}, f32[6,256]{1,0:T(8,128)S(1)}) custom-call(f32[4,128]{1,0:T(4,128)S(1)} %fusion.30.count_ref, bf16[256,384]{1,0:T(8,128)(2,1)S(1)} %collective-permute-done.6.qg_ref.refs_0_, bf16[2,384,384]{2,1,0:T(8,128)(2,1)S(1)} %copy-done, ...), custom_call_target="tpu_custom_call" | custom-call | flops 150994944 | bytes 419200 | tf_op jit(solution)/shard_map/pallas_call | solution.py:294
  43.2 2.6 %collective-permute-done.7 = f32[4,6,256]{2,1,0:T(8,128)S(1)} collective-permute-done((f32[4,6,256]{2,1,0:T(8,128)S(1)}, f32[4,6,256]{2,1,0:T(8,128)S(1)}, u32[]{:S(2)}, u32[]{:S(2)}) %collective-permute-start.7) | collective-permute-done | bytes 24608 | tf_op jit(solution)/shard_map/ppermute | solution.py:319
  45.9 2.9 %collective-permute-start.8 = (f32[4,6,256]{2,1,0:T(8,128)S(1)}, f32[4,6,256]{2,1,0:T(8,128)S(1)}, u32[]{:S(2)}, u32[]{:S(2)}) collective-permute-start(f32[4,6,256]{2,1,0:T(8,128)S(1)} %pad_maximum_fusion.9), channel_id=1, source_target_pairs={{0,8},{1,9},{2,10},{3,11},{4,12},{5,13},{6,14},{7,15},{8,0},{9,1},... | collective-permute-start | bytes 73736 | tf_op jit(solution)/shard_map/ppermute | solution.py:319
  48.8 2.0 %collective-permute-done.8 = f32[4,6,256]{2,1,0:T(8,128)S(1)} collective-permute-done((f32[4,6,256]{2,1,0:T(8,128)S(1)}, f32[4,6,256]{2,1,0:T(8,128)S(1)}, u32[]{:S(2)}, u32[]{:S(2)}) %collective-permute-start.8) | collective-permute-done | bytes 24608 | tf_op jit(solution)/shard_map/ppermute | solution.py:319
  50.9 3.0 %collective-permute-start.9 = (bf16[2,192,256]{2,1,0:T(8,128)(2,1)S(1)}, bf16[2,192,256]{2,1,0:T(8,128)(2,1)S(1)}, u32[]{:S(2)}, u32[]{:S(2)}) collective-permute-start(bf16[2,192,256]{2,1,0:T(8,128)(2,1)S(1)} %pad_maximum_fusion.3), channel_id=1, source_target_pairs={{0,8},{1,9},{2,10},{3,11},{4,12},{5,13},{6,14},{7,15},{8,0},{9,1},... | collective-permute-start | bytes 589832 | tf_op jit(solution)/shard_map/ppermute | solution.py:319
  53.9 6.3 %shard_map.111 = (f32[4,192,256]{2,1,0:T(8,128)S(1)}, bf16[2,384,384]{2,1,0:T(8,128)(2,1)S(1)}) custom-call(f32[4,128]{1,0:T(4,128)S(1)} %fusion.30.count_ref, bf16[256,384]{1,0:T(8,128)(2,1)S(1)} %collective-permute-done.6.qg_ref.refs_0_, bf16[256,384]{1,0:T(8,128)(2,1)S(1)} %collective-permute-done.4.qg_ref.refs_1_.refs_0_, ...), custom_call_target="tpu_custom_call" | custom-call | flops 528482304 | bytes 494848 | tf_op jit(solution)/shard_map/pallas_call | solution.py:294
  60.2 1.6 %collective-permute-start.11 = (bf16[2,384,384]{2,1,0:T(8,128)(2,1)S(1)}, bf16[2,384,384]{2,1,0:T(8,128)(2,1)S(1)}, u32[]{:S(2)}, u32[]{:S(2)}) collective-permute-start(bf16[2,384,384]{2,1,0:T(8,128)(2,1)S(1)} %get-tuple-element.72), channel_id=1, source_target_pairs={{0,2},{1,3},{2,0},{3,1},{4,6},{5,7},{6,4},{7,5},{8,10},{9,11},{10,... | collective-permute-start | bytes 1769480 | tf_op jit(solution)/shard_map/ppermute | solution.py:319
  61.8 1.7 %shard_map.112 = (bf16[1,192,256]{2,1,0:T(8,128)(2,1)S(1)}, f32[2,384,384]{2,1,0:T(8,128)S(1)}) custom-call(f32[4,128]{1,0:T(4,128)S(1)} %fusion.30.count_ref, bf16[256,384]{1,0:T(8,128)(2,1)S(1)} %collective-permute-done.6.qg_ref.refs_0_, f32[6,256]{1,0:T(8,128)S(1)} %get-tuple-element.104.refs_4_.refs_1_, bf16[2,384,384]{2,1,0:T(8,128)(2,1)S(1)} %copy-done, ...), custom_call_target="tpu_custom_call" | custom-call | flops 132120576 | bytes 504832 | tf_op jit(solution)/shard_map/pallas_call | solution.py:294
  63.5 3.8 %collective-permute-start.12 = (bf16[192,256]{1,0:T(8,128)(2,1)S(1)}, bf16[192,256]{1,0:T(8,128)(2,1)S(1)}, u32[]{:S(2)}, u32[]{:S(2)}) collective-permute-start(bf16[192,256]{1,0:T(8,128)(2,1)S(1)} %bitcast.105), channel_id=1, source_target_pairs={{0,4},{1,5},{2,6},{3,7},{4,0},{5,1},{6,2},{7,3},{8,12},{9,13},{10,... | collective-permute-start | bytes 294920 | tf_op jit(solution)/shard_map/ppermute | solution.py:319
  67.4 1.7 %shard_map.113 = (f32[1,192,256]{2,1,0:T(8,128)S(1)}, f32[2,384,384]{2,1,0:T(8,128)S(1)}) custom-call(f32[4,128]{1,0:T(4,128)S(1)} %fusion.30.count_ref, bf16[256,384]{1,0:T(8,128)(2,1)S(1)} %collective-permute-done.4.qg_ref.refs_1_.refs_0_, f32[6,256]{1,0:T(8,128)S(1)} %get-tuple-element.105.refs_5_.refs_1_, bf16[2,384,384]{2,1,0:T(8,128)(2,1)S(1)} %copy-done, ...), custom_call_target="tpu_custom_call" | custom-call | flops 132120576 | bytes 664576 | tf_op jit(solution)/shard_map/pallas_call | solution.py:294
  70.6 1.7 %shard_map.114 = (bf16[1,192,256]{2,1,0:T(8,128)(2,1)S(1)}, f32[2,384,384]{2,1,0:T(8,128)S(1)}) custom-call(f32[4,128]{1,0:T(4,128)S(1)} %fusion.30.count_ref, bf16[256,384]{1,0:T(8,128)(2,1)S(1)} %collective-permute-done.5.qg_ref.refs_2_.refs_0_, f32[6,256]{1,0:T(8,128)S(1)} %get-tuple-element.106.refs_6_.refs_1_, bf16[2,384,384]{2,1,0:T(8,128)(2,1)S(1)} %copy-done, ...), custom_call_target="tpu_custom_call" | custom-call | flops 132120576 | bytes 652288 | tf_op jit(solution)/shard_map/pallas_call | solution.py:294
  74.6 1.7 %shard_map.115 = (f32[1,192,256]{2,1,0:T(8,128)S(1)}, bf16[2,384,384]{2,1,0:T(8,128)(2,1)S(1)}) custom-call(f32[4,128]{1,0:T(4,128)S(1)} %fusion.30.count_ref, bf16[256,384]{1,0:T(8,128)(2,1)S(1)} %pad_maximum_fusion.2.qg_ref.refs_3_.refs_0_, f32[6,256]{1,0:T(8,128)S(1)} %get-tuple-element.103.refs_7_.refs_1_, bf16[2,384,384]{2,1,0:T(8,128)(2,1)S(1)} %copy-done, ...), custom_call_target="tpu_custom_call" | custom-call | flops 132120576 | bytes 590848 | tf_op jit(solution)/shard_map/pallas_call | solution.py:294
  77.0 3.3 %collective-permute-done.14 = bf16[192,256]{1,0:T(8,128)(2,1)S(1)} collective-permute-done((bf16[192,256]{1,0:T(8,128)(2,1)S(1)}, bf16[192,256]{1,0:T(8,128)(2,1)S(1)}, u32[]{:S(2)}, u32[]{:S(2)}) %collective-permute-start.14) | collective-permute-done | bytes 98336 | tf_op jit(solution)/shard_map/ppermute | solution.py:319
  82.6 2.2 %shard_map.116 = bf16[384,768]{1,0:T(8,128)(2,1)} custom-call(s32[1]{0:T(128)} %bitcast.place_ref, bf16[2,384,384]{2,1,0:T(8,128)(2,1)S(1)} %get-tuple-element.86.near_ref, bf16[2,384,384]{2,1,0:T(8,128)(2,1)S(1)} %collective-permute-done.11.far_ref, bf16[2,384,384]{2,1,0:T(8,128)(2,1)S(1)} %collective-permute-done.16.core_ref, ...), custom_call_target="tpu_custom_call" | custom-call | flops 113246208 | bytes 589824 | tf_op jit(solution)/shard_map/pallas_call | solution.py:294
  (78 shorter events, 18.2 us)
Async XLA Ops:
  7.2 3.9 %collective-permute-start = (bf16[2,80,384]{2,1,0:T(8,128)(2,1)}, bf16[2,80,384]{2,1,0:T(8,128)(2,1)S(1)}, u32[]{:S(2)}, u32[]{:S(2)}) collective-permute-start(bf16[2,80,384]{2,1,0:T(8,128)(2,1)} %get-tuple-element.49), channel_id=1, source_target_pairs={{0,1},{1,0},{2,3},{3,2},{4,5},{5,4},{6,7},{7,6},{8,9},{9,8},{10,11... | collective-permute-start | bytes 368648 | tf_op jit(solution)/shard_map/ppermute | solution.py:319
  7.7 6.5 %collective-permute-start.2 = (bf16[2,384,384]{2,1,0:T(8,128)(2,1)}, bf16[2,384,384]{2,1,0:T(8,128)(2,1)S(1)}, u32[]{:S(2)}, u32[]{:S(2)}) collective-permute-start(bf16[2,384,384]{2,1,0:T(8,128)(2,1)} %get-tuple-element.52), channel_id=1, source_target_pairs={{0,1},{1,0},{2,3},{3,2},{4,5},{5,4},{6,7},{7,6},{8,9},{9,8},{10,11... | collective-permute-start | bytes 1769480 | tf_op jit(solution)/shard_map/ppermute | solution.py:319
  11.1 7.1 %collective-permute-start.1 = (bf16[2,80,384]{2,1,0:T(8,128)(2,1)S(1)}, bf16[2,80,384]{2,1,0:T(8,128)(2,1)S(1)}, u32[]{:S(2)}, u32[]{:S(2)}) collective-permute-start(bf16[2,80,384]{2,1,0:T(8,128)(2,1)S(1)} %pad_maximum_fusion.6), channel_id=1, source_target_pairs={{0,2},{1,3},{2,0},{3,1},{4,6},{5,7},{6,4},{7,5},{8,10},{9,11},{10,... | collective-permute-start | bytes 368648 | tf_op jit(solution)/shard_map/ppermute | solution.py:319
  14.1 9.0 %copy-start.3 = (bf16[768,768]{1,0:T(8,128)(2,1)S(1)}, bf16[768,768]{1,0:T(8,128)(2,1)}, u32[]{:S(2)}) copy-start(bf16[768,768]{1,0:T(8,128)(2,1)} %w_key_ref) | copy-start | bytes 3538948
  14.2 8.9 %copy-start.4 = (bf16[768,768]{1,0:T(8,128)(2,1)S(1)}, bf16[768,768]{1,0:T(8,128)(2,1)}, u32[]{:S(2)}) copy-start(bf16[768,768]{1,0:T(8,128)(2,1)} %w_value_ref) | copy-start | bytes 3538948
  14.3 16.0 %collective-permute-start.3 = (bf16[2,384,384]{2,1,0:T(8,128)(2,1)S(1)}, bf16[2,384,384]{2,1,0:T(8,128)(2,1)S(1)}, u32[]{:S(2)}, u32[]{:S(2)}) collective-permute-start(bf16[2,384,384]{2,1,0:T(8,128)(2,1)S(1)} %pad_maximum_fusion), channel_id=1, source_target_pairs={{0,2},{1,3},{2,0},{3,1},{4,6},{5,7},{6,4},{7,5},{8,10},{9,11},{10,... | collective-permute-start | bytes 1769480 | tf_op jit(solution)/shard_map/ppermute | solution.py:319
  18.3 18.8 %collective-permute-start.5 = (bf16[256,384]{1,0:T(8,128)(2,1)S(1)}, bf16[256,384]{1,0:T(8,128)(2,1)S(1)}, u32[]{:S(2)}, u32[]{:S(2)}) collective-permute-start(bf16[256,384]{1,0:T(8,128)(2,1)S(1)} %pad_maximum_fusion.2.qg_ref.refs_3_.refs_0_), channel_id=1, source_target_pairs={{0,4},{1,5},{2,6},{3,7},{4,0},{5,1},{6,2},{7,3},{8,12},{9,13},{10,... | collective-permute-start | bytes 589832 | tf_op jit(solution)/shard_map/ppermute | solution.py:319
  20.5 12.4 %collective-permute-start.4 = (bf16[256,384]{1,0:T(8,128)(2,1)S(1)}, bf16[256,384]{1,0:T(8,128)(2,1)S(1)}, u32[]{:S(2)}, u32[]{:S(2)}) collective-permute-start(bf16[256,384]{1,0:T(8,128)(2,1)S(1)} %pad_maximum_fusion.2.qg_ref.refs_3_.refs_0_), channel_id=1, source_target_pairs={{0,8},{1,9},{2,10},{3,11},{4,12},{5,13},{6,14},{7,15},{8,0},{9,1},... | collective-permute-start | bytes 589832 | tf_op jit(solution)/shard_map/ppermute | solution.py:319
  32.9 6.6 %collective-permute-start.6 = (bf16[256,384]{1,0:T(8,128)(2,1)S(1)}, bf16[256,384]{1,0:T(8,128)(2,1)S(1)}, u32[]{:S(2)}, u32[]{:S(2)}) collective-permute-start(bf16[256,384]{1,0:T(8,128)(2,1)S(1)} %collective-permute-done.4.qg_ref.refs_1_.refs_0_), channel_id=1, source_target_pairs={{0,4},{1,5},{2,6},{3,7},{4,0},{5,1},{6,2},{7,3},{8,12},{9,13},{10,... | collective-permute-start | bytes 589832 | tf_op jit(solution)/shard_map/ppermute | solution.py:319
  41.8 4.0 %collective-permute-start.7 = (f32[4,6,256]{2,1,0:T(8,128)S(1)}, f32[4,6,256]{2,1,0:T(8,128)S(1)}, u32[]{:S(2)}, u32[]{:S(2)}) collective-permute-start(f32[4,6,256]{2,1,0:T(8,128)S(1)} %pad_maximum_fusion.7), channel_id=1, source_target_pairs={{0,4},{1,5},{2,6},{3,7},{4,0},{5,1},{6,2},{7,3},{8,12},{9,13},{10,... | collective-permute-start | bytes 73736 | tf_op jit(solution)/shard_map/ppermute | solution.py:319
  45.9 4.9 %collective-permute-start.8 = (f32[4,6,256]{2,1,0:T(8,128)S(1)}, f32[4,6,256]{2,1,0:T(8,128)S(1)}, u32[]{:S(2)}, u32[]{:S(2)}) collective-permute-start(f32[4,6,256]{2,1,0:T(8,128)S(1)} %pad_maximum_fusion.9), channel_id=1, source_target_pairs={{0,8},{1,9},{2,10},{3,11},{4,12},{5,13},{6,14},{7,15},{8,0},{9,1},... | collective-permute-start | bytes 73736 | tf_op jit(solution)/shard_map/ppermute | solution.py:319
  50.9 10.9 %collective-permute-start.9 = (bf16[2,192,256]{2,1,0:T(8,128)(2,1)S(1)}, bf16[2,192,256]{2,1,0:T(8,128)(2,1)S(1)}, u32[]{:S(2)}, u32[]{:S(2)}) collective-permute-start(bf16[2,192,256]{2,1,0:T(8,128)(2,1)S(1)} %pad_maximum_fusion.3), channel_id=1, source_target_pairs={{0,8},{1,9},{2,10},{3,11},{4,12},{5,13},{6,14},{7,15},{8,0},{9,1},... | collective-permute-start | bytes 589832 | tf_op jit(solution)/shard_map/ppermute | solution.py:319
  60.2 14.3 %collective-permute-start.11 = (bf16[2,384,384]{2,1,0:T(8,128)(2,1)S(1)}, bf16[2,384,384]{2,1,0:T(8,128)(2,1)S(1)}, u32[]{:S(2)}, u32[]{:S(2)}) collective-permute-start(bf16[2,384,384]{2,1,0:T(8,128)(2,1)S(1)} %get-tuple-element.72), channel_id=1, source_target_pairs={{0,2},{1,3},{2,0},{3,1},{4,6},{5,7},{6,4},{7,5},{8,10},{9,11},{10,... | collective-permute-start | bytes 1769480 | tf_op jit(solution)/shard_map/ppermute | solution.py:319
  63.5 7.0 %collective-permute-start.12 = (bf16[192,256]{1,0:T(8,128)(2,1)S(1)}, bf16[192,256]{1,0:T(8,128)(2,1)S(1)}, u32[]{:S(2)}, u32[]{:S(2)}) collective-permute-start(bf16[192,256]{1,0:T(8,128)(2,1)S(1)} %bitcast.105), channel_id=1, source_target_pairs={{0,4},{1,5},{2,6},{3,7},{4,0},{5,1},{6,2},{7,3},{8,12},{9,13},{10,... | collective-permute-start | bytes 294920 | tf_op jit(solution)/shard_map/ppermute | solution.py:319
  67.3 7.2 %collective-permute-start.10 = (bf16[192,256]{1,0:T(8,128)(2,1)S(1)}, bf16[192,256]{1,0:T(8,128)(2,1)S(1)}, u32[]{:S(2)}, u32[]{:S(2)}) collective-permute-start(bf16[192,256]{1,0:T(8,128)(2,1)S(1)} %fusion.1), channel_id=1, source_target_pairs={{0,4},{1,5},{2,6},{3,7},{4,0},{5,1},{6,2},{7,3},{8,12},{9,13},{10,... | collective-permute-start | bytes 294920 | tf_op jit(solution)/shard_map/ppermute | solution.py:319
  72.3 4.7 %collective-permute-start.13 = (bf16[192,256]{1,0:T(8,128)(2,1)S(1)}, bf16[192,256]{1,0:T(8,128)(2,1)S(1)}, u32[]{:S(2)}, u32[]{:S(2)}) collective-permute-start(bf16[192,256]{1,0:T(8,128)(2,1)S(1)} %bitcast.104), channel_id=1, source_target_pairs={{0,4},{1,5},{2,6},{3,7},{4,0},{5,1},{6,2},{7,3},{8,12},{9,13},{10,... | collective-permute-start | bytes 294920 | tf_op jit(solution)/shard_map/ppermute | solution.py:319
  73.7 6.6 %collective-permute-start.14 = (bf16[192,256]{1,0:T(8,128)(2,1)S(1)}, bf16[192,256]{1,0:T(8,128)(2,1)S(1)}, u32[]{:S(2)}, u32[]{:S(2)}) collective-permute-start(bf16[192,256]{1,0:T(8,128)(2,1)S(1)} %fusion.4), channel_id=1, source_target_pairs={{0,8},{1,9},{2,10},{3,11},{4,12},{5,13},{6,14},{7,15},{8,0},{9,1},... | collective-permute-start | bytes 294920 | tf_op jit(solution)/shard_map/ppermute | solution.py:319
  80.5 2.1 %collective-permute-start.16 = (bf16[2,384,384]{2,1,0:T(8,128)(2,1)S(1)}, bf16[2,384,384]{2,1,0:T(8,128)(2,1)S(1)}, u32[]{:S(2)}, u32[]{:S(2)}) collective-permute-start(bf16[2,384,384]{2,1,0:T(8,128)(2,1)S(1)} %pad_maximum_fusion.1), channel_id=1, source_target_pairs={{0,1},{1,0},{2,3},{3,2},{4,5},{5,4},{6,7},{7,6},{8,9},{9,8},{10,11... | collective-permute-start | bytes 1769480 | tf_op jit(solution)/shard_map/ppermute | solution.py:319
  80.7 5.3 %collective-permute-start.15 = (bf16[2,192,128]{2,1,0:T(8,128)(2,1)S(1)}, bf16[2,192,128]{2,1,0:T(8,128)(2,1)S(1)}, u32[]{:S(2)}, u32[]{:S(2)}) collective-permute-start(bf16[2,192,128]{2,1,0:T(8,128)(2,1)S(1)} %get-tuple-element.93), channel_id=1, source_target_pairs={{0,2},{1,3},{2,0},{3,1},{4,6},{5,7},{6,4},{7,5},{8,10},{9,11},{10,... | collective-permute-start | bytes 294920 | tf_op jit(solution)/shard_map/ppermute | solution.py:319
  81.6 6.0 %copy-start.5 = (bf16[64,768]{1,0:T(8,128)(2,1)S(1)}, bf16[64,768]{1,0:T(8,128)(2,1)}, u32[]{:S(2)}) copy-start(bf16[64,768]{1,0:T(8,128)(2,1)} %latents_ref.1) | copy-start | bytes 294916
  81.6 6.0 %copy-start.6 = (bf16[64,768]{1,0:T(8,128)(2,1)S(1)}, bf16[64,768]{1,0:T(8,128)(2,1)}, u32[]{:S(2)}) copy-start(bf16[64,768]{1,0:T(8,128)(2,1)} %d_out_ref.1) | copy-start | bytes 294916
  82.6 5.0 %copy-start.1 = (bf16[768,768]{1,0:T(8,128)(2,1)S(1)}, bf16[768,768]{1,0:T(8,128)(2,1)}, u32[]{:S(2)}) copy-start(bf16[768,768]{1,0:T(8,128)(2,1)} %w_query_ref.1) | copy-start | bytes 3538948
  82.6 5.0 %copy-start.2 = (bf16[768,768]{1,0:T(8,128)(2,1)S(1)}, bf16[768,768]{1,0:T(8,128)(2,1)}, u32[]{:S(2)}) copy-start(bf16[768,768]{1,0:T(8,128)(2,1)} %w_out_ref.1) | copy-start | bytes 3538948
  86.1 1.5 %collective-permute-start.17 = (bf16[2,2,192,64]{3,2,1,0:T(8,128)(2,1)S(1)}, bf16[2,2,192,64]{3,2,1,0:T(8,128)(2,1)S(1)}, u32[]{:S(2)}, u32[]{:S(2)}) collective-permute-start(bf16[2,2,192,64]{3,2,1,0:T(8,128)(2,1)S(1)} %pad_maximum_fusion.5), channel_id=1, source_target_pairs={{0,1},{1,0},{2,3},{3,2},{4,5},{5,4},{6,7},{7,6},{8,9},{9,8},{10,11... | collective-permute-start | bytes 294920 | tf_op jit(solution)/shard_map/ppermute | solution.py:319
  (1 other events, 1.1 us)

commit v8 on v7

--- a/solution.py
+++ b/solution.py
@@ -114,6 +114,20 @@
             out_ref[quarter, i * mine : (i + 1) * mine, :] = turned[quarter * mine : (quarter + 1) * mine]
 
 
+def pair_kernel(keep_ref, core_ref, out_ref):
+    out_ref[0] = keep_ref[1]
+    out_ref[1] = core_ref[1]
+
+
+def chunk_kernel(keep_ref, core_ref, far_ref, out_ref, count_ref):
+    own, mine = out_ref.shape[0] // TEAM, out_ref.shape[1] // 2
+    blocks = keep_ref.at[0], core_ref.at[0], far_ref.at[0], far_ref.at[1]
+    for i, ref in enumerate(blocks):
+        out_ref[i * own : (i + 1) * own, :] = ref[:own, :]
+        row = ref[own:, :].astype(F32)[:1, :]
+        count_ref[i : i + 1, :] = 16 * row[:, :LANES] + row[:, mine : mine + LANES]
+
+
 def turn_kernel(picks, *refs):
     for i, (ref, which) in enumerate(picks):
         refs[-1][i] = refs[ref][which].T
@@ -124,18 +138,24 @@
     return slot >= count
 
 
-def forward_kernel(
-    count_ref, qg_ref, keep_ref, core_ref, far_ref, near_t_ref, far_t_ref,
-    numer_ref, max_ref, stat_ref, score_ref, weight_ref
-):
+def forward_kernel(blocks, count_ref, qg_ref, *refs):
+    kv_refs, kv_t_refs = {}, {}
+    if 0 in blocks:
+        keep_ref, core_ref, near_t_ref, *refs = refs
+        kv_refs.update({0: keep_ref.at[0], 1: core_ref.at[0]})
+        kv_t_refs.update({0: near_t_ref.at[0], 1: near_t_ref.at[1]})
+    if 2 in blocks:
+        far_ref, far_t_ref, *refs = refs
+        kv_refs.update({2: far_ref.at[0], 3: far_ref.at[1]})
+        kv_t_refs.update({2: far_t_ref.at[0], 3: far_t_ref.at[1]})
+    before = refs[:2] if blocks[0] else ()
+    numer_ref, stat_ref, score_ref, weight_ref = refs[len(before) :]
     rows = qg_ref.shape[0]
-    slots = keep_ref.shape[1]
-    dim = keep_ref.shape[2] // (2 * MINE)
+    slots = kv_refs[blocks[0]].shape[0]
+    dim = qg_ref.shape[1] // (2 * MINE)
     depth = score_ref.shape[0]
-    kv_refs = [keep_ref.at[0], core_ref.at[0], far_ref.at[0], far_ref.at[1]]
-    kv_t_refs = [near_t_ref.at[0], near_t_ref.at[1], far_t_ref.at[0], far_t_ref.at[1]]
     slot = lax.broadcasted_iota(jnp.int32, (slots, rows), 0).astype(F32)
-    units = [(head, block) for head in range(MINE) for block in range(TEAM)]
+    units = [(head, block) for head in range(MINE) for block in blocks]
     tops, totals, numers = {}, {}, {}
 
     def score(step):
@@ -156,20 +176,25 @@
         part = MINE + head
         at = slice(part * dim, (part + 1) * dim)
         numers[step] = dot(kv_t_refs[block][at, :], weight_ref[step % depth])
-        if block < TEAM - 1:
+        if block != blocks[-1]:
             return
-        steps = range(step - TEAM + 1, step + 1)
+        steps = list(range(step - len(blocks) + 1, step + 1))
+        own_rows = slice(head * dim, (head + 1) * dim)
+        if before:
+            steps.append(-1)
+            numers[-1] = before[0][own_rows, :]
+            tops[-1] = before[1][head : head + 1, :]
+            totals[-1] = before[1][MINE + head : MINE + head + 1, :]
         top = functools.reduce(jnp.maximum, [tops[s] for s in steps])
         scale = {s: jnp.exp(tops[s] - top) for s in steps}
         total = sum(scale[s] * totals[s] for s in steps)
         numer = sum(scale[s] * numers[s] for s in steps)
-        numer_ref[head * dim : (head + 1) * dim, :] = numer
+        numer_ref[own_rows, :] = numer
         half = part % 2 * dim
         grad_t = qg_ref[:, lanes_of(part)].astype(F32).T[half : half + dim, :]
         inner = jnp.sum(grad_t * numer, axis=0, keepdims=True)
-        max_ref[head : head + 1, :] = top
-        stat_ref[head : head + 1, :] = top + jnp.log(total)
-        stat_ref[MINE + head : MINE + head + 1, :] = inner / total
+        for i, row in enumerate((top, total, top + jnp.log(total), inner / total)):
+            stat_ref[i * MINE + head : i * MINE + head + 1, :] = row
 
     for step in range(len(units) + 2):
         if step < len(units):
@@ -330,13 +355,16 @@
         grant=60,
     )
     core_qg = swap(send_qg, 1)
-    far_qg = swap(jnp.stack([keep_qg[1], core_qg[1]]), 2)
     core = swap(send, 1)
-    far = swap(jnp.stack([keep[1], core[1]]), 2)
-    blocks = [keep_qg[0], core_qg[0], far_qg[0], far_qg[1]]
-    qg = jnp.concatenate([a[:own] for a in blocks], axis=0)
-    tail = jnp.concatenate([a[own : own + 1] for a in blocks], axis=0).astype(F32)
-    count = 16 * tail[:, :LANES] + tail[:, mine : mine + LANES]
+    (far_qg,) = call(pair_kernel, [keep_qg, core_qg], [shape(keep_qg.shape, BF16)])
+    far_qg, core = lax.optimization_barrier((far_qg, core))
+    far_qg = swap(far_qg, 2)
+    far = swap(call(pair_kernel, [keep, core], [shape(keep.shape, BF16)])[0], 2)
+    qg, count = call(
+        chunk_kernel,
+        [keep_qg, core_qg, far_qg],
+        [shape((TEAM * own, 2 * mine), BF16), shape((TEAM, LANES), F32)],
+    )
     for mask in middle:
         qg = jnp.concatenate([qg, swap(qg, mask)], axis=0)
     qg, w_key, w_value = lax.optimization_barrier((qg, w_key, w_value))
@@ -346,24 +374,33 @@
     turned = [shape((2, 2 * mine, slots), BF16)]
     (near_t,) = call(functools.partial(turn_kernel, ((0, 0), (1, 0))), [keep, core], turned)
     near_t, weights = lax.optimization_barrier((near_t, weights))
-    (far_t,) = call(functools.partial(turn_kernel, ((0, 0), (0, 1))), [far], turned)
     rows = qg[0].shape[0]
     team_slots = TEAM * slots
     work = 2 * rows * team_slots * mine
 
-    numer, tops, stats = [None] * 4, [None] * 4, [None] * 4
-    for p in range(4):
-        if p == 2:
-            qg[2], stats[0] = lax.optimization_barrier((qg[2], stats[0]))
-            qg.append(swap(qg[2], near_bit))
-        numer[p], tops[p], stats[p] = call(
-            forward_kernel,
-            [count, qg[p], keep, core, far, near_t, far_t],
-            [shape((mine, rows), F32), shape((MINE, rows), F32), shape((2 * MINE, rows), F32)],
+    def forward(p, blocks, before=()):
+        return call(
+            functools.partial(forward_kernel, blocks),
+            [count, qg[p]]
+            + ([keep, core, near_t] if 0 in blocks else [])
+            + ([far, far_t] if 2 in blocks else [])
+            + list(before),
+            [shape((mine, rows), F32), shape((4 * MINE, rows), F32)],
             [pltpu.VMEM((3, slots, rows), F32), pltpu.VMEM((3, slots, rows), BF16)],
-            flops=8 * work,
-            exps=rows * team_slots * MINE,
+            flops=2 * work * len(blocks),
+            exps=rows * slots * len(blocks) * MINE,
         )
+
+    early = [forward(p, (0, 1)) for p in range(2)]
+    (early, far) = lax.optimization_barrier((early, far))
+    (far_t,) = call(functools.partial(turn_kernel, ((0, 0), (0, 1))), [far], turned)
+    done = [forward(p, (2, 3), early[p]) for p in range(2)]
+    qg[2], done[0] = lax.optimization_barrier((qg[2], done[0]))
+    qg.append(swap(qg[2], near_bit))
+    done += [forward(p, (0, 1, 2, 3)) for p in (2, 3)]
+    numer = [d[0] for d in done]
+    tops = [d[1][:MINE] for d in done]
+    stats = [d[1][2 * MINE :] for d in done]
 
     def merge(*parts):
         lse = [p[..., :MINE, :] for p in parts]
@@ -428,7 +465,7 @@
     far_q = swap(sent, far_bit)
     gq, total = backward((1,), 0, BF16, [total], [partial])
     near_q = swap(gq[0], near_bit)
-    came_far, total = lax.optimization_barrier((came_far, total))
+    came_far, far_q, total = lax.optimization_barrier((came_far, far_q, total))
     gq, gkv_near = backward((0,), 0, F32, [total], [partial], True)
     attended = add(add(scaled(0), near_a), came_a[1])
     grad_query = add(add(gq[0], near_q), far_q)

time: 89.4 us -> 97.7 us (1.093)
  waiting for transfers between devices: 23.4 us -> 43.3 us
  starting transfers between devices: 26.2 us -> 16.2 us
  local copies, waits for them, and re-layouts: 4.03 us -> 2.34 us
    ppermute x18, waiting for transfers between devices: 23.4 us -> 43.3 us  [swap(): return lax.ppermute(array, 'pts', [(i, i ^ mask) for i in range(size)])]
    ppermute x18, starting transfers between devices: 26.2 us -> 16.2 us  [swap(): return lax.ppermute(array, 'pts', [(i, i ^ mask) for i in range(size)])]
    slice x10 -> x0, local copies, waits for them, and re-layouts: 3.39 us -> none  [the longest x2 1.02 us: body(): far = swap(jnp.stack([keep[1], core[1]]), 2)]
    unnamed x14 -> x20, local copies, waits for them, and re-layouts: 0.35 us -> 2.03 us
    pallas_call x15 -> x20, Pallas kernels: 33.1 us -> 33.5 us  [call(): pl.pallas_call(kernel, in_specs=[smem if a.dtype == jnp.int32 else other...]
  transfers between devices with their start and end apart: 18 -> 18, of which waited for: 10 -> 12; matrix products, arithmetic and copies ran while one was open for 4% -> 0% of each run, Pallas kernels for 26% -> 24%
where the time goes in v8:
time: 97.7 us; the launch traced here: 97.5 us
  waiting for transfers between devices  43.3 us (44%)
  Pallas kernels  33.5 us (34%)
  starting transfers between devices  16.2 us (17%)
  local copies, waits for them, and re-layouts  2.34 us (2%)
  between operations  1.69 us (2%)
    ppermute x18, waiting for transfers between devices, swap(): return lax.ppermute(array, 'pts', [(i, i ^ mask) for i in range(size)])  43.3 us
    pallas_call x20, Pallas kernels, call(): pl.pallas_call(kernel, in_specs=[smem if a.dtype == jnp.int32 else other...  33.5 us
    ppermute x18, starting transfers between devices, swap(): return lax.ppermute(array, 'pts', [(i, i ^ mask) for i in range(size)])  16.2 us
    unnamed x20, local copies, waits for them, and re-layouts  2.03 us
  transfers between devices with their start and end apart: 18, of which 12 were waited for; matrix products, arithmetic and copies ran while one was open for 0% of the time, Pallas kernels for 24%

profile of v8, /device:TPU:0, one launch (start us, length us, event | category | flops | bytes accessed | tf_op | source)
XLA Modules:
  0.0 97.5 jit_solution(1542741019045546993)
XLA Ops:
  1.3 5.9 %shard_map.103 = (bf16[2,80,384]{2,1,0:T(8,128)(2,1)}, bf16[2,80,384]{2,1,0:T(8,128)(2,1)}, bf16[2,384,384]{2,1,0:T(8,128)(2,1)}, bf16[2,384,384]{2,1,0:T(8,128)(2,1)}) custom-call(s32[1]{0:T(128)} %bitcast.place_ref, s32[1]{0:T(128)S(6)} %copy.11.count_ref, bf16[64,768]{1,0:T(8,128)(2,1)} %latents_ref.1, bf16[64,768]{1,0:T(8,128)(2,1)} %d_out_ref.1, ...), custom_call_target="tpu_custom_call" | custom-call | flops 132120576 | bytes 866305 | tf_op jit(solution)/shard_map/pallas_call | solution.py:319
  7.7 1.9 %collective-permute-done.core_ref = bf16[2,80,384]{2,1,0:T(8,128)(2,1)S(1)} collective-permute-done((bf16[2,80,384]{2,1,0:T(8,128)(2,1)}, bf16[2,80,384]{2,1,0:T(8,128)(2,1)S(1)}, u32[]{:S(2)}, u32[]{:S(2)}) %collective-permute-start) | collective-permute-done | bytes 122912 | tf_op jit(solution)/shard_map/ppermute | solution.py:344
  11.8 2.9 %collective-permute-start.5 = (bf16[2,384,384]{2,1,0:T(8,128)(2,1)S(1)}, bf16[2,384,384]{2,1,0:T(8,128)(2,1)S(1)}, u32[]{:S(2)}, u32[]{:S(2)}) collective-permute-start(bf16[2,384,384]{2,1,0:T(8,128)(2,1)S(1)} %shard_map.110), channel_id=1, source_target_pairs={{0,2},{1,3},{2,0},{3,1},{4,6},{5,7},{6,4},{7,5},{8,10},{9,11},{10,... | collective-permute-start | bytes 1769480 | tf_op jit(solution)/shard_map/ppermute | solution.py:344
  14.8 16.2 %collective-permute-done.2.far_ref = bf16[2,80,384]{2,1,0:T(8,128)(2,1)S(1)} collective-permute-done((bf16[2,80,384]{2,1,0:T(8,128)(2,1)S(1)}, bf16[2,80,384]{2,1,0:T(8,128)(2,1)S(1)}, u32[]{:S(2)}, u32[]{:S(2)}) %collective-permute-start.2) | collective-permute-done | bytes 122912 | tf_op jit(solution)/shard_map/ppermute | solution.py:344
  31.1 1.9 %collective-permute-start.4 = (bf16[256,384]{1,0:T(8,128)(2,1)S(1)}, bf16[256,384]{1,0:T(8,128)(2,1)S(1)}, u32[]{:S(2)}, u32[]{:S(2)}) collective-permute-start(bf16[256,384]{1,0:T(8,128)(2,1)S(1)} %get-tuple-element.64.qg_ref.refs_3_.refs_0_), channel_id=1, source_target_pairs={{0,4},{1,5},{2,6},{3,7},{4,0},{5,1},{6,2},{7,3},{8,12},{9,13},{10,... | collective-permute-start | bytes 589832 | tf_op jit(solution)/shard_map/ppermute | solution.py:344
  32.9 2.6 %collective-permute-start.3 = (bf16[256,384]{1,0:T(8,128)(2,1)S(1)}, bf16[256,384]{1,0:T(8,128)(2,1)S(1)}, u32[]{:S(2)}, u32[]{:S(2)}) collective-permute-start(bf16[256,384]{1,0:T(8,128)(2,1)S(1)} %get-tuple-element.64.qg_ref.refs_3_.refs_0_), channel_id=1, source_target_pairs={{0,8},{1,9},{2,10},{3,11},{4,12},{5,13},{6,14},{7,15},{8,0},{9,1},... | collective-permute-start | bytes 589832 | tf_op jit(solution)/shard_map/ppermute | solution.py:344
  37.7 4.0 %collective-permute-done.4.qg_ref.refs_2_.refs_0_ = bf16[256,384]{1,0:T(8,128)(2,1)S(1)} collective-permute-done((bf16[256,384]{1,0:T(8,128)(2,1)S(1)}, bf16[256,384]{1,0:T(8,128)(2,1)S(1)}, u32[]{:S(2)}, u32[]{:S(2)}) %collective-permute-start.4) | collective-permute-done | bytes 196640 | tf_op jit(solution)/shard_map/ppermute | solution.py:344
  44.5 2.3 %shard_map.114 = (f32[192,256]{1,0:T(8,128)S(1)}, f32[12,256]{1,0:T(8,128)S(1)}) custom-call(f32[4,128]{1,0:T(4,128)S(1)} %get-tuple-element.65.count_ref, bf16[256,384]{1,0:T(8,128)(2,1)S(1)} %collective-permute-done.3.qg_ref.refs_1_.refs_0_, bf16[2,384,384]{2,1,0:T(8,128)(2,1)S(1)} %copy-done.1, ...), custom_call_target="tpu_custom_call" | custom-call | flops 150994944 | bytes 419584 | tf_op jit(solution)/shard_map/pallas_call | solution.py:319
  48.1 2.0 %collective-permute-done.6.qg_ref.refs_0_ = bf16[256,384]{1,0:T(8,128)(2,1)S(1)} collective-permute-done((bf16[256,384]{1,0:T(8,128)(2,1)S(1)}, bf16[256,384]{1,0:T(8,128)(2,1)S(1)}, u32[]{:S(2)}, u32[]{:S(2)}) %collective-permute-start.6) | collective-permute-done | bytes 196640 | tf_op jit(solution)/shard_map/ppermute | solution.py:344
  50.1 2.3 %shard_map.115 = (f32[192,256]{1,0:T(8,128)S(1)}, f32[12,256]{1,0:T(8,128)S(1)}) custom-call(f32[4,128]{1,0:T(4,128)S(1)} %get-tuple-element.65.count_ref, bf16[256,384]{1,0:T(8,128)(2,1)S(1)} %collective-permute-done.6.qg_ref.refs_0_, bf16[2,384,384]{2,1,0:T(8,128)(2,1)S(1)} %copy-done.1, ...), custom_call_target="tpu_custom_call" | custom-call | flops 150994944 | bytes 419584 | tf_op jit(solution)/shard_map/pallas_call | solution.py:319
  52.6 4.0 %collective-permute-done.7 = f32[4,6,256]{2,1,0:T(8,128)S(1)} collective-permute-done((f32[4,6,256]{2,1,0:T(8,128)S(1)}, f32[4,6,256]{2,1,0:T(8,128)S(1)}, u32[]{:S(2)}, u32[]{:S(2)}) %collective-permute-start.7) | collective-permute-done | bytes 24608 | tf_op jit(solution)/shard_map/ppermute | solution.py:344
  57.9 5.8 %collective-permute-done.8 = f32[4,6,256]{2,1,0:T(8,128)S(1)} collective-permute-done((f32[4,6,256]{2,1,0:T(8,128)S(1)}, f32[4,6,256]{2,1,0:T(8,128)S(1)}, u32[]{:S(2)}, u32[]{:S(2)}) %collective-permute-start.8) | collective-permute-done | bytes 24608 | tf_op jit(solution)/shard_map/ppermute | solution.py:344
  63.9 6.3 %shard_map.116 = (f32[4,192,256]{2,1,0:T(8,128)S(1)}, bf16[2,384,384]{2,1,0:T(8,128)(2,1)S(1)}) custom-call(f32[4,128]{1,0:T(4,128)S(1)} %get-tuple-element.65.count_ref, bf16[256,384]{1,0:T(8,128)(2,1)S(1)} %collective-permute-done.6.qg_ref.refs_0_, bf16[256,384]{1,0:T(8,128)(2,1)S(1)} %collective-permute-done.3.qg_ref.refs_1_.refs_0_, ...), custom_call_target="tpu_custom_call" | custom-call | flops 528482304 | bytes 494848 | tf_op jit(solution)/shard_map/pallas_call | solution.py:319
  70.2 1.5 %collective-permute-start.11 = (bf16[2,384,384]{2,1,0:T(8,128)(2,1)S(1)}, bf16[2,384,384]{2,1,0:T(8,128)(2,1)S(1)}, u32[]{:S(2)}, u32[]{:S(2)}) collective-permute-start(bf16[2,384,384]{2,1,0:T(8,128)(2,1)S(1)} %get-tuple-element.93), channel_id=1, source_target_pairs={{0,2},{1,3},{2,0},{3,1},{4,6},{5,7},{6,4},{7,5},{8,10},{9,11},{10,... | collective-permute-start | bytes 1769480 | tf_op jit(solution)/shard_map/ppermute | solution.py:344
  72.6 1.7 %shard_map.117 = (bf16[1,192,256]{2,1,0:T(8,128)(2,1)S(1)}, f32[2,384,384]{2,1,0:T(8,128)S(1)}) custom-call(f32[4,128]{1,0:T(4,128)S(1)} %get-tuple-element.65.count_ref, bf16[256,384]{1,0:T(8,128)(2,1)S(1)} %collective-permute-done.6.qg_ref.refs_0_, f32[6,256]{1,0:T(8,128)S(1)} %get-tuple-element.122.refs_4_.refs_1_, bf16[2,384,384]{2,1,0:T(8,128)(2,1)S(1)} %copy-done.1, ...), custom_call_target="tpu_custom_call" | custom-call | flops 132120576 | bytes 504832 | tf_op jit(solution)/shard_map/pallas_call | solution.py:319
  74.3 2.6 %collective-permute-start.12 = (bf16[192,256]{1,0:T(8,128)(2,1)S(1)}, bf16[192,256]{1,0:T(8,128)(2,1)S(1)}, u32[]{:S(2)}, u32[]{:S(2)}) collective-permute-start(bf16[192,256]{1,0:T(8,128)(2,1)S(1)} %bitcast.89), channel_id=1, source_target_pairs={{0,4},{1,5},{2,6},{3,7},{4,0},{5,1},{6,2},{7,3},{8,12},{9,13},{10,... | collective-permute-start | bytes 294920 | tf_op jit(solution)/shard_map/ppermute | solution.py:344
  77.0 1.7 %shard_map.118 = (f32[1,192,256]{2,1,0:T(8,128)S(1)}, f32[2,384,384]{2,1,0:T(8,128)S(1)}) custom-call(f32[4,128]{1,0:T(4,128)S(1)} %get-tuple-element.65.count_ref, bf16[256,384]{1,0:T(8,128)(2,1)S(1)} %collective-permute-done.3.qg_ref.refs_1_.refs_0_, f32[6,256]{1,0:T(8,128)S(1)} %get-tuple-element.123.refs_5_.refs_1_, bf16[2,384,384]{2,1,0:T(8,128)(2,1)S(1)} %copy-done.1, ...), custom_call_target="tpu_custom_call" | custom-call | flops 132120576 | bytes 664576 | tf_op jit(solution)/shard_map/pallas_call | solution.py:319
  78.7 1.7 %collective-permute-done.12 = bf16[192,256]{1,0:T(8,128)(2,1)S(1)} collective-permute-done((bf16[192,256]{1,0:T(8,128)(2,1)S(1)}, bf16[192,256]{1,0:T(8,128)(2,1)S(1)}, u32[]{:S(2)}, u32[]{:S(2)}) %collective-permute-start.12) | collective-permute-done | bytes 98336 | tf_op jit(solution)/shard_map/ppermute | solution.py:344
  81.8 1.7 %shard_map.119 = (bf16[1,192,256]{2,1,0:T(8,128)(2,1)S(1)}, f32[2,384,384]{2,1,0:T(8,128)S(1)}) custom-call(f32[4,128]{1,0:T(4,128)S(1)} %get-tuple-element.65.count_ref, bf16[256,384]{1,0:T(8,128)(2,1)S(1)} %collective-permute-done.4.qg_ref.refs_2_.refs_0_, f32[6,256]{1,0:T(8,128)S(1)} %get-tuple-element.124.refs_6_.refs_1_, ...), custom_call_target="tpu_custom_call" | custom-call | flops 132120576 | bytes 652288 | tf_op jit(solution)/shard_map/pallas_call | solution.py:319
  84.5 2.6 %collective-permute-done.13 = bf16[192,256]{1,0:T(8,128)(2,1)S(1)} collective-permute-done((bf16[192,256]{1,0:T(8,128)(2,1)S(1)}, bf16[192,256]{1,0:T(8,128)(2,1)S(1)}, u32[]{:S(2)}, u32[]{:S(2)}) %collective-permute-start.13) | collective-permute-done | bytes 98336 | tf_op jit(solution)/shard_map/ppermute | solution.py:344
  87.1 1.7 %shard_map.120 = (f32[1,192,256]{2,1,0:T(8,128)S(1)}, bf16[2,384,384]{2,1,0:T(8,128)(2,1)S(1)}) custom-call(f32[4,128]{1,0:T(4,128)S(1)} %get-tuple-element.65.count_ref, bf16[256,384]{1,0:T(8,128)(2,1)S(1)} %get-tuple-element.64.qg_ref.refs_3_.refs_0_, f32[6,256]{1,0:T(8,128)S(1)} %get-tuple-element.121.refs_7_.refs_1_, bf16[2,384,384]{2,1,0:T(8,128)(2,1)S(1)} %copy-done.1, ...), custom_call_target="tpu_custom_call" | custom-call | flops 132120576 | bytes 590848 | tf_op jit(solution)/shard_map/pallas_call | solution.py:319
  89.4 1.7 %collective-permute-done.16.core_ref = bf16[2,384,384]{2,1,0:T(8,128)(2,1)S(1)} collective-permute-done((bf16[2,384,384]{2,1,0:T(8,128)(2,1)S(1)}, bf16[2,384,384]{2,1,0:T(8,128)(2,1)S(1)}, u32[]{:S(2)}, u32[]{:S(2)}) %collective-permute-start.16) | collective-permute-done | bytes 589856 | tf_op jit(solution)/shard_map/ppermute | solution.py:344
  91.1 2.2 %shard_map.121 = bf16[384,768]{1,0:T(8,128)(2,1)} custom-call(s32[1]{0:T(128)} %bitcast.place_ref, bf16[2,384,384]{2,1,0:T(8,128)(2,1)S(1)} %get-tuple-element.108.near_ref, bf16[2,384,384]{2,1,0:T(8,128)(2,1)S(1)} %collective-permute-done.11.far_ref, bf16[2,384,384]{2,1,0:T(8,128)(2,1)S(1)} %collective-permute-done.16.core_ref, ...), custom_call_target="tpu_custom_call" | custom-call | flops 113246208 | bytes 589824 | tf_op jit(solution)/shard_map/pallas_call | solution.py:319
  94.6 1.4 %collective-permute-done.17.core_ref = bf16[2,2,192,64]{3,2,1,0:T(8,128)(2,1)S(1)} collective-permute-done((bf16[2,2,192,64]{3,2,1,0:T(8,128)(2,1)S(1)}, bf16[2,2,192,64]{3,2,1,0:T(8,128)(2,1)S(1)}, u32[]{:S(2)}, u32[]{:S(2)}) %collective-permute-start.17) | collective-permute-done | bytes 98336 | tf_op jit(solution)/shard_map/ppermute | solution.py:344
  (79 shorter events, 17.0 us)
Async XLA Ops:
  7.1 3.5 %collective-permute-start.1 = (bf16[2,384,384]{2,1,0:T(8,128)(2,1)}, bf16[2,384,384]{2,1,0:T(8,128)(2,1)S(1)}, u32[]{:S(2)}, u32[]{:S(2)}) collective-permute-start(bf16[2,384,384]{2,1,0:T(8,128)(2,1)} %get-tuple-element.61), channel_id=1, source_target_pairs={{0,1},{1,0},{2,3},{3,2},{4,5},{5,4},{6,7},{7,6},{8,9},{9,8},{10,11... | collective-permute-start | bytes 1769480 | tf_op jit(solution)/shard_map/ppermute | solution.py:344
  7.7 2.0 %collective-permute-start = (bf16[2,80,384]{2,1,0:T(8,128)(2,1)}, bf16[2,80,384]{2,1,0:T(8,128)(2,1)S(1)}, u32[]{:S(2)}, u32[]{:S(2)}) collective-permute-start(bf16[2,80,384]{2,1,0:T(8,128)(2,1)} %get-tuple-element.60), channel_id=1, source_target_pairs={{0,1},{1,0},{2,3},{3,2},{4,5},{5,4},{6,7},{7,6},{8,9},{9,8},{10,11... | collective-permute-start | bytes 368648 | tf_op jit(solution)/shard_map/ppermute | solution.py:344
  10.6 20.4 %copy-start.7 = (bf16[2,80,384]{2,1,0:T(8,128)(2,1)S(1)}, bf16[2,80,384]{2,1,0:T(8,128)(2,1)}, u32[]{:S(2)}) copy-start(bf16[2,80,384]{2,1,0:T(8,128)(2,1)} %get-tuple-element.59.keep_ref) | copy-start | bytes 368644
  11.7 23.8 %copy-start.1 = (bf16[2,384,384]{2,1,0:T(8,128)(2,1)S(1)}, bf16[2,384,384]{2,1,0:T(8,128)(2,1)}, u32[]{:S(2)}) copy-start(bf16[2,384,384]{2,1,0:T(8,128)(2,1)} %get-tuple-element.66.refs_0_.keep_ref.refs_2_) | copy-start | bytes 1769476
  11.7 24.0 %copy-start.5 = (bf16[768,768]{1,0:T(8,128)(2,1)S(1)}, bf16[768,768]{1,0:T(8,128)(2,1)}, u32[]{:S(2)}) copy-start(bf16[768,768]{1,0:T(8,128)(2,1)} %w_value_ref) | copy-start | bytes 3538948
  11.8 24.0 %copy-start.4 = (bf16[768,768]{1,0:T(8,128)(2,1)S(1)}, bf16[768,768]{1,0:T(8,128)(2,1)}, u32[]{:S(2)}) copy-start(bf16[768,768]{1,0:T(8,128)(2,1)} %w_key_ref) | copy-start | bytes 3538948
  11.8 31.1 %collective-permute-start.5 = (bf16[2,384,384]{2,1,0:T(8,128)(2,1)S(1)}, bf16[2,384,384]{2,1,0:T(8,128)(2,1)S(1)}, u32[]{:S(2)}, u32[]{:S(2)}) collective-permute-start(bf16[2,384,384]{2,1,0:T(8,128)(2,1)S(1)} %shard_map.110), channel_id=1, source_target_pairs={{0,2},{1,3},{2,0},{3,1},{4,6},{5,7},{6,4},{7,5},{8,10},{9,11},{10,... | collective-permute-start | bytes 1769480 | tf_op jit(solution)/shard_map/ppermute | solution.py:344
  14.7 16.3 %collective-permute-start.2 = (bf16[2,80,384]{2,1,0:T(8,128)(2,1)S(1)}, bf16[2,80,384]{2,1,0:T(8,128)(2,1)S(1)}, u32[]{:S(2)}, u32[]{:S(2)}) collective-permute-start(bf16[2,80,384]{2,1,0:T(8,128)(2,1)S(1)} %shard_map.104), channel_id=1, source_target_pairs={{0,2},{1,3},{2,0},{3,1},{4,6},{5,7},{6,4},{7,5},{8,10},{9,11},{10,... | collective-permute-start | bytes 368648 | tf_op jit(solution)/shard_map/ppermute | solution.py:344
  31.1 10.6 %collective-permute-start.4 = (bf16[256,384]{1,0:T(8,128)(2,1)S(1)}, bf16[256,384]{1,0:T(8,128)(2,1)S(1)}, u32[]{:S(2)}, u32[]{:S(2)}) collective-permute-start(bf16[256,384]{1,0:T(8,128)(2,1)S(1)} %get-tuple-element.64.qg_ref.refs_3_.refs_0_), channel_id=1, source_target_pairs={{0,4},{1,5},{2,6},{3,7},{4,0},{5,1},{6,2},{7,3},{8,12},{9,13},{10,... | collective-permute-start | bytes 589832 | tf_op jit(solution)/shard_map/ppermute | solution.py:344
  32.9 11.4 %collective-permute-start.3 = (bf16[256,384]{1,0:T(8,128)(2,1)S(1)}, bf16[256,384]{1,0:T(8,128)(2,1)S(1)}, u32[]{:S(2)}, u32[]{:S(2)}) collective-permute-start(bf16[256,384]{1,0:T(8,128)(2,1)S(1)} %get-tuple-element.64.qg_ref.refs_3_.refs_0_), channel_id=1, source_target_pairs={{0,8},{1,9},{2,10},{3,11},{4,12},{5,13},{6,14},{7,15},{8,0},{9,1},... | collective-permute-start | bytes 589832 | tf_op jit(solution)/shard_map/ppermute | solution.py:344
  44.4 5.7 %collective-permute-start.6 = (bf16[256,384]{1,0:T(8,128)(2,1)S(1)}, bf16[256,384]{1,0:T(8,128)(2,1)S(1)}, u32[]{:S(2)}, u32[]{:S(2)}) collective-permute-start(bf16[256,384]{1,0:T(8,128)(2,1)S(1)} %collective-permute-done.3.qg_ref.refs_1_.refs_0_), channel_id=1, source_target_pairs={{0,4},{1,5},{2,6},{3,7},{4,0},{5,1},{6,2},{7,3},{8,12},{9,13},{10,... | collective-permute-start | bytes 589832 | tf_op jit(solution)/shard_map/ppermute | solution.py:344
  52.5 4.1 %collective-permute-start.7 = (f32[4,6,256]{2,1,0:T(8,128)S(1)}, f32[4,6,256]{2,1,0:T(8,128)S(1)}, u32[]{:S(2)}, u32[]{:S(2)}) collective-permute-start(f32[4,6,256]{2,1,0:T(8,128)S(1)} %pad_maximum_fusion.4), channel_id=1, source_target_pairs={{0,4},{1,5},{2,6},{3,7},{4,0},{5,1},{6,2},{7,3},{8,12},{9,13},{10,... | collective-permute-start | bytes 73736 | tf_op jit(solution)/shard_map/ppermute | solution.py:344
  56.6 7.0 %collective-permute-start.8 = (f32[4,6,256]{2,1,0:T(8,128)S(1)}, f32[4,6,256]{2,1,0:T(8,128)S(1)}, u32[]{:S(2)}, u32[]{:S(2)}) collective-permute-start(f32[4,6,256]{2,1,0:T(8,128)S(1)} %pad_maximum_fusion.6), channel_id=1, source_target_pairs={{0,8},{1,9},{2,10},{3,11},{4,12},{5,13},{6,14},{7,15},{8,0},{9,1},... | collective-permute-start | bytes 73736 | tf_op jit(solution)/shard_map/ppermute | solution.py:344
  63.8 8.8 %collective-permute-start.9 = (bf16[2,192,256]{2,1,0:T(8,128)(2,1)S(1)}, bf16[2,192,256]{2,1,0:T(8,128)(2,1)S(1)}, u32[]{:S(2)}, u32[]{:S(2)}) collective-permute-start(bf16[2,192,256]{2,1,0:T(8,128)(2,1)S(1)} %pad_maximum_fusion.1), channel_id=1, source_target_pairs={{0,8},{1,9},{2,10},{3,11},{4,12},{5,13},{6,14},{7,15},{8,0},{9,1},... | collective-permute-start | bytes 589832 | tf_op jit(solution)/shard_map/ppermute | solution.py:344
  70.2 16.9 %collective-permute-start.11 = (bf16[2,384,384]{2,1,0:T(8,128)(2,1)S(1)}, bf16[2,384,384]{2,1,0:T(8,128)(2,1)S(1)}, u32[]{:S(2)}, u32[]{:S(2)}) collective-permute-start(bf16[2,384,384]{2,1,0:T(8,128)(2,1)S(1)} %get-tuple-element.93), channel_id=1, source_target_pairs={{0,2},{1,3},{2,0},{3,1},{4,6},{5,7},{6,4},{7,5},{8,10},{9,11},{10,... | collective-permute-start | bytes 1769480 | tf_op jit(solution)/shard_map/ppermute | solution.py:344
  74.3 6.1 %collective-permute-start.12 = (bf16[192,256]{1,0:T(8,128)(2,1)S(1)}, bf16[192,256]{1,0:T(8,128)(2,1)S(1)}, u32[]{:S(2)}, u32[]{:S(2)}) collective-permute-start(bf16[192,256]{1,0:T(8,128)(2,1)S(1)} %bitcast.89), channel_id=1, source_target_pairs={{0,4},{1,5},{2,6},{3,7},{4,0},{5,1},{6,2},{7,3},{8,12},{9,13},{10,... | collective-permute-start | bytes 294920 | tf_op jit(solution)/shard_map/ppermute | solution.py:344
  76.9 7.5 %collective-permute-start.10 = (bf16[192,256]{1,0:T(8,128)(2,1)S(1)}, bf16[192,256]{1,0:T(8,128)(2,1)S(1)}, u32[]{:S(2)}, u32[]{:S(2)}) collective-permute-start(bf16[192,256]{1,0:T(8,128)(2,1)S(1)} %fusion.1), channel_id=1, source_target_pairs={{0,4},{1,5},{2,6},{3,7},{4,0},{5,1},{6,2},{7,3},{8,12},{9,13},{10,... | collective-permute-start | bytes 294920 | tf_op jit(solution)/shard_map/ppermute | solution.py:344
  80.4 6.6 %collective-permute-start.13 = (bf16[192,256]{1,0:T(8,128)(2,1)S(1)}, bf16[192,256]{1,0:T(8,128)(2,1)S(1)}, u32[]{:S(2)}, u32[]{:S(2)}) collective-permute-start(bf16[192,256]{1,0:T(8,128)(2,1)S(1)} %fusion.4), channel_id=1, source_target_pairs={{0,8},{1,9},{2,10},{3,11},{4,12},{5,13},{6,14},{7,15},{8,0},{9,1},... | collective-permute-start | bytes 294920 | tf_op jit(solution)/shard_map/ppermute | solution.py:344
  83.5 5.3 %collective-permute-start.14 = (bf16[192,256]{1,0:T(8,128)(2,1)S(1)}, bf16[192,256]{1,0:T(8,128)(2,1)S(1)}, u32[]{:S(2)}, u32[]{:S(2)}) collective-permute-start(bf16[192,256]{1,0:T(8,128)(2,1)S(1)} %bitcast.88), channel_id=1, source_target_pairs={{0,4},{1,5},{2,6},{3,7},{4,0},{5,1},{6,2},{7,3},{8,12},{9,13},{10,... | collective-permute-start | bytes 294920 | tf_op jit(solution)/shard_map/ppermute | solution.py:344
  89.0 2.1 %collective-permute-start.16 = (bf16[2,384,384]{2,1,0:T(8,128)(2,1)S(1)}, bf16[2,384,384]{2,1,0:T(8,128)(2,1)S(1)}, u32[]{:S(2)}, u32[]{:S(2)}) collective-permute-start(bf16[2,384,384]{2,1,0:T(8,128)(2,1)S(1)} %pad_maximum_fusion), channel_id=1, source_target_pairs={{0,1},{1,0},{2,3},{3,2},{4,5},{5,4},{6,7},{7,6},{8,9},{9,8},{10,11... | collective-permute-start | bytes 1769480 | tf_op jit(solution)/shard_map/ppermute | solution.py:344
  89.2 5.3 %collective-permute-start.15 = (bf16[2,192,128]{2,1,0:T(8,128)(2,1)S(1)}, bf16[2,192,128]{2,1,0:T(8,128)(2,1)S(1)}, u32[]{:S(2)}, u32[]{:S(2)}) collective-permute-start(bf16[2,192,128]{2,1,0:T(8,128)(2,1)S(1)} %get-tuple-element.115), channel_id=1, source_target_pairs={{0,2},{1,3},{2,0},{3,1},{4,6},{5,7},{6,4},{7,5},{8,10},{9,11},{10,... | collective-permute-start | bytes 294920 | tf_op jit(solution)/shard_map/ppermute | solution.py:344
  89.3 6.7 %copy-start.8 = (bf16[64,768]{1,0:T(8,128)(2,1)S(1)}, bf16[64,768]{1,0:T(8,128)(2,1)}, u32[]{:S(2)}) copy-start(bf16[64,768]{1,0:T(8,128)(2,1)} %latents_ref.1) | copy-start | bytes 294916
  89.4 6.7 %copy-start.9 = (bf16[64,768]{1,0:T(8,128)(2,1)S(1)}, bf16[64,768]{1,0:T(8,128)(2,1)}, u32[]{:S(2)}) copy-start(bf16[64,768]{1,0:T(8,128)(2,1)} %d_out_ref.1) | copy-start | bytes 294916
  94.6 1.5 %collective-permute-start.17 = (bf16[2,2,192,64]{3,2,1,0:T(8,128)(2,1)S(1)}, bf16[2,2,192,64]{3,2,1,0:T(8,128)(2,1)S(1)}, u32[]{:S(2)}, u32[]{:S(2)}) collective-permute-start(bf16[2,2,192,64]{3,2,1,0:T(8,128)(2,1)S(1)} %pad_maximum_fusion.3), channel_id=1, source_target_pairs={{0,1},{1,0},{2,3},{3,2},{4,5},{5,4},{6,7},{7,6},{8,9},{9,8},{10,11... | collective-permute-start | bytes 294920 | tf_op jit(solution)/shard_map/ppermute | solution.py:344
  (4 other events, 12.0 us)

commit v9 on v8

--- a/solution.py
+++ b/solution.py
@@ -38,22 +38,21 @@
     return jnp.where(low if part % 2 == 0 else ~low, array, jnp.zeros_like(array))
 
 
-def team_place(place_ref, quarter):
-    relative = (place_ref[0] % TEAM) ^ quarter
-    return relative % 2, relative // 2
-
-
-def store_quarters(place_ref, keep_ref, send_ref, one, two, at):
+def store_quarters(place_ref, near_refs, far_ref, one, two, at):
     mine = one.shape[1] // TEAM
     for quarter in range(TEAM):
         cols = slice(quarter * mine, (quarter + 1) * mine)
         piece = jnp.concatenate([one[:, cols], two[:, cols]], axis=1)
-        core, across = team_place(place_ref, quarter)
-        for ref, which in ((keep_ref, 0), (send_ref, 1)):
-
-            @pl.when(core == which)
+        relative = (place_ref[0] % TEAM) ^ quarter
+        for which, ref in enumerate(near_refs):
+
+            @pl.when(relative == which)
             def _():
-                ref[across, at, :] = piece
+                ref[at, :] = piece
+
+        @pl.when(relative >= 2)
+        def _():
+            far_ref[relative % 2, at, :] = piece
 
 
 def load(source, target, sems, pieces):
@@ -66,10 +65,15 @@
     return copies
 
 
-def project_kernel(
-    place_ref, count_ref, latents_hbm, d_out_hbm, points_hbm, w_query_hbm, w_out_hbm, w_key_hbm, w_value_hbm,
-    keep_qg_ref, send_qg_ref, keep_ref, send_ref,
-    latents_ref, d_out_ref, points_ref, w_query_ref, w_out_ref, w_key_ref, w_value_ref, sems
+def wait(*groups):
+    for group in groups:
+        for copy in group:
+            copy.wait()
+
+
+def rows_kernel(
+    place_ref, count_ref, latents_hbm, d_out_hbm, w_query_hbm, w_out_hbm,
+    keep_ref, core_ref, far_ref, latents_ref, d_out_ref, w_query_ref, w_out_ref, sems
 ):
     pieces = sems.shape[1]
     own = latents_ref.shape[0]
@@ -78,32 +82,34 @@
         load(w_query_hbm, w_query_ref, sems.at[1], pieces),
         load(d_out_hbm, d_out_ref, sems.at[2], 1),
         load(w_out_hbm, w_out_ref, sems.at[3], pieces),
-        load(points_hbm, points_ref, sems.at[4], pieces),
-        load(w_key_hbm, w_key_ref, sems.at[5], pieces),
-        load(w_value_hbm, w_value_ref, sems.at[6], pieces),
     ]
-
-    def arrived(*which):
-        for i in which:
-            for copy in loads[i]:
-                copy.wait()
-
-    extra = keep_qg_ref.shape[1] - own, keep_qg_ref.shape[2]
+    extra = keep_ref.shape[0] - own, keep_ref.shape[1]
     first = lax.broadcasted_iota(jnp.int32, extra, 1) < extra[1] // 2
     count = jnp.where(first, count_ref[0] // 16, count_ref[0] % 16).astype(F32).astype(BF16)
-    for ref in (keep_qg_ref, send_qg_ref):
-        for across in range(2):
-            ref[across, own:, :] = count
-    arrived(0, 1)
+    for ref in (keep_ref, core_ref, far_ref.at[0], far_ref.at[1]):
+        ref[own:, :] = count
+    wait(*loads[:2])
     query = dot(latents_ref[...], w_query_ref[...]).astype(BF16)
-    arrived(2, 3)
+    wait(*loads[2:])
     grad = dot_nt(d_out_ref[...], w_out_ref[...]).astype(BF16)
-    store_quarters(place_ref, keep_qg_ref, send_qg_ref, query, grad, slice(0, own))
-    arrived(4, 5)
+    store_quarters(place_ref, (keep_ref, core_ref), far_ref, query, grad, slice(0, own))
+
+
+def slots_kernel(
+    place_ref, points_hbm, w_key_hbm, w_value_hbm,
+    keep_ref, core_ref, far_ref, points_ref, w_key_ref, w_value_ref, sems
+):
+    pieces = sems.shape[1]
+    loads = [
+        load(points_hbm, points_ref, sems.at[0], pieces),
+        load(w_key_hbm, w_key_ref, sems.at[1], pieces),
+        load(w_value_hbm, w_value_ref, sems.at[2], pieces),
+    ]
+    wait(*loads[:2])
     keys = dot(points_ref[...], w_key_ref[...]).astype(BF16) * jnp.asarray(0.125, BF16)
-    arrived(6)
+    wait(*loads[2:])
     values = dot(points_ref[...], w_value_ref[...]).astype(BF16)
-    store_quarters(place_ref, keep_ref, send_ref, keys, values, slice(0, keys.shape[0]))
+    store_quarters(place_ref, (keep_ref, core_ref), far_ref, keys, values, slice(0, keys.shape[0]))
 
 
 def weights_kernel(w_key_ref, w_value_ref, out_ref):
@@ -114,15 +120,9 @@
             out_ref[quarter, i * mine : (i + 1) * mine, :] = turned[quarter * mine : (quarter + 1) * mine]
 
 
-def pair_kernel(keep_ref, core_ref, out_ref):
-    out_ref[0] = keep_ref[1]
-    out_ref[1] = core_ref[1]
-
-
-def chunk_kernel(keep_ref, core_ref, far_ref, out_ref, count_ref):
+def chunk_kernel(keep_ref, core_ref, far_ref, diagonal_ref, out_ref, count_ref):
     own, mine = out_ref.shape[0] // TEAM, out_ref.shape[1] // 2
-    blocks = keep_ref.at[0], core_ref.at[0], far_ref.at[0], far_ref.at[1]
-    for i, ref in enumerate(blocks):
+    for i, ref in enumerate((keep_ref, core_ref, far_ref.at[0], diagonal_ref.at[1])):
         out_ref[i * own : (i + 1) * own, :] = ref[:own, :]
         row = ref[own:, :].astype(F32)[:1, :]
         count_ref[i : i + 1, :] = 16 * row[:, :LANES] + row[:, mine : mine + LANES]
@@ -130,7 +130,7 @@
 
 def turn_kernel(picks, *refs):
     for i, (ref, which) in enumerate(picks):
-        refs[-1][i] = refs[ref][which].T
+        refs[-1][i] = (refs[ref][...] if which is None else refs[ref][which]).T
 
 
 def dead_slots(slot, count_ref, block):
@@ -142,11 +142,11 @@
     kv_refs, kv_t_refs = {}, {}
     if 0 in blocks:
         keep_ref, core_ref, near_t_ref, *refs = refs
-        kv_refs.update({0: keep_ref.at[0], 1: core_ref.at[0]})
+        kv_refs.update({0: keep_ref, 1: core_ref})
         kv_t_refs.update({0: near_t_ref.at[0], 1: near_t_ref.at[1]})
     if 2 in blocks:
-        far_ref, far_t_ref, *refs = refs
-        kv_refs.update({2: far_ref.at[0], 3: far_ref.at[1]})
+        far_ref, diagonal_ref, far_t_ref, *refs = refs
+        kv_refs.update({2: far_ref.at[0], 3: diagonal_ref.at[1]})
         kv_t_refs.update({2: far_t_ref.at[0], 3: far_t_ref.at[1]})
     before = refs[:2] if blocks[0] else ()
     numer_ref, stat_ref, score_ref, weight_ref = refs[len(before) :]
@@ -208,7 +208,7 @@
 def backward_kernel(chunks, start, side, first, last, count_ref, *refs):
     qg_refs, stat_refs, refs = refs[:chunks], refs[chunks : 2 * chunks], refs[2 * chunks :]
     even_ref, odd_ref, kv_t_ref, *refs = refs
-    kv_refs = even_ref.at[0], odd_ref.at[side]
+    kv_refs = (even_ref.at[0], odd_ref.at[1]) if side else (even_ref, odd_ref)
     if not first:
         sum_in_ref, *refs = refs
     gq_in_ref = None
@@ -216,7 +216,7 @@
         gq_in_ref, *refs = refs
     gq_ref, sum_ref, total_ref, score_ref, gw_ref, prob_ref, ds_ref = refs
     rows = qg_refs[0].shape[0]
-    slots, dim = even_ref.shape[1], even_ref.shape[2] // (2 * MINE)
+    slots, dim = even_ref.shape[-2], even_ref.shape[-1] // (2 * MINE)
     depth = score_ref.shape[0]
     slot = lax.broadcasted_iota(jnp.int32, (slots, rows), 0).astype(F32)
     low = low_lanes((slots, LANES))
@@ -343,26 +343,30 @@
     def swap(array, mask):
         return lax.ppermute(array, "pts", [(i, i ^ mask) for i in range(size)])
 
-    each = own + 16
-    inputs = [latents, d_out, points, w_query, w_out, w_key, w_value]
-    keep_qg, send_qg, keep, send = call(
-        project_kernel,
-        [place, counts] + inputs,
-        [shape((2, each, 2 * mine), BF16)] * 2 + [shape((2, slots, 2 * mine), BF16)] * 2,
-        [pltpu.VMEM(a.shape, BF16) for a in inputs] + [pltpu.SemaphoreType.DMA((len(inputs), 4))],
-        flops=4 * (own + slots) * width * width,
-        space=pltpu.HBM,
-        grant=60,
+    def project(kernel, scalars, inputs, rows):
+        return call(
+            kernel,
+            scalars + inputs,
+            [shape((rows, 2 * mine), BF16)] * 2 + [shape((2, rows, 2 * mine), BF16)],
+            [pltpu.VMEM(a.shape, BF16) for a in inputs] + [pltpu.SemaphoreType.DMA((len(inputs), 4))],
+            flops=4 * rows * width * width,
+            space=pltpu.HBM,
+            grant=60,
+        )
+
+    keep_qg, core_qg, far_qg = project(
+        rows_kernel, [place, counts], [latents, d_out, w_query, w_out], own + 16
     )
-    core_qg = swap(send_qg, 1)
-    core = swap(send, 1)
-    (far_qg,) = call(pair_kernel, [keep_qg, core_qg], [shape(keep_qg.shape, BF16)])
-    far_qg, core = lax.optimization_barrier((far_qg, core))
+    keep_qg, points = lax.optimization_barrier((keep_qg, points))
     far_qg = swap(far_qg, 2)
-    far = swap(call(pair_kernel, [keep, core], [shape(keep.shape, BF16)])[0], 2)
+    core_qg = swap(core_qg, 1)
+    keep, core, far = project(slots_kernel, [place], [points, w_key, w_value], slots)
+    far_qg, far = lax.optimization_barrier((far_qg, far))
+    far = swap(far, 2)
+    core = swap(core, 1)
     qg, count = call(
         chunk_kernel,
-        [keep_qg, core_qg, far_qg],
+        [keep_qg, core_qg, far_qg, swap(far_qg, 1)],
         [shape((TEAM * own, 2 * mine), BF16), shape((TEAM, LANES), F32)],
     )
     for mask in middle:
@@ -372,7 +376,7 @@
     qg = [qg, swap(qg, near_bit), far_qg]
     (weights,) = call(weights_kernel, [w_key, w_value], [shape((TEAM, 2 * mine, width), BF16)])
     turned = [shape((2, 2 * mine, slots), BF16)]
-    (near_t,) = call(functools.partial(turn_kernel, ((0, 0), (1, 0))), [keep, core], turned)
+    (near_t,) = call(functools.partial(turn_kernel, ((0, None), (1, None))), [keep, core], turned)
     near_t, weights = lax.optimization_barrier((near_t, weights))
     rows = qg[0].shape[0]
     team_slots = TEAM * slots
@@ -383,7 +387,7 @@
             functools.partial(forward_kernel, blocks),
             [count, qg[p]]
             + ([keep, core, near_t] if 0 in blocks else [])
-            + ([far, far_t] if 2 in blocks else [])
+            + ([far, diagonal, far_t] if 2 in blocks else [])
             + list(before),
             [shape((mine, rows), F32), shape((4 * MINE, rows), F32)],
             [pltpu.VMEM((3, slots, rows), F32), pltpu.VMEM((3, slots, rows), BF16)],
@@ -392,11 +396,11 @@
         )
 
     early = [forward(p, (0, 1)) for p in range(2)]
-    (early, far) = lax.optimization_barrier((early, far))
-    (far_t,) = call(functools.partial(turn_kernel, ((0, 0), (0, 1))), [far], turned)
+    early, far, qg[2] = lax.optimization_barrier((early, far, qg[2]))
+    qg.append(swap(qg[2], near_bit))
+    diagonal = swap(far, 1)
+    (far_t,) = call(functools.partial(turn_kernel, ((0, 0), (1, 1))), [far, diagonal], turned)
     done = [forward(p, (2, 3), early[p]) for p in range(2)]
-    qg[2], done[0] = lax.optimization_barrier((qg[2], done[0]))
-    qg.append(swap(qg[2], near_bit))
     done += [forward(p, (0, 1, 2, 3)) for p in (2, 3)]
     numer = [d[0] for d in done]
     tops = [d[1][:MINE] for d in done]
@@ -442,7 +446,7 @@
             [count]
             + [qg[p] for p in chunks]
             + [final[p] for p in chunks]
-            + ([far, far, far_t] if side else [keep, core, near_t])
+            + ([far, diagonal, far_t] if side else [keep, core, near_t])
             + list(sums)
             + list(partial),
             [shape((len(chunks), mine, rows), kind), shape(kept, BF16 if last else F32)],

time: 97.7 us -> 81 us (0.83)
  waiting for transfers between devices: 43.3 us -> 21.8 us
  starting transfers between devices: 16.2 us -> 20.5 us
  Pallas kernels: 33.5 us -> 36.1 us
  local copies, waits for them, and re-layouts: 2.34 us -> 0.34 us
    ppermute x18 -> x20, waiting for transfers between devices: 43.3 us -> 21.8 us  [swap(): return lax.ppermute(array, 'pts', [(i, i ^ mask) for i in range(size)])]
    ppermute x18 -> x20, starting transfers between devices: 16.2 us -> 20.5 us  [swap(): return lax.ppermute(array, 'pts', [(i, i ^ mask) for i in range(size)])]
    pallas_call x20 -> x19, Pallas kernels: 33.5 us -> 36.1 us  [call(): pl.pallas_call(kernel, in_specs=[smem if a.dtype == jnp.int32 else other...]
    unnamed x20 -> x18, local copies, waits for them, and re-layouts: 2.03 us -> 0.04 us
  transfers between devices with their start and end apart: 18 -> 20, of which waited for: 12 -> 13; matrix products, arithmetic and copies ran while one was open for 0% -> 0% of each run, Pallas kernels for 24% -> 36%
where the time goes in v9:
time: 81 us; the launch traced here: 80.8 us
  Pallas kernels  36.1 us (45%)
  waiting for transfers between devices  21.8 us (27%)
  starting transfers between devices  20.5 us (25%)
  between operations  1.64 us (2%)
    pallas_call x19, Pallas kernels, call(): pl.pallas_call(kernel, in_specs=[smem if a.dtype == jnp.int32 else other...  36.1 us
    ppermute x20, waiting for transfers between devices, swap(): return lax.ppermute(array, 'pts', [(i, i ^ mask) for i in range(size)])  21.8 us
    ppermute x20, starting transfers between devices, swap(): return lax.ppermute(array, 'pts', [(i, i ^ mask) for i in range(size)])  20.5 us
  transfers between devices with their start and end apart: 20, of which 13 were waited for; matrix products, arithmetic and copies ran while one was open for 0% of the time, Pallas kernels for 36%

profile of v9, /device:TPU:0, one launch (start us, length us, event | category | flops | bytes accessed | tf_op | source)
XLA Modules:
  0.0 80.8 jit_solution(9670886505181988716)
XLA Ops:
  1.3 3.3 %shard_map.103 = (bf16[80,384]{1,0:T(8,128)(2,1)}, bf16[80,384]{1,0:T(8,128)(2,1)}, bf16[2,80,384]{2,1,0:T(8,128)(2,1)}) custom-call(s32[1]{0:T(128)} %bitcast.place_ref, s32[1]{0:T(128)S(6)} %copy.11.count_ref, bf16[64,768]{1,0:T(8,128)(2,1)} %latents_ref.1, bf16[64,768]{1,0:T(8,128)(2,1)} %d_out_ref.1, bf16[768,768]{1,0:T(8,128)(2,1)} %w_query_ref.1, ...), custom_call_target="tpu_custom_call" | custom-call | flops 23592960 | bytes 350209 | tf_op jit(solution)/shard_map/pallas_call | solution.py:319
  4.6 3.0 %collective-permute-start.1 = (bf16[2,80,384]{2,1,0:T(8,128)(2,1)}, bf16[2,80,384]{2,1,0:T(8,128)(2,1)S(1)}, u32[]{:S(2)}, u32[]{:S(2)}) collective-permute-start(bf16[2,80,384]{2,1,0:T(8,128)(2,1)} %get-tuple-element.64), channel_id=1, source_target_pairs={{0,2},{1,3},{2,0},{3,1},{4,6},{5,7},{6,4},{7,5},{8,10},{9,11},{10,... | collective-permute-start | bytes 368648 | tf_op jit(solution)/shard_map/ppermute | solution.py:344
  7.6 5.0 %shard_map.104 = (bf16[384,384]{1,0:T(8,128)(2,1)}, bf16[384,384]{1,0:T(8,128)(2,1)}, bf16[2,384,384]{2,1,0:T(8,128)(2,1)}) custom-call(s32[1]{0:T(128)} %bitcast.place_ref, bf16[384,768]{1,0:T(8,128)(2,1)} %points_hbm, bf16[768,768]{1,0:T(8,128)(2,1)} %w_key_ref, bf16[768,768]{1,0:T(8,128)(2,1)} %w_value_ref), custom_call_target="tpu_custom_call" | custom-call | flops 113246208 | bytes 516096 | tf_op jit(solution)/shard_map/pallas_call | solution.py:319
  14.8 2.0 %collective-permute-start.4 = (bf16[256,384]{1,0:T(8,128)(2,1)S(1)}, bf16[256,384]{1,0:T(8,128)(2,1)S(1)}, u32[]{:S(2)}, u32[]{:S(2)}) collective-permute-start(bf16[256,384]{1,0:T(8,128)(2,1)S(1)} %get-tuple-element.70.qg_ref.refs_3_.refs_0_), channel_id=1, source_target_pairs={{0,4},{1,5},{2,6},{3,7},{4,0},{5,1},{6,2},{7,3},{8,12},{9,13},{10,... | collective-permute-start | bytes 589832 | tf_op jit(solution)/shard_map/ppermute | solution.py:344
  16.8 2.6 %collective-permute-start.6 = (bf16[256,384]{1,0:T(8,128)(2,1)S(1)}, bf16[256,384]{1,0:T(8,128)(2,1)S(1)}, u32[]{:S(2)}, u32[]{:S(2)}) collective-permute-start(bf16[256,384]{1,0:T(8,128)(2,1)S(1)} %get-tuple-element.70.qg_ref.refs_3_.refs_0_), channel_id=1, source_target_pairs={{0,8},{1,9},{2,10},{3,11},{4,12},{5,13},{6,14},{7,15},{8,0},{9,1},... | collective-permute-start | bytes 589832 | tf_op jit(solution)/shard_map/ppermute | solution.py:344
  21.6 4.6 %collective-permute-done.4.qg_ref.refs_2_.refs_0_ = bf16[256,384]{1,0:T(8,128)(2,1)S(1)} collective-permute-done((bf16[256,384]{1,0:T(8,128)(2,1)S(1)}, bf16[256,384]{1,0:T(8,128)(2,1)S(1)}, u32[]{:S(2)}, u32[]{:S(2)}) %collective-permute-start.4) | collective-permute-done | bytes 196640 | tf_op jit(solution)/shard_map/ppermute | solution.py:344
  29.3 1.4 %collective-permute-done.7.refs_1_.refs_4_.refs_9_ = bf16[2,384,384]{2,1,0:T(8,128)(2,1)S(1)} collective-permute-done((bf16[2,384,384]{2,1,0:T(8,128)(2,1)S(1)}, bf16[2,384,384]{2,1,0:T(8,128)(2,1)S(1)}, u32[]{:S(2)}, u32[]{:S(2)}) %collective-permute-start.7) | collective-permute-done | bytes 589856 | tf_op jit(solution)/shard_map/ppermute | solution.py:344
  30.9 2.4 %shard_map.113 = (f32[192,256]{1,0:T(8,128)S(1)}, f32[12,256]{1,0:T(8,128)S(1)}) custom-call(f32[4,128]{1,0:T(4,128)S(1)} %get-tuple-element.68.count_ref, bf16[256,384]{1,0:T(8,128)(2,1)S(1)} %collective-permute-done.6.qg_ref.refs_1_.refs_0_, bf16[384,384]{1,0:T(8,128)(2,1)S(1)} %copy-done, bf16[384,384]{1,0:T(8,128)(2,1)S(1)} %collective-permute-done.3.refs_1_.refs_3_, ...), custom_call_target="tpu_custom_call" | custom-call | flops 150994944 | bytes 419584 | tf_op jit(solution)/shard_map/pallas_call | solution.py:319
  36.0 2.3 %shard_map.114 = (f32[192,256]{1,0:T(8,128)S(1)}, f32[12,256]{1,0:T(8,128)S(1)}) custom-call(f32[4,128]{1,0:T(4,128)S(1)} %get-tuple-element.68.count_ref, bf16[256,384]{1,0:T(8,128)(2,1)S(1)} %collective-permute-done.8.qg_ref.refs_0_, bf16[384,384]{1,0:T(8,128)(2,1)S(1)} %copy-done, bf16[384,384]{1,0:T(8,128)(2,1)S(1)} %collective-permute-done.3.refs_1_.refs_3_, ...), custom_call_target="tpu_custom_call" | custom-call | flops 150994944 | bytes 419584 | tf_op jit(solution)/shard_map/pallas_call | solution.py:319
  39.0 3.3 %collective-permute-done.9 = f32[4,6,256]{2,1,0:T(8,128)S(1)} collective-permute-done((f32[4,6,256]{2,1,0:T(8,128)S(1)}, f32[4,6,256]{2,1,0:T(8,128)S(1)}, u32[]{:S(2)}, u32[]{:S(2)}) %collective-permute-start.9) | collective-permute-done | bytes 24608 | tf_op jit(solution)/shard_map/ppermute | solution.py:344
  42.4 1.7 %collective-permute-start.10 = (f32[4,6,256]{2,1,0:T(8,128)S(1)}, f32[4,6,256]{2,1,0:T(8,128)S(1)}, u32[]{:S(2)}, u32[]{:S(2)}) collective-permute-start(f32[4,6,256]{2,1,0:T(8,128)S(1)} %pad_maximum_fusion.6), channel_id=1, source_target_pairs={{0,8},{1,9},{2,10},{3,11},{4,12},{5,13},{6,14},{7,15},{8,0},{9,1},... | collective-permute-start | bytes 73736 | tf_op jit(solution)/shard_map/ppermute | solution.py:344
  44.1 3.5 %collective-permute-done.10 = f32[4,6,256]{2,1,0:T(8,128)S(1)} collective-permute-done((f32[4,6,256]{2,1,0:T(8,128)S(1)}, f32[4,6,256]{2,1,0:T(8,128)S(1)}, u32[]{:S(2)}, u32[]{:S(2)}) %collective-permute-start.10) | collective-permute-done | bytes 24608 | tf_op jit(solution)/shard_map/ppermute | solution.py:344
  49.2 6.5 %shard_map.115 = (f32[4,192,256]{2,1,0:T(8,128)S(1)}, bf16[2,384,384]{2,1,0:T(8,128)(2,1)S(1)}) custom-call(f32[4,128]{1,0:T(4,128)S(1)} %get-tuple-element.68.count_ref, bf16[256,384]{1,0:T(8,128)(2,1)S(1)} %collective-permute-done.8.qg_ref.refs_0_, bf16[256,384]{1,0:T(8,128)(2,1)S(1)} %collective-permute-done.6.qg_ref.refs_1_.refs_0_, ...), custom_call_target="tpu_custom_call" | custom-call | flops 528482304 | bytes 494848 | tf_op jit(solution)/shard_map/pallas_call | solution.py:319
  57.3 1.7 %shard_map.116 = (bf16[1,192,256]{2,1,0:T(8,128)(2,1)S(1)}, f32[2,384,384]{2,1,0:T(8,128)S(1)}) custom-call(f32[4,128]{1,0:T(4,128)S(1)} %get-tuple-element.68.count_ref, bf16[256,384]{1,0:T(8,128)(2,1)S(1)} %collective-permute-done.8.qg_ref.refs_0_, f32[6,256]{1,0:T(8,128)S(1)} %get-tuple-element.126.refs_4_.refs_1_, bf16[384,384]{1,0:T(8,128)(2,1)S(1)} %copy-done, ...), custom_call_target="tpu_custom_call" | custom-call | flops 132120576 | bytes 431104 | tf_op jit(solution)/shard_map/pallas_call | solution.py:319
  59.0 1.4 %collective-permute-start.14 = (bf16[192,256]{1,0:T(8,128)(2,1)S(1)}, bf16[192,256]{1,0:T(8,128)(2,1)S(1)}, u32[]{:S(2)}, u32[]{:S(2)}) collective-permute-start(bf16[192,256]{1,0:T(8,128)(2,1)S(1)} %bitcast.89), channel_id=1, source_target_pairs={{0,4},{1,5},{2,6},{3,7},{4,0},{5,1},{6,2},{7,3},{8,12},{9,13},{10,... | collective-permute-start | bytes 294920 | tf_op jit(solution)/shard_map/ppermute | solution.py:344
  61.2 1.7 %shard_map.117 = (f32[1,192,256]{2,1,0:T(8,128)S(1)}, f32[2,384,384]{2,1,0:T(8,128)S(1)}) custom-call(f32[4,128]{1,0:T(4,128)S(1)} %get-tuple-element.68.count_ref, bf16[256,384]{1,0:T(8,128)(2,1)S(1)} %collective-permute-done.6.qg_ref.refs_1_.refs_0_, f32[6,256]{1,0:T(8,128)S(1)} %get-tuple-element.127.refs_5_.refs_1_, bf16[384,384]{1,0:T(8,128)(2,1)S(1)} %copy-done, ...), custom_call_target="tpu_custom_call" | custom-call | flops 132120576 | bytes 590848 | tf_op jit(solution)/shard_map/pallas_call | solution.py:319
  63.7 1.6 %collective-permute-start.15 = (bf16[192,256]{1,0:T(8,128)(2,1)S(1)}, bf16[192,256]{1,0:T(8,128)(2,1)S(1)}, u32[]{:S(2)}, u32[]{:S(2)}) collective-permute-start(bf16[192,256]{1,0:T(8,128)(2,1)S(1)} %fusion.4), channel_id=1, source_target_pairs={{0,8},{1,9},{2,10},{3,11},{4,12},{5,13},{6,14},{7,15},{8,0},{9,1},... | collective-permute-start | bytes 294920 | tf_op jit(solution)/shard_map/ppermute | solution.py:344
  65.3 1.7 %shard_map.118 = (bf16[1,192,256]{2,1,0:T(8,128)(2,1)S(1)}, f32[2,384,384]{2,1,0:T(8,128)S(1)}) custom-call(f32[4,128]{1,0:T(4,128)S(1)} %get-tuple-element.68.count_ref, bf16[256,384]{1,0:T(8,128)(2,1)S(1)} %collective-permute-done.4.qg_ref.refs_2_.refs_0_, f32[6,256]{1,0:T(8,128)S(1)} %get-tuple-element.128.refs_6_.refs_1_, bf16[384,384]{1,0:T(8,128)(2,1)S(1)} %copy-done, ...), custom_call_target="tpu_custom_call" | custom-call | flops 132120576 | bytes 578560 | tf_op jit(solution)/shard_map/pallas_call | solution.py:319
  67.0 1.4 %collective-permute-start.16 = (bf16[192,256]{1,0:T(8,128)(2,1)S(1)}, bf16[192,256]{1,0:T(8,128)(2,1)S(1)}, u32[]{:S(2)}, u32[]{:S(2)}) collective-permute-start(bf16[192,256]{1,0:T(8,128)(2,1)S(1)} %bitcast.88), channel_id=1, source_target_pairs={{0,4},{1,5},{2,6},{3,7},{4,0},{5,1},{6,2},{7,3},{8,12},{9,13},{10,... | collective-permute-start | bytes 294920 | tf_op jit(solution)/shard_map/ppermute | solution.py:344
  68.5 1.8 %collective-permute-done.15 = bf16[192,256]{1,0:T(8,128)(2,1)S(1)} collective-permute-done((bf16[192,256]{1,0:T(8,128)(2,1)S(1)}, bf16[192,256]{1,0:T(8,128)(2,1)S(1)}, u32[]{:S(2)}, u32[]{:S(2)}) %collective-permute-start.15) | collective-permute-done | bytes 98336 | tf_op jit(solution)/shard_map/ppermute | solution.py:344
  70.4 1.7 %shard_map.119 = (f32[1,192,256]{2,1,0:T(8,128)S(1)}, bf16[2,384,384]{2,1,0:T(8,128)(2,1)S(1)}) custom-call(f32[4,128]{1,0:T(4,128)S(1)} %get-tuple-element.68.count_ref, bf16[256,384]{1,0:T(8,128)(2,1)S(1)} %get-tuple-element.70.qg_ref.refs_3_.refs_0_, f32[6,256]{1,0:T(8,128)S(1)} %get-tuple-element.125.refs_7_.refs_1_, bf16[384,384]{1,0:T(8,128)(2,1)S(1)} %copy-done, ...), custom_call_target="tpu_custom_call" | custom-call | flops 132120576 | bytes 517120 | tf_op jit(solution)/shard_map/pallas_call | solution.py:319
  74.4 2.2 %shard_map.120 = bf16[384,768]{1,0:T(8,128)(2,1)} custom-call(s32[1]{0:T(128)} %bitcast.place_ref, bf16[2,384,384]{2,1,0:T(8,128)(2,1)S(1)} %get-tuple-element.112.near_ref, bf16[2,384,384]{2,1,0:T(8,128)(2,1)S(1)} %collective-permute-done.13.far_ref, bf16[2,384,384]{2,1,0:T(8,128)(2,1)S(1)} %collective-permute-done.18.core_ref, ...), custom_call_target="tpu_custom_call" | custom-call | flops 113246208 | bytes 589824 | tf_op jit(solution)/shard_map/pallas_call | solution.py:319
  77.9 1.4 %collective-permute-done.19.core_ref = bf16[2,2,192,64]{3,2,1,0:T(8,128)(2,1)S(1)} collective-permute-done((bf16[2,2,192,64]{3,2,1,0:T(8,128)(2,1)S(1)}, bf16[2,2,192,64]{3,2,1,0:T(8,128)(2,1)S(1)}, u32[]{:S(2)}, u32[]{:S(2)}) %collective-permute-start.19) | collective-permute-done | bytes 98336 | tf_op jit(solution)/shard_map/ppermute | solution.py:344
  79.4 1.4 %shard_map.121 = (bf16[64,768]{1,0:T(8,128)(2,1)}, bf16[64,768]{1,0:T(8,128)(2,1)}) custom-call(s32[1]{0:T(128)} %bitcast.place_ref, bf16[2,192,128]{2,1,0:T(8,128)(2,1)S(1)} %get-tuple-element.120.near_ref, bf16[2,192,128]{2,1,0:T(8,128)(2,1)S(1)} %collective-permute-done.17.far_ref, bf16[2,2,192,64]{3,2,1,0:T(8,128)(2,1)S(1)} %collective-permute-done.19.core_ref, ...), custom_call_target="tpu_custom_call" | custom-call | flops 18874368 | bytes 380928 | tf_op jit(solution)/shard_map/pallas_call | solution.py:319
  (79 shorter events, 19.5 us)
Async XLA Ops:
  4.6 8.0 %collective-permute-start.1 = (bf16[2,80,384]{2,1,0:T(8,128)(2,1)}, bf16[2,80,384]{2,1,0:T(8,128)(2,1)S(1)}, u32[]{:S(2)}, u32[]{:S(2)}) collective-permute-start(bf16[2,80,384]{2,1,0:T(8,128)(2,1)} %get-tuple-element.64), channel_id=1, source_target_pairs={{0,2},{1,3},{2,0},{3,1},{4,6},{5,7},{6,4},{7,5},{8,10},{9,11},{10,... | collective-permute-start | bytes 368648 | tf_op jit(solution)/shard_map/ppermute | solution.py:344
  7.6 5.8 %copy-start.8 = (bf16[80,384]{1,0:T(8,128)(2,1)S(1)}, bf16[80,384]{1,0:T(8,128)(2,1)}, u32[]{:S(2)}) copy-start(bf16[80,384]{1,0:T(8,128)(2,1)} %get-tuple-element.63) | copy-start | bytes 184324
  7.6 7.1 %copy-start.7 = (bf16[80,384]{1,0:T(8,128)(2,1)S(1)}, bf16[80,384]{1,0:T(8,128)(2,1)}, u32[]{:S(2)}) copy-start(bf16[80,384]{1,0:T(8,128)(2,1)} %get-tuple-element.62.keep_ref) | copy-start | bytes 184324
  7.6 11.8 %copy-start.3 = (bf16[768,768]{1,0:T(8,128)(2,1)S(1)}, bf16[768,768]{1,0:T(8,128)(2,1)}, u32[]{:S(2)}) copy-start(bf16[768,768]{1,0:T(8,128)(2,1)} %w_key_ref) | copy-start | bytes 3538948
  7.6 11.8 %copy-start.4 = (bf16[768,768]{1,0:T(8,128)(2,1)S(1)}, bf16[768,768]{1,0:T(8,128)(2,1)}, u32[]{:S(2)}) copy-start(bf16[768,768]{1,0:T(8,128)(2,1)} %w_value_ref) | copy-start | bytes 3538948
  12.6 16.0 %collective-permute-start.5 = (bf16[2,384,384]{2,1,0:T(8,128)(2,1)}, bf16[2,384,384]{2,1,0:T(8,128)(2,1)S(1)}, u32[]{:S(2)}, u32[]{:S(2)}) collective-permute-start(bf16[2,384,384]{2,1,0:T(8,128)(2,1)} %get-tuple-element.80), channel_id=1, source_target_pairs={{0,2},{1,3},{2,0},{3,1},{4,6},{5,7},{6,4},{7,5},{8,10},{9,11},{10,... | collective-permute-start | bytes 1769480 | tf_op jit(solution)/shard_map/ppermute | solution.py:344
  12.9 1.8 %collective-permute-start.2 = (bf16[2,80,384]{2,1,0:T(8,128)(2,1)S(1)}, bf16[2,80,384]{2,1,0:T(8,128)(2,1)S(1)}, u32[]{:S(2)}, u32[]{:S(2)}) collective-permute-start(bf16[2,80,384]{2,1,0:T(8,128)(2,1)S(1)} %collective-permute-done.1.far_ref), channel_id=1, source_target_pairs={{0,1},{1,0},{2,3},{3,2},{4,5},{5,4},{6,7},{7,6},{8,9},{9,8},{10,11... | collective-permute-start | bytes 368648 | tf_op jit(solution)/shard_map/ppermute | solution.py:344
  12.9 7.2 %collective-permute-start.3 = (bf16[384,384]{1,0:T(8,128)(2,1)}, bf16[384,384]{1,0:T(8,128)(2,1)S(1)}, u32[]{:S(2)}, u32[]{:S(2)}) collective-permute-start(bf16[384,384]{1,0:T(8,128)(2,1)} %get-tuple-element.72), channel_id=1, source_target_pairs={{0,1},{1,0},{2,3},{3,2},{4,5},{5,4},{6,7},{7,6},{8,9},{9,8},{10,11... | collective-permute-start | bytes 884744 | tf_op jit(solution)/shard_map/ppermute | solution.py:344
  13.4 1.3 %collective-permute-start = (bf16[80,384]{1,0:T(8,128)(2,1)S(1)}, bf16[80,384]{1,0:T(8,128)(2,1)S(1)}, u32[]{:S(2)}, u32[]{:S(2)}) collective-permute-start(bf16[80,384]{1,0:T(8,128)(2,1)S(1)} %copy-done.8), channel_id=1, source_target_pairs={{0,1},{1,0},{2,3},{3,2},{4,5},{5,4},{6,7},{7,6},{8,9},{9,8},{10,11... | collective-permute-start | bytes 184328 | tf_op jit(solution)/shard_map/ppermute | solution.py:344
  14.8 11.3 %collective-permute-start.4 = (bf16[256,384]{1,0:T(8,128)(2,1)S(1)}, bf16[256,384]{1,0:T(8,128)(2,1)S(1)}, u32[]{:S(2)}, u32[]{:S(2)}) collective-permute-start(bf16[256,384]{1,0:T(8,128)(2,1)S(1)} %get-tuple-element.70.qg_ref.refs_3_.refs_0_), channel_id=1, source_target_pairs={{0,4},{1,5},{2,6},{3,7},{4,0},{5,1},{6,2},{7,3},{8,12},{9,13},{10,... | collective-permute-start | bytes 589832 | tf_op jit(solution)/shard_map/ppermute | solution.py:344
  16.8 11.8 %collective-permute-start.6 = (bf16[256,384]{1,0:T(8,128)(2,1)S(1)}, bf16[256,384]{1,0:T(8,128)(2,1)S(1)}, u32[]{:S(2)}, u32[]{:S(2)}) collective-permute-start(bf16[256,384]{1,0:T(8,128)(2,1)S(1)} %get-tuple-element.70.qg_ref.refs_3_.refs_0_), channel_id=1, source_target_pairs={{0,8},{1,9},{2,10},{3,11},{4,12},{5,13},{6,14},{7,15},{8,0},{9,1},... | collective-permute-start | bytes 589832 | tf_op jit(solution)/shard_map/ppermute | solution.py:344
  28.7 2.0 %collective-permute-start.7 = (bf16[2,384,384]{2,1,0:T(8,128)(2,1)S(1)}, bf16[2,384,384]{2,1,0:T(8,128)(2,1)S(1)}, u32[]{:S(2)}, u32[]{:S(2)}) collective-permute-start(bf16[2,384,384]{2,1,0:T(8,128)(2,1)S(1)} %collective-permute-done.5.refs_0_.refs_3_.refs_8_), channel_id=1, source_target_pairs={{0,1},{1,0},{2,3},{3,2},{4,5},{5,4},{6,7},{7,6},{8,9},{9,8},{10,11... | collective-permute-start | bytes 1769480 | tf_op jit(solution)/shard_map/ppermute | solution.py:344
  28.7 7.3 %collective-permute-start.8 = (bf16[256,384]{1,0:T(8,128)(2,1)S(1)}, bf16[256,384]{1,0:T(8,128)(2,1)S(1)}, u32[]{:S(2)}, u32[]{:S(2)}) collective-permute-start(bf16[256,384]{1,0:T(8,128)(2,1)S(1)} %collective-permute-done.6.qg_ref.refs_1_.refs_0_), channel_id=1, source_target_pairs={{0,4},{1,5},{2,6},{3,7},{4,0},{5,1},{6,2},{7,3},{8,12},{9,13},{10,... | collective-permute-start | bytes 589832 | tf_op jit(solution)/shard_map/ppermute | solution.py:344
  38.4 4.0 %collective-permute-start.9 = (f32[4,6,256]{2,1,0:T(8,128)S(1)}, f32[4,6,256]{2,1,0:T(8,128)S(1)}, u32[]{:S(2)}, u32[]{:S(2)}) collective-permute-start(f32[4,6,256]{2,1,0:T(8,128)S(1)} %pad_maximum_fusion.4), channel_id=1, source_target_pairs={{0,4},{1,5},{2,6},{3,7},{4,0},{5,1},{6,2},{7,3},{8,12},{9,13},{10,... | collective-permute-start | bytes 73736 | tf_op jit(solution)/shard_map/ppermute | solution.py:344
  42.4 5.2 %collective-permute-start.10 = (f32[4,6,256]{2,1,0:T(8,128)S(1)}, f32[4,6,256]{2,1,0:T(8,128)S(1)}, u32[]{:S(2)}, u32[]{:S(2)}) collective-permute-start(f32[4,6,256]{2,1,0:T(8,128)S(1)} %pad_maximum_fusion.6), channel_id=1, source_target_pairs={{0,8},{1,9},{2,10},{3,11},{4,12},{5,13},{6,14},{7,15},{8,0},{9,1},... | collective-permute-start | bytes 73736 | tf_op jit(solution)/shard_map/ppermute | solution.py:344
  47.8 9.5 %collective-permute-start.11 = (bf16[2,192,256]{2,1,0:T(8,128)(2,1)S(1)}, bf16[2,192,256]{2,1,0:T(8,128)(2,1)S(1)}, u32[]{:S(2)}, u32[]{:S(2)}) collective-permute-start(bf16[2,192,256]{2,1,0:T(8,128)(2,1)S(1)} %pad_maximum_fusion.1), channel_id=1, source_target_pairs={{0,8},{1,9},{2,10},{3,11},{4,12},{5,13},{6,14},{7,15},{8,0},{9,1},... | collective-permute-start | bytes 589832 | tf_op jit(solution)/shard_map/ppermute | solution.py:344
  55.6 14.7 %collective-permute-start.13 = (bf16[2,384,384]{2,1,0:T(8,128)(2,1)S(1)}, bf16[2,384,384]{2,1,0:T(8,128)(2,1)S(1)}, u32[]{:S(2)}, u32[]{:S(2)}) collective-permute-start(bf16[2,384,384]{2,1,0:T(8,128)(2,1)S(1)} %get-tuple-element.97), channel_id=1, source_target_pairs={{0,2},{1,3},{2,0},{3,1},{4,6},{5,7},{6,4},{7,5},{8,10},{9,11},{10,... | collective-permute-start | bytes 1769480 | tf_op jit(solution)/shard_map/ppermute | solution.py:344
  59.0 4.7 %collective-permute-start.14 = (bf16[192,256]{1,0:T(8,128)(2,1)S(1)}, bf16[192,256]{1,0:T(8,128)(2,1)S(1)}, u32[]{:S(2)}, u32[]{:S(2)}) collective-permute-start(bf16[192,256]{1,0:T(8,128)(2,1)S(1)} %bitcast.89), channel_id=1, source_target_pairs={{0,4},{1,5},{2,6},{3,7},{4,0},{5,1},{6,2},{7,3},{8,12},{9,13},{10,... | collective-permute-start | bytes 294920 | tf_op jit(solution)/shard_map/ppermute | solution.py:344
  60.5 8.0 %collective-permute-start.12 = (bf16[192,256]{1,0:T(8,128)(2,1)S(1)}, bf16[192,256]{1,0:T(8,128)(2,1)S(1)}, u32[]{:S(2)}, u32[]{:S(2)}) collective-permute-start(bf16[192,256]{1,0:T(8,128)(2,1)S(1)} %fusion.1), channel_id=1, source_target_pairs={{0,4},{1,5},{2,6},{3,7},{4,0},{5,1},{6,2},{7,3},{8,12},{9,13},{10,... | collective-permute-start | bytes 294920 | tf_op jit(solution)/shard_map/ppermute | solution.py:344
  63.7 6.6 %collective-permute-start.15 = (bf16[192,256]{1,0:T(8,128)(2,1)S(1)}, bf16[192,256]{1,0:T(8,128)(2,1)S(1)}, u32[]{:S(2)}, u32[]{:S(2)}) collective-permute-start(bf16[192,256]{1,0:T(8,128)(2,1)S(1)} %fusion.4), channel_id=1, source_target_pairs={{0,8},{1,9},{2,10},{3,11},{4,12},{5,13},{6,14},{7,15},{8,0},{9,1},... | collective-permute-start | bytes 294920 | tf_op jit(solution)/shard_map/ppermute | solution.py:344
  67.0 5.1 %collective-permute-start.16 = (bf16[192,256]{1,0:T(8,128)(2,1)S(1)}, bf16[192,256]{1,0:T(8,128)(2,1)S(1)}, u32[]{:S(2)}, u32[]{:S(2)}) collective-permute-start(bf16[192,256]{1,0:T(8,128)(2,1)S(1)} %bitcast.88), channel_id=1, source_target_pairs={{0,4},{1,5},{2,6},{3,7},{4,0},{5,1},{6,2},{7,3},{8,12},{9,13},{10,... | collective-permute-start | bytes 294920 | tf_op jit(solution)/shard_map/ppermute | solution.py:344
  72.3 2.1 %collective-permute-start.18 = (bf16[2,384,384]{2,1,0:T(8,128)(2,1)S(1)}, bf16[2,384,384]{2,1,0:T(8,128)(2,1)S(1)}, u32[]{:S(2)}, u32[]{:S(2)}) collective-permute-start(bf16[2,384,384]{2,1,0:T(8,128)(2,1)S(1)} %pad_maximum_fusion), channel_id=1, source_target_pairs={{0,1},{1,0},{2,3},{3,2},{4,5},{5,4},{6,7},{7,6},{8,9},{9,8},{10,11... | collective-permute-start | bytes 1769480 | tf_op jit(solution)/shard_map/ppermute | solution.py:344
  72.4 5.3 %collective-permute-start.17 = (bf16[2,192,128]{2,1,0:T(8,128)(2,1)S(1)}, bf16[2,192,128]{2,1,0:T(8,128)(2,1)S(1)}, u32[]{:S(2)}, u32[]{:S(2)}) collective-permute-start(bf16[2,192,128]{2,1,0:T(8,128)(2,1)S(1)} %get-tuple-element.119), channel_id=1, source_target_pairs={{0,2},{1,3},{2,0},{3,1},{4,6},{5,7},{6,4},{7,5},{8,10},{9,11},{10,... | collective-permute-start | bytes 294920 | tf_op jit(solution)/shard_map/ppermute | solution.py:344
  77.8 1.5 %collective-permute-start.19 = (bf16[2,2,192,64]{3,2,1,0:T(8,128)(2,1)S(1)}, bf16[2,2,192,64]{3,2,1,0:T(8,128)(2,1)S(1)}, u32[]{:S(2)}, u32[]{:S(2)}) collective-permute-start(bf16[2,2,192,64]{3,2,1,0:T(8,128)(2,1)S(1)} %pad_maximum_fusion.3), channel_id=1, source_target_pairs={{0,1},{1,0},{2,3},{3,2},{4,5},{5,4},{6,7},{7,6},{8,9},{9,8},{10,11... | collective-permute-start | bytes 294920 | tf_op jit(solution)/shard_map/ppermute | solution.py:344
  (5 other events, 26.3 us)

commit v10 on v9

--- a/solution.py
+++ b/solution.py
@@ -95,19 +95,8 @@
     store_quarters(place_ref, (keep_ref, core_ref), far_ref, query, grad, slice(0, own))
 
 
-def slots_kernel(
-    place_ref, points_hbm, w_key_hbm, w_value_hbm,
-    keep_ref, core_ref, far_ref, points_ref, w_key_ref, w_value_ref, sems
-):
-    pieces = sems.shape[1]
-    loads = [
-        load(points_hbm, points_ref, sems.at[0], pieces),
-        load(w_key_hbm, w_key_ref, sems.at[1], pieces),
-        load(w_value_hbm, w_value_ref, sems.at[2], pieces),
-    ]
-    wait(*loads[:2])
+def slots_kernel(place_ref, points_ref, w_key_ref, w_value_ref, keep_ref, core_ref, far_ref):
     keys = dot(points_ref[...], w_key_ref[...]).astype(BF16) * jnp.asarray(0.125, BF16)
-    wait(*loads[2:])
     values = dot(points_ref[...], w_value_ref[...]).astype(BF16)
     store_quarters(place_ref, (keep_ref, core_ref), far_ref, keys, values, slice(0, keys.shape[0]))
 
@@ -343,24 +332,25 @@
     def swap(array, mask):
         return lax.ppermute(array, "pts", [(i, i ^ mask) for i in range(size)])
 
-    def project(kernel, scalars, inputs, rows):
-        return call(
-            kernel,
-            scalars + inputs,
-            [shape((rows, 2 * mine), BF16)] * 2 + [shape((2, rows, 2 * mine), BF16)],
-            [pltpu.VMEM(a.shape, BF16) for a in inputs] + [pltpu.SemaphoreType.DMA((len(inputs), 4))],
-            flops=4 * rows * width * width,
-            space=pltpu.HBM,
-            grant=60,
-        )
-
-    keep_qg, core_qg, far_qg = project(
-        rows_kernel, [place, counts], [latents, d_out, w_query, w_out], own + 16
+    def pieces(rows):
+        return [shape((rows, 2 * mine), BF16)] * 2 + [shape((2, rows, 2 * mine), BF16)]
+
+    inputs = [latents, d_out, w_query, w_out]
+    keep_qg, core_qg, far_qg = call(
+        rows_kernel,
+        [place, counts] + inputs,
+        pieces(own + 16),
+        [pltpu.VMEM(a.shape, BF16) for a in inputs] + [pltpu.SemaphoreType.DMA((len(inputs), 4))],
+        flops=4 * own * width * width,
+        space=pltpu.HBM,
+        grant=60,
     )
-    keep_qg, points = lax.optimization_barrier((keep_qg, points))
+    keep_qg, then_place = lax.optimization_barrier((keep_qg, place))
     far_qg = swap(far_qg, 2)
     core_qg = swap(core_qg, 1)
-    keep, core, far = project(slots_kernel, [place], [points, w_key, w_value], slots)
+    keep, core, far = call(
+        slots_kernel, [then_place, points, w_key, w_value], pieces(slots), flops=4 * slots * width * width
+    )
     far_qg, far = lax.optimization_barrier((far_qg, far))
     far = swap(far, 2)
     core = swap(core, 1)

time: 81 us -> 80.6 us (level)
  Pallas kernels: 36.1 us -> 32.8 us
  waiting for transfers between devices: 21.8 us -> 25 us
  starting transfers between devices: 20.5 us -> 19.2 us
  local copies, waits for them, and re-layouts: 0.34 us -> 1.4 us
    pallas_call x19, Pallas kernels: 36.1 us -> 32.8 us  [call(): pl.pallas_call(kernel, in_specs=[smem if a.dtype == jnp.int32 else other...]
    ppermute x20, waiting for transfers between devices: 21.8 us -> 25 us  [swap(): return lax.ppermute(array, 'pts', [(i, i ^ mask) for i in range(size)])]
    ppermute x20, starting transfers between devices: 20.5 us -> 19.2 us  [swap(): return lax.ppermute(array, 'pts', [(i, i ^ mask) for i in range(size)])]
    unnamed x18, local copies, waits for them, and re-layouts: 0.04 us -> 1.1 us
  transfers between devices with their start and end apart: 20 -> 20, of which waited for: 13 -> 14; matrix products, arithmetic and copies ran while one was open for 0% -> 0% of each run, Pallas kernels for 36% -> 32%
where the time goes in v10:
time: 80.6 us; the launch traced here: 80.5 us
  Pallas kernels  32.8 us (41%)
  waiting for transfers between devices  25 us (31%)
  starting transfers between devices  19.2 us (24%)
  between operations  1.64 us (2%)
  local copies, waits for them, and re-layouts  1.4 us (2%)
    pallas_call x19, Pallas kernels, call(): pl.pallas_call(kernel, in_specs=[smem if a.dtype == jnp.int32 else other...  32.8 us
    ppermute x20, waiting for transfers between devices, swap(): return lax.ppermute(array, 'pts', [(i, i ^ mask) for i in range(size)])  25 us
    ppermute x20, starting transfers between devices, swap(): return lax.ppermute(array, 'pts', [(i, i ^ mask) for i in range(size)])  19.2 us
  transfers between devices with their start and end apart: 20, of which 14 were waited for; matrix products, arithmetic and copies ran while one was open for 0% of the time, Pallas kernels for 32%

profile of v10, /device:TPU:0, one launch (start us, length us, event | category | flops | bytes accessed | tf_op | source)
XLA Modules:
  0.0 80.5 jit_solution(16955838149092252558)
XLA Ops:
  1.3 3.5 %shard_map.103 = (bf16[80,384]{1,0:T(8,128)(2,1)}, bf16[80,384]{1,0:T(8,128)(2,1)}, bf16[2,80,384]{2,1,0:T(8,128)(2,1)}) custom-call(s32[1]{0:T(128)} %bitcast.place_ref, s32[1]{0:T(128)S(6)} %copy.11.count_ref, bf16[64,768]{1,0:T(8,128)(2,1)} %latents_ref.1, bf16[64,768]{1,0:T(8,128)(2,1)} %d_out_ref.1, bf16[768,768]{1,0:T(8,128)(2,1)} %w_query_ref.1, ...), custom_call_target="tpu_custom_call" | custom-call | flops 18874368 | bytes 350209 | tf_op jit(solution)/shard_map/pallas_call | solution.py:308
  4.8 3.0 %collective-permute-start.1 = (bf16[2,80,384]{2,1,0:T(8,128)(2,1)}, bf16[2,80,384]{2,1,0:T(8,128)(2,1)S(1)}, u32[]{:S(2)}, u32[]{:S(2)}) collective-permute-start(bf16[2,80,384]{2,1,0:T(8,128)(2,1)} %get-tuple-element.64), channel_id=1, source_target_pairs={{0,2},{1,3},{2,0},{3,1},{4,6},{5,7},{6,4},{7,5},{8,10},{9,11},{10,... | collective-permute-start | bytes 368648 | tf_op jit(solution)/shard_map/ppermute | solution.py:333
  8.9 1.6 %shard_map.104 = (bf16[384,384]{1,0:T(8,128)(2,1)S(1)}, bf16[384,384]{1,0:T(8,128)(2,1)S(1)}, bf16[2,384,384]{2,1,0:T(8,128)(2,1)S(1)}) custom-call(s32[1]{0:T(128)} %bitcast.place_ref, bf16[384,768]{1,0:T(8,128)(2,1)S(1)} %copy-done.4, bf16[768,768]{1,0:T(8,128)(2,1)S(1)} %copy-done.2, bf16[768,768]{1,0:T(8,128)(2,1)S(1)} %copy-done.3), custom_call_target="tpu_custom_call" | custom-call | flops 113246208 | bytes 516096 | tf_op jit(solution)/shard_map/pallas_call | solution.py:308
  11.3 1.7 %collective-permute-start.5 = (bf16[2,384,384]{2,1,0:T(8,128)(2,1)S(1)}, bf16[2,384,384]{2,1,0:T(8,128)(2,1)S(1)}, u32[]{:S(2)}, u32[]{:S(2)}) collective-permute-start(bf16[2,384,384]{2,1,0:T(8,128)(2,1)S(1)} %get-tuple-element.80), channel_id=1, source_target_pairs={{0,2},{1,3},{2,0},{3,1},{4,6},{5,7},{6,4},{7,5},{8,10},{9,11},{10,... | collective-permute-start | bytes 1769480 | tf_op jit(solution)/shard_map/ppermute | solution.py:333
  15.0 1.6 %collective-permute-start.4 = (bf16[256,384]{1,0:T(8,128)(2,1)S(1)}, bf16[256,384]{1,0:T(8,128)(2,1)S(1)}, u32[]{:S(2)}, u32[]{:S(2)}) collective-permute-start(bf16[256,384]{1,0:T(8,128)(2,1)S(1)} %get-tuple-element.70.qg_ref.refs_3_.refs_0_), channel_id=1, source_target_pairs={{0,4},{1,5},{2,6},{3,7},{4,0},{5,1},{6,2},{7,3},{8,12},{9,13},{10,... | collective-permute-start | bytes 589832 | tf_op jit(solution)/shard_map/ppermute | solution.py:333
  16.6 2.6 %collective-permute-start.6 = (bf16[256,384]{1,0:T(8,128)(2,1)S(1)}, bf16[256,384]{1,0:T(8,128)(2,1)S(1)}, u32[]{:S(2)}, u32[]{:S(2)}) collective-permute-start(bf16[256,384]{1,0:T(8,128)(2,1)S(1)} %get-tuple-element.70.qg_ref.refs_3_.refs_0_), channel_id=1, source_target_pairs={{0,8},{1,9},{2,10},{3,11},{4,12},{5,13},{6,14},{7,15},{8,0},{9,1},... | collective-permute-start | bytes 589832 | tf_op jit(solution)/shard_map/ppermute | solution.py:333
  21.4 4.9 %collective-permute-done.4.qg_ref.refs_2_.refs_0_ = bf16[256,384]{1,0:T(8,128)(2,1)S(1)} collective-permute-done((bf16[256,384]{1,0:T(8,128)(2,1)S(1)}, bf16[256,384]{1,0:T(8,128)(2,1)S(1)}, u32[]{:S(2)}, u32[]{:S(2)}) %collective-permute-start.4) | collective-permute-done | bytes 196640 | tf_op jit(solution)/shard_map/ppermute | solution.py:333
  29.1 1.6 %collective-permute-done.7.refs_1_.refs_4_.refs_9_ = bf16[2,384,384]{2,1,0:T(8,128)(2,1)S(1)} collective-permute-done((bf16[2,384,384]{2,1,0:T(8,128)(2,1)S(1)}, bf16[2,384,384]{2,1,0:T(8,128)(2,1)S(1)}, u32[]{:S(2)}, u32[]{:S(2)}) %collective-permute-start.7) | collective-permute-done | bytes 589856 | tf_op jit(solution)/shard_map/ppermute | solution.py:333
  30.9 2.3 %shard_map.113 = (f32[192,256]{1,0:T(8,128)S(1)}, f32[12,256]{1,0:T(8,128)S(1)}) custom-call(f32[4,128]{1,0:T(4,128)S(1)} %get-tuple-element.68.count_ref, bf16[256,384]{1,0:T(8,128)(2,1)S(1)} %collective-permute-done.6.qg_ref.refs_1_.refs_0_, bf16[384,384]{1,0:T(8,128)(2,1)S(1)} %get-tuple-element.71.refs_0_.refs_2_, ...), custom_call_target="tpu_custom_call" | custom-call | flops 150994944 | bytes 419584 | tf_op jit(solution)/shard_map/pallas_call | solution.py:308
  36.0 2.3 %shard_map.114 = (f32[192,256]{1,0:T(8,128)S(1)}, f32[12,256]{1,0:T(8,128)S(1)}) custom-call(f32[4,128]{1,0:T(4,128)S(1)} %get-tuple-element.68.count_ref, bf16[256,384]{1,0:T(8,128)(2,1)S(1)} %collective-permute-done.8.qg_ref.refs_0_, bf16[384,384]{1,0:T(8,128)(2,1)S(1)} %get-tuple-element.71.refs_0_.refs_2_, ...), custom_call_target="tpu_custom_call" | custom-call | flops 150994944 | bytes 419584 | tf_op jit(solution)/shard_map/pallas_call | solution.py:308
  38.9 3.5 %collective-permute-done.9 = f32[4,6,256]{2,1,0:T(8,128)S(1)} collective-permute-done((f32[4,6,256]{2,1,0:T(8,128)S(1)}, f32[4,6,256]{2,1,0:T(8,128)S(1)}, u32[]{:S(2)}, u32[]{:S(2)}) %collective-permute-start.9) | collective-permute-done | bytes 24608 | tf_op jit(solution)/shard_map/ppermute | solution.py:333
  43.8 3.8 %collective-permute-done.10 = f32[4,6,256]{2,1,0:T(8,128)S(1)} collective-permute-done((f32[4,6,256]{2,1,0:T(8,128)S(1)}, f32[4,6,256]{2,1,0:T(8,128)S(1)}, u32[]{:S(2)}, u32[]{:S(2)}) %collective-permute-start.10) | collective-permute-done | bytes 24608 | tf_op jit(solution)/shard_map/ppermute | solution.py:333
  48.8 6.4 %shard_map.115 = (f32[4,192,256]{2,1,0:T(8,128)S(1)}, bf16[2,384,384]{2,1,0:T(8,128)(2,1)S(1)}) custom-call(f32[4,128]{1,0:T(4,128)S(1)} %get-tuple-element.68.count_ref, bf16[256,384]{1,0:T(8,128)(2,1)S(1)} %collective-permute-done.8.qg_ref.refs_0_, bf16[256,384]{1,0:T(8,128)(2,1)S(1)} %collective-permute-done.6.qg_ref.refs_1_.refs_0_, ...), custom_call_target="tpu_custom_call" | custom-call | flops 528482304 | bytes 494848 | tf_op jit(solution)/shard_map/pallas_call | solution.py:308
  57.0 1.7 %shard_map.116 = (bf16[1,192,256]{2,1,0:T(8,128)(2,1)S(1)}, f32[2,384,384]{2,1,0:T(8,128)S(1)}) custom-call(f32[4,128]{1,0:T(4,128)S(1)} %get-tuple-element.68.count_ref, bf16[256,384]{1,0:T(8,128)(2,1)S(1)} %collective-permute-done.8.qg_ref.refs_0_, f32[6,256]{1,0:T(8,128)S(1)} %get-tuple-element.126.refs_4_.refs_1_, ...), custom_call_target="tpu_custom_call" | custom-call | flops 132120576 | bytes 431104 | tf_op jit(solution)/shard_map/pallas_call | solution.py:308
  60.9 1.7 %shard_map.117 = (f32[1,192,256]{2,1,0:T(8,128)S(1)}, f32[2,384,384]{2,1,0:T(8,128)S(1)}) custom-call(f32[4,128]{1,0:T(4,128)S(1)} %get-tuple-element.68.count_ref, bf16[256,384]{1,0:T(8,128)(2,1)S(1)} %collective-permute-done.6.qg_ref.refs_1_.refs_0_, f32[6,256]{1,0:T(8,128)S(1)} %get-tuple-element.127.refs_5_.refs_1_, ...), custom_call_target="tpu_custom_call" | custom-call | flops 132120576 | bytes 590848 | tf_op jit(solution)/shard_map/pallas_call | solution.py:308
  63.4 1.5 %collective-permute-start.15 = (bf16[192,256]{1,0:T(8,128)(2,1)S(1)}, bf16[192,256]{1,0:T(8,128)(2,1)S(1)}, u32[]{:S(2)}, u32[]{:S(2)}) collective-permute-start(bf16[192,256]{1,0:T(8,128)(2,1)S(1)} %fusion.4), channel_id=1, source_target_pairs={{0,8},{1,9},{2,10},{3,11},{4,12},{5,13},{6,14},{7,15},{8,0},{9,1},... | collective-permute-start | bytes 294920 | tf_op jit(solution)/shard_map/ppermute | solution.py:333
  64.9 1.7 %shard_map.118 = (bf16[1,192,256]{2,1,0:T(8,128)(2,1)S(1)}, f32[2,384,384]{2,1,0:T(8,128)S(1)}) custom-call(f32[4,128]{1,0:T(4,128)S(1)} %get-tuple-element.68.count_ref, bf16[256,384]{1,0:T(8,128)(2,1)S(1)} %collective-permute-done.4.qg_ref.refs_2_.refs_0_, f32[6,256]{1,0:T(8,128)S(1)} %get-tuple-element.128.refs_6_.refs_1_, ...), custom_call_target="tpu_custom_call" | custom-call | flops 132120576 | bytes 578560 | tf_op jit(solution)/shard_map/pallas_call | solution.py:308
  66.7 1.4 %collective-permute-start.16 = (bf16[192,256]{1,0:T(8,128)(2,1)S(1)}, bf16[192,256]{1,0:T(8,128)(2,1)S(1)}, u32[]{:S(2)}, u32[]{:S(2)}) collective-permute-start(bf16[192,256]{1,0:T(8,128)(2,1)S(1)} %bitcast.88), channel_id=1, source_target_pairs={{0,4},{1,5},{2,6},{3,7},{4,0},{5,1},{6,2},{7,3},{8,12},{9,13},{10,... | collective-permute-start | bytes 294920 | tf_op jit(solution)/shard_map/ppermute | solution.py:333
  68.2 1.9 %collective-permute-done.15 = bf16[192,256]{1,0:T(8,128)(2,1)S(1)} collective-permute-done((bf16[192,256]{1,0:T(8,128)(2,1)S(1)}, bf16[192,256]{1,0:T(8,128)(2,1)S(1)}, u32[]{:S(2)}, u32[]{:S(2)}) %collective-permute-start.15) | collective-permute-done | bytes 98336 | tf_op jit(solution)/shard_map/ppermute | solution.py:333
  70.0 1.7 %shard_map.119 = (f32[1,192,256]{2,1,0:T(8,128)S(1)}, bf16[2,384,384]{2,1,0:T(8,128)(2,1)S(1)}) custom-call(f32[4,128]{1,0:T(4,128)S(1)} %get-tuple-element.68.count_ref, bf16[256,384]{1,0:T(8,128)(2,1)S(1)} %get-tuple-element.70.qg_ref.refs_3_.refs_0_, f32[6,256]{1,0:T(8,128)S(1)} %get-tuple-element.125.refs_7_.refs_1_, ...), custom_call_target="tpu_custom_call" | custom-call | flops 132120576 | bytes 517120 | tf_op jit(solution)/shard_map/pallas_call | solution.py:308
  72.6 1.4 %collective-permute-done.18.core_ref = bf16[2,384,384]{2,1,0:T(8,128)(2,1)S(1)} collective-permute-done((bf16[2,384,384]{2,1,0:T(8,128)(2,1)S(1)}, bf16[2,384,384]{2,1,0:T(8,128)(2,1)S(1)}, u32[]{:S(2)}, u32[]{:S(2)}) %collective-permute-start.18) | collective-permute-done | bytes 589856 | tf_op jit(solution)/shard_map/ppermute | solution.py:333
  74.1 2.2 %shard_map.120 = bf16[384,768]{1,0:T(8,128)(2,1)} custom-call(s32[1]{0:T(128)} %bitcast.place_ref, bf16[2,384,384]{2,1,0:T(8,128)(2,1)S(1)} %get-tuple-element.112.near_ref, bf16[2,384,384]{2,1,0:T(8,128)(2,1)S(1)} %collective-permute-done.13.far_ref, bf16[2,384,384]{2,1,0:T(8,128)(2,1)S(1)} %collective-permute-done.18.core_ref, ...), custom_call_target="tpu_custom_call" | custom-call | flops 113246208 | bytes 589824 | tf_op jit(solution)/shard_map/pallas_call | solution.py:308
  77.6 1.4 %collective-permute-done.19.core_ref = bf16[2,2,192,64]{3,2,1,0:T(8,128)(2,1)S(1)} collective-permute-done((bf16[2,2,192,64]{3,2,1,0:T(8,128)(2,1)S(1)}, bf16[2,2,192,64]{3,2,1,0:T(8,128)(2,1)S(1)}, u32[]{:S(2)}, u32[]{:S(2)}) %collective-permute-start.19) | collective-permute-done | bytes 98336 | tf_op jit(solution)/shard_map/ppermute | solution.py:333
  79.0 1.4 %shard_map.121 = (bf16[64,768]{1,0:T(8,128)(2,1)}, bf16[64,768]{1,0:T(8,128)(2,1)}) custom-call(s32[1]{0:T(128)} %bitcast.place_ref, bf16[2,192,128]{2,1,0:T(8,128)(2,1)S(1)} %get-tuple-element.120.near_ref, bf16[2,192,128]{2,1,0:T(8,128)(2,1)S(1)} %collective-permute-done.17.far_ref, bf16[2,2,192,64]{3,2,1,0:T(8,128)(2,1)S(1)} %collective-permute-done.19.core_ref, ...), custom_call_target="tpu_custom_call" | custom-call | flops 18874368 | bytes 380928 | tf_op jit(solution)/shard_map/pallas_call | solution.py:308
  (79 shorter events, 21.8 us)
Async XLA Ops:
  1.3 6.5 %copy-start.2 = (bf16[768,768]{1,0:T(8,128)(2,1)S(1)}, bf16[768,768]{1,0:T(8,128)(2,1)}, u32[]{:S(2)}) copy-start(bf16[768,768]{1,0:T(8,128)(2,1)} %w_key_ref.2) | copy-start | bytes 3538948
  1.3 6.5 %copy-start.3 = (bf16[768,768]{1,0:T(8,128)(2,1)S(1)}, bf16[768,768]{1,0:T(8,128)(2,1)}, u32[]{:S(2)}) copy-start(bf16[768,768]{1,0:T(8,128)(2,1)} %w_value_ref.2) | copy-start | bytes 3538948
  4.8 6.5 %collective-permute-start.1 = (bf16[2,80,384]{2,1,0:T(8,128)(2,1)}, bf16[2,80,384]{2,1,0:T(8,128)(2,1)S(1)}, u32[]{:S(2)}, u32[]{:S(2)}) collective-permute-start(bf16[2,80,384]{2,1,0:T(8,128)(2,1)} %get-tuple-element.64), channel_id=1, source_target_pairs={{0,2},{1,3},{2,0},{3,1},{4,6},{5,7},{6,4},{7,5},{8,10},{9,11},{10,... | collective-permute-start | bytes 368648 | tf_op jit(solution)/shard_map/ppermute | solution.py:333
  11.3 17.3 %collective-permute-start.5 = (bf16[2,384,384]{2,1,0:T(8,128)(2,1)S(1)}, bf16[2,384,384]{2,1,0:T(8,128)(2,1)S(1)}, u32[]{:S(2)}, u32[]{:S(2)}) collective-permute-start(bf16[2,384,384]{2,1,0:T(8,128)(2,1)S(1)} %get-tuple-element.80), channel_id=1, source_target_pairs={{0,2},{1,3},{2,0},{3,1},{4,6},{5,7},{6,4},{7,5},{8,10},{9,11},{10,... | collective-permute-start | bytes 1769480 | tf_op jit(solution)/shard_map/ppermute | solution.py:333
  13.1 1.8 %collective-permute-start.2 = (bf16[2,80,384]{2,1,0:T(8,128)(2,1)S(1)}, bf16[2,80,384]{2,1,0:T(8,128)(2,1)S(1)}, u32[]{:S(2)}, u32[]{:S(2)}) collective-permute-start(bf16[2,80,384]{2,1,0:T(8,128)(2,1)S(1)} %collective-permute-done.1.far_ref), channel_id=1, source_target_pairs={{0,1},{1,0},{2,3},{3,2},{4,5},{5,4},{6,7},{7,6},{8,9},{9,8},{10,11... | collective-permute-start | bytes 368648 | tf_op jit(solution)/shard_map/ppermute | solution.py:333
  13.1 6.8 %collective-permute-start.3 = (bf16[384,384]{1,0:T(8,128)(2,1)S(1)}, bf16[384,384]{1,0:T(8,128)(2,1)S(1)}, u32[]{:S(2)}, u32[]{:S(2)}) collective-permute-start(bf16[384,384]{1,0:T(8,128)(2,1)S(1)} %get-tuple-element.72), channel_id=1, source_target_pairs={{0,1},{1,0},{2,3},{3,2},{4,5},{5,4},{6,7},{7,6},{8,9},{9,8},{10,11... | collective-permute-start | bytes 884744 | tf_op jit(solution)/shard_map/ppermute | solution.py:333
  13.6 1.3 %collective-permute-start = (bf16[80,384]{1,0:T(8,128)(2,1)S(1)}, bf16[80,384]{1,0:T(8,128)(2,1)S(1)}, u32[]{:S(2)}, u32[]{:S(2)}) collective-permute-start(bf16[80,384]{1,0:T(8,128)(2,1)S(1)} %copy-done.8), channel_id=1, source_target_pairs={{0,1},{1,0},{2,3},{3,2},{4,5},{5,4},{6,7},{7,6},{8,9},{9,8},{10,11... | collective-permute-start | bytes 184328 | tf_op jit(solution)/shard_map/ppermute | solution.py:333
  15.0 11.3 %collective-permute-start.4 = (bf16[256,384]{1,0:T(8,128)(2,1)S(1)}, bf16[256,384]{1,0:T(8,128)(2,1)S(1)}, u32[]{:S(2)}, u32[]{:S(2)}) collective-permute-start(bf16[256,384]{1,0:T(8,128)(2,1)S(1)} %get-tuple-element.70.qg_ref.refs_3_.refs_0_), channel_id=1, source_target_pairs={{0,4},{1,5},{2,6},{3,7},{4,0},{5,1},{6,2},{7,3},{8,12},{9,13},{10,... | collective-permute-start | bytes 589832 | tf_op jit(solution)/shard_map/ppermute | solution.py:333
  16.6 12.0 %collective-permute-start.6 = (bf16[256,384]{1,0:T(8,128)(2,1)S(1)}, bf16[256,384]{1,0:T(8,128)(2,1)S(1)}, u32[]{:S(2)}, u32[]{:S(2)}) collective-permute-start(bf16[256,384]{1,0:T(8,128)(2,1)S(1)} %get-tuple-element.70.qg_ref.refs_3_.refs_0_), channel_id=1, source_target_pairs={{0,8},{1,9},{2,10},{3,11},{4,12},{5,13},{6,14},{7,15},{8,0},{9,1},... | collective-permute-start | bytes 589832 | tf_op jit(solution)/shard_map/ppermute | solution.py:333
  28.7 2.0 %collective-permute-start.7 = (bf16[2,384,384]{2,1,0:T(8,128)(2,1)S(1)}, bf16[2,384,384]{2,1,0:T(8,128)(2,1)S(1)}, u32[]{:S(2)}, u32[]{:S(2)}) collective-permute-start(bf16[2,384,384]{2,1,0:T(8,128)(2,1)S(1)} %collective-permute-done.5.refs_0_.refs_3_.refs_8_), channel_id=1, source_target_pairs={{0,1},{1,0},{2,3},{3,2},{4,5},{5,4},{6,7},{7,6},{8,9},{9,8},{10,11... | collective-permute-start | bytes 1769480 | tf_op jit(solution)/shard_map/ppermute | solution.py:333
  28.7 7.3 %collective-permute-start.8 = (bf16[256,384]{1,0:T(8,128)(2,1)S(1)}, bf16[256,384]{1,0:T(8,128)(2,1)S(1)}, u32[]{:S(2)}, u32[]{:S(2)}) collective-permute-start(bf16[256,384]{1,0:T(8,128)(2,1)S(1)} %collective-permute-done.6.qg_ref.refs_1_.refs_0_), channel_id=1, source_target_pairs={{0,4},{1,5},{2,6},{3,7},{4,0},{5,1},{6,2},{7,3},{8,12},{9,13},{10,... | collective-permute-start | bytes 589832 | tf_op jit(solution)/shard_map/ppermute | solution.py:333
  38.4 4.0 %collective-permute-start.9 = (f32[4,6,256]{2,1,0:T(8,128)S(1)}, f32[4,6,256]{2,1,0:T(8,128)S(1)}, u32[]{:S(2)}, u32[]{:S(2)}) collective-permute-start(f32[4,6,256]{2,1,0:T(8,128)S(1)} %pad_maximum_fusion.4), channel_id=1, source_target_pairs={{0,4},{1,5},{2,6},{3,7},{4,0},{5,1},{6,2},{7,3},{8,12},{9,13},{10,... | collective-permute-start | bytes 73736 | tf_op jit(solution)/shard_map/ppermute | solution.py:333
  42.4 5.1 %collective-permute-start.10 = (f32[4,6,256]{2,1,0:T(8,128)S(1)}, f32[4,6,256]{2,1,0:T(8,128)S(1)}, u32[]{:S(2)}, u32[]{:S(2)}) collective-permute-start(f32[4,6,256]{2,1,0:T(8,128)S(1)} %pad_maximum_fusion.6), channel_id=1, source_target_pairs={{0,8},{1,9},{2,10},{3,11},{4,12},{5,13},{6,14},{7,15},{8,0},{9,1},... | collective-permute-start | bytes 73736 | tf_op jit(solution)/shard_map/ppermute | solution.py:333
  47.7 9.3 %collective-permute-start.11 = (bf16[2,192,256]{2,1,0:T(8,128)(2,1)S(1)}, bf16[2,192,256]{2,1,0:T(8,128)(2,1)S(1)}, u32[]{:S(2)}, u32[]{:S(2)}) collective-permute-start(bf16[2,192,256]{2,1,0:T(8,128)(2,1)S(1)} %pad_maximum_fusion.1), channel_id=1, source_target_pairs={{0,8},{1,9},{2,10},{3,11},{4,12},{5,13},{6,14},{7,15},{8,0},{9,1},... | collective-permute-start | bytes 589832 | tf_op jit(solution)/shard_map/ppermute | solution.py:333
  55.3 14.8 %collective-permute-start.13 = (bf16[2,384,384]{2,1,0:T(8,128)(2,1)S(1)}, bf16[2,384,384]{2,1,0:T(8,128)(2,1)S(1)}, u32[]{:S(2)}, u32[]{:S(2)}) collective-permute-start(bf16[2,384,384]{2,1,0:T(8,128)(2,1)S(1)} %get-tuple-element.97), channel_id=1, source_target_pairs={{0,2},{1,3},{2,0},{3,1},{4,6},{5,7},{6,4},{7,5},{8,10},{9,11},{10,... | collective-permute-start | bytes 1769480 | tf_op jit(solution)/shard_map/ppermute | solution.py:333
  58.7 4.7 %collective-permute-start.14 = (bf16[192,256]{1,0:T(8,128)(2,1)S(1)}, bf16[192,256]{1,0:T(8,128)(2,1)S(1)}, u32[]{:S(2)}, u32[]{:S(2)}) collective-permute-start(bf16[192,256]{1,0:T(8,128)(2,1)S(1)} %bitcast.89), channel_id=1, source_target_pairs={{0,4},{1,5},{2,6},{3,7},{4,0},{5,1},{6,2},{7,3},{8,12},{9,13},{10,... | collective-permute-start | bytes 294920 | tf_op jit(solution)/shard_map/ppermute | solution.py:333
  59.5 8.7 %collective-permute-start.12 = (bf16[192,256]{1,0:T(8,128)(2,1)S(1)}, bf16[192,256]{1,0:T(8,128)(2,1)S(1)}, u32[]{:S(2)}, u32[]{:S(2)}) collective-permute-start(bf16[192,256]{1,0:T(8,128)(2,1)S(1)} %fusion.1), channel_id=1, source_target_pairs={{0,4},{1,5},{2,6},{3,7},{4,0},{5,1},{6,2},{7,3},{8,12},{9,13},{10,... | collective-permute-start | bytes 294920 | tf_op jit(solution)/shard_map/ppermute | solution.py:333
  63.4 6.6 %collective-permute-start.15 = (bf16[192,256]{1,0:T(8,128)(2,1)S(1)}, bf16[192,256]{1,0:T(8,128)(2,1)S(1)}, u32[]{:S(2)}, u32[]{:S(2)}) collective-permute-start(bf16[192,256]{1,0:T(8,128)(2,1)S(1)} %fusion.4), channel_id=1, source_target_pairs={{0,8},{1,9},{2,10},{3,11},{4,12},{5,13},{6,14},{7,15},{8,0},{9,1},... | collective-permute-start | bytes 294920 | tf_op jit(solution)/shard_map/ppermute | solution.py:333
  66.7 5.1 %collective-permute-start.16 = (bf16[192,256]{1,0:T(8,128)(2,1)S(1)}, bf16[192,256]{1,0:T(8,128)(2,1)S(1)}, u32[]{:S(2)}, u32[]{:S(2)}) collective-permute-start(bf16[192,256]{1,0:T(8,128)(2,1)S(1)} %bitcast.88), channel_id=1, source_target_pairs={{0,4},{1,5},{2,6},{3,7},{4,0},{5,1},{6,2},{7,3},{8,12},{9,13},{10,... | collective-permute-start | bytes 294920 | tf_op jit(solution)/shard_map/ppermute | solution.py:333
  72.0 2.1 %collective-permute-start.18 = (bf16[2,384,384]{2,1,0:T(8,128)(2,1)S(1)}, bf16[2,384,384]{2,1,0:T(8,128)(2,1)S(1)}, u32[]{:S(2)}, u32[]{:S(2)}) collective-permute-start(bf16[2,384,384]{2,1,0:T(8,128)(2,1)S(1)} %pad_maximum_fusion), channel_id=1, source_target_pairs={{0,1},{1,0},{2,3},{3,2},{4,5},{5,4},{6,7},{7,6},{8,9},{9,8},{10,11... | collective-permute-start | bytes 1769480 | tf_op jit(solution)/shard_map/ppermute | solution.py:333
  72.1 5.3 %collective-permute-start.17 = (bf16[2,192,128]{2,1,0:T(8,128)(2,1)S(1)}, bf16[2,192,128]{2,1,0:T(8,128)(2,1)S(1)}, u32[]{:S(2)}, u32[]{:S(2)}) collective-permute-start(bf16[2,192,128]{2,1,0:T(8,128)(2,1)S(1)} %get-tuple-element.119), channel_id=1, source_target_pairs={{0,2},{1,3},{2,0},{3,1},{4,6},{5,7},{6,4},{7,5},{8,10},{9,11},{10,... | collective-permute-start | bytes 294920 | tf_op jit(solution)/shard_map/ppermute | solution.py:333
  72.6 6.4 %copy-start.5 = (bf16[64,768]{1,0:T(8,128)(2,1)S(1)}, bf16[64,768]{1,0:T(8,128)(2,1)}, u32[]{:S(2)}) copy-start(bf16[64,768]{1,0:T(8,128)(2,1)} %latents_ref.1) | copy-start | bytes 294916
  72.6 6.4 %copy-start.6 = (bf16[64,768]{1,0:T(8,128)(2,1)S(1)}, bf16[64,768]{1,0:T(8,128)(2,1)}, u32[]{:S(2)}) copy-start(bf16[64,768]{1,0:T(8,128)(2,1)} %d_out_ref.1) | copy-start | bytes 294916
  77.5 1.5 %collective-permute-start.19 = (bf16[2,2,192,64]{3,2,1,0:T(8,128)(2,1)S(1)}, bf16[2,2,192,64]{3,2,1,0:T(8,128)(2,1)S(1)}, u32[]{:S(2)}, u32[]{:S(2)}) collective-permute-start(bf16[2,2,192,64]{3,2,1,0:T(8,128)(2,1)S(1)} %pad_maximum_fusion.3), channel_id=1, source_target_pairs={{0,1},{1,0},{2,3},{3,2},{4,5},{5,4},{6,7},{7,6},{8,9},{9,8},{10,11... | collective-permute-start | bytes 294920 | tf_op jit(solution)/shard_map/ppermute | solution.py:333
  (5 other events, 21.8 us)

commit v11 on v10

--- a/solution.py
+++ b/solution.py
@@ -269,17 +269,14 @@
             score(step)
 
 
-def queries_kernel(
-    place_ref, near_ref, far_ref, core_ref, latents_ref, d_out_ref, w_out_ref, w_query_ref,
-    result_ref, d_latents_ref, joined_ref
-):
-    own = latents_ref.shape[0]
-    mine = near_ref.shape[1]
+def queries_kernel(place_ref, *refs):
+    pieces, refs = refs[:TEAM], refs[TEAM:]
+    latents_ref, d_out_ref, w_out_ref, w_query_ref, result_ref, d_latents_ref, joined_ref = refs
+    mine = pieces[0].shape[1]
     for kind in range(2):
         for relative in range(TEAM):
-            core, across = relative % 2, relative // 2
             quarter = (place_ref[0] % TEAM) ^ relative
-            piece = core_ref[across, kind] if core else (near_ref, far_ref)[across][kind, :, :own]
+            piece = pieces[relative][kind]
             joined_ref[pl.ds(pl.multiple_of(quarter * mine, mine), mine), :] = piece.astype(F32)
         joined = joined_ref[...].T.astype(BF16)
         if kind == 0:
@@ -451,9 +448,8 @@
     partial, gkv_far = backward(order, 1, F32, last=True)
     came_a, partial = lax.optimization_barrier((came_a, partial))
     came_far = swap(gkv_far, 2)
-    near_a = swap(add(scaled(1), came_a[0]).astype(BF16), near_bit)
     gq, total = backward((3,), 0, BF16, partial=[partial])
-    came = swap(gq[0], near_bit)
+    came, near_a = swap(jnp.stack([gq[0], add(scaled(1), came_a[0]).astype(BF16)]), near_bit)
     gq, total = backward((2,), 0, F32, [total], [partial])
     sent, total = lax.optimization_barrier((add(gq[0], came).astype(BF16), total))
     far_q = swap(sent, far_bit)
@@ -469,8 +465,8 @@
         half = both.shape[-1] // 2
         both = add(both[..., :half], swap(both[..., half:].astype(BF16), mask))
     both, came_far = lax.optimization_barrier((both.astype(BF16), came_far))
-    far_both = swap(both[..., 2 * own :], 2)
-    near_both = both[..., : 2 * own]
+    pieces_both = [both[..., i * own : (i + 1) * own] for i in range(TEAM)]
+    pieces_both[1:] = [swap(pieces_both[i], i) for i in range(1, TEAM)]
 
     core_gkv = swap(jnp.stack([gkv_near[1], came_far[1]]), 1)
     (d_points,) = call(
@@ -479,11 +475,10 @@
         [shape((slots, width), BF16)],
         flops=4 * slots * width * width,
     )
-    far_both, d_points = lax.optimization_barrier((far_both, d_points))
-    core_both = swap(jnp.stack([near_both[..., own:], far_both[..., own:]]), 1)
+    *pieces_both, d_points = lax.optimization_barrier((*pieces_both, d_points))
     result, d_latents = call(
         queries_kernel,
-        [place, near_both, far_both, core_both, latents, d_out, w_out, w_query],
+        [place] + pieces_both + [latents, d_out, w_out, w_query],
         [shape((own, width), BF16)] * 2,
         [pltpu.VMEM((width, own), F32)],
         flops=4 * own * width * width,

time: 80.6 us -> 82.2 us (1.020)
  waiting for transfers between devices: 25 us -> 26.3 us
    ppermute x20, waiting for transfers between devices: 25 us -> 26.3 us  [swap(): return lax.ppermute(array, 'pts', [(i, i ^ mask) for i in range(size)])]
  transfers between devices with their start and end apart: 20 -> 20, of which waited for: 14 -> 12; matrix products, arithmetic and copies ran while one was open for 0% -> 0% of each run, Pallas kernels for 32% -> 31%
where the time goes in v11:
time: 82.2 us; the launch traced here: 82 us
  Pallas kernels  32.8 us (40%)
  waiting for transfers between devices  26.3 us (32%)
  starting transfers between devices  19.6 us (24%)
  between operations  1.62 us (2%)
  local copies, waits for them, and re-layouts  1.3 us (2%)
    pallas_call x19, Pallas kernels, call(): pl.pallas_call(kernel, in_specs=[smem if a.dtype == jnp.int32 else other...  32.8 us
    ppermute x20, waiting for transfers between devices, swap(): return lax.ppermute(array, 'pts', [(i, i ^ mask) for i in range(size)])  26.3 us
    ppermute x20, starting transfers between devices, swap(): return lax.ppermute(array, 'pts', [(i, i ^ mask) for i in range(size)])  19.6 us
  transfers between devices with their start and end apart: 20, of which 12 were waited for; matrix products, arithmetic and copies ran while one was open for 0% of the time, Pallas kernels for 31%

profile of v11, /device:TPU:0, one launch (start us, length us, event | category | flops | bytes accessed | tf_op | source)
XLA Modules:
  0.0 82.0 jit_solution(789291861891904947)
XLA Ops:
  1.3 3.5 %shard_map.103 = (bf16[80,384]{1,0:T(8,128)(2,1)}, bf16[80,384]{1,0:T(8,128)(2,1)}, bf16[2,80,384]{2,1,0:T(8,128)(2,1)}) custom-call(s32[1]{0:T(128)} %bitcast.place_ref, s32[1]{0:T(128)S(6)} %copy.11.count_ref, bf16[64,768]{1,0:T(8,128)(2,1)} %refs_4_.1, bf16[64,768]{1,0:T(8,128)(2,1)} %refs_5_.1, bf16[768,768]{1,0:T(8,128)(2,1)} %refs_7_.1, ...), custom_call_target="tpu_custom_call" | custom-call | flops 18874368 | bytes 350209 | tf_op jit(solution)/shard_map/pallas_call | solution.py:305
  4.8 3.0 %collective-permute-start.1 = (bf16[2,80,384]{2,1,0:T(8,128)(2,1)}, bf16[2,80,384]{2,1,0:T(8,128)(2,1)S(1)}, u32[]{:S(2)}, u32[]{:S(2)}) collective-permute-start(bf16[2,80,384]{2,1,0:T(8,128)(2,1)} %get-tuple-element.67), channel_id=1, source_target_pairs={{0,2},{1,3},{2,0},{3,1},{4,6},{5,7},{6,4},{7,5},{8,10},{9,11},{10,... | collective-permute-start | bytes 368648 | tf_op jit(solution)/shard_map/ppermute | solution.py:330
  8.9 1.6 %shard_map.104 = (bf16[384,384]{1,0:T(8,128)(2,1)S(1)}, bf16[384,384]{1,0:T(8,128)(2,1)S(1)}, bf16[2,384,384]{2,1,0:T(8,128)(2,1)S(1)}) custom-call(s32[1]{0:T(128)} %bitcast.place_ref, bf16[384,768]{1,0:T(8,128)(2,1)S(1)} %copy-done.4, bf16[768,768]{1,0:T(8,128)(2,1)S(1)} %copy-done.2, bf16[768,768]{1,0:T(8,128)(2,1)S(1)} %copy-done.3), custom_call_target="tpu_custom_call" | custom-call | flops 113246208 | bytes 516096 | tf_op jit(solution)/shard_map/pallas_call | solution.py:305
  11.3 1.7 %collective-permute-start.5 = (bf16[2,384,384]{2,1,0:T(8,128)(2,1)S(1)}, bf16[2,384,384]{2,1,0:T(8,128)(2,1)S(1)}, u32[]{:S(2)}, u32[]{:S(2)}) collective-permute-start(bf16[2,384,384]{2,1,0:T(8,128)(2,1)S(1)} %get-tuple-element.83), channel_id=1, source_target_pairs={{0,2},{1,3},{2,0},{3,1},{4,6},{5,7},{6,4},{7,5},{8,10},{9,11},{10,... | collective-permute-start | bytes 1769480 | tf_op jit(solution)/shard_map/ppermute | solution.py:330
  15.0 1.6 %collective-permute-start.4 = (bf16[256,384]{1,0:T(8,128)(2,1)S(1)}, bf16[256,384]{1,0:T(8,128)(2,1)S(1)}, u32[]{:S(2)}, u32[]{:S(2)}) collective-permute-start(bf16[256,384]{1,0:T(8,128)(2,1)S(1)} %get-tuple-element.73.qg_ref.refs_3_.refs_0_), channel_id=1, source_target_pairs={{0,4},{1,5},{2,6},{3,7},{4,0},{5,1},{6,2},{7,3},{8,12},{9,13},{10,... | collective-permute-start | bytes 589832 | tf_op jit(solution)/shard_map/ppermute | solution.py:330
  16.6 2.6 %collective-permute-start.6 = (bf16[256,384]{1,0:T(8,128)(2,1)S(1)}, bf16[256,384]{1,0:T(8,128)(2,1)S(1)}, u32[]{:S(2)}, u32[]{:S(2)}) collective-permute-start(bf16[256,384]{1,0:T(8,128)(2,1)S(1)} %get-tuple-element.73.qg_ref.refs_3_.refs_0_), channel_id=1, source_target_pairs={{0,8},{1,9},{2,10},{3,11},{4,12},{5,13},{6,14},{7,15},{8,0},{9,1},... | collective-permute-start | bytes 589832 | tf_op jit(solution)/shard_map/ppermute | solution.py:330
  21.4 4.9 %collective-permute-done.4.qg_ref.refs_2_.refs_0_ = bf16[256,384]{1,0:T(8,128)(2,1)S(1)} collective-permute-done((bf16[256,384]{1,0:T(8,128)(2,1)S(1)}, bf16[256,384]{1,0:T(8,128)(2,1)S(1)}, u32[]{:S(2)}, u32[]{:S(2)}) %collective-permute-start.4) | collective-permute-done | bytes 196640 | tf_op jit(solution)/shard_map/ppermute | solution.py:330
  29.1 1.6 %collective-permute-done.7.refs_1_.refs_4_.refs_9_ = bf16[2,384,384]{2,1,0:T(8,128)(2,1)S(1)} collective-permute-done((bf16[2,384,384]{2,1,0:T(8,128)(2,1)S(1)}, bf16[2,384,384]{2,1,0:T(8,128)(2,1)S(1)}, u32[]{:S(2)}, u32[]{:S(2)}) %collective-permute-start.7) | collective-permute-done | bytes 589856 | tf_op jit(solution)/shard_map/ppermute | solution.py:330
  30.9 2.3 %shard_map.113 = (f32[192,256]{1,0:T(8,128)S(1)}, f32[12,256]{1,0:T(8,128)S(1)}) custom-call(f32[4,128]{1,0:T(4,128)S(1)} %get-tuple-element.71.count_ref, bf16[256,384]{1,0:T(8,128)(2,1)S(1)} %collective-permute-done.6.qg_ref.refs_1_.refs_0_, bf16[384,384]{1,0:T(8,128)(2,1)S(1)} %get-tuple-element.74.refs_0_.refs_2_, ...), custom_call_target="tpu_custom_call" | custom-call | flops 150994944 | bytes 419584 | tf_op jit(solution)/shard_map/pallas_call | solution.py:305
  36.0 2.3 %shard_map.114 = (f32[192,256]{1,0:T(8,128)S(1)}, f32[12,256]{1,0:T(8,128)S(1)}) custom-call(f32[4,128]{1,0:T(4,128)S(1)} %get-tuple-element.71.count_ref, bf16[256,384]{1,0:T(8,128)(2,1)S(1)} %collective-permute-done.8.qg_ref.refs_0_, bf16[384,384]{1,0:T(8,128)(2,1)S(1)} %get-tuple-element.74.refs_0_.refs_2_, ...), custom_call_target="tpu_custom_call" | custom-call | flops 150994944 | bytes 419584 | tf_op jit(solution)/shard_map/pallas_call | solution.py:305
  38.9 3.5 %collective-permute-done.9 = f32[4,6,256]{2,1,0:T(8,128)S(1)} collective-permute-done((f32[4,6,256]{2,1,0:T(8,128)S(1)}, f32[4,6,256]{2,1,0:T(8,128)S(1)}, u32[]{:S(2)}, u32[]{:S(2)}) %collective-permute-start.9) | collective-permute-done | bytes 24608 | tf_op jit(solution)/shard_map/ppermute | solution.py:330
  43.8 3.8 %collective-permute-done.10 = f32[4,6,256]{2,1,0:T(8,128)S(1)} collective-permute-done((f32[4,6,256]{2,1,0:T(8,128)S(1)}, f32[4,6,256]{2,1,0:T(8,128)S(1)}, u32[]{:S(2)}, u32[]{:S(2)}) %collective-permute-start.10) | collective-permute-done | bytes 24608 | tf_op jit(solution)/shard_map/ppermute | solution.py:330
  48.8 6.4 %shard_map.115 = (f32[4,192,256]{2,1,0:T(8,128)S(1)}, bf16[2,384,384]{2,1,0:T(8,128)(2,1)S(1)}) custom-call(f32[4,128]{1,0:T(4,128)S(1)} %get-tuple-element.71.count_ref, bf16[256,384]{1,0:T(8,128)(2,1)S(1)} %collective-permute-done.8.qg_ref.refs_0_, bf16[256,384]{1,0:T(8,128)(2,1)S(1)} %collective-permute-done.6.qg_ref.refs_1_.refs_0_, ...), custom_call_target="tpu_custom_call" | custom-call | flops 528482304 | bytes 494848 | tf_op jit(solution)/shard_map/pallas_call | solution.py:305
  57.0 1.7 %shard_map.116 = (bf16[1,192,256]{2,1,0:T(8,128)(2,1)S(1)}, f32[2,384,384]{2,1,0:T(8,128)S(1)}) custom-call(f32[4,128]{1,0:T(4,128)S(1)} %get-tuple-element.71.count_ref, bf16[256,384]{1,0:T(8,128)(2,1)S(1)} %collective-permute-done.8.qg_ref.refs_0_, f32[6,256]{1,0:T(8,128)S(1)} %get-tuple-element.134.refs_4_.refs_1_, ...), custom_call_target="tpu_custom_call" | custom-call | flops 132120576 | bytes 431104 | tf_op jit(solution)/shard_map/pallas_call | solution.py:305
  59.5 1.7 %shard_map.117 = (f32[1,192,256]{2,1,0:T(8,128)S(1)}, f32[2,384,384]{2,1,0:T(8,128)S(1)}) custom-call(f32[4,128]{1,0:T(4,128)S(1)} %get-tuple-element.71.count_ref, bf16[256,384]{1,0:T(8,128)(2,1)S(1)} %collective-permute-done.6.qg_ref.refs_1_.refs_0_, f32[6,256]{1,0:T(8,128)S(1)} %get-tuple-element.135.refs_5_.refs_1_, ...), custom_call_target="tpu_custom_call" | custom-call | flops 132120576 | bytes 590848 | tf_op jit(solution)/shard_map/pallas_call | solution.py:305
  61.2 3.3 %collective-permute-done.12 = bf16[2,192,256]{2,1,0:T(8,128)(2,1)S(1)} collective-permute-done((bf16[2,192,256]{2,1,0:T(8,128)(2,1)S(1)}, bf16[2,192,256]{2,1,0:T(8,128)(2,1)S(1)}, u32[]{:S(2)}, u32[]{:S(2)}) %collective-permute-start.12) | collective-permute-done | bytes 196640 | tf_op jit(solution)/shard_map/ppermute | solution.py:330
  65.5 1.7 %shard_map.118 = (bf16[1,192,256]{2,1,0:T(8,128)(2,1)S(1)}, f32[2,384,384]{2,1,0:T(8,128)S(1)}) custom-call(f32[4,128]{1,0:T(4,128)S(1)} %get-tuple-element.71.count_ref, bf16[256,384]{1,0:T(8,128)(2,1)S(1)} %collective-permute-done.4.qg_ref.refs_2_.refs_0_, f32[6,256]{1,0:T(8,128)S(1)} %get-tuple-element.136.refs_6_.refs_1_, ...), custom_call_target="tpu_custom_call" | custom-call | flops 132120576 | bytes 578560 | tf_op jit(solution)/shard_map/pallas_call | solution.py:305
  67.3 1.9 %collective-permute-start.15 = (bf16[192,256]{1,0:T(8,128)(2,1)S(1)}, bf16[192,256]{1,0:T(8,128)(2,1)S(1)}, u32[]{:S(2)}, u32[]{:S(2)}) collective-permute-start(bf16[192,256]{1,0:T(8,128)(2,1)S(1)} %bitcast.85), channel_id=1, source_target_pairs={{0,4},{1,5},{2,6},{3,7},{4,0},{5,1},{6,2},{7,3},{8,12},{9,13},{10,... | collective-permute-start | bytes 294920 | tf_op jit(solution)/shard_map/ppermute | solution.py:330
  69.3 1.9 %collective-permute-done.14 = bf16[192,256]{1,0:T(8,128)(2,1)S(1)} collective-permute-done((bf16[192,256]{1,0:T(8,128)(2,1)S(1)}, bf16[192,256]{1,0:T(8,128)(2,1)S(1)}, u32[]{:S(2)}, u32[]{:S(2)}) %collective-permute-start.14) | collective-permute-done | bytes 98336 | tf_op jit(solution)/shard_map/ppermute | solution.py:330
  71.1 1.7 %shard_map.119 = (f32[1,192,256]{2,1,0:T(8,128)S(1)}, bf16[2,384,384]{2,1,0:T(8,128)(2,1)S(1)}) custom-call(f32[4,128]{1,0:T(4,128)S(1)} %get-tuple-element.71.count_ref, bf16[256,384]{1,0:T(8,128)(2,1)S(1)} %get-tuple-element.73.qg_ref.refs_3_.refs_0_, f32[6,256]{1,0:T(8,128)S(1)} %get-tuple-element.133.refs_7_.refs_1_, ...), custom_call_target="tpu_custom_call" | custom-call | flops 132120576 | bytes 517120 | tf_op jit(solution)/shard_map/pallas_call | solution.py:305
  73.8 1.7 %collective-permute-start.17 = (bf16[2,192,64]{2,1,0:T(8,128)(2,1)S(1)}, bf16[2,192,64]{2,1,0:T(8,128)(2,1)S(1)}, u32[]{:S(2)}, u32[]{:S(2)}) collective-permute-start(bf16[2,192,64]{2,1,0:T(8,128)(2,1)S(1)} %get-tuple-element.126), channel_id=1, source_target_pairs={{0,2},{1,3},{2,0},{3,1},{4,6},{5,7},{6,4},{7,5},{8,10},{9,11},{10,... | collective-permute-start | bytes 147464 | tf_op jit(solution)/shard_map/ppermute | solution.py:330
  75.6 2.2 %shard_map.120 = bf16[384,768]{1,0:T(8,128)(2,1)} custom-call(s32[1]{0:T(128)} %bitcast.place_ref, bf16[2,384,384]{2,1,0:T(8,128)(2,1)S(1)} %get-tuple-element.115.near_ref, bf16[2,384,384]{2,1,0:T(8,128)(2,1)S(1)} %collective-permute-done.13.far_ref, bf16[2,384,384]{2,1,0:T(8,128)(2,1)S(1)} %collective-permute-done.19.core_ref, ...), custom_call_target="tpu_custom_call" | custom-call | flops 113246208 | bytes 589824 | tf_op jit(solution)/shard_map/pallas_call | solution.py:305
  77.8 2.7 %collective-permute-done.17.refs_2_ = bf16[2,192,64]{2,1,0:T(8,128)(2,1)S(1)} collective-permute-done((bf16[2,192,64]{2,1,0:T(8,128)(2,1)S(1)}, bf16[2,192,64]{2,1,0:T(8,128)(2,1)S(1)}, u32[]{:S(2)}, u32[]{:S(2)}) %collective-permute-start.17) | collective-permute-done | bytes 49184 | tf_op jit(solution)/shard_map/ppermute | solution.py:330
  80.6 1.4 %shard_map.121 = (bf16[64,768]{1,0:T(8,128)(2,1)}, bf16[64,768]{1,0:T(8,128)(2,1)}) custom-call(s32[1]{0:T(128)} %bitcast.place_ref, bf16[2,192,64]{2,1,0:T(8,128)(2,1)S(1)} %get-tuple-element.118.refs_0_, bf16[2,192,64]{2,1,0:T(8,128)(2,1)S(1)} %collective-permute-done.16.refs_1_, bf16[2,192,64]{2,1,0:T(8,128)(2,1)S(1)} %collective-permute-done.17.refs_2_, ...), custom_call_target="tpu_custom_call" | custom-call | flops 18874368 | bytes 368640 | tf_op jit(solution)/shard_map/pallas_call | solution.py:305
  (77 shorter events, 19.6 us)
Async XLA Ops:
  1.3 6.5 %copy-start.2 = (bf16[768,768]{1,0:T(8,128)(2,1)S(1)}, bf16[768,768]{1,0:T(8,128)(2,1)}, u32[]{:S(2)}) copy-start(bf16[768,768]{1,0:T(8,128)(2,1)} %w_key_ref.2) | copy-start | bytes 3538948
  1.3 6.5 %copy-start.3 = (bf16[768,768]{1,0:T(8,128)(2,1)S(1)}, bf16[768,768]{1,0:T(8,128)(2,1)}, u32[]{:S(2)}) copy-start(bf16[768,768]{1,0:T(8,128)(2,1)} %w_value_ref.2) | copy-start | bytes 3538948
  4.8 6.5 %collective-permute-start.1 = (bf16[2,80,384]{2,1,0:T(8,128)(2,1)}, bf16[2,80,384]{2,1,0:T(8,128)(2,1)S(1)}, u32[]{:S(2)}, u32[]{:S(2)}) collective-permute-start(bf16[2,80,384]{2,1,0:T(8,128)(2,1)} %get-tuple-element.67), channel_id=1, source_target_pairs={{0,2},{1,3},{2,0},{3,1},{4,6},{5,7},{6,4},{7,5},{8,10},{9,11},{10,... | collective-permute-start | bytes 368648 | tf_op jit(solution)/shard_map/ppermute | solution.py:330
  8.9 6.1 %copy-start.7 = (bf16[80,384]{1,0:T(8,128)(2,1)S(1)}, bf16[80,384]{1,0:T(8,128)(2,1)}, u32[]{:S(2)}) copy-start(bf16[80,384]{1,0:T(8,128)(2,1)} %get-tuple-element.65.keep_ref) | copy-start | bytes 184324
  11.3 17.3 %collective-permute-start.5 = (bf16[2,384,384]{2,1,0:T(8,128)(2,1)S(1)}, bf16[2,384,384]{2,1,0:T(8,128)(2,1)S(1)}, u32[]{:S(2)}, u32[]{:S(2)}) collective-permute-start(bf16[2,384,384]{2,1,0:T(8,128)(2,1)S(1)} %get-tuple-element.83), channel_id=1, source_target_pairs={{0,2},{1,3},{2,0},{3,1},{4,6},{5,7},{6,4},{7,5},{8,10},{9,11},{10,... | collective-permute-start | bytes 1769480 | tf_op jit(solution)/shard_map/ppermute | solution.py:330
  13.1 1.8 %collective-permute-start.2 = (bf16[2,80,384]{2,1,0:T(8,128)(2,1)S(1)}, bf16[2,80,384]{2,1,0:T(8,128)(2,1)S(1)}, u32[]{:S(2)}, u32[]{:S(2)}) collective-permute-start(bf16[2,80,384]{2,1,0:T(8,128)(2,1)S(1)} %collective-permute-done.1.far_ref), channel_id=1, source_target_pairs={{0,1},{1,0},{2,3},{3,2},{4,5},{5,4},{6,7},{7,6},{8,9},{9,8},{10,11... | collective-permute-start | bytes 368648 | tf_op jit(solution)/shard_map/ppermute | solution.py:330
  13.1 6.8 %collective-permute-start.3 = (bf16[384,384]{1,0:T(8,128)(2,1)S(1)}, bf16[384,384]{1,0:T(8,128)(2,1)S(1)}, u32[]{:S(2)}, u32[]{:S(2)}) collective-permute-start(bf16[384,384]{1,0:T(8,128)(2,1)S(1)} %get-tuple-element.75), channel_id=1, source_target_pairs={{0,1},{1,0},{2,3},{3,2},{4,5},{5,4},{6,7},{7,6},{8,9},{9,8},{10,11... | collective-permute-start | bytes 884744 | tf_op jit(solution)/shard_map/ppermute | solution.py:330
  13.6 1.3 %collective-permute-start = (bf16[80,384]{1,0:T(8,128)(2,1)S(1)}, bf16[80,384]{1,0:T(8,128)(2,1)S(1)}, u32[]{:S(2)}, u32[]{:S(2)}) collective-permute-start(bf16[80,384]{1,0:T(8,128)(2,1)S(1)} %copy-done.8), channel_id=1, source_target_pairs={{0,1},{1,0},{2,3},{3,2},{4,5},{5,4},{6,7},{7,6},{8,9},{9,8},{10,11... | collective-permute-start | bytes 184328 | tf_op jit(solution)/shard_map/ppermute | solution.py:330
  15.0 11.3 %collective-permute-start.4 = (bf16[256,384]{1,0:T(8,128)(2,1)S(1)}, bf16[256,384]{1,0:T(8,128)(2,1)S(1)}, u32[]{:S(2)}, u32[]{:S(2)}) collective-permute-start(bf16[256,384]{1,0:T(8,128)(2,1)S(1)} %get-tuple-element.73.qg_ref.refs_3_.refs_0_), channel_id=1, source_target_pairs={{0,4},{1,5},{2,6},{3,7},{4,0},{5,1},{6,2},{7,3},{8,12},{9,13},{10,... | collective-permute-start | bytes 589832 | tf_op jit(solution)/shard_map/ppermute | solution.py:330
  16.6 12.0 %collective-permute-start.6 = (bf16[256,384]{1,0:T(8,128)(2,1)S(1)}, bf16[256,384]{1,0:T(8,128)(2,1)S(1)}, u32[]{:S(2)}, u32[]{:S(2)}) collective-permute-start(bf16[256,384]{1,0:T(8,128)(2,1)S(1)} %get-tuple-element.73.qg_ref.refs_3_.refs_0_), channel_id=1, source_target_pairs={{0,8},{1,9},{2,10},{3,11},{4,12},{5,13},{6,14},{7,15},{8,0},{9,1},... | collective-permute-start | bytes 589832 | tf_op jit(solution)/shard_map/ppermute | solution.py:330
  28.7 2.0 %collective-permute-start.7 = (bf16[2,384,384]{2,1,0:T(8,128)(2,1)S(1)}, bf16[2,384,384]{2,1,0:T(8,128)(2,1)S(1)}, u32[]{:S(2)}, u32[]{:S(2)}) collective-permute-start(bf16[2,384,384]{2,1,0:T(8,128)(2,1)S(1)} %collective-permute-done.5.refs_0_.refs_3_.refs_8_), channel_id=1, source_target_pairs={{0,1},{1,0},{2,3},{3,2},{4,5},{5,4},{6,7},{7,6},{8,9},{9,8},{10,11... | collective-permute-start | bytes 1769480 | tf_op jit(solution)/shard_map/ppermute | solution.py:330
  28.7 7.3 %collective-permute-start.8 = (bf16[256,384]{1,0:T(8,128)(2,1)S(1)}, bf16[256,384]{1,0:T(8,128)(2,1)S(1)}, u32[]{:S(2)}, u32[]{:S(2)}) collective-permute-start(bf16[256,384]{1,0:T(8,128)(2,1)S(1)} %collective-permute-done.6.qg_ref.refs_1_.refs_0_), channel_id=1, source_target_pairs={{0,4},{1,5},{2,6},{3,7},{4,0},{5,1},{6,2},{7,3},{8,12},{9,13},{10,... | collective-permute-start | bytes 589832 | tf_op jit(solution)/shard_map/ppermute | solution.py:330
  38.4 4.0 %collective-permute-start.9 = (f32[4,6,256]{2,1,0:T(8,128)S(1)}, f32[4,6,256]{2,1,0:T(8,128)S(1)}, u32[]{:S(2)}, u32[]{:S(2)}) collective-permute-start(f32[4,6,256]{2,1,0:T(8,128)S(1)} %pad_maximum_fusion.4), channel_id=1, source_target_pairs={{0,4},{1,5},{2,6},{3,7},{4,0},{5,1},{6,2},{7,3},{8,12},{9,13},{10,... | collective-permute-start | bytes 73736 | tf_op jit(solution)/shard_map/ppermute | solution.py:330
  42.4 5.1 %collective-permute-start.10 = (f32[4,6,256]{2,1,0:T(8,128)S(1)}, f32[4,6,256]{2,1,0:T(8,128)S(1)}, u32[]{:S(2)}, u32[]{:S(2)}) collective-permute-start(f32[4,6,256]{2,1,0:T(8,128)S(1)} %pad_maximum_fusion.6), channel_id=1, source_target_pairs={{0,8},{1,9},{2,10},{3,11},{4,12},{5,13},{6,14},{7,15},{8,0},{9,1},... | collective-permute-start | bytes 73736 | tf_op jit(solution)/shard_map/ppermute | solution.py:330
  47.7 9.3 %collective-permute-start.11 = (bf16[2,192,256]{2,1,0:T(8,128)(2,1)S(1)}, bf16[2,192,256]{2,1,0:T(8,128)(2,1)S(1)}, u32[]{:S(2)}, u32[]{:S(2)}) collective-permute-start(bf16[2,192,256]{2,1,0:T(8,128)(2,1)S(1)} %pad_maximum_fusion.1), channel_id=1, source_target_pairs={{0,8},{1,9},{2,10},{3,11},{4,12},{5,13},{6,14},{7,15},{8,0},{9,1},... | collective-permute-start | bytes 589832 | tf_op jit(solution)/shard_map/ppermute | solution.py:330
  55.3 15.9 %collective-permute-start.13 = (bf16[2,384,384]{2,1,0:T(8,128)(2,1)S(1)}, bf16[2,384,384]{2,1,0:T(8,128)(2,1)S(1)}, u32[]{:S(2)}, u32[]{:S(2)}) collective-permute-start(bf16[2,384,384]{2,1,0:T(8,128)(2,1)S(1)} %get-tuple-element.102), channel_id=1, source_target_pairs={{0,2},{1,3},{2,0},{3,1},{4,6},{5,7},{6,4},{7,5},{8,10},{9,11},{10,... | collective-permute-start | bytes 1769480 | tf_op jit(solution)/shard_map/ppermute | solution.py:330
  58.7 5.7 %collective-permute-start.12 = (bf16[2,192,256]{2,1,0:T(8,128)(2,1)S(1)}, bf16[2,192,256]{2,1,0:T(8,128)(2,1)S(1)}, u32[]{:S(2)}, u32[]{:S(2)}) collective-permute-start(bf16[2,192,256]{2,1,0:T(8,128)(2,1)S(1)} %pad_maximum_fusion.2), channel_id=1, source_target_pairs={{0,4},{1,5},{2,6},{3,7},{4,0},{5,1},{6,2},{7,3},{8,12},{9,13},{10,... | collective-permute-start | bytes 589832 | tf_op jit(solution)/shard_map/ppermute | solution.py:330
  64.5 6.6 %collective-permute-start.14 = (bf16[192,256]{1,0:T(8,128)(2,1)S(1)}, bf16[192,256]{1,0:T(8,128)(2,1)S(1)}, u32[]{:S(2)}, u32[]{:S(2)}) collective-permute-start(bf16[192,256]{1,0:T(8,128)(2,1)S(1)} %fusion.6), channel_id=1, source_target_pairs={{0,8},{1,9},{2,10},{3,11},{4,12},{5,13},{6,14},{7,15},{8,0},{9,1},... | collective-permute-start | bytes 294920 | tf_op jit(solution)/shard_map/ppermute | solution.py:330
  67.3 5.6 %collective-permute-start.15 = (bf16[192,256]{1,0:T(8,128)(2,1)S(1)}, bf16[192,256]{1,0:T(8,128)(2,1)S(1)}, u32[]{:S(2)}, u32[]{:S(2)}) collective-permute-start(bf16[192,256]{1,0:T(8,128)(2,1)S(1)} %bitcast.85), channel_id=1, source_target_pairs={{0,4},{1,5},{2,6},{3,7},{4,0},{5,1},{6,2},{7,3},{8,12},{9,13},{10,... | collective-permute-start | bytes 294920 | tf_op jit(solution)/shard_map/ppermute | solution.py:330
  73.1 2.5 %collective-permute-start.19 = (bf16[2,384,384]{2,1,0:T(8,128)(2,1)S(1)}, bf16[2,384,384]{2,1,0:T(8,128)(2,1)S(1)}, u32[]{:S(2)}, u32[]{:S(2)}) collective-permute-start(bf16[2,384,384]{2,1,0:T(8,128)(2,1)S(1)} %pad_maximum_fusion), channel_id=1, source_target_pairs={{0,1},{1,0},{2,3},{3,2},{4,5},{5,4},{6,7},{7,6},{8,9},{9,8},{10,11... | collective-permute-start | bytes 1769480 | tf_op jit(solution)/shard_map/ppermute | solution.py:330
  73.3 4.5 %collective-permute-start.18 = (bf16[2,192,64]{2,1,0:T(8,128)(2,1)S(1)}, bf16[2,192,64]{2,1,0:T(8,128)(2,1)S(1)}, u32[]{:S(2)}, u32[]{:S(2)}) collective-permute-start(bf16[2,192,64]{2,1,0:T(8,128)(2,1)S(1)} %get-tuple-element.125), channel_id=1, source_target_pairs={{0,3},{1,2},{2,1},{3,0},{4,7},{5,6},{6,5},{7,4},{8,11},{9,10},{10,... | collective-permute-start | bytes 147464 | tf_op jit(solution)/shard_map/ppermute | solution.py:330
  73.8 6.8 %collective-permute-start.17 = (bf16[2,192,64]{2,1,0:T(8,128)(2,1)S(1)}, bf16[2,192,64]{2,1,0:T(8,128)(2,1)S(1)}, u32[]{:S(2)}, u32[]{:S(2)}) collective-permute-start(bf16[2,192,64]{2,1,0:T(8,128)(2,1)S(1)} %get-tuple-element.126), channel_id=1, source_target_pairs={{0,2},{1,3},{2,0},{3,1},{4,6},{5,7},{6,4},{7,5},{8,10},{9,11},{10,... | collective-permute-start | bytes 147464 | tf_op jit(solution)/shard_map/ppermute | solution.py:330
  75.5 5.1 %copy-start.6 = (bf16[64,768]{1,0:T(8,128)(2,1)S(1)}, bf16[64,768]{1,0:T(8,128)(2,1)}, u32[]{:S(2)}) copy-start(bf16[64,768]{1,0:T(8,128)(2,1)} %refs_5_.1) | copy-start | bytes 294916
  75.5 5.1 %collective-permute-start.16 = (bf16[2,192,64]{2,1,0:T(8,128)(2,1)S(1)}, bf16[2,192,64]{2,1,0:T(8,128)(2,1)S(1)}, u32[]{:S(2)}, u32[]{:S(2)}) collective-permute-start(bf16[2,192,64]{2,1,0:T(8,128)(2,1)S(1)} %get-tuple-element.127), channel_id=1, source_target_pairs={{0,1},{1,0},{2,3},{3,2},{4,5},{5,4},{6,7},{7,6},{8,9},{9,8},{10,11... | collective-permute-start | bytes 147464 | tf_op jit(solution)/shard_map/ppermute | solution.py:330
  (5 other events, 21.0 us)

commit v12 on v10

--- a/solution.py
+++ b/solution.py
@@ -49,6 +49,9 @@
             @pl.when(relative == which)
             def _():
                 ref[at, :] = piece
+
+        if far_ref is None:
+            continue
 
         @pl.when(relative >= 2)
         def _():
@@ -95,10 +98,10 @@
     store_quarters(place_ref, (keep_ref, core_ref), far_ref, query, grad, slice(0, own))
 
 
-def slots_kernel(place_ref, points_ref, w_key_ref, w_value_ref, keep_ref, core_ref, far_ref):
+def slots_kernel(place_ref, points_ref, w_key_ref, w_value_ref, *piece_refs):
     keys = dot(points_ref[...], w_key_ref[...]).astype(BF16) * jnp.asarray(0.125, BF16)
     values = dot(points_ref[...], w_value_ref[...]).astype(BF16)
-    store_quarters(place_ref, (keep_ref, core_ref), far_ref, keys, values, slice(0, keys.shape[0]))
+    store_quarters(place_ref, piece_refs, None, keys, values, slice(0, keys.shape[0]))
 
 
 def weights_kernel(w_key_ref, w_value_ref, out_ref):
@@ -135,7 +138,7 @@
         kv_t_refs.update({0: near_t_ref.at[0], 1: near_t_ref.at[1]})
     if 2 in blocks:
         far_ref, diagonal_ref, far_t_ref, *refs = refs
-        kv_refs.update({2: far_ref.at[0], 3: diagonal_ref.at[1]})
+        kv_refs.update({2: far_ref, 3: diagonal_ref})
         kv_t_refs.update({2: far_t_ref.at[0], 3: far_t_ref.at[1]})
     before = refs[:2] if blocks[0] else ()
     numer_ref, stat_ref, score_ref, weight_ref = refs[len(before) :]
@@ -197,7 +200,7 @@
 def backward_kernel(chunks, start, side, first, last, count_ref, *refs):
     qg_refs, stat_refs, refs = refs[:chunks], refs[chunks : 2 * chunks], refs[2 * chunks :]
     even_ref, odd_ref, kv_t_ref, *refs = refs
-    kv_refs = (even_ref.at[0], odd_ref.at[1]) if side else (even_ref, odd_ref)
+    kv_refs = even_ref, odd_ref
     if not first:
         sum_in_ref, *refs = refs
     gq_in_ref = None
@@ -348,10 +351,11 @@
     keep_qg, then_place = lax.optimization_barrier((keep_qg, place))
     far_qg = swap(far_qg, 2)
     core_qg = swap(core_qg, 1)
-    keep, core, far = call(
-        slots_kernel, [then_place, points, w_key, w_value], pieces(slots), flops=4 * slots * width * width
+    keep, core, far, diagonal = call(
+        slots_kernel, [then_place, points, w_key, w_value], [shape((slots, 2 * mine), BF16)] * 4, flops=4 * slots * width * width
     )
-    far_qg, far = lax.optimization_barrier((far_qg, far))
+    far_qg, diagonal = lax.optimization_barrier((far_qg, diagonal))
+    diagonal = swap(diagonal, 2)
     far = swap(far, 2)
     core = swap(core, 1)
     qg, count = call(
@@ -367,7 +371,7 @@
     (weights,) = call(weights_kernel, [w_key, w_value], [shape((TEAM, 2 * mine, width), BF16)])
     turned = [shape((2, 2 * mine, slots), BF16)]
     (near_t,) = call(functools.partial(turn_kernel, ((0, None), (1, None))), [keep, core], turned)
-    near_t, weights = lax.optimization_barrier((near_t, weights))
+    near_t, weights, diagonal = lax.optimization_barrier((near_t, weights, diagonal))
     rows = qg[0].shape[0]
     team_slots = TEAM * slots
     work = 2 * rows * team_slots * mine
@@ -388,8 +392,8 @@
     early = [forward(p, (0, 1)) for p in range(2)]
     early, far, qg[2] = lax.optimization_barrier((early, far, qg[2]))
     qg.append(swap(qg[2], near_bit))
-    diagonal = swap(far, 1)
-    (far_t,) = call(functools.partial(turn_kernel, ((0, 0), (1, 1))), [far, diagonal], turned)
+    diagonal = swap(diagonal, 1)
+    (far_t,) = call(functools.partial(turn_kernel, ((0, None), (1, None))), [far, diagonal], turned)
     done = [forward(p, (2, 3), early[p]) for p in range(2)]
     done += [forward(p, (0, 1, 2, 3)) for p in (2, 3)]
     numer = [d[0] for d in done]

time: 80.6 us -> 87.8 us (1.089)
  waiting for transfers between devices: 25 us -> 29 us
  starting transfers between devices: 19.2 us -> 22.4 us
    ppermute x20 -> x21, waiting for transfers between devices: 25 us -> 29 us  [swap(): return lax.ppermute(array, 'pts', [(i, i ^ mask) for i in range(size)])]
    ppermute x20 -> x21, starting transfers between devices: 19.2 us -> 22.4 us  [swap(): return lax.ppermute(array, 'pts', [(i, i ^ mask) for i in range(size)])]
  transfers between devices with their start and end apart: 20 -> 21, of which waited for: 14 -> 13; matrix products, arithmetic and copies ran while one was open for 0% -> 0% of each run, Pallas kernels for 32% -> 29%
where the time goes in v12:
time: 87.8 us; the launch traced here: 87.6 us
  Pallas kernels  32.8 us (37%)
  waiting for transfers between devices  29 us (33%)
  starting transfers between devices  22.4 us (26%)
  between operations  1.65 us (2%)
  local copies, waits for them, and re-layouts  1.4 us (2%)
    pallas_call x19, Pallas kernels, call(): pl.pallas_call(kernel, in_specs=[smem if a.dtype == jnp.int32 else other...  32.8 us
    ppermute x21, waiting for transfers between devices, swap(): return lax.ppermute(array, 'pts', [(i, i ^ mask) for i in range(size)])  29 us
    ppermute x21, starting transfers between devices, swap(): return lax.ppermute(array, 'pts', [(i, i ^ mask) for i in range(size)])  22.4 us
  transfers between devices with their start and end apart: 21, of which 13 were waited for; matrix products, arithmetic and copies ran while one was open for 0% of the time, Pallas kernels for 29%

profile of v12, /device:TPU:0, one launch (start us, length us, event | category | flops | bytes accessed | tf_op | source)
XLA Modules:
  0.0 87.6 jit_solution(12527858401290464683)
XLA Ops:
  1.3 3.5 %shard_map.103 = (bf16[80,384]{1,0:T(8,128)(2,1)}, bf16[80,384]{1,0:T(8,128)(2,1)}, bf16[2,80,384]{2,1,0:T(8,128)(2,1)}) custom-call(s32[1]{0:T(128)} %bitcast.place_ref, s32[1]{0:T(128)S(6)} %copy.11.count_ref, bf16[64,768]{1,0:T(8,128)(2,1)} %latents_ref.1, bf16[64,768]{1,0:T(8,128)(2,1)} %d_out_ref.1, bf16[768,768]{1,0:T(8,128)(2,1)} %w_query_ref.1, ...), custom_call_target="tpu_custom_call" | custom-call | flops 18874368 | bytes 350209 | tf_op jit(solution)/shard_map/pallas_call | solution.py:311
  4.8 3.0 %collective-permute-start.1 = (bf16[2,80,384]{2,1,0:T(8,128)(2,1)}, bf16[2,80,384]{2,1,0:T(8,128)(2,1)S(1)}, u32[]{:S(2)}, u32[]{:S(2)}) collective-permute-start(bf16[2,80,384]{2,1,0:T(8,128)(2,1)} %get-tuple-element.66), channel_id=1, source_target_pairs={{0,2},{1,3},{2,0},{3,1},{4,6},{5,7},{6,4},{7,5},{8,10},{9,11},{10,... | collective-permute-start | bytes 368648 | tf_op jit(solution)/shard_map/ppermute | solution.py:336
  8.9 1.6 %shard_map.104 = (bf16[384,384]{1,0:T(8,128)(2,1)S(1)}, bf16[384,384]{1,0:T(8,128)(2,1)S(1)}, bf16[384,384]{1,0:T(8,128)(2,1)S(1)}, bf16[384,384]{1,0:T(8,128)(2,1)S(1)}) custom-call(s32[1]{0:T(128)} %bitcast.place_ref, bf16[384,768]{1,0:T(8,128)(2,1)S(1)} %copy-done.4, bf16[768,768]{1,0:T(8,128)(2,1)S(1)} %copy-done.2, bf16[768,768]{1,0:T(8,128)(2,1)S(1)} %copy-done.3), custom_call_target="tpu_custom_call" | custom-call | flops 113246208 | bytes 516096 | tf_op jit(solution)/shard_map/pallas_call | solution.py:311
  11.3 1.7 %collective-permute-start.4 = (bf16[384,384]{1,0:T(8,128)(2,1)S(1)}, bf16[384,384]{1,0:T(8,128)(2,1)S(1)}, u32[]{:S(2)}, u32[]{:S(2)}) collective-permute-start(bf16[384,384]{1,0:T(8,128)(2,1)S(1)} %get-tuple-element.77), channel_id=1, source_target_pairs={{0,2},{1,3},{2,0},{3,1},{4,6},{5,7},{6,4},{7,5},{8,10},{9,11},{10,... | collective-permute-start | bytes 884744 | tf_op jit(solution)/shard_map/ppermute | solution.py:336
  15.5 5.8 %collective-permute-done.4 = bf16[384,384]{1,0:T(8,128)(2,1)S(1)} collective-permute-done((bf16[384,384]{1,0:T(8,128)(2,1)S(1)}, bf16[384,384]{1,0:T(8,128)(2,1)S(1)}, u32[]{:S(2)}, u32[]{:S(2)}) %collective-permute-start.4) | collective-permute-done | bytes 294944 | tf_op jit(solution)/shard_map/ppermute | solution.py:336
  21.2 1.9 %collective-permute-start.5 = (bf16[256,384]{1,0:T(8,128)(2,1)S(1)}, bf16[256,384]{1,0:T(8,128)(2,1)S(1)}, u32[]{:S(2)}, u32[]{:S(2)}) collective-permute-start(bf16[256,384]{1,0:T(8,128)(2,1)S(1)} %get-tuple-element.72.qg_ref.refs_3_.refs_0_), channel_id=1, source_target_pairs={{0,4},{1,5},{2,6},{3,7},{4,0},{5,1},{6,2},{7,3},{8,12},{9,13},{10,... | collective-permute-start | bytes 589832 | tf_op jit(solution)/shard_map/ppermute | solution.py:336
  23.1 2.6 %collective-permute-start.7 = (bf16[256,384]{1,0:T(8,128)(2,1)S(1)}, bf16[256,384]{1,0:T(8,128)(2,1)S(1)}, u32[]{:S(2)}, u32[]{:S(2)}) collective-permute-start(bf16[256,384]{1,0:T(8,128)(2,1)S(1)} %get-tuple-element.72.qg_ref.refs_3_.refs_0_), channel_id=1, source_target_pairs={{0,8},{1,9},{2,10},{3,11},{4,12},{5,13},{6,14},{7,15},{8,0},{9,1},... | collective-permute-start | bytes 589832 | tf_op jit(solution)/shard_map/ppermute | solution.py:336
  26.9 5.8 %collective-permute-done.5.qg_ref.refs_2_.refs_0_ = bf16[256,384]{1,0:T(8,128)(2,1)S(1)} collective-permute-done((bf16[256,384]{1,0:T(8,128)(2,1)S(1)}, bf16[256,384]{1,0:T(8,128)(2,1)S(1)}, u32[]{:S(2)}, u32[]{:S(2)}) %collective-permute-start.5) | collective-permute-done | bytes 196640 | tf_op jit(solution)/shard_map/ppermute | solution.py:336
  35.9 2.4 %shard_map.113 = (f32[192,256]{1,0:T(8,128)S(1)}, f32[12,256]{1,0:T(8,128)S(1)}) custom-call(f32[4,128]{1,0:T(4,128)S(1)} %get-tuple-element.70.count_ref, bf16[256,384]{1,0:T(8,128)(2,1)S(1)} %collective-permute-done.7.qg_ref.refs_1_.refs_0_, bf16[384,384]{1,0:T(8,128)(2,1)S(1)} %get-tuple-element.73.refs_0_.refs_2_, ...), custom_call_target="tpu_custom_call" | custom-call | flops 150994944 | bytes 345856 | tf_op jit(solution)/shard_map/pallas_call | solution.py:311
  41.0 2.4 %shard_map.114 = (f32[192,256]{1,0:T(8,128)S(1)}, f32[12,256]{1,0:T(8,128)S(1)}) custom-call(f32[4,128]{1,0:T(4,128)S(1)} %get-tuple-element.70.count_ref, bf16[256,384]{1,0:T(8,128)(2,1)S(1)} %collective-permute-done.9.qg_ref.refs_0_, bf16[384,384]{1,0:T(8,128)(2,1)S(1)} %get-tuple-element.73.refs_0_.refs_2_, ...), custom_call_target="tpu_custom_call" | custom-call | flops 150994944 | bytes 345856 | tf_op jit(solution)/shard_map/pallas_call | solution.py:311
  43.3 1.6 %collective-permute-start.10 = (f32[4,6,256]{2,1,0:T(8,128)S(1)}, f32[4,6,256]{2,1,0:T(8,128)S(1)}, u32[]{:S(2)}, u32[]{:S(2)}) collective-permute-start(f32[4,6,256]{2,1,0:T(8,128)S(1)} %pad_maximum_fusion.4), channel_id=1, source_target_pairs={{0,4},{1,5},{2,6},{3,7},{4,0},{5,1},{6,2},{7,3},{8,12},{9,13},{10,... | collective-permute-start | bytes 73736 | tf_op jit(solution)/shard_map/ppermute | solution.py:336
  44.9 2.4 %collective-permute-done.10 = f32[4,6,256]{2,1,0:T(8,128)S(1)} collective-permute-done((f32[4,6,256]{2,1,0:T(8,128)S(1)}, f32[4,6,256]{2,1,0:T(8,128)S(1)}, u32[]{:S(2)}, u32[]{:S(2)}) %collective-permute-start.10) | collective-permute-done | bytes 24608 | tf_op jit(solution)/shard_map/ppermute | solution.py:336
  47.4 2.6 %collective-permute-start.11 = (f32[4,6,256]{2,1,0:T(8,128)S(1)}, f32[4,6,256]{2,1,0:T(8,128)S(1)}, u32[]{:S(2)}, u32[]{:S(2)}) collective-permute-start(f32[4,6,256]{2,1,0:T(8,128)S(1)} %pad_maximum_fusion.6), channel_id=1, source_target_pairs={{0,8},{1,9},{2,10},{3,11},{4,12},{5,13},{6,14},{7,15},{8,0},{9,1},... | collective-permute-start | bytes 73736 | tf_op jit(solution)/shard_map/ppermute | solution.py:336
  50.0 2.3 %collective-permute-done.11 = f32[4,6,256]{2,1,0:T(8,128)S(1)} collective-permute-done((f32[4,6,256]{2,1,0:T(8,128)S(1)}, f32[4,6,256]{2,1,0:T(8,128)S(1)}, u32[]{:S(2)}, u32[]{:S(2)}) %collective-permute-start.11) | collective-permute-done | bytes 24608 | tf_op jit(solution)/shard_map/ppermute | solution.py:336
  52.4 2.7 %collective-permute-start.12 = (bf16[2,192,256]{2,1,0:T(8,128)(2,1)S(1)}, bf16[2,192,256]{2,1,0:T(8,128)(2,1)S(1)}, u32[]{:S(2)}, u32[]{:S(2)}) collective-permute-start(bf16[2,192,256]{2,1,0:T(8,128)(2,1)S(1)} %pad_maximum_fusion.1), channel_id=1, source_target_pairs={{0,8},{1,9},{2,10},{3,11},{4,12},{5,13},{6,14},{7,15},{8,0},{9,1},... | collective-permute-start | bytes 589832 | tf_op jit(solution)/shard_map/ppermute | solution.py:336
  55.1 6.4 %shard_map.115 = (f32[4,192,256]{2,1,0:T(8,128)S(1)}, bf16[2,384,384]{2,1,0:T(8,128)(2,1)S(1)}) custom-call(f32[4,128]{1,0:T(4,128)S(1)} %get-tuple-element.70.count_ref, bf16[256,384]{1,0:T(8,128)(2,1)S(1)} %collective-permute-done.9.qg_ref.refs_0_, bf16[256,384]{1,0:T(8,128)(2,1)S(1)} %collective-permute-done.7.qg_ref.refs_1_.refs_0_, ...), custom_call_target="tpu_custom_call" | custom-call | flops 528482304 | bytes 421120 | tf_op jit(solution)/shard_map/pallas_call | solution.py:311
  63.1 1.7 %shard_map.116 = (bf16[1,192,256]{2,1,0:T(8,128)(2,1)S(1)}, f32[2,384,384]{2,1,0:T(8,128)S(1)}) custom-call(f32[4,128]{1,0:T(4,128)S(1)} %get-tuple-element.70.count_ref, bf16[256,384]{1,0:T(8,128)(2,1)S(1)} %collective-permute-done.9.qg_ref.refs_0_, f32[6,256]{1,0:T(8,128)S(1)} %get-tuple-element.130.refs_4_.refs_1_, ...), custom_call_target="tpu_custom_call" | custom-call | flops 132120576 | bytes 431104 | tf_op jit(solution)/shard_map/pallas_call | solution.py:311
  67.0 1.7 %shard_map.117 = (f32[1,192,256]{2,1,0:T(8,128)S(1)}, f32[2,384,384]{2,1,0:T(8,128)S(1)}) custom-call(f32[4,128]{1,0:T(4,128)S(1)} %get-tuple-element.70.count_ref, bf16[256,384]{1,0:T(8,128)(2,1)S(1)} %collective-permute-done.7.qg_ref.refs_1_.refs_0_, f32[6,256]{1,0:T(8,128)S(1)} %get-tuple-element.131.refs_5_.refs_1_, ...), custom_call_target="tpu_custom_call" | custom-call | flops 132120576 | bytes 590848 | tf_op jit(solution)/shard_map/pallas_call | solution.py:311
  68.7 1.9 %collective-permute-done.15 = bf16[192,256]{1,0:T(8,128)(2,1)S(1)} collective-permute-done((bf16[192,256]{1,0:T(8,128)(2,1)S(1)}, bf16[192,256]{1,0:T(8,128)(2,1)S(1)}, u32[]{:S(2)}, u32[]{:S(2)}) %collective-permute-start.15) | collective-permute-done | bytes 98336 | tf_op jit(solution)/shard_map/ppermute | solution.py:336
  70.7 1.7 %shard_map.118 = (bf16[1,192,256]{2,1,0:T(8,128)(2,1)S(1)}, f32[2,384,384]{2,1,0:T(8,128)S(1)}) custom-call(f32[4,128]{1,0:T(4,128)S(1)} %get-tuple-element.70.count_ref, bf16[256,384]{1,0:T(8,128)(2,1)S(1)} %collective-permute-done.5.qg_ref.refs_2_.refs_0_, f32[6,256]{1,0:T(8,128)S(1)} %get-tuple-element.132.refs_6_.refs_1_, ...), custom_call_target="tpu_custom_call" | custom-call | flops 132120576 | bytes 578560 | tf_op jit(solution)/shard_map/pallas_call | solution.py:311
  73.5 3.7 %collective-permute-done.16 = bf16[192,256]{1,0:T(8,128)(2,1)S(1)} collective-permute-done((bf16[192,256]{1,0:T(8,128)(2,1)S(1)}, bf16[192,256]{1,0:T(8,128)(2,1)S(1)}, u32[]{:S(2)}, u32[]{:S(2)}) %collective-permute-start.16) | collective-permute-done | bytes 98336 | tf_op jit(solution)/shard_map/ppermute | solution.py:336
  77.2 1.7 %shard_map.119 = (f32[1,192,256]{2,1,0:T(8,128)S(1)}, bf16[2,384,384]{2,1,0:T(8,128)(2,1)S(1)}) custom-call(f32[4,128]{1,0:T(4,128)S(1)} %get-tuple-element.70.count_ref, bf16[256,384]{1,0:T(8,128)(2,1)S(1)} %get-tuple-element.72.qg_ref.refs_3_.refs_0_, f32[6,256]{1,0:T(8,128)S(1)} %get-tuple-element.129.refs_7_.refs_1_, ...), custom_call_target="tpu_custom_call" | custom-call | flops 132120576 | bytes 517120 | tf_op jit(solution)/shard_map/pallas_call | solution.py:311
  79.5 1.7 %collective-permute-done.19.core_ref = bf16[2,384,384]{2,1,0:T(8,128)(2,1)S(1)} collective-permute-done((bf16[2,384,384]{2,1,0:T(8,128)(2,1)S(1)}, bf16[2,384,384]{2,1,0:T(8,128)(2,1)S(1)}, u32[]{:S(2)}, u32[]{:S(2)}) %collective-permute-start.19) | collective-permute-done | bytes 589856 | tf_op jit(solution)/shard_map/ppermute | solution.py:336
  81.2 2.2 %shard_map.120 = bf16[384,768]{1,0:T(8,128)(2,1)} custom-call(s32[1]{0:T(128)} %bitcast.place_ref, bf16[2,384,384]{2,1,0:T(8,128)(2,1)S(1)} %get-tuple-element.116.near_ref, bf16[2,384,384]{2,1,0:T(8,128)(2,1)S(1)} %collective-permute-done.14.far_ref, bf16[2,384,384]{2,1,0:T(8,128)(2,1)S(1)} %collective-permute-done.19.core_ref, ...), custom_call_target="tpu_custom_call" | custom-call | flops 113246208 | bytes 589824 | tf_op jit(solution)/shard_map/pallas_call | solution.py:311
  (81 shorter events, 21.2 us)
Async XLA Ops:
  1.3 6.5 %copy-start.2 = (bf16[768,768]{1,0:T(8,128)(2,1)S(1)}, bf16[768,768]{1,0:T(8,128)(2,1)}, u32[]{:S(2)}) copy-start(bf16[768,768]{1,0:T(8,128)(2,1)} %w_key_ref.2) | copy-start | bytes 3538948
  4.8 6.5 %collective-permute-start.1 = (bf16[2,80,384]{2,1,0:T(8,128)(2,1)}, bf16[2,80,384]{2,1,0:T(8,128)(2,1)S(1)}, u32[]{:S(2)}, u32[]{:S(2)}) collective-permute-start(bf16[2,80,384]{2,1,0:T(8,128)(2,1)} %get-tuple-element.66), channel_id=1, source_target_pairs={{0,2},{1,3},{2,0},{3,1},{4,6},{5,7},{6,4},{7,5},{8,10},{9,11},{10,... | collective-permute-start | bytes 368648 | tf_op jit(solution)/shard_map/ppermute | solution.py:336
  10.4 4.8 %collective-permute-start.3 = (bf16[384,384]{1,0:T(8,128)(2,1)S(1)}, bf16[384,384]{1,0:T(8,128)(2,1)S(1)}, u32[]{:S(2)}, u32[]{:S(2)}) collective-permute-start(bf16[384,384]{1,0:T(8,128)(2,1)S(1)} %get-tuple-element.74), channel_id=1, source_target_pairs={{0,1},{1,0},{2,3},{3,2},{4,5},{5,4},{6,7},{7,6},{8,9},{9,8},{10,11... | collective-permute-start | bytes 884744 | tf_op jit(solution)/shard_map/ppermute | solution.py:336
  11.3 9.9 %collective-permute-start.4 = (bf16[384,384]{1,0:T(8,128)(2,1)S(1)}, bf16[384,384]{1,0:T(8,128)(2,1)S(1)}, u32[]{:S(2)}, u32[]{:S(2)}) collective-permute-start(bf16[384,384]{1,0:T(8,128)(2,1)S(1)} %get-tuple-element.77), channel_id=1, source_target_pairs={{0,2},{1,3},{2,0},{3,1},{4,6},{5,7},{6,4},{7,5},{8,10},{9,11},{10,... | collective-permute-start | bytes 884744 | tf_op jit(solution)/shard_map/ppermute | solution.py:336
  13.1 1.4 %collective-permute-start.2 = (bf16[2,80,384]{2,1,0:T(8,128)(2,1)S(1)}, bf16[2,80,384]{2,1,0:T(8,128)(2,1)S(1)}, u32[]{:S(2)}, u32[]{:S(2)}) collective-permute-start(bf16[2,80,384]{2,1,0:T(8,128)(2,1)S(1)} %collective-permute-done.1.far_ref), channel_id=1, source_target_pairs={{0,1},{1,0},{2,3},{3,2},{4,5},{5,4},{6,7},{7,6},{8,9},{9,8},{10,11... | collective-permute-start | bytes 368648 | tf_op jit(solution)/shard_map/ppermute | solution.py:336
  13.1 1.4 %collective-permute-start = (bf16[80,384]{1,0:T(8,128)(2,1)S(1)}, bf16[80,384]{1,0:T(8,128)(2,1)S(1)}, u32[]{:S(2)}, u32[]{:S(2)}) collective-permute-start(bf16[80,384]{1,0:T(8,128)(2,1)S(1)} %copy-done.8), channel_id=1, source_target_pairs={{0,1},{1,0},{2,3},{3,2},{4,5},{5,4},{6,7},{7,6},{8,9},{9,8},{10,11... | collective-permute-start | bytes 184328 | tf_op jit(solution)/shard_map/ppermute | solution.py:336
  13.6 20.4 %collective-permute-start.6 = (bf16[384,384]{1,0:T(8,128)(2,1)S(1)}, bf16[384,384]{1,0:T(8,128)(2,1)S(1)}, u32[]{:S(2)}, u32[]{:S(2)}) collective-permute-start(bf16[384,384]{1,0:T(8,128)(2,1)S(1)} %get-tuple-element.83), channel_id=1, source_target_pairs={{0,2},{1,3},{2,0},{3,1},{4,6},{5,7},{6,4},{7,5},{8,10},{9,11},{10,... | collective-permute-start | bytes 884744 | tf_op jit(solution)/shard_map/ppermute | solution.py:336
  21.2 14.5 %collective-permute-start.8 = (bf16[384,384]{1,0:T(8,128)(2,1)S(1)}, bf16[384,384]{1,0:T(8,128)(2,1)S(1)}, u32[]{:S(2)}, u32[]{:S(2)}) collective-permute-start(bf16[384,384]{1,0:T(8,128)(2,1)S(1)} %collective-permute-done.4), channel_id=1, source_target_pairs={{0,1},{1,0},{2,3},{3,2},{4,5},{5,4},{6,7},{7,6},{8,9},{9,8},{10,11... | collective-permute-start | bytes 884744 | tf_op jit(solution)/shard_map/ppermute | solution.py:336
  21.2 11.5 %collective-permute-start.5 = (bf16[256,384]{1,0:T(8,128)(2,1)S(1)}, bf16[256,384]{1,0:T(8,128)(2,1)S(1)}, u32[]{:S(2)}, u32[]{:S(2)}) collective-permute-start(bf16[256,384]{1,0:T(8,128)(2,1)S(1)} %get-tuple-element.72.qg_ref.refs_3_.refs_0_), channel_id=1, source_target_pairs={{0,4},{1,5},{2,6},{3,7},{4,0},{5,1},{6,2},{7,3},{8,12},{9,13},{10,... | collective-permute-start | bytes 589832 | tf_op jit(solution)/shard_map/ppermute | solution.py:336
  23.1 12.2 %collective-permute-start.7 = (bf16[256,384]{1,0:T(8,128)(2,1)S(1)}, bf16[256,384]{1,0:T(8,128)(2,1)S(1)}, u32[]{:S(2)}, u32[]{:S(2)}) collective-permute-start(bf16[256,384]{1,0:T(8,128)(2,1)S(1)} %get-tuple-element.72.qg_ref.refs_3_.refs_0_), channel_id=1, source_target_pairs={{0,8},{1,9},{2,10},{3,11},{4,12},{5,13},{6,14},{7,15},{8,0},{9,1},... | collective-permute-start | bytes 589832 | tf_op jit(solution)/shard_map/ppermute | solution.py:336
  35.3 5.7 %collective-permute-start.9 = (bf16[256,384]{1,0:T(8,128)(2,1)S(1)}, bf16[256,384]{1,0:T(8,128)(2,1)S(1)}, u32[]{:S(2)}, u32[]{:S(2)}) collective-permute-start(bf16[256,384]{1,0:T(8,128)(2,1)S(1)} %collective-permute-done.7.qg_ref.refs_1_.refs_0_), channel_id=1, source_target_pairs={{0,4},{1,5},{2,6},{3,7},{4,0},{5,1},{6,2},{7,3},{8,12},{9,13},{10,... | collective-permute-start | bytes 589832 | tf_op jit(solution)/shard_map/ppermute | solution.py:336
  43.3 4.0 %collective-permute-start.10 = (f32[4,6,256]{2,1,0:T(8,128)S(1)}, f32[4,6,256]{2,1,0:T(8,128)S(1)}, u32[]{:S(2)}, u32[]{:S(2)}) collective-permute-start(f32[4,6,256]{2,1,0:T(8,128)S(1)} %pad_maximum_fusion.4), channel_id=1, source_target_pairs={{0,4},{1,5},{2,6},{3,7},{4,0},{5,1},{6,2},{7,3},{8,12},{9,13},{10,... | collective-permute-start | bytes 73736 | tf_op jit(solution)/shard_map/ppermute | solution.py:336
  47.4 4.9 %collective-permute-start.11 = (f32[4,6,256]{2,1,0:T(8,128)S(1)}, f32[4,6,256]{2,1,0:T(8,128)S(1)}, u32[]{:S(2)}, u32[]{:S(2)}) collective-permute-start(f32[4,6,256]{2,1,0:T(8,128)S(1)} %pad_maximum_fusion.6), channel_id=1, source_target_pairs={{0,8},{1,9},{2,10},{3,11},{4,12},{5,13},{6,14},{7,15},{8,0},{9,1},... | collective-permute-start | bytes 73736 | tf_op jit(solution)/shard_map/ppermute | solution.py:336
  52.4 10.7 %collective-permute-start.12 = (bf16[2,192,256]{2,1,0:T(8,128)(2,1)S(1)}, bf16[2,192,256]{2,1,0:T(8,128)(2,1)S(1)}, u32[]{:S(2)}, u32[]{:S(2)}) collective-permute-start(bf16[2,192,256]{2,1,0:T(8,128)(2,1)S(1)} %pad_maximum_fusion.1), channel_id=1, source_target_pairs={{0,8},{1,9},{2,10},{3,11},{4,12},{5,13},{6,14},{7,15},{8,0},{9,1},... | collective-permute-start | bytes 589832 | tf_op jit(solution)/shard_map/ppermute | solution.py:336
  61.5 15.6 %collective-permute-start.14 = (bf16[2,384,384]{2,1,0:T(8,128)(2,1)S(1)}, bf16[2,384,384]{2,1,0:T(8,128)(2,1)S(1)}, u32[]{:S(2)}, u32[]{:S(2)}) collective-permute-start(bf16[2,384,384]{2,1,0:T(8,128)(2,1)S(1)} %get-tuple-element.101), channel_id=1, source_target_pairs={{0,2},{1,3},{2,0},{3,1},{4,6},{5,7},{6,4},{7,5},{8,10},{9,11},{10,... | collective-permute-start | bytes 1769480 | tf_op jit(solution)/shard_map/ppermute | solution.py:336
  64.8 5.8 %collective-permute-start.15 = (bf16[192,256]{1,0:T(8,128)(2,1)S(1)}, bf16[192,256]{1,0:T(8,128)(2,1)S(1)}, u32[]{:S(2)}, u32[]{:S(2)}) collective-permute-start(bf16[192,256]{1,0:T(8,128)(2,1)S(1)} %bitcast.89), channel_id=1, source_target_pairs={{0,4},{1,5},{2,6},{3,7},{4,0},{5,1},{6,2},{7,3},{8,12},{9,13},{10,... | collective-permute-start | bytes 294920 | tf_op jit(solution)/shard_map/ppermute | solution.py:336
  66.0 7.5 %collective-permute-start.13 = (bf16[192,256]{1,0:T(8,128)(2,1)S(1)}, bf16[192,256]{1,0:T(8,128)(2,1)S(1)}, u32[]{:S(2)}, u32[]{:S(2)}) collective-permute-start(bf16[192,256]{1,0:T(8,128)(2,1)S(1)} %fusion.1), channel_id=1, source_target_pairs={{0,4},{1,5},{2,6},{3,7},{4,0},{5,1},{6,2},{7,3},{8,12},{9,13},{10,... | collective-permute-start | bytes 294920 | tf_op jit(solution)/shard_map/ppermute | solution.py:336
  70.6 6.5 %collective-permute-start.16 = (bf16[192,256]{1,0:T(8,128)(2,1)S(1)}, bf16[192,256]{1,0:T(8,128)(2,1)S(1)}, u32[]{:S(2)}, u32[]{:S(2)}) collective-permute-start(bf16[192,256]{1,0:T(8,128)(2,1)S(1)} %fusion.4), channel_id=1, source_target_pairs={{0,8},{1,9},{2,10},{3,11},{4,12},{5,13},{6,14},{7,15},{8,0},{9,1},... | collective-permute-start | bytes 294920 | tf_op jit(solution)/shard_map/ppermute | solution.py:336
  72.4 6.5 %collective-permute-start.17 = (bf16[192,256]{1,0:T(8,128)(2,1)S(1)}, bf16[192,256]{1,0:T(8,128)(2,1)S(1)}, u32[]{:S(2)}, u32[]{:S(2)}) collective-permute-start(bf16[192,256]{1,0:T(8,128)(2,1)S(1)} %bitcast.88), channel_id=1, source_target_pairs={{0,4},{1,5},{2,6},{3,7},{4,0},{5,1},{6,2},{7,3},{8,12},{9,13},{10,... | collective-permute-start | bytes 294920 | tf_op jit(solution)/shard_map/ppermute | solution.py:336
  79.1 2.1 %collective-permute-start.19 = (bf16[2,384,384]{2,1,0:T(8,128)(2,1)S(1)}, bf16[2,384,384]{2,1,0:T(8,128)(2,1)S(1)}, u32[]{:S(2)}, u32[]{:S(2)}) collective-permute-start(bf16[2,384,384]{2,1,0:T(8,128)(2,1)S(1)} %pad_maximum_fusion), channel_id=1, source_target_pairs={{0,1},{1,0},{2,3},{3,2},{4,5},{5,4},{6,7},{7,6},{8,9},{9,8},{10,11... | collective-permute-start | bytes 1769480 | tf_op jit(solution)/shard_map/ppermute | solution.py:336
  79.3 5.3 %collective-permute-start.18 = (bf16[2,192,128]{2,1,0:T(8,128)(2,1)S(1)}, bf16[2,192,128]{2,1,0:T(8,128)(2,1)S(1)}, u32[]{:S(2)}, u32[]{:S(2)}) collective-permute-start(bf16[2,192,128]{2,1,0:T(8,128)(2,1)S(1)} %get-tuple-element.123), channel_id=1, source_target_pairs={{0,2},{1,3},{2,0},{3,1},{4,6},{5,7},{6,4},{7,5},{8,10},{9,11},{10,... | collective-permute-start | bytes 294920 | tf_op jit(solution)/shard_map/ppermute | solution.py:336
  79.4 6.7 %copy-start.5 = (bf16[64,768]{1,0:T(8,128)(2,1)S(1)}, bf16[64,768]{1,0:T(8,128)(2,1)}, u32[]{:S(2)}) copy-start(bf16[64,768]{1,0:T(8,128)(2,1)} %latents_ref.1) | copy-start | bytes 294916
  79.5 6.7 %copy-start.6 = (bf16[64,768]{1,0:T(8,128)(2,1)S(1)}, bf16[64,768]{1,0:T(8,128)(2,1)}, u32[]{:S(2)}) copy-start(bf16[64,768]{1,0:T(8,128)(2,1)} %d_out_ref.1) | copy-start | bytes 294916
  84.7 1.5 %collective-permute-start.20 = (bf16[2,2,192,64]{3,2,1,0:T(8,128)(2,1)S(1)}, bf16[2,2,192,64]{3,2,1,0:T(8,128)(2,1)S(1)}, u32[]{:S(2)}, u32[]{:S(2)}) collective-permute-start(bf16[2,2,192,64]{3,2,1,0:T(8,128)(2,1)S(1)} %pad_maximum_fusion.3), channel_id=1, source_target_pairs={{0,1},{1,0},{2,3},{3,2},{4,5},{5,4},{6,7},{7,6},{8,9},{9,8},{10,11... | collective-permute-start | bytes 294920 | tf_op jit(solution)/shard_map/ppermute | solution.py:336
  (6 other events, 27.4 us)
